TPU v7x, 128 devices: a whole 4x4x4 slice. The times are simulated.
128 devices in a mesh: tx: 32 (over y, x, core), ty: 4 (over z).
Axes of the slice: x: 4, y: 4, z: 4, core: 2. Of those that a mesh axis runs over, the one named last changes fastest.
Arguments:
- points: bfloat16 [524288, 128], P(('tx', 'ty')), may hold values from -6 to 6
- embed_weight: bfloat16 [128, 512], replicated, may hold values from -0.5 to 0.5
- inner_weights: bfloat16 [1, 512, 512], replicated, may hold values from -0.25 to 0.25
- output_weight: bfloat16 [512, 128], replicated, may hold values from -0.25 to 0.25
- counts: int32 [128, 512], replicated, may hold values from 1 to 16, as said below
- point_order: int32 [128, 4096], P(('tx', 'ty')), may hold values from 0 to 4095, each once within a row
- inducing: bfloat16 [128, 128], replicated, may hold values from -6 to 6
- first_proj: bfloat16 [4, 128, 128], replicated, may hold values from -0.5 to 0.5
- second_proj: bfloat16 [4, 128, 128], replicated, may hold values from -0.5 to 0.5
- mixing: bfloat16 [8, 128, 128], replicated, may hold values from -0.1875 to 0.1875
Outputs:
- encoded: bfloat16 [524288, 128], P(('tx', 'ty'))
Inputs may be any that keep to these rules, and one draw needn't show every extreme that they name: Row s sums to 4096. For every source s and every device, the counts of s in the 4 tiles that device holds sum to exactly 32, and one of those 4 entries equals 16. Row s is a permutation of the local points of source s: the points of tile g are point_order[s, offsets[s, g] + c] for c below counts[s, g].
All inputs are finite; a program needn't handle non-finite values.
Results may differ from a plain program's by a relative error of at most 0.025.
Values may be sent and summed in bfloat16 or wider, within the bound.
A program may use at most 64 MiB of HBM per device.

v0:
```python
import math

import jax
import jax.numpy as jnp
from jax import lax
from jax.sharding import PartitionSpec as P

HEADS = 2
TLX = 2
TLY = 2


sharpness = 32.0
epsilon = 1e-06
neighbour_steps = ((-1, -1), (-1, 0), (-1, 1), (0, -1), (0, 1), (1, -1), (1, 0), (1, 1))


def padded_2(block, sides, width):
    for axis, dim in sides:
        count = lax.axis_size(axis)
        forward = [(i, i + 1) for i in range(count - 1)]
        backward = [(target, source) for source, target in forward]
        low = lax.ppermute(
            lax.slice_in_dim(block, block.shape[dim] - width, None, axis=dim), axis, forward
        )
        high = lax.ppermute(lax.slice_in_dim(block, 0, width, axis=dim), axis, backward)
        block = jnp.concatenate([low, block, high], axis=dim)
    return block


def unit_heads(projected, head_count):
    pieces = projected.reshape(
        projected.shape[:-1] + (head_count, projected.shape[-1] // head_count)
    )
    magnitude = jnp.sqrt(jnp.sum(pieces * pieces, axis=-1, keepdims=True) + epsilon)
    return (pieces / magnitude).reshape(projected.shape).astype(jnp.bfloat16)


def attend(query_rows, key_rows, value_rows, weight_mask):
    head_width = query_rows.shape[-1] // HEADS
    outputs = []
    for head_id in range(HEADS):
        lower = head_id * head_width
        upper = lower + head_width
        scores = jnp.dot(
            query_rows[:, lower:upper],
            key_rows[:, lower:upper].T,
            preferred_element_type=jnp.float32,
        )
        weights = jnp.exp(sharpness * scores) * weight_mask[None, :]
        totals = jnp.sum(weights, axis=1, keepdims=True)
        numer = jnp.dot(
            weights.astype(jnp.bfloat16),
            value_rows[:, lower:upper],
            preferred_element_type=jnp.float32,
        )
        outputs.append(numer / totals)
    return jnp.concatenate(outputs, axis=1).astype(jnp.bfloat16)


def block_layout(tallies, quota):
    before = jnp.cumsum(tallies, axis=0) - tallies
    through = (before + tallies).T
    slot_ids = jnp.arange(quota, dtype=jnp.int32)
    which = jnp.sum((slot_ids[None, :, None] >= through[:, None, :]).astype(jnp.int32), axis=2)
    base = jnp.take_along_axis(before.T, which, axis=1)
    return (before, which, slot_ids[None, :] - base)


def local_rows(index, source_rows, block):
    column_ids = jnp.arange(source_rows.shape[0], dtype=jnp.int32)

    def pick_block(index_block):
        table = (index_block[:, None] == column_ids[None, :]).astype(jnp.bfloat16)
        return jnp.dot(table, source_rows, preferred_element_type=jnp.float32).astype(jnp.bfloat16)

    picked = lax.map(pick_block, index.reshape(-1, block))
    return picked.reshape(index.shape[0], source_rows.shape[1])


def place_rows(index, rows, total, block):
    target_ids = jnp.arange(total, dtype=jnp.int32).reshape(-1, block)

    def place_block(target_block):
        table = (target_block[:, None] == index[None, :]).astype(jnp.bfloat16)
        return jnp.dot(table, rows, preferred_element_type=jnp.float32).astype(jnp.bfloat16)

    placed = lax.map(place_block, target_ids)
    return placed.reshape(total, rows.shape[1])


def slot_table(tallies, before, capacity, quota):
    slot_ids = jnp.arange(capacity, dtype=jnp.int32)
    packed_ids = jnp.arange(quota, dtype=jnp.int32)
    starts = before.T
    live = slot_ids[None, None, :] < tallies.T[:, :, None]
    hits = (
        packed_ids[None, None, None, :] == starts[:, :, None, None] + slot_ids[None, None, :, None]
    )
    return (hits & live[..., None]).astype(jnp.bfloat16)


def expand(blocks, table):
    return jnp.einsum("otcq,oqe->toce", table, blocks, preferred_element_type=jnp.float32).astype(
        jnp.bfloat16
    )


def collapse(slots, table):
    return jnp.einsum("otcq,toce->oqe", table, slots, preferred_element_type=jnp.float32).astype(
        jnp.bfloat16
    )


def body(
    points,
    embed_weight,
    inner_weights,
    output_weight,
    counts,
    point_order,
    inducing,
    first_proj,
    second_proj,
    mixing,
):
    along_x = lax.axis_size("tx")
    along_y = lax.axis_size("ty")
    devices = along_x * along_y
    index_x = lax.axis_index("tx")
    index_y = lax.axis_index("ty")
    own_index = index_x * along_y + index_y
    point_count = points.shape[0]
    capacity = 2 * point_count // counts.shape[1]
    per_device = TLX * TLY
    width = output_weight.shape[1]
    tile_rows = devices * capacity
    quota = point_count // devices
    block = math.gcd(512, point_count)
    hidden = jax.nn.silu(jnp.dot(points, embed_weight, preferred_element_type=jnp.float32)).astype(
        jnp.bfloat16
    )
    hidden = jax.nn.silu(
        jnp.dot(hidden, inner_weights[0], preferred_element_type=jnp.float32)
    ).astype(jnp.bfloat16)
    features = jnp.dot(hidden, output_weight, preferred_element_type=jnp.float32).astype(
        jnp.bfloat16
    )
    own_counts = lax.dynamic_index_in_dim(counts, own_index, 0, keepdims=False)
    own_offsets = jnp.cumsum(own_counts) - own_counts

    def by_owner(table):
        return (
            table.reshape(along_x, TLX, along_y, TLY)
            .transpose(1, 3, 0, 2)
            .reshape(per_device, devices)
        )

    slot_ids = jnp.arange(capacity, dtype=jnp.int32)
    send_counts = by_owner(own_counts)
    send_starts = by_owner(own_offsets)
    inbound = counts.reshape(devices, along_x, TLX, along_y, TLY)
    inbound = lax.dynamic_index_in_dim(inbound, index_x, 1, keepdims=False)
    inbound = lax.dynamic_index_in_dim(inbound, index_y, 2, keepdims=False)
    inbound = inbound.transpose(1, 2, 0).reshape(per_device, devices)
    live_slots = slot_ids[None, None, :] < inbound[:, :, None]
    key_mask = live_slots.astype(jnp.float32).reshape(per_device, tile_rows)
    send_before, send_which, send_within = block_layout(send_counts, quota)
    packed_pos = jnp.take_along_axis(send_starts.T, send_which, axis=1) + send_within
    packed_index = point_order[0][packed_pos].reshape(-1)
    packed = local_rows(packed_index, features, block).reshape(devices, quota, width)
    send_table = slot_table(send_counts, send_before, capacity, quota)
    outgoing = expand(packed, send_table)
    arrived = lax.all_to_all(outgoing, ("tx", "ty"), split_axis=1, concat_axis=1, tiled=True)
    arrived = arrived.reshape(per_device, tile_rows, width)
    all_rows = arrived.reshape(per_device * tile_rows, width)
    first_keys = unit_heads(
        jnp.dot(all_rows, first_proj[1], preferred_element_type=jnp.float32), HEADS
    ).reshape(per_device, tile_rows, width)
    first_values = (
        jnp.dot(all_rows, first_proj[2], preferred_element_type=jnp.float32)
        .astype(jnp.bfloat16)
        .reshape(per_device, tile_rows, width)
    )
    inducing_queries = unit_heads(
        jnp.dot(inducing, first_proj[0], preferred_element_type=jnp.float32), HEADS
    )
    first_attended = jax.vmap(attend, in_axes=(None, 0, 0, 0))(
        inducing_queries, first_keys, first_values, key_mask
    )
    summary = (
        inducing.astype(jnp.float32)[None]
        + jnp.einsum(
            "tic,ce->tie", first_attended, first_proj[3], preferred_element_type=jnp.float32
        )
    ).astype(jnp.bfloat16)
    tile_grid = summary.reshape(TLX, TLY, summary.shape[1], width)
    padded = padded_2(tile_grid, (("tx", 0), ("ty", 1)), 1)
    stacked = jnp.stack(
        [
            padded[1 + steps[0] : 1 + steps[0] + TLX, 1 + steps[1] : 1 + steps[1] + TLY]
            for steps in neighbour_steps
        ]
    )
    mixture = tile_grid.astype(jnp.float32) + jnp.einsum(
        "dxyic,dce->xyie", stacked, mixing, preferred_element_type=jnp.float32
    )
    mixture = mixture.astype(jnp.bfloat16).reshape(per_device * summary.shape[1], width)
    point_queries = unit_heads(
        jnp.dot(all_rows, second_proj[0], preferred_element_type=jnp.float32), HEADS
    ).reshape(per_device, tile_rows, width)
    second_keys = unit_heads(
        jnp.dot(mixture, second_proj[1], preferred_element_type=jnp.float32), HEADS
    ).reshape(per_device, -1, width)
    second_values = (
        jnp.dot(mixture, second_proj[2], preferred_element_type=jnp.float32)
        .astype(jnp.bfloat16)
        .reshape(per_device, -1, width)
    )
    every_key = jnp.ones((second_keys.shape[1],), jnp.float32)
    second_attended = jax.vmap(attend, in_axes=(0, 0, 0, None))(
        point_queries, second_keys, second_values, every_key
    )
    result = (
        arrived.astype(jnp.float32)
        + jnp.einsum(
            "trc,ce->tre", second_attended, second_proj[3], preferred_element_type=jnp.float32
        )
    ).astype(jnp.bfloat16)
    result_slots = result.reshape(per_device, devices, capacity, width)
    coming = lax.all_to_all(result_slots, ("tx", "ty"), split_axis=1, concat_axis=1, tiled=True)
    returned = collapse(coming, send_table)
    return place_rows(packed_index, returned.reshape(point_count, width), point_count, block)


def solution(mesh):
    placed = (P(("tx", "ty"), None), P(), P(), P(), P(), P(("tx", "ty"), None), P(), P(), P(), P())
    return jax.shard_map(
        body, mesh=mesh, in_specs=placed, out_specs=P(("tx", "ty"), None), check_vma=False
    )
```

profile of v0, /device:TPU:1, one launch (start us, length us, event | category | flops | bytes accessed | tf_op | source)
XLA Modules:
  0.0 279.4 jit_solution(15943603343116851955)
XLA Ops:
  0.0 0.5 broadcast.183
  0.5 1.4 fusion.117
  3.1 0.5 copy.58
  3.8 0.5 copy.55
  5.2 26.7 %gather_fusion.2 = s32[4096]{0:T(1024)S(1)} fusion(s32[128,4]{1,0:T(8,128)S(1)} %subtract_bitcast_fusion.1, s32[4096]{0:T(1024)S(1)} %reshape.218), kind=kCustom, calls=%fused_computation.1.clone | custom fusion | bytes 65536 | tf_op jit(solution)/shard_map/jit(take_along_axis)/gather | solution.py:66
  31.9 33.1 %gather_fusion.1 = s32[4096]{0:T(1024)S(1)} fusion(s32[128,4]{0,1:T(4,128)S(1)} %bitcast.236, s32[4096]{0:T(1024)S(1)} %reshape.218), kind=kCustom, calls=%fused_computation.clone | custom fusion | bytes 65536 | tf_op jit(solution)/shard_map/jit(take_along_axis)/gather | solution.py:169
  65.8 23.0 %gather_fusion = s32[4096]{0:T(1024)S(1)} fusion(s32[4096]{0:T(1024)S(1)} %bitcast.237, s32[4096]{0:T(1024)S(1)} %broadcast_clamp_fusion), kind=kCustom, calls=%fused_computation.2 | custom fusion | bytes 49152 | tf_op jit(solution)/shard_map/gather | solution.py:170
  88.9 6.4 %fusion.21 = f32[4096,512]{1,0:T(8,128)} fusion(bf16[4096,128]{1,0:T(8,128)(2,1)S(1)} %copy-done, bf16[128,512]{1,0:T(8,128)(2,1)S(1)} %copy-done.18, bf16[1,512,512]{2,1,0:T(8,128)(2,1)S(1)} %copy-done.17), kind=kOutput, calls=%fused_computation.38 | convolution fusion | flops 2694840320 | bytes 10092544 | tf_op jit(solution)/shard_map/dot_general | solution.py:144
  95.3 5.7 %convolution_convert_fusion.1 = bf16[4096,128]{1,0:T(8,128)(2,1)S(1)} fusion(bf16[512,128]{1,0:T(8,128)(2,1)S(1)} %copy-done.19, f32[4096,512]{1,0:T(8,128)} %fusion.21), kind=kOutput, calls=%fused_computation.22 | convolution fusion | flops 547880960 | bytes 9568256 | tf_op jit(solution)/shard_map/dot_general | solution.py:146
  101.1 12.9 %while.22 = (s32[]{:T(128)}, bf16[8,512,128]{2,1,0:T(8,128)(2,1)S(1)}, s32[8,512]{1,0:T(8,128)S(1)}, bf16[4096,128]{1,0:T(8,128)(2,1)S(1)}, s32[]{:T(128)}) while((s32[]{:T(128)}, bf16[8,512,128]{2,1,0:T(8,128)(2,1)S(1)}, s32[8,512]{1,0:T(8,128)S(1)}, bf16[4096,128]{1,0:T(8,128)(2,1)S(1)}, s32[]{:T(128)}) %tuple.56), condition=%wide.region_5.7_spmd.clone, body=%wide.region_4.6_spmd.clone.sunk | while | flops 539033600 | bytes 1185861 | solution.py:77
  101.1 1.6 fusion.148
  102.8 1.6 fusion.148
  104.4 1.6 fusion.148
  106.0 1.6 fusion.148
  107.6 1.6 fusion.148
  109.2 1.6 fusion.148
  110.8 1.6 fusion.148
  112.4 1.6 fusion.148
  114.4 5.1 %convert_bitcast_fusion = bf16[4,128,16,128]{3,2,0,1:T(8,128)(2,1)} fusion(bf16[128,32,128,1]{2,1,3,0:T(8,128)(2,1)S(1)} %bitcast.252, s32[128,4,16]{2,1,0:T(4,128)S(1)} %iota_add_fusion, pred[128,4,16]{2,1,0:T(4,128)(4,1)S(1)} %iota_compare_fusion.9), kind=kOutput, calls=%fused_computation.65 | convolution fusion | flops 68681728 | bytes 3186688 | tf_op jit(solution)/shard_map/otcq,oqe->toce/dot_general | solution.py:104
  119.5 12.0 %all-to-all-start = ((bf16[4,128,16,128]{3,2,0,1:T(8,128)(2,1)}), bf16[4,128,16,128]{3,2,0,1:T(8,128)(2,1)}, u32[]{:S(2)}, u32[]{:S(2)}) async-start(bf16[4,128,16,128]{3,2,0,1:T(8,128)(2,1)} %convert_bitcast_fusion), calls=%async_computation | async-start | bytes 4194304 | tf_op jit(solution)/shard_map/all_to_all | solution.py:174
  132.4 0.7 copy.85
  133.4 0.6 compare_convert_fusion
  134.1 27.6 %all-to-all-done = bf16[4,128,16,128]{3,2,0,1:T(8,128)(2,1)} async-done(((bf16[4,128,16,128]{3,2,0,1:T(8,128)(2,1)}), bf16[4,128,16,128]{3,2,0,1:T(8,128)(2,1)}, u32[]{:S(2)}, u32[]{:S(2)}) %all-to-all-start) | async-done | bytes 2097184 | tf_op jit(solution)/shard_map/all_to_all | solution.py:174
  161.7 2.0 copy.67
  163.6 0.7 multiply_reduce_fusion
  164.5 1.7 divide_convert_fusion
  166.1 4.5 %convert_element_type.119 = bf16[4,2048,128]{1,0,2:T(4,128)(2,1)} reshape(bf16[8192,2,64]{0,2,1:T(8,128)(2,1)} %divide_convert_fusion) | data formatting | bytes 4194304 | tf_op jit(solution)/shard_map/convert_element_type | solution.py:36
  170.6 2.5 fusion.119
  173.2 0.7 convolution_convert_fusion
  173.9 1.6 fusion.77
  175.5 2.7 bitcast_reduce_fusion.1
  178.2 1.9 fusion.64
  180.1 1.1 fusion.70
  181.5 2.8 collective-permute-start
  184.3 2.1 collective-permute-start.1
  186.4 0.7 multiply_reduce_fusion.1
  187.3 0.4 divide_convert_fusion.1
  187.6 2.8 convert_element_type.114
  190.5 2.5 collective-permute-start.2
  192.9 1.3 collective-permute-start.3
  194.2 2.6 fusion.118
  196.8 3.9 %copy.66 = f32[4,128,16,128]{3,2,1,0:T(8,128)} copy(bf16[4,128,16,128]{3,2,0,1:T(8,128)(2,1)} %all-to-all-done) | data formatting | bytes 6291456 | tf_op jit(solution)/shard_map/convert_element_type | solution.py:225
  201.1 0.4 fusion.60
  202.1 2.0 fusion.27
  204.1 2.0 fusion.29
  206.1 0.9 fusion.33
  207.1 0.9 fusion.34
  208.0 1.3 copy-done.3
  209.2 0.8 fusion.20
  210.1 2.0 copy.94
  212.1 8.4 %all-to-all-start.1 = ((bf16[4,128,16,128]{3,2,0,1:T(8,128)(2,1)}), bf16[4,128,16,128]{3,2,0,1:T(8,128)(2,1)S(1)}, u32[]{:S(2)}, u32[]{:S(2)}) async-start(bf16[4,128,16,128]{3,2,0,1:T(8,128)(2,1)} %copy.94), calls=%async_computation.1 | async-start | bytes 4194304 | tf_op jit(solution)/shard_map/all_to_all | solution.py:231
  220.7 30.4 %all-to-all-done.1 = bf16[4,128,16,128]{3,2,0,1:T(8,128)(2,1)S(1)} async-done(((bf16[4,128,16,128]{3,2,0,1:T(8,128)(2,1)}), bf16[4,128,16,128]{3,2,0,1:T(8,128)(2,1)S(1)}, u32[]{:S(2)}, u32[]{:S(2)}) %all-to-all-start.1) | async-done | bytes 2097184 | tf_op jit(solution)/shard_map/all_to_all | solution.py:231
  251.0 5.7 %bitcast_convert_fusion.4 = bf16[128,32,128]{2,1,0:T(8,128)(2,1)} fusion(bf16[4,128,16,128]{3,2,0,1:T(8,128)(2,1)S(1)} %all-to-all-done.1, s32[128,4,16]{2,1,0:T(4,128)S(1)} %iota_add_fusion, pred[128,4,16]{2,1,0:T(4,128)(4,1)S(1)} %copy-done.16), kind=kOutput, calls=%fused_computation.58 | convolution fusion | flops 68157440 | bytes 3186688 | tf_op jit(solution)/shard_map/otcq,toce->oqe/dot_general | solution.py:110
  256.8 20.9 %while.23 = (s32[]{:T(128)}, bf16[8,512,128]{2,1,0:T(8,128)(2,1)S(1)}, s32[8,512]{1,0:T(8,128)S(1)}, s32[128,32]{1,0:T(8,128)}, bf16[4096,128]{1,0:T(8,128)(2,1)}, /*index=5*/s32[4096]{0:T(1024)S(1)}, s32[]{:T(128)}) while((s32[]{:T(128)}, bf16[8,512,128]{2,1,0:T(8,128)(2,1)S(1)}, s32[8,512]{1,0:T(8,128)S(1)}, ...), condition=%wide.wide.region_15.17_spmd, body=%wide.wide.region_14.16_spmd.sunk | while | flops 539033600 | bytes 1202261 | solution.py:88
  256.9 2.6 fusion.151
  259.5 2.6 fusion.151
  262.1 2.6 fusion.151
  264.7 2.6 fusion.151
  267.3 2.6 fusion.151
  269.9 2.6 fusion.151
  272.6 2.6 fusion.151
  275.2 2.6 fusion.151
  277.8 0.9 copy-done.4
  278.7 0.6 copy-done.1
  (129 shorter events, 6.1 us)
Async XLA Ops:
  0.0 88.8 %copy-start = (bf16[4096,128]{1,0:T(8,128)(2,1)S(1)}, bf16[4096,128]{1,0:T(8,128)(2,1)}, u32[]{:S(2)}) copy-start(bf16[4096,128]{1,0:T(8,128)(2,1)} %param.16) | copy-start | bytes 3145732
  65.1 0.7 copy-start.2
  65.8 23.1 %copy-start.17 = (bf16[1,512,512]{2,1,0:T(8,128)(2,1)S(1)}, bf16[1,512,512]{2,1,0:T(8,128)(2,1)}, u32[]{:S(2)}) copy-start(bf16[1,512,512]{2,1,0:T(8,128)(2,1)} %param.18) | copy-start | bytes 1572868
  65.8 23.1 %copy-start.18 = (bf16[128,512]{1,0:T(8,128)(2,1)S(1)}, bf16[128,512]{1,0:T(8,128)(2,1)}, u32[]{:S(2)}) copy-start(bf16[128,512]{1,0:T(8,128)(2,1)} %param.17) | copy-start | bytes 393220
  88.9 6.4 %copy-start.19 = (bf16[512,128]{1,0:T(8,128)(2,1)S(1)}, bf16[512,128]{1,0:T(8,128)(2,1)}, u32[]{:S(2)}) copy-start(bf16[512,128]{1,0:T(8,128)(2,1)} %param.19) | copy-start | bytes 393220
  114.3 5.1 %copy-start.15 = (pred[128,4,16]{2,1,0:T(4,128)(4,1)}, pred[128,4,16]{2,1,0:T(4,128)(4,1)S(1)}, u32[]{:S(2)}) copy-start(pred[128,4,16]{2,1,0:T(4,128)(4,1)S(1)} %iota_compare_fusion.9) | copy-start | bytes 24580
  119.5 12.0 %copy-start.5 = (s32[128,512]{1,0:T(8,128)S(1)}, s32[128,512]{1,0:T(8,128)}, u32[]{:S(2)}) copy-start(s32[128,512]{1,0:T(8,128)} %param.20) | copy-start | bytes 786436
  119.5 12.2 %copy-start.11 = (bf16[4,128,128]{2,1,0:T(8,128)(2,1)S(1)}, bf16[4,128,128]{2,1,0:T(8,128)(2,1)}, u32[]{:S(2)}) copy-start(bf16[4,128,128]{2,1,0:T(8,128)(2,1)} %param.23) | copy-start | bytes 393220
  119.5 12.8 %copy-start.13 = (bf16[128,128]{1,0:T(8,128)(2,1)S(1)}, bf16[128,128]{1,0:T(8,128)(2,1)}, u32[]{:S(2)}) copy-start(bf16[128,128]{1,0:T(8,128)(2,1)} %param.22) | copy-start | bytes 98308
  119.5 12.8 %copy-start.9 = (bf16[4,128,128]{2,1,0:T(8,128)(2,1)S(1)}, bf16[4,128,128]{2,1,0:T(8,128)(2,1)}, u32[]{:S(2)}) copy-start(bf16[4,128,128]{2,1,0:T(8,128)(2,1)} %param.24) | copy-start | bytes 393220
  119.5 42.2 %all-to-all-start = ((bf16[4,128,16,128]{3,2,0,1:T(8,128)(2,1)}), bf16[4,128,16,128]{3,2,0,1:T(8,128)(2,1)}, u32[]{:S(2)}, u32[]{:S(2)}) async-start(bf16[4,128,16,128]{3,2,0,1:T(8,128)(2,1)} %convert_bitcast_fusion), calls=%async_computation | async-start | bytes 4194304 | tf_op jit(solution)/shard_map/all_to_all | solution.py:174
  170.6 2.5 copy-start.12
  173.8 1.7 copy-start.8
  181.5 8.9 %collective-permute-start = (bf16[1,2,128,128]{3,2,1,0:T(8,128)(2,1)S(1)}, bf16[1,2,128,128]{3,2,1,0:T(8,128)(2,1)S(1)}, u32[]{:S(2)}, u32[]{:S(2)}) collective-permute-start(bf16[1,2,128,128]{3,2,1,0:T(8,128)(2,1)S(1)} %get-tuple-element.106), channel_id=1, source_target_pairs={{0,4},{4,8},{8,12},{12,16},{16,20},{20,24},{24,28},{28,32},{32,36}... | collective-permute-start | bytes 196616 | tf_op jit(solution)/shard_map/ppermute | solution.py:23
  184.3 6.1 %collective-permute-start.1 = (bf16[1,2,128,128]{3,2,1,0:T(8,128)(2,1)S(1)}, bf16[1,2,128,128]{3,2,1,0:T(8,128)(2,1)S(1)}, u32[]{:S(2)}, u32[]{:S(2)}) collective-permute-start(bf16[1,2,128,128]{3,2,1,0:T(8,128)(2,1)S(1)} %get-tuple-element.107), channel_id=1, source_target_pairs={{4,0},{8,4},{12,8},{16,12},{20,16},{24,20},{28,24},{32,28},{36,32}... | collective-permute-start | bytes 196616 | tf_op jit(solution)/shard_map/ppermute | solution.py:26
  190.5 10.3 %collective-permute-start.2 = (bf16[4,1,128,128]{3,2,1,0:T(8,128)(2,1)S(1)}, bf16[4,1,128,128]{3,2,1,0:T(8,128)(2,1)S(1)}, u32[]{:S(2)}, u32[]{:S(2)}) collective-permute-start(bf16[4,1,128,128]{3,2,1,0:T(8,128)(2,1)S(1)} %get-tuple-element.101), channel_id=1, source_target_pairs={{0,1},{1,2},{2,3},{4,5},{5,6},{6,7},{8,9},{9,10},{10,11},{12,13},{... | collective-permute-start | bytes 393224 | tf_op jit(solution)/shard_map/ppermute | solution.py:23
  192.9 7.8 %collective-permute-start.3 = (bf16[4,1,128,128]{3,2,1,0:T(8,128)(2,1)S(1)}, bf16[4,1,128,128]{3,2,1,0:T(8,128)(2,1)S(1)}, u32[]{:S(2)}, u32[]{:S(2)}) collective-permute-start(bf16[4,1,128,128]{3,2,1,0:T(8,128)(2,1)S(1)} %get-tuple-element.100), channel_id=1, source_target_pairs={{1,0},{2,1},{3,2},{5,4},{6,5},{7,6},{9,8},{10,9},{11,10},{13,12},{... | collective-permute-start | bytes 393224 | tf_op jit(solution)/shard_map/ppermute | solution.py:26
  196.8 4.2 %copy-start.7 = (bf16[8,128,128]{2,1,0:T(8,128)(2,1)S(1)}, bf16[8,128,128]{2,1,0:T(8,128)(2,1)}, u32[]{:S(2)}) copy-start(bf16[8,128,128]{2,1,0:T(8,128)(2,1)} %param.25) | copy-start | bytes 786436
  196.8 4.7 %copy-start.14 = (bf16[128,128]{1,0:T(8,128)(2,1)S(1)}, bf16[128,128]{1,0:T(8,128)(2,1)}, u32[]{:S(2)}) copy-start(bf16[128,128]{1,0:T(8,128)(2,1)} %copy.85) | copy-start | bytes 98308
  200.8 1.1 copy-start.10
  207.1 2.2 copy-start.3
  210.1 41.0 %copy-start.16 = (pred[128,4,16]{2,1,0:T(4,128)(4,1)S(1)}, pred[128,4,16]{2,1,0:T(4,128)(4,1)}, u32[]{:S(2)}) copy-start(pred[128,4,16]{2,1,0:T(4,128)(4,1)} %copy-done.15) | copy-start | bytes 24580
  212.1 39.0 %all-to-all-start.1 = ((bf16[4,128,16,128]{3,2,0,1:T(8,128)(2,1)}), bf16[4,128,16,128]{3,2,0,1:T(8,128)(2,1)S(1)}, u32[]{:S(2)}, u32[]{:S(2)}) async-start(bf16[4,128,16,128]{3,2,0,1:T(8,128)(2,1)} %copy.94), calls=%async_computation.1 | async-start | bytes 4194304 | tf_op jit(solution)/shard_map/all_to_all | solution.py:231
  220.6 36.1 %copy-start.6 = (s32[128,32]{1,0:T(8,128)}, s32[128,32]{1,0:T(8,128)S(1)}, u32[]{:S(2)}) copy-start(s32[128,32]{1,0:T(8,128)S(1)} %reshape.197) | copy-start | bytes 49156
  277.8 1.0 copy-start.4
  277.8 1.6 copy-start.1
where the time goes:
time: 280 us; the launch traced here: 279 us
  local copies, waits for them, and re-layouts  113 us (40%)
  matrix products  73.6 us (26%)
  waiting for transfers between devices  58 us (21%)
  starting transfers between devices  29.1 us (10%)
  other arithmetic  4.16 us (1%)
    gather x5, local copies, waits for them, and re-layouts, body(): jnp.take_along_axis(send_starts.T, send_which, axis=1) + send_within  33.4 us
    all_to_all x1, waiting for transfers between devices, body(): lax.all_to_all(result_slots, ('tx', 'ty'), split_axis=1, concat_axis=1, t...  30.4 us
    all_to_all x1, waiting for transfers between devices, body(): lax.all_to_all(outgoing, ('tx', 'ty'), split_axis=1, concat_axis=1, tiled...  27.6 us
    gather x3, local copies, waits for them, and re-layouts, block_layout(): base = jnp.take_along_axis(before.T, which, axis=1)  26.9 us
    gather x2, local copies, waits for them, and re-layouts, body(): packed_index = point_order[0][packed_pos].reshape(-1)  23.1 us
    dot_general x8, matrix products, place_block(): jnp.dot(table, rows, preferred_element_type=jnp.float32)  20.7 us
    dot_general x8, matrix products, pick_block(): jnp.dot(table, source_rows, preferred_element_type=jnp.float32)  12.7 us
    all_to_all x1, starting transfers between devices, body(): lax.all_to_all(outgoing, ('tx', 'ty'), split_axis=1, concat_axis=1, tiled...  12 us
  transfers between devices with their start and end apart: 6, of which 2 were waited for; matrix products, arithmetic and copies ran while one was open for 5% of the time, Pallas kernels for 0%

commit v1 on v0

v1 whole, which is shorter than its diff:
```python
import jax
import jax.numpy as jnp
from jax import lax
from jax.sharding import PartitionSpec as P

HEADS = 2
TLX = 2
TLY = 2


sharpness = 32.0
epsilon = 1e-06
neighbour_steps = ((-1, -1), (-1, 0), (-1, 1), (0, -1), (0, 1), (1, -1), (1, 0), (1, 1))


def padded_2(block, sides, width):
    for axis, dim in sides:
        count = lax.axis_size(axis)
        forward = [(i, i + 1) for i in range(count - 1)]
        backward = [(target, source) for source, target in forward]
        low = lax.ppermute(
            lax.slice_in_dim(block, block.shape[dim] - width, None, axis=dim), axis, forward
        )
        high = lax.ppermute(lax.slice_in_dim(block, 0, width, axis=dim), axis, backward)
        block = jnp.concatenate([low, block, high], axis=dim)
    return block


def unit_heads(projected, head_count):
    pieces = projected.reshape(
        projected.shape[:-1] + (head_count, projected.shape[-1] // head_count)
    )
    magnitude = jnp.sqrt(jnp.sum(pieces * pieces, axis=-1, keepdims=True) + epsilon)
    return (pieces / magnitude).reshape(projected.shape).astype(jnp.bfloat16)


def gather_rows(order, rows, block):
    column_ids = jnp.arange(rows.shape[0], dtype=jnp.int32)

    def pick_block(index_block):
        table = (index_block[:, None] == column_ids[None, :]).astype(jnp.bfloat16)
        return jnp.dot(table, rows, preferred_element_type=jnp.float32).astype(jnp.bfloat16)

    picked = lax.map(pick_block, order.reshape(-1, block))
    return picked.reshape(order.shape[0], rows.shape[1])


def scatter_rows(order, rows, block):
    target_ids = jnp.arange(rows.shape[0], dtype=jnp.int32).reshape(-1, block)

    def place_block(target_block):
        table = (target_block[:, None] == order[None, :]).astype(jnp.bfloat16)
        return jnp.dot(table, rows, preferred_element_type=jnp.float32).astype(jnp.bfloat16)

    placed = lax.map(place_block, target_ids)
    return placed.reshape(rows.shape[0], rows.shape[1])


def body(
    points,
    embed_weight,
    inner_weights,
    output_weight,
    counts,
    point_order,
    inducing,
    first_proj,
    second_proj,
    mixing,
):
    along_x = lax.axis_size("tx")
    along_y = lax.axis_size("ty")
    devices = along_x * along_y
    index_x = lax.axis_index("tx")
    index_y = lax.axis_index("ty")
    own_index = index_x * along_y + index_y
    point_count = points.shape[0]
    per_device = TLX * TLY
    width = output_weight.shape[1]
    quota = point_count // devices
    band = quota * along_y
    head_width = width // HEADS
    inducing_count = inducing.shape[0]

    hidden = jax.nn.silu(jnp.dot(points, embed_weight, preferred_element_type=jnp.float32)).astype(
        jnp.bfloat16
    )
    for layer_id in range(inner_weights.shape[0]):
        hidden = jax.nn.silu(
            jnp.dot(hidden, inner_weights[layer_id], preferred_element_type=jnp.float32)
        ).astype(jnp.bfloat16)
    features = jnp.dot(hidden, output_weight, preferred_element_type=jnp.float32).astype(
        jnp.bfloat16
    )

    own_counts = lax.dynamic_index_in_dim(counts, own_index, 0, keepdims=False)
    own_offsets = jnp.cumsum(own_counts) - own_counts
    grid_counts = own_counts.reshape(along_x, TLX, along_y, TLY)
    grid_offsets = own_offsets.reshape(along_x, TLX, along_y, TLY)
    band_start = grid_offsets[:, 0, 0, 0][:, None]
    first_len = grid_counts[:, 0, :, 0] + grid_counts[:, 0, :, 1]
    first_start = grid_offsets[:, 0, :, 0] - band_start
    second_start = grid_offsets[:, 1, :, 0] - band_start
    slot_ids = jnp.arange(quota, dtype=jnp.int32)
    local_pos = jnp.where(
        slot_ids[None, None, :] < first_len[:, :, None],
        first_start[:, :, None] + slot_ids[None, None, :],
        second_start[:, :, None] + slot_ids[None, None, :] - first_len[:, :, None],
    ).reshape(along_x, band)
    band_ids = jnp.arange(band, dtype=jnp.int32)
    band_table = (local_pos[:, :, None] == band_ids[None, None, :]).astype(jnp.bfloat16)

    order = point_order[0]
    ordered = gather_rows(order, features, 512).reshape(along_x, band, width)
    outgoing = jnp.einsum(
        "xrp,xpe->xre", band_table, ordered, preferred_element_type=jnp.float32
    ).astype(jnp.bfloat16)
    outgoing = outgoing.reshape(devices, quota, width)
    arrived = lax.all_to_all(outgoing, ("tx", "ty"), split_axis=0, concat_axis=0, tiled=True)
    all_rows = arrived.reshape(devices * quota, width)

    inbound = counts.reshape(devices, along_x, TLX, along_y, TLY)
    inbound = lax.dynamic_index_in_dim(inbound, index_x, 1, keepdims=False)
    inbound = lax.dynamic_index_in_dim(inbound, index_y, 2, keepdims=False)
    inbound = inbound.reshape(devices, per_device)
    through = jnp.cumsum(inbound, axis=1)
    row_tile = jnp.sum(
        (slot_ids[None, :, None] >= through[:, None, : per_device - 1]).astype(jnp.int32), axis=2
    ).reshape(-1)
    tile_ids = jnp.arange(per_device, dtype=jnp.int32)
    row_mask = (row_tile[:, None] == tile_ids[None, :]).astype(jnp.float32)

    first_keys = unit_heads(
        jnp.dot(all_rows, first_proj[1], preferred_element_type=jnp.float32), HEADS
    )
    first_values = jnp.dot(all_rows, first_proj[2], preferred_element_type=jnp.float32).astype(
        jnp.bfloat16
    )
    inducing_queries = unit_heads(
        jnp.dot(inducing, first_proj[0], preferred_element_type=jnp.float32), HEADS
    )
    masked_values = first_values[:, None, :] * row_mask.astype(jnp.bfloat16)[:, :, None]
    heads_out = []
    for head_id in range(HEADS):
        lower = head_id * head_width
        upper = lower + head_width
        scores = jnp.dot(
            inducing_queries[:, lower:upper],
            first_keys[:, lower:upper].T,
            preferred_element_type=jnp.float32,
        )
        weights = jnp.exp(sharpness * scores)
        totals = jnp.dot(weights, row_mask, precision=lax.Precision.HIGHEST)
        numer = jnp.dot(
            weights.astype(jnp.bfloat16),
            masked_values[:, :, lower:upper].reshape(-1, per_device * head_width),
            preferred_element_type=jnp.float32,
        ).reshape(inducing_count, per_device, head_width)
        heads_out.append(numer / totals[:, :, None])
    first_attended = (
        jnp.concatenate(heads_out, axis=2).astype(jnp.bfloat16).transpose(1, 0, 2)
    )
    summary = (
        inducing.astype(jnp.float32)[None]
        + jnp.einsum(
            "tic,ce->tie", first_attended, first_proj[3], preferred_element_type=jnp.float32
        )
    ).astype(jnp.bfloat16)
    tile_grid = summary.reshape(TLX, TLY, inducing_count, width)
    padded = padded_2(tile_grid, (("tx", 0), ("ty", 1)), 1)
    stacked = jnp.stack(
        [
            padded[1 + steps[0] : 1 + steps[0] + TLX, 1 + steps[1] : 1 + steps[1] + TLY]
            for steps in neighbour_steps
        ]
    )
    mixture = tile_grid.astype(jnp.float32) + jnp.einsum(
        "dxyic,dce->xyie", stacked, mixing, preferred_element_type=jnp.float32
    )
    mixture = mixture.astype(jnp.bfloat16).reshape(per_device * inducing_count, width)

    point_queries = unit_heads(
        jnp.dot(all_rows, second_proj[0], preferred_element_type=jnp.float32), HEADS
    )
    second_keys = unit_heads(
        jnp.dot(mixture, second_proj[1], preferred_element_type=jnp.float32), HEADS
    )
    second_values = jnp.dot(mixture, second_proj[2], preferred_element_type=jnp.float32).astype(
        jnp.bfloat16
    )
    key_mask = jnp.repeat(row_mask, inducing_count, axis=1)
    heads_out = []
    for head_id in range(HEADS):
        lower = head_id * head_width
        upper = lower + head_width
        scores = jnp.dot(
            point_queries[:, lower:upper],
            second_keys[:, lower:upper].T,
            preferred_element_type=jnp.float32,
        )
        weights = jnp.exp(sharpness * scores) * key_mask
        totals = jnp.sum(weights, axis=1, keepdims=True)
        numer = jnp.dot(
            weights.astype(jnp.bfloat16),
            second_values[:, lower:upper],
            preferred_element_type=jnp.float32,
        )
        heads_out.append(numer / totals)
    second_attended = jnp.concatenate(heads_out, axis=1).astype(jnp.bfloat16)
    result = (
        all_rows.astype(jnp.float32)
        + jnp.dot(second_attended, second_proj[3], preferred_element_type=jnp.float32)
    ).astype(jnp.bfloat16)

    coming = lax.all_to_all(
        result.reshape(devices, quota, width), ("tx", "ty"), split_axis=0, concat_axis=0, tiled=True
    )
    returned = jnp.einsum(
        "xrp,xre->xpe",
        band_table,
        coming.reshape(along_x, band, width),
        preferred_element_type=jnp.float32,
    ).astype(jnp.bfloat16)
    return scatter_rows(order, returned.reshape(point_count, width), 512)


def solution(mesh):
    placed = (P(("tx", "ty"), None), P(), P(), P(), P(), P(("tx", "ty"), None), P(), P(), P(), P())
    return jax.shard_map(
        body, mesh=mesh, in_specs=placed, out_specs=P(("tx", "ty"), None), check_vma=False
    )
```

time: 280 us -> 158 us (0.56)
  local copies, waits for them, and re-layouts: 113 us -> 8.97 us
  waiting for transfers between devices: 58 us -> 44.7 us
    gather x10 -> x0, local copies, waits for them, and re-layouts: 83.4 us -> none  [the longest x5 33.4 us: body(): jnp.take_along_axis(send_starts.T, send_which, axis=1) + send_within]
    all_to_all x2, waiting for transfers between devices: 58 us -> 37.6 us  [the longest x1 19.4 us: body(): lax.all_to_all(result.reshape(devices, quota, width), ('tx', 'ty'), split...]
    dot_general x8, matrix products: 20.7 us -> 10.9 us  [place_block(): jnp.dot(table, rows, preferred_element_type=jnp.float32)]
    convert_element_type x4 -> x1, local copies, waits for them, and re-layouts: 11.2 us -> 1.48 us  [body(): jnp.dot(all_rows, first_proj[2], preferred_element_type=jnp.float32)]
    ppermute x2, waiting for transfers between devices: 0.01 us -> 6.91 us  [padded_2(): lax.ppermute(lax.slice_in_dim(block, 0, width, axis=dim), axis, backward)]
    dot_general x20 -> x22, matrix products: 43.9 us -> 49.2 us  [the longest x8 22.5 us: pick_block(): jnp.dot(table, rows, preferred_element_type=jnp.float32)]
    slice x4 -> x5, local copies, waits for them, and re-layouts: 5.2 us -> 0.97 us  [the longest x1 0.68 us: body(): band_start = grid_offsets[:, 0, 0, 0][:, None]]
  transfers between devices with their start and end apart: 6 -> 6, of which waited for: 2 -> 5; matrix products, arithmetic and copies ran while one was open for 5% -> 1% of each run, Pallas kernels for 0% -> 0%
where the time goes in v1:
time: 158 us; the launch traced here: 157 us
  matrix products  71.1 us (45%)
  waiting for transfers between devices  44.7 us (28%)
  starting transfers between devices  28.1 us (18%)
  local copies, waits for them, and re-layouts  8.97 us (6%)
  other arithmetic  3.02 us (2%)
    dot_general x8, matrix products, pick_block(): jnp.dot(table, rows, preferred_element_type=jnp.float32)  22.5 us
    all_to_all x1, waiting for transfers between devices, body(): lax.all_to_all(result.reshape(devices, quota, width), ('tx', 'ty'), split...  19.4 us
    all_to_all x1, waiting for transfers between devices, body(): lax.all_to_all(outgoing, ('tx', 'ty'), split_axis=0, concat_axis=0, tiled...  18.2 us
    all_to_all x1, starting transfers between devices, body(): lax.all_to_all(outgoing, ('tx', 'ty'), split_axis=0, concat_axis=0, tiled...  11.5 us
    dot_general x8, matrix products, place_block(): jnp.dot(table, rows, preferred_element_type=jnp.float32)  10.9 us
    dot_general x1, matrix products, body(): jnp.dot(hidden, inner_weights[layer_id], preferred_element_type=jnp.float32)  8.83 us
    all_to_all x1, starting transfers between devices, body(): lax.all_to_all(result.reshape(devices, quota, width), ('tx', 'ty'), split...  7.99 us
    ppermute x2, waiting for transfers between devices, padded_2(): lax.ppermute(lax.slice_in_dim(block, 0, width, axis=dim), axis, backward)  6.91 us
  transfers between devices with their start and end apart: 6, of which 5 were waited for; matrix products, arithmetic and copies ran while one was open for 1% of the time, Pallas kernels for 0%

profile of v1, /device:TPU:1, one launch (start us, length us, event | category | flops | bytes accessed | tf_op | source)
XLA Modules:
  0.0 157.0 jit_solution(1427958555098266817)
XLA Ops:
  0.0 0.5 broadcast.133
  0.5 1.4 fusion.100
  1.9 0.3 reduce-window.9
  2.3 0.2 reshape.270
  2.8 0.2 reshape.268
  3.1 0.7 slice_reduce_fusion
  5.2 1.4 reduce.10
  6.7 8.8 %fusion.29 = f32[4096,512]{1,0:T(8,128)} fusion(bf16[4096,128]{1,0:T(8,128)(2,1)S(1)} %copy-done, bf16[128,512]{1,0:T(8,128)(2,1)} %param.15, bf16[1,512,512]{2,1,0:T(8,128)(2,1)} %param.16), kind=kOutput, calls=%fused_computation.36 | convolution fusion | flops 2694840320 | bytes 10092544 | tf_op jit(solution)/shard_map/dot_general | solution.py:90
  15.5 6.7 %convolution_convert_fusion.1 = bf16[4096,128]{1,0:T(8,128)(2,1)} fusion(bf16[512,128]{1,0:T(8,128)(2,1)S(1)} %copy-done.11, f32[4096,512]{1,0:T(8,128)} %fusion.29), kind=kOutput, calls=%fused_computation.31 | convolution fusion | flops 547880960 | bytes 9568256 | tf_op jit(solution)/shard_map/dot_general | solution.py:92
  22.3 22.7 %while.22 = (s32[]{:T(128)}, bf16[8,512,128]{2,1,0:T(8,128)(2,1)S(1)}, s32[8,512]{1,0:T(8,128)S(1)}, bf16[4096,128]{1,0:T(8,128)(2,1)}, s32[]{:T(128)}) while((s32[]{:T(128)}, bf16[8,512,128]{2,1,0:T(8,128)(2,1)S(1)}, s32[8,512]{1,0:T(8,128)S(1)}, bf16[4096,128]{1,0:T(8,128)(2,1)}, s32[]{:T(128)}) %tuple.50), condition=%wide.region_3.4_spmd.clone, body=%wide.region_2.3_spmd.clone.sunk | while | flops 539033600 | bytes 1185861 | solution.py:44
  22.3 2.8 %fusion.133 = bf16[8,512,128]{2,1,0:T(8,128)(2,1)S(1)} fusion(bf16[8,512,128]{2,1,0:T(8,128)(2,1)S(1)} %get-tuple-element.181, s32[]{:T(128)} %get-tuple-element.180, bf16[4096,128]{1,0:T(8,128)(2,1)} %get-tuple-element.188, s32[512]{0:T(512)S(1)} %bitcast.244), kind=kOutput, calls=%fused_computation.14.clone.1 | convolution fusion | flops 539033600 | bytes 1181700 | tf_op jit(solution)/shard_map/while/body/eval_jaxpr/dot_general | solution.py:42
  25.2 2.8 %fusion.133 = bf16[8,512,128]{2,1,0:T(8,128)(2,1)S(1)} fusion(bf16[8,512,128]{2,1,0:T(8,128)(2,1)S(1)} %get-tuple-element.181, s32[]{:T(128)} %get-tuple-element.180, bf16[4096,128]{1,0:T(8,128)(2,1)} %get-tuple-element.188, s32[512]{0:T(512)S(1)} %bitcast.244), kind=kOutput, calls=%fused_computation.14.clone.1 | convolution fusion | flops 539033600 | bytes 1181700 | tf_op jit(solution)/shard_map/while/body/eval_jaxpr/dot_general | solution.py:42
  28.0 2.8 %fusion.133 = bf16[8,512,128]{2,1,0:T(8,128)(2,1)S(1)} fusion(bf16[8,512,128]{2,1,0:T(8,128)(2,1)S(1)} %get-tuple-element.181, s32[]{:T(128)} %get-tuple-element.180, bf16[4096,128]{1,0:T(8,128)(2,1)} %get-tuple-element.188, s32[512]{0:T(512)S(1)} %bitcast.244), kind=kOutput, calls=%fused_computation.14.clone.1 | convolution fusion | flops 539033600 | bytes 1181700 | tf_op jit(solution)/shard_map/while/body/eval_jaxpr/dot_general | solution.py:42
  30.8 2.8 %fusion.133 = bf16[8,512,128]{2,1,0:T(8,128)(2,1)S(1)} fusion(bf16[8,512,128]{2,1,0:T(8,128)(2,1)S(1)} %get-tuple-element.181, s32[]{:T(128)} %get-tuple-element.180, bf16[4096,128]{1,0:T(8,128)(2,1)} %get-tuple-element.188, s32[512]{0:T(512)S(1)} %bitcast.244), kind=kOutput, calls=%fused_computation.14.clone.1 | convolution fusion | flops 539033600 | bytes 1181700 | tf_op jit(solution)/shard_map/while/body/eval_jaxpr/dot_general | solution.py:42
  33.7 2.8 %fusion.133 = bf16[8,512,128]{2,1,0:T(8,128)(2,1)S(1)} fusion(bf16[8,512,128]{2,1,0:T(8,128)(2,1)S(1)} %get-tuple-element.181, s32[]{:T(128)} %get-tuple-element.180, bf16[4096,128]{1,0:T(8,128)(2,1)} %get-tuple-element.188, s32[512]{0:T(512)S(1)} %bitcast.244), kind=kOutput, calls=%fused_computation.14.clone.1 | convolution fusion | flops 539033600 | bytes 1181700 | tf_op jit(solution)/shard_map/while/body/eval_jaxpr/dot_general | solution.py:42
  36.5 2.8 %fusion.133 = bf16[8,512,128]{2,1,0:T(8,128)(2,1)S(1)} fusion(bf16[8,512,128]{2,1,0:T(8,128)(2,1)S(1)} %get-tuple-element.181, s32[]{:T(128)} %get-tuple-element.180, bf16[4096,128]{1,0:T(8,128)(2,1)} %get-tuple-element.188, s32[512]{0:T(512)S(1)} %bitcast.244), kind=kOutput, calls=%fused_computation.14.clone.1 | convolution fusion | flops 539033600 | bytes 1181700 | tf_op jit(solution)/shard_map/while/body/eval_jaxpr/dot_general | solution.py:42
  39.4 2.8 %fusion.133 = bf16[8,512,128]{2,1,0:T(8,128)(2,1)S(1)} fusion(bf16[8,512,128]{2,1,0:T(8,128)(2,1)S(1)} %get-tuple-element.181, s32[]{:T(128)} %get-tuple-element.180, bf16[4096,128]{1,0:T(8,128)(2,1)} %get-tuple-element.188, s32[512]{0:T(512)S(1)} %bitcast.244), kind=kOutput, calls=%fused_computation.14.clone.1 | convolution fusion | flops 539033600 | bytes 1181700 | tf_op jit(solution)/shard_map/while/body/eval_jaxpr/dot_general | solution.py:42
  42.2 2.8 %fusion.133 = bf16[8,512,128]{2,1,0:T(8,128)(2,1)S(1)} fusion(bf16[8,512,128]{2,1,0:T(8,128)(2,1)S(1)} %get-tuple-element.181, s32[]{:T(128)} %get-tuple-element.180, bf16[4096,128]{1,0:T(8,128)(2,1)} %get-tuple-element.188, s32[512]{0:T(512)S(1)} %bitcast.244), kind=kOutput, calls=%fused_computation.14.clone.1 | convolution fusion | flops 539033600 | bytes 1181700 | tf_op jit(solution)/shard_map/while/body/eval_jaxpr/dot_general | solution.py:42
  45.1 1.7 %fusion.36 = bf16[32,128,128]{2,1,0:T(8,128)(2,1)} fusion(bf16[32,128,128]{2,1,0:T(8,128)(2,1)S(1)} %bitcast.231, s32[32,128]{1,0:T(8,128)S(1)} %subtract_select_fusion), kind=kOutput, calls=%fused_computation.50 | convolution fusion | flops 135266304 | bytes 2113536 | tf_op jit(solution)/shard_map/xrp,xpe->xre/dot_general | solution.py:115
  46.8 11.5 %all-to-all-start = ((bf16[128,32,128]{2,1,0:T(8,128)(2,1)}), bf16[128,32,128]{2,1,0:T(8,128)(2,1)S(1)}, u32[]{:S(2)}, u32[]{:S(2)}) async-start(bf16[128,32,128]{2,1,0:T(8,128)(2,1)} %bitcast.9), calls=%async_computation | async-start | bytes 2097152 | tf_op jit(solution)/shard_map/all_to_all | solution.py:119
  59.5 18.2 %all-to-all-done = bf16[128,32,128]{2,1,0:T(8,128)(2,1)S(1)} async-done(((bf16[128,32,128]{2,1,0:T(8,128)(2,1)}), bf16[128,32,128]{2,1,0:T(8,128)(2,1)S(1)}, u32[]{:S(2)}, u32[]{:S(2)}) %all-to-all-start) | async-done | bytes 1048608 | tf_op jit(solution)/shard_map/all_to_all | solution.py:119
  77.7 0.5 multiply_reduce_fusion
  78.2 0.2 divide_convert_fusion
  78.4 0.5 fusion.25
  78.9 2.0 %fusion.24 = f32[128,4096]{1,0:T(8,128)} fusion(bf16[4096,128]{0,1:T(8,128)(2,1)S(1)} %bitcast.229, bf16[128,128]{0,1:T(8,128)(2,1)S(1)} %bitcast.239), kind=kOutput, calls=%fused_computation.26 | convolution fusion | flops 67633152 | bytes 2637824 | tf_op jit(solution)/shard_map/dot_general | solution.py:147
  80.9 1.1 fusion.79
  81.9 1.4 convolution_convert_fusion
  83.3 1.5 copy.81
  84.8 2.8 %fusion.78 = f32[128,4]{0,1:T(4,128)S(1)} fusion(f32[128,4096]{1,0:T(8,128)} %fusion.24, s32[4096]{0:T(1024)S(1)} %eq.67), kind=kOutput, calls=%fused_computation.114 | convolution fusion | flops 25182208 | bytes 2115584 | tf_op jit(solution)/shard_map/dot_general | solution.py:153
  87.6 0.3 broadcast_multiply_fusion
  87.9 0.7 fusion.44
  88.7 0.6 copy-done.1
  89.2 0.7 fusion.43
  89.9 1.0 fusion.39
  90.9 2.7 %collective-permute-start = (bf16[1,2,128,128]{3,2,1,0:T(8,128)(2,1)S(1)}, bf16[1,2,128,128]{3,2,1,0:T(8,128)(2,1)S(1)}, u32[]{:S(2)}, u32[]{:S(2)}) collective-permute-start(bf16[1,2,128,128]{3,2,1,0:T(8,128)(2,1)S(1)} %get-tuple-element.101), channel_id=1, source_target_pairs={{0,4},{4,8},{8,12},{12,16},{16,20},{20,24},{24,28},{28,32},{32,36}... | collective-permute-start | bytes 196616 | tf_op jit(solution)/shard_map/ppermute | solution.py:21
  93.6 1.9 %collective-permute-start.1 = (bf16[1,2,128,128]{3,2,1,0:T(8,128)(2,1)S(1)}, bf16[1,2,128,128]{3,2,1,0:T(8,128)(2,1)S(1)}, u32[]{:S(2)}, u32[]{:S(2)}) collective-permute-start(bf16[1,2,128,128]{3,2,1,0:T(8,128)(2,1)S(1)} %get-tuple-element.102), channel_id=1, source_target_pairs={{4,0},{8,4},{12,8},{16,12},{20,16},{24,20},{28,24},{32,28},{36,32}... | collective-permute-start | bytes 196616 | tf_op jit(solution)/shard_map/ppermute | solution.py:24
  95.6 0.5 multiply_reduce_fusion.1
  96.1 3.1 %collective-permute-done.1 = bf16[1,2,128,128]{3,2,1,0:T(8,128)(2,1)S(1)} collective-permute-done((bf16[1,2,128,128]{3,2,1,0:T(8,128)(2,1)S(1)}, bf16[1,2,128,128]{3,2,1,0:T(8,128)(2,1)S(1)}, u32[]{:S(2)}, u32[]{:S(2)}) %collective-permute-start.1) | collective-permute-done | bytes 65568 | tf_op jit(solution)/shard_map/ppermute | solution.py:24
  99.3 2.4 %collective-permute-start.2 = (bf16[4,1,128,128]{3,2,1,0:T(8,128)(2,1)S(1)}, bf16[4,1,128,128]{3,2,1,0:T(8,128)(2,1)S(1)}, u32[]{:S(2)}, u32[]{:S(2)}) collective-permute-start(bf16[4,1,128,128]{3,2,1,0:T(8,128)(2,1)S(1)} %get-tuple-element.98), channel_id=1, source_target_pairs={{0,1},{1,2},{2,3},{4,5},{5,6},{6,7},{8,9},{9,10},{10,11},{12,13},{... | collective-permute-start | bytes 393224 | tf_op jit(solution)/shard_map/ppermute | solution.py:21
  101.7 1.5 collective-permute-start.3
  103.3 0.2 divide_convert_fusion.1
  103.4 0.2 collective-permute-done.2
  103.7 3.8 %collective-permute-done.3 = bf16[4,1,128,128]{3,2,1,0:T(8,128)(2,1)S(1)} collective-permute-done((bf16[4,1,128,128]{3,2,1,0:T(8,128)(2,1)S(1)}, bf16[4,1,128,128]{3,2,1,0:T(8,128)(2,1)S(1)}, u32[]{:S(2)}, u32[]{:S(2)}) %collective-permute-start.3) | collective-permute-done | bytes 131104 | tf_op jit(solution)/shard_map/ppermute | solution.py:24
  107.7 0.4 fusion.40
  108.2 0.2 multiply_reduce_fusion.2
  108.4 0.2 convolution_convert_fusion.2
  108.7 1.3 fusion.54
  110.0 3.6 %fusion.20 = (f32[4096]{0:T(1024)S(1)}, f32[4096]{0:T(1024)S(1)}, bf16[4096,512]{0,1:T(8,128)(2,1)S(1)}, bf16[4096,512]{0,1:T(8,128)(2,1)S(1)}) fusion(f32[4096,4]{0,1:T(4,128)S(1)} %get-tuple-element.107, f32[4096,512]{0,1:T(8,128)S(1)} %fusion.54, bf16[512,128]{0,1:T(8,128)(2,1)S(1)} %bitcast.236, bf16[4096,128]{0,1:T(8,128)(2,1)S(1)} %bitcast.227), kind=kOutput, calls=%fused_computation.20 | convolution fusion | flops 285204480 | bytes 17465344 | tf_op jit(solution)/shard_map/dot_general | solution.py:196
  113.6 0.8 fusion.27
  114.5 0.8 fusion.28
  115.3 1.5 fusion.26
  116.8 8.0 %all-to-all-start.1 = ((bf16[128,32,128]{2,1,0:T(8,128)(2,1)}), bf16[128,32,128]{2,1,0:T(8,128)(2,1)S(1)}, u32[]{:S(2)}, u32[]{:S(2)}) async-start(bf16[128,32,128]{2,1,0:T(8,128)(2,1)} %bitcast.71), calls=%async_computation.1 | async-start | bytes 2097152 | tf_op jit(solution)/shard_map/all_to_all | solution.py:215
  124.8 19.4 %all-to-all-done.1 = bf16[128,32,128]{2,1,0:T(8,128)(2,1)S(1)} async-done(((bf16[128,32,128]{2,1,0:T(8,128)(2,1)}), bf16[128,32,128]{2,1,0:T(8,128)(2,1)S(1)}, u32[]{:S(2)}, u32[]{:S(2)}) %all-to-all-start.1) | async-done | bytes 1048608 | tf_op jit(solution)/shard_map/all_to_all | solution.py:215
  144.2 0.5 fusion.37
  144.8 11.1 %while.21 = (s32[]{:T(128)}, bf16[8,512,128]{2,1,0:T(8,128)(2,1)S(1)}, s32[8,512]{1,0:T(8,128)S(1)}, s32[1,4096]{1,0:T(1,128)S(1)}, bf16[4096,128]{1,0:T(8,128)(2,1)S(1)}, /*index=5*/s32[]{:T(128)}) while((s32[]{:T(128)}, bf16[8,512,128]{2,1,0:T(8,128)(2,1)S(1)}, s32[8,512]{1,0:T(8,128)S(1)}, s32[1,4096]{1,0:T(1,128)S(1)}, ...), condition=%wide.region_13.14_spmd, body=%wide.region_12.13_spmd.sunk | while | flops 539033600 | bytes 1202253 | solution.py:55
  144.9 1.4 fusion.131
  146.3 1.4 fusion.131
  147.7 1.4 fusion.131
  149.0 1.4 fusion.131
  150.4 1.4 fusion.131
  151.8 1.4 fusion.131
  153.2 1.4 fusion.131
  154.6 1.4 fusion.131
  156.0 1.0 copy-done.4
  (100 shorter events, 3.8 us)
Async XLA Ops:
  0.0 6.6 %copy-start = (bf16[4096,128]{1,0:T(8,128)(2,1)S(1)}, bf16[4096,128]{1,0:T(8,128)(2,1)}, u32[]{:S(2)}) copy-start(bf16[4096,128]{1,0:T(8,128)(2,1)} %param.14) | copy-start | bytes 3145732
  6.6 8.8 %copy-start.11 = (bf16[512,128]{1,0:T(8,128)(2,1)S(1)}, bf16[512,128]{1,0:T(8,128)(2,1)}, u32[]{:S(2)}) copy-start(bf16[512,128]{1,0:T(8,128)(2,1)} %param.17) | copy-start | bytes 393220
  45.0 13.3 %copy-start.5 = (s32[128,512]{1,0:T(8,128)S(1)}, s32[128,512]{1,0:T(8,128)}, u32[]{:S(2)}) copy-start(s32[128,512]{1,0:T(8,128)} %param.18) | copy-start | bytes 786436
  45.0 13.4 %copy-start.8 = (bf16[4,128,128]{2,1,0:T(8,128)(2,1)S(1)}, bf16[4,128,128]{2,1,0:T(8,128)(2,1)}, u32[]{:S(2)}) copy-start(bf16[4,128,128]{2,1,0:T(8,128)(2,1)} %param.21) | copy-start | bytes 393220
  45.0 13.7 %copy-start.9 = (bf16[128,128]{1,0:T(8,128)(2,1)S(1)}, bf16[128,128]{1,0:T(8,128)(2,1)}, u32[]{:S(2)}) copy-start(bf16[128,128]{1,0:T(8,128)(2,1)} %param.20) | copy-start | bytes 98308
  45.0 14.1 %copy-start.7 = (bf16[4,128,128]{2,1,0:T(8,128)(2,1)S(1)}, bf16[4,128,128]{2,1,0:T(8,128)(2,1)}, u32[]{:S(2)}) copy-start(bf16[4,128,128]{2,1,0:T(8,128)(2,1)} %param.22) | copy-start | bytes 393220
  46.8 30.9 %all-to-all-start = ((bf16[128,32,128]{2,1,0:T(8,128)(2,1)}), bf16[128,32,128]{2,1,0:T(8,128)(2,1)S(1)}, u32[]{:S(2)}, u32[]{:S(2)}) async-start(bf16[128,32,128]{2,1,0:T(8,128)(2,1)} %bitcast.9), calls=%async_computation | async-start | bytes 2097152 | tf_op jit(solution)/shard_map/all_to_all | solution.py:119
  78.9 2.0 %copy-start.2 = (f32[128,4096]{1,0:T(8,128)}, f32[128,4096]{1,0:T(8,128)S(1)}, u32[]{:S(2)}) copy-start(f32[128,4096]{1,0:T(8,128)S(1)} %fusion.25) | copy-start | bytes 6291460
  84.8 3.1 %copy-start.3 = (f32[128,4096]{1,0:T(8,128)S(1)}, f32[128,4096]{1,0:T(8,128)}, u32[]{:S(2)}) copy-start(f32[128,4096]{1,0:T(8,128)} %copy-done.2) | copy-start | bytes 6291460
  87.6 1.6 %copy-start.1 = (f32[128,4096]{1,0:T(8,128)S(1)}, f32[128,4096]{1,0:T(8,128)}, u32[]{:S(2)}) copy-start(f32[128,4096]{1,0:T(8,128)} %fusion.24) | copy-start | bytes 6291460
  90.9 5.2 %collective-permute-start = (bf16[1,2,128,128]{3,2,1,0:T(8,128)(2,1)S(1)}, bf16[1,2,128,128]{3,2,1,0:T(8,128)(2,1)S(1)}, u32[]{:S(2)}, u32[]{:S(2)}) collective-permute-start(bf16[1,2,128,128]{3,2,1,0:T(8,128)(2,1)S(1)} %get-tuple-element.101), channel_id=1, source_target_pairs={{0,4},{4,8},{8,12},{12,16},{16,20},{20,24},{24,28},{28,32},{32,36}... | collective-permute-start | bytes 196616 | tf_op jit(solution)/shard_map/ppermute | solution.py:21
  93.6 5.6 %collective-permute-start.1 = (bf16[1,2,128,128]{3,2,1,0:T(8,128)(2,1)S(1)}, bf16[1,2,128,128]{3,2,1,0:T(8,128)(2,1)S(1)}, u32[]{:S(2)}, u32[]{:S(2)}) collective-permute-start(bf16[1,2,128,128]{3,2,1,0:T(8,128)(2,1)S(1)} %get-tuple-element.102), channel_id=1, source_target_pairs={{4,0},{8,4},{12,8},{16,12},{20,16},{24,20},{28,24},{32,28},{36,32}... | collective-permute-start | bytes 196616 | tf_op jit(solution)/shard_map/ppermute | solution.py:24
  96.0 11.7 %copy-start.6 = (bf16[8,128,128]{2,1,0:T(8,128)(2,1)S(1)}, bf16[8,128,128]{2,1,0:T(8,128)(2,1)}, u32[]{:S(2)}) copy-start(bf16[8,128,128]{2,1,0:T(8,128)(2,1)} %param.23) | copy-start | bytes 786436
  99.3 4.4 %collective-permute-start.2 = (bf16[4,1,128,128]{3,2,1,0:T(8,128)(2,1)S(1)}, bf16[4,1,128,128]{3,2,1,0:T(8,128)(2,1)S(1)}, u32[]{:S(2)}, u32[]{:S(2)}) collective-permute-start(bf16[4,1,128,128]{3,2,1,0:T(8,128)(2,1)S(1)} %get-tuple-element.98), channel_id=1, source_target_pairs={{0,1},{1,2},{2,3},{4,5},{5,6},{6,7},{8,9},{9,10},{10,11},{12,13},{... | collective-permute-start | bytes 393224 | tf_op jit(solution)/shard_map/ppermute | solution.py:21
  101.7 5.7 %collective-permute-start.3 = (bf16[4,1,128,128]{3,2,1,0:T(8,128)(2,1)S(1)}, bf16[4,1,128,128]{3,2,1,0:T(8,128)(2,1)S(1)}, u32[]{:S(2)}, u32[]{:S(2)}) collective-permute-start(bf16[4,1,128,128]{3,2,1,0:T(8,128)(2,1)S(1)} %get-tuple-element.97), channel_id=1, source_target_pairs={{1,0},{2,1},{3,2},{5,4},{6,5},{7,6},{9,8},{10,9},{11,10},{13,12},{... | collective-permute-start | bytes 393224 | tf_op jit(solution)/shard_map/ppermute | solution.py:24
  115.3 29.5 %copy-start.10 = (s32[1,4096]{1,0:T(1,128)S(1)}, s32[1,4096]{1,0:T(1,128)}, u32[]{:S(2)}) copy-start(s32[1,4096]{1,0:T(1,128)} %param.19) | copy-start | bytes 49156
  116.8 27.4 %all-to-all-start.1 = ((bf16[128,32,128]{2,1,0:T(8,128)(2,1)}), bf16[128,32,128]{2,1,0:T(8,128)(2,1)S(1)}, u32[]{:S(2)}, u32[]{:S(2)}) async-start(bf16[128,32,128]{2,1,0:T(8,128)(2,1)} %bitcast.71), calls=%async_computation.1 | async-start | bytes 2097152 | tf_op jit(solution)/shard_map/all_to_all | solution.py:215
  156.0 1.0 copy-start.4

commit v2 on v1

--- a/solution.py
+++ b/solution.py
@@ -1,6 +1,10 @@
+import functools
+
 import jax
 import jax.numpy as jnp
 from jax import lax
+from jax.experimental import pallas as pl
+from jax.experimental.pallas import tpu as pltpu
 from jax.sharding import PartitionSpec as P
 
 HEADS = 2
@@ -11,6 +15,48 @@
 sharpness = 32.0
 epsilon = 1e-06
 neighbour_steps = ((-1, -1), (-1, 0), (-1, 1), (0, -1), (0, 1), (1, -1), (1, 0), (1, 1))
+
+
+def exchange_kernel(n, ny, x_ref, o_ref, send_sem, recv_sem, local_sem):
+    me = lax.axis_index("tx") * ny + lax.axis_index("ty")
+
+    def copy_to(d):
+        return pltpu.make_async_remote_copy(
+            src_ref=x_ref.at[d], dst_ref=o_ref.at[me], send_sem=send_sem.at[d],
+            recv_sem=recv_sem.at[me], device_id=(d // ny, d % ny),
+            device_id_type=pl.DeviceIdType.MESH)
+
+    def copy_from(s):
+        return pltpu.make_async_remote_copy(
+            src_ref=x_ref.at[s], dst_ref=o_ref.at[s], send_sem=send_sem.at[s],
+            recv_sem=recv_sem.at[s], device_id=(s // ny, s % ny),
+            device_id_type=pl.DeviceIdType.MESH)
+
+    local = pltpu.make_async_copy(x_ref.at[me], o_ref.at[me], local_sem)
+    local.start()
+
+    def start(k, carry):
+        copy_to(lax.rem(me + k, n)).start()
+        return carry
+    lax.fori_loop(1, n, start, 0)
+
+    def finish(k, carry):
+        copy_to(lax.rem(me + k, n)).wait_send()
+        copy_from(lax.rem(me + n - k, n)).wait_recv()
+        return carry
+    lax.fori_loop(1, n, finish, 0)
+    local.wait()
+
+def exchange(x, nx, ny):
+    n = nx * ny
+    return pl.pallas_call(
+        functools.partial(exchange_kernel, n, ny),
+        out_shape=jax.ShapeDtypeStruct(x.shape, x.dtype),
+        in_specs=[pl.BlockSpec(memory_space=pltpu.VMEM)],
+        out_specs=pl.BlockSpec(memory_space=pltpu.VMEM),
+        scratch_shapes=[pltpu.SemaphoreType.DMA((n,)), pltpu.SemaphoreType.DMA((n,)), pltpu.SemaphoreType.DMA],
+        compiler_params=pltpu.CompilerParams(has_side_effects=True),
+    )(x)
 
 
 def padded_2(block, sides, width):
@@ -116,7 +162,7 @@
         "xrp,xpe->xre", band_table, ordered, preferred_element_type=jnp.float32
     ).astype(jnp.bfloat16)
     outgoing = outgoing.reshape(devices, quota, width)
-    arrived = lax.all_to_all(outgoing, ("tx", "ty"), split_axis=0, concat_axis=0, tiled=True)
+    arrived = exchange(outgoing, along_x, along_y)
     all_rows = arrived.reshape(devices * quota, width)
 
     inbound = counts.reshape(devices, along_x, TLX, along_y, TLY)
@@ -212,9 +258,7 @@
         + jnp.dot(second_attended, second_proj[3], preferred_element_type=jnp.float32)
     ).astype(jnp.bfloat16)
 
-    coming = lax.all_to_all(
-        result.reshape(devices, quota, width), ("tx", "ty"), split_axis=0, concat_axis=0, tiled=True
-    )
+    coming = exchange(result.reshape(devices, quota, width), along_x, along_y)
     returned = jnp.einsum(
         "xrp,xre->xpe",
         band_table,

time: 158 us -> 181 us (1.15)
  Pallas kernels: 0 us -> 67.2 us
  waiting for transfers between devices: 44.7 us -> 6.55 us
  starting transfers between devices: 28.1 us -> 9.34 us
  matrix products: 71.1 us -> 78.8 us
  local copies, waits for them, and re-layouts: 8.97 us -> 12.5 us
    pallas_call x0 -> x2, Pallas kernels: none -> 67.2 us  [exchange(): pl.pallas_call(functools.partial(exchange_kernel, n, ny), out_shape=jax.S...]
    all_to_all x2 -> x0, waiting for transfers between devices: 37.6 us -> none  [the longest x1 19.4 us: body(): lax.all_to_all(result.reshape(devices, quota, width), ('tx', 'ty'), split...]
    all_to_all x2 -> x0, starting transfers between devices: 19.5 us -> none  [the longest x1 11.5 us: body(): lax.all_to_all(outgoing, ('tx', 'ty'), split_axis=0, concat_axis=0, tiled...]
  transfers between devices with their start and end apart: 6 -> 4, of which waited for: 5 -> 2; matrix products, arithmetic and copies ran while one was open for 1% -> 1% of each run, Pallas kernels for 0% -> 0%
where the time goes in v2:
time: 181 us; the launch traced here: 179 us
  matrix products  78.8 us (44%)
  Pallas kernels  67.2 us (37%)
  local copies, waits for them, and re-layouts  12.5 us (7%)
  starting transfers between devices  9.34 us (5%)
  waiting for transfers between devices  6.55 us (4%)
  other arithmetic  3.97 us (2%)
    pallas_call x2, Pallas kernels, exchange(): pl.pallas_call(functools.partial(exchange_kernel, n, ny), out_shape=jax.S...  67.2 us
    dot_general x8, matrix products, pick_block(): jnp.dot(table, rows, preferred_element_type=jnp.float32)  22.5 us
    dot_general x8, matrix products, place_block(): jnp.dot(table, rows, preferred_element_type=jnp.float32)  10.9 us
    dot_general x1, matrix products, body(): jnp.dot(hidden, inner_weights[layer_id], preferred_element_type=jnp.float32)  8.81 us
    dot_general x1, matrix products, body(): jnp.dot(hidden, output_weight, preferred_element_type=jnp.float32)  6.67 us
    ppermute x2, waiting for transfers between devices, padded_2(): lax.ppermute(lax.slice_in_dim(block, 0, width, axis=dim), axis, backward)  6.55 us
    ppermute x2, starting transfers between devices, padded_2(): lax.ppermute(lax.slice_in_dim(block, block.shape[dim] - width, None, axis...  5.92 us
    dot_general x2, matrix products, body(): totals = jnp.dot(weights, row_mask, precision=lax.Precision.HIGHEST)  5.42 us
  transfers between devices with their start and end apart: 4, of which 2 were waited for; matrix products, arithmetic and copies ran while one was open for 1% of the time, Pallas kernels for 0%

profile of v2, /device:TPU:1, one launch (start us, length us, event | category | flops | bytes accessed | tf_op | source)
XLA Modules:
  0.0 179.4 jit_solution(9231750066693235065)
XLA Ops:
  0.0 0.5 broadcast.133
  0.5 1.4 fusion.100
  1.9 0.3 reduce-window.9
  3.1 0.7 slice_reduce_fusion
  3.9 1.1 copy.82
  6.3 1.4 reduce.10
  7.7 8.8 %fusion.29 = f32[4096,512]{1,0:T(8,128)} fusion(bf16[4096,128]{1,0:T(8,128)(2,1)S(1)} %copy-done, bf16[128,512]{1,0:T(8,128)(2,1)} %param.15, bf16[1,512,512]{2,1,0:T(8,128)(2,1)} %param.16), kind=kOutput, calls=%fused_computation.36 | convolution fusion | flops 2694840320 | bytes 10092544 | tf_op jit(solution)/shard_map/dot_general | solution.py:136
  16.6 6.7 %convolution_convert_fusion.1 = bf16[4096,128]{1,0:T(8,128)(2,1)} fusion(bf16[512,128]{1,0:T(8,128)(2,1)S(1)} %copy-done.11, f32[4096,512]{1,0:T(8,128)} %fusion.29), kind=kOutput, calls=%fused_computation.31 | convolution fusion | flops 547880960 | bytes 9568256 | tf_op jit(solution)/shard_map/dot_general | solution.py:138
  23.4 22.7 %while.22 = (s32[]{:T(128)}, bf16[8,512,128]{2,1,0:T(8,128)(2,1)S(1)}, s32[8,512]{1,0:T(8,128)S(1)}, bf16[4096,128]{1,0:T(8,128)(2,1)}, s32[]{:T(128)}) while((s32[]{:T(128)}, bf16[8,512,128]{2,1,0:T(8,128)(2,1)S(1)}, s32[8,512]{1,0:T(8,128)S(1)}, bf16[4096,128]{1,0:T(8,128)(2,1)}, s32[]{:T(128)}) %tuple.50), condition=%wide.region_3.4_spmd.clone, body=%wide.region_2.3_spmd.clone.sunk | while | flops 539033600 | bytes 1185861 | solution.py:90
  23.4 2.8 %fusion.133 = bf16[8,512,128]{2,1,0:T(8,128)(2,1)S(1)} fusion(bf16[8,512,128]{2,1,0:T(8,128)(2,1)S(1)} %get-tuple-element.181, s32[]{:T(128)} %get-tuple-element.180, bf16[4096,128]{1,0:T(8,128)(2,1)} %get-tuple-element.188, s32[512]{0:T(512)S(1)} %bitcast.246), kind=kOutput, calls=%fused_computation.14.clone.1 | convolution fusion | flops 539033600 | bytes 1181700 | tf_op jit(solution)/shard_map/while/body/eval_jaxpr/dot_general | solution.py:88
  26.2 2.8 %fusion.133 = bf16[8,512,128]{2,1,0:T(8,128)(2,1)S(1)} fusion(bf16[8,512,128]{2,1,0:T(8,128)(2,1)S(1)} %get-tuple-element.181, s32[]{:T(128)} %get-tuple-element.180, bf16[4096,128]{1,0:T(8,128)(2,1)} %get-tuple-element.188, s32[512]{0:T(512)S(1)} %bitcast.246), kind=kOutput, calls=%fused_computation.14.clone.1 | convolution fusion | flops 539033600 | bytes 1181700 | tf_op jit(solution)/shard_map/while/body/eval_jaxpr/dot_general | solution.py:88
  29.1 2.8 %fusion.133 = bf16[8,512,128]{2,1,0:T(8,128)(2,1)S(1)} fusion(bf16[8,512,128]{2,1,0:T(8,128)(2,1)S(1)} %get-tuple-element.181, s32[]{:T(128)} %get-tuple-element.180, bf16[4096,128]{1,0:T(8,128)(2,1)} %get-tuple-element.188, s32[512]{0:T(512)S(1)} %bitcast.246), kind=kOutput, calls=%fused_computation.14.clone.1 | convolution fusion | flops 539033600 | bytes 1181700 | tf_op jit(solution)/shard_map/while/body/eval_jaxpr/dot_general | solution.py:88
  31.9 2.8 %fusion.133 = bf16[8,512,128]{2,1,0:T(8,128)(2,1)S(1)} fusion(bf16[8,512,128]{2,1,0:T(8,128)(2,1)S(1)} %get-tuple-element.181, s32[]{:T(128)} %get-tuple-element.180, bf16[4096,128]{1,0:T(8,128)(2,1)} %get-tuple-element.188, s32[512]{0:T(512)S(1)} %bitcast.246), kind=kOutput, calls=%fused_computation.14.clone.1 | convolution fusion | flops 539033600 | bytes 1181700 | tf_op jit(solution)/shard_map/while/body/eval_jaxpr/dot_general | solution.py:88
  34.7 2.8 %fusion.133 = bf16[8,512,128]{2,1,0:T(8,128)(2,1)S(1)} fusion(bf16[8,512,128]{2,1,0:T(8,128)(2,1)S(1)} %get-tuple-element.181, s32[]{:T(128)} %get-tuple-element.180, bf16[4096,128]{1,0:T(8,128)(2,1)} %get-tuple-element.188, s32[512]{0:T(512)S(1)} %bitcast.246), kind=kOutput, calls=%fused_computation.14.clone.1 | convolution fusion | flops 539033600 | bytes 1181700 | tf_op jit(solution)/shard_map/while/body/eval_jaxpr/dot_general | solution.py:88
  37.6 2.8 %fusion.133 = bf16[8,512,128]{2,1,0:T(8,128)(2,1)S(1)} fusion(bf16[8,512,128]{2,1,0:T(8,128)(2,1)S(1)} %get-tuple-element.181, s32[]{:T(128)} %get-tuple-element.180, bf16[4096,128]{1,0:T(8,128)(2,1)} %get-tuple-element.188, s32[512]{0:T(512)S(1)} %bitcast.246), kind=kOutput, calls=%fused_computation.14.clone.1 | convolution fusion | flops 539033600 | bytes 1181700 | tf_op jit(solution)/shard_map/while/body/eval_jaxpr/dot_general | solution.py:88
  40.4 2.8 %fusion.133 = bf16[8,512,128]{2,1,0:T(8,128)(2,1)S(1)} fusion(bf16[8,512,128]{2,1,0:T(8,128)(2,1)S(1)} %get-tuple-element.181, s32[]{:T(128)} %get-tuple-element.180, bf16[4096,128]{1,0:T(8,128)(2,1)} %get-tuple-element.188, s32[512]{0:T(512)S(1)} %bitcast.246), kind=kOutput, calls=%fused_computation.14.clone.1 | convolution fusion | flops 539033600 | bytes 1181700 | tf_op jit(solution)/shard_map/while/body/eval_jaxpr/dot_general | solution.py:88
  43.3 2.8 %fusion.133 = bf16[8,512,128]{2,1,0:T(8,128)(2,1)S(1)} fusion(bf16[8,512,128]{2,1,0:T(8,128)(2,1)S(1)} %get-tuple-element.181, s32[]{:T(128)} %get-tuple-element.180, bf16[4096,128]{1,0:T(8,128)(2,1)} %get-tuple-element.188, s32[512]{0:T(512)S(1)} %bitcast.246), kind=kOutput, calls=%fused_computation.14.clone.1 | convolution fusion | flops 539033600 | bytes 1181700 | tf_op jit(solution)/shard_map/while/body/eval_jaxpr/dot_general | solution.py:88
  46.1 1.7 fusion.36
  47.8 35.5 %shard_map.100 = bf16[128,32,128]{2,1,0:T(8,128)(2,1)} custom-call(bf16[128,32,128]{2,1,0:T(8,128)(2,1)} %bitcast.233), custom_call_target="tpu_custom_call" | custom-call | tf_op jit(solution)/shard_map/pallas_call | solution.py:52
  83.4 0.6 slice_bitcast_fusion.22
  84.1 1.7 multiply_reduce_fusion
  85.9 0.9 copy.79
  86.7 0.9 multiply_reduce_fusion.3
  87.9 1.8 fusion.25
  89.7 1.8 %fusion.24 = f32[128,4096]{1,0:T(8,128)} fusion(bf16[4096,128]{0,1:T(8,128)(2,1)S(1)} %bitcast.229, bf16[128,128]{0,1:T(8,128)(2,1)S(1)} %bitcast.241), kind=kOutput, calls=%fused_computation.26 | convolution fusion | flops 67633152 | bytes 2637824 | tf_op jit(solution)/shard_map/dot_general | solution.py:193
  91.8 2.6 %fusion.79 = f32[128,4]{0,1:T(4,128)S(1)} fusion(f32[128,4096]{1,0:T(8,128)} %fusion.25, s32[4096]{0:T(1024)S(1)} %eq.67), kind=kOutput, calls=%fused_computation.115 | convolution fusion | flops 25182208 | bytes 2115584 | tf_op jit(solution)/shard_map/dot_general | solution.py:199
  94.5 2.2 %convolution_convert_fusion = bf16[4096,128]{1,0:T(8,128)(2,1)} fusion(bf16[4096,128]{1,0:T(8,128)(2,1)S(1)} %bitcast.218, bf16[4,128,128]{2,1,0:T(8,128)(2,1)} %param.21), kind=kOutput, calls=%fused_computation.30 | convolution fusion | flops 134742016 | bytes 2129920 | tf_op jit(solution)/shard_map/dot_general | solution.py:182
  96.6 1.5 copy.81
  98.1 2.8 %fusion.78 = f32[128,4]{0,1:T(4,128)S(1)} fusion(f32[128,4096]{1,0:T(8,128)} %fusion.24, s32[4096]{0:T(1024)S(1)} %eq.67), kind=kOutput, calls=%fused_computation.114 | convolution fusion | flops 25182208 | bytes 2115584 | tf_op jit(solution)/shard_map/dot_general | solution.py:199
  100.9 0.3 broadcast_multiply_fusion
  101.3 0.7 fusion.44
  102.0 0.6 copy-done.2
  102.5 0.7 fusion.43
  103.2 1.0 fusion.39
  104.2 2.8 %collective-permute-start = (bf16[1,2,128,128]{3,2,1,0:T(8,128)(2,1)S(1)}, bf16[1,2,128,128]{3,2,1,0:T(8,128)(2,1)S(1)}, u32[]{:S(2)}, u32[]{:S(2)}) collective-permute-start(bf16[1,2,128,128]{3,2,1,0:T(8,128)(2,1)S(1)} %get-tuple-element.101), channel_id=1, source_target_pairs={{0,4},{4,8},{8,12},{12,16},{16,20},{20,24},{24,28},{28,32},{32,36}... | collective-permute-start | bytes 196616 | tf_op jit(solution)/shard_map/ppermute | solution.py:67
  107.0 1.9 %collective-permute-start.1 = (bf16[1,2,128,128]{3,2,1,0:T(8,128)(2,1)S(1)}, bf16[1,2,128,128]{3,2,1,0:T(8,128)(2,1)S(1)}, u32[]{:S(2)}, u32[]{:S(2)}) collective-permute-start(bf16[1,2,128,128]{3,2,1,0:T(8,128)(2,1)S(1)} %get-tuple-element.102), channel_id=1, source_target_pairs={{4,0},{8,4},{12,8},{16,12},{20,16},{24,20},{28,24},{32,28},{36,32}... | collective-permute-start | bytes 196616 | tf_op jit(solution)/shard_map/ppermute | solution.py:70
  108.9 0.6 slice_bitcast_fusion.20
  109.7 0.5 multiply_reduce_fusion.1
  110.2 2.4 %collective-permute-done.1 = bf16[1,2,128,128]{3,2,1,0:T(8,128)(2,1)S(1)} collective-permute-done((bf16[1,2,128,128]{3,2,1,0:T(8,128)(2,1)S(1)}, bf16[1,2,128,128]{3,2,1,0:T(8,128)(2,1)S(1)}, u32[]{:S(2)}, u32[]{:S(2)}) %collective-permute-start.1) | collective-permute-done | bytes 65568 | tf_op jit(solution)/shard_map/ppermute | solution.py:70
  112.6 0.7 fusion.101
  113.3 3.2 %collective-permute-start.2 = (bf16[4,1,128,128]{3,2,1,0:T(8,128)(2,1)}, bf16[4,1,128,128]{3,2,1,0:T(8,128)(2,1)}, u32[]{:S(2)}, u32[]{:S(2)}) collective-permute-start(bf16[4,1,128,128]{3,2,1,0:T(8,128)(2,1)} %get-tuple-element.98), channel_id=1, source_target_pairs={{0,1},{1,2},{2,3},{4,5},{5,6},{6,7},{8,9},{9,10},{10,11},{12,13},{... | collective-permute-start | bytes 393224 | tf_op jit(solution)/shard_map/ppermute | solution.py:67
  116.5 1.5 collective-permute-start.3
  118.3 4.2 %collective-permute-done.3 = bf16[4,1,128,128]{3,2,1,0:T(8,128)(2,1)} collective-permute-done((bf16[4,1,128,128]{3,2,1,0:T(8,128)(2,1)}, bf16[4,1,128,128]{3,2,1,0:T(8,128)(2,1)}, u32[]{:S(2)}, u32[]{:S(2)}) %collective-permute-start.3) | collective-permute-done | bytes 131104 | tf_op jit(solution)/shard_map/ppermute | solution.py:70
  122.5 1.0 pad_maximum_fusion
  123.7 1.4 fusion.40
  125.1 0.2 multiply_reduce_fusion.2
  125.4 0.2 convolution_convert_fusion.2
  125.6 1.3 fusion.54
  126.9 3.6 %fusion.20 = (f32[4096]{0:T(1024)S(1)}, f32[4096]{0:T(1024)S(1)}, bf16[4096,512]{0,1:T(8,128)(2,1)S(1)}, bf16[4096,512]{0,1:T(8,128)(2,1)S(1)}) fusion(f32[4096,4]{0,1:T(4,128)S(1)} %get-tuple-element.107, f32[4096,512]{0,1:T(8,128)S(1)} %fusion.54, bf16[512,128]{0,1:T(8,128)(2,1)S(1)} %bitcast.238, bf16[4096,128]{0,1:T(8,128)(2,1)S(1)} %bitcast.227), kind=kOutput, calls=%fused_computation.20 | convolution fusion | flops 285204480 | bytes 17465344 | tf_op jit(solution)/shard_map/dot_general | solution.py:242
  130.6 0.8 fusion.27
  131.4 0.8 fusion.28
  132.3 1.5 fusion.26
  133.7 31.7 %shard_map.101 = bf16[128,32,128]{2,1,0:T(8,128)(2,1)} custom-call(bf16[128,32,128]{2,1,0:T(8,128)(2,1)} %bitcast.230), custom_call_target="tpu_custom_call" | custom-call | tf_op jit(solution)/shard_map/pallas_call | solution.py:52
  165.4 1.7 fusion.37
  167.3 11.1 %while.21 = (s32[]{:T(128)}, bf16[8,512,128]{2,1,0:T(8,128)(2,1)S(1)}, s32[8,512]{1,0:T(8,128)S(1)}, s32[1,4096]{1,0:T(1,128)S(1)}, bf16[4096,128]{1,0:T(8,128)(2,1)S(1)}, /*index=5*/s32[]{:T(128)}) while((s32[]{:T(128)}, bf16[8,512,128]{2,1,0:T(8,128)(2,1)S(1)}, s32[8,512]{1,0:T(8,128)S(1)}, s32[1,4096]{1,0:T(1,128)S(1)}, ...), condition=%wide.region_13.14_spmd, body=%wide.region_12.13_spmd.sunk | while | flops 539033600 | bytes 1202253 | solution.py:101
  167.3 1.4 fusion.131
  168.7 1.4 fusion.131
  170.1 1.4 fusion.131
  171.5 1.4 fusion.131
  172.9 1.4 fusion.131
  174.3 1.4 fusion.131
  175.7 1.4 fusion.131
  177.0 1.4 fusion.131
  178.4 1.0 copy-done.4
  (98 shorter events, 4.0 us)
Async XLA Ops:
  0.0 7.7 %copy-start = (bf16[4096,128]{1,0:T(8,128)(2,1)S(1)}, bf16[4096,128]{1,0:T(8,128)(2,1)}, u32[]{:S(2)}) copy-start(bf16[4096,128]{1,0:T(8,128)(2,1)} %param.14) | copy-start | bytes 3145732
  7.7 8.8 %copy-start.11 = (bf16[512,128]{1,0:T(8,128)(2,1)S(1)}, bf16[512,128]{1,0:T(8,128)(2,1)}, u32[]{:S(2)}) copy-start(bf16[512,128]{1,0:T(8,128)(2,1)} %param.17) | copy-start | bytes 393220
  46.1 37.3 %copy-start.7 = (bf16[4,128,128]{2,1,0:T(8,128)(2,1)S(1)}, bf16[4,128,128]{2,1,0:T(8,128)(2,1)}, u32[]{:S(2)}) copy-start(bf16[4,128,128]{2,1,0:T(8,128)(2,1)} %param.21) | copy-start | bytes 393220
  87.7 3.8 %copy-start.8 = (bf16[128,128]{1,0:T(8,128)(2,1)S(1)}, bf16[128,128]{1,0:T(8,128)(2,1)}, u32[]{:S(2)}) copy-start(bf16[128,128]{1,0:T(8,128)(2,1)} %param.20) | copy-start | bytes 98308
  87.9 6.6 %copy-start.1 = (bf16[128,32,128]{2,1,0:T(8,128)(2,1)S(1)}, bf16[128,32,128]{2,1,0:T(8,128)(2,1)}, u32[]{:S(2)}) copy-start(bf16[128,32,128]{2,1,0:T(8,128)(2,1)} %shard_map.100) | copy-start | bytes 3145732
  98.1 3.1 %copy-start.3 = (f32[128,4096]{1,0:T(8,128)S(1)}, f32[128,4096]{1,0:T(8,128)}, u32[]{:S(2)}) copy-start(f32[128,4096]{1,0:T(8,128)} %fusion.25) | copy-start | bytes 6291460
  100.9 1.6 copy-start.2
  101.2 7.7 %copy-start.5 = (bf16[4,128,128]{2,1,0:T(8,128)(2,1)S(1)}, bf16[4,128,128]{2,1,0:T(8,128)(2,1)}, u32[]{:S(2)}) copy-start(bf16[4,128,128]{2,1,0:T(8,128)(2,1)} %param.22) | copy-start | bytes 393220
  104.2 5.9 %collective-permute-start = (bf16[1,2,128,128]{3,2,1,0:T(8,128)(2,1)S(1)}, bf16[1,2,128,128]{3,2,1,0:T(8,128)(2,1)S(1)}, u32[]{:S(2)}, u32[]{:S(2)}) collective-permute-start(bf16[1,2,128,128]{3,2,1,0:T(8,128)(2,1)S(1)} %get-tuple-element.101), channel_id=1, source_target_pairs={{0,4},{4,8},{8,12},{12,16},{16,20},{20,24},{24,28},{28,32},{32,36}... | collective-permute-start | bytes 196616 | tf_op jit(solution)/shard_map/ppermute | solution.py:67
  107.0 5.6 %collective-permute-start.1 = (bf16[1,2,128,128]{3,2,1,0:T(8,128)(2,1)S(1)}, bf16[1,2,128,128]{3,2,1,0:T(8,128)(2,1)S(1)}, u32[]{:S(2)}, u32[]{:S(2)}) collective-permute-start(bf16[1,2,128,128]{3,2,1,0:T(8,128)(2,1)S(1)} %get-tuple-element.102), channel_id=1, source_target_pairs={{4,0},{8,4},{12,8},{16,12},{20,16},{24,20},{28,24},{32,28},{36,32}... | collective-permute-start | bytes 196616 | tf_op jit(solution)/shard_map/ppermute | solution.py:70
  110.2 8.0 %copy-start.9 = (bf16[128,128]{0,1:T(8,128)(2,1)S(1)}, bf16[128,128]{0,1:T(8,128)(2,1)}, u32[]{:S(2)}) copy-start(bf16[128,128]{0,1:T(8,128)(2,1)} %get-tuple-element.99) | copy-start | bytes 98308
  113.3 5.0 %collective-permute-start.2 = (bf16[4,1,128,128]{3,2,1,0:T(8,128)(2,1)}, bf16[4,1,128,128]{3,2,1,0:T(8,128)(2,1)}, u32[]{:S(2)}, u32[]{:S(2)}) collective-permute-start(bf16[4,1,128,128]{3,2,1,0:T(8,128)(2,1)} %get-tuple-element.98), channel_id=1, source_target_pairs={{0,1},{1,2},{2,3},{4,5},{5,6},{6,7},{8,9},{9,10},{10,11},{12,13},{... | collective-permute-start | bytes 393224 | tf_op jit(solution)/shard_map/ppermute | solution.py:67
  116.5 6.0 %collective-permute-start.3 = (bf16[4,1,128,128]{3,2,1,0:T(8,128)(2,1)}, bf16[4,1,128,128]{3,2,1,0:T(8,128)(2,1)}, u32[]{:S(2)}, u32[]{:S(2)}) collective-permute-start(bf16[4,1,128,128]{3,2,1,0:T(8,128)(2,1)} %get-tuple-element.97), channel_id=1, source_target_pairs={{1,0},{2,1},{3,2},{5,4},{6,5},{7,6},{9,8},{10,9},{11,10},{13,12},{... | collective-permute-start | bytes 393224 | tf_op jit(solution)/shard_map/ppermute | solution.py:70
  118.3 7.1 %copy-start.6 = (bf16[4,128,128]{2,1,0:T(8,128)(2,1)S(1)}, bf16[4,128,128]{2,1,0:T(8,128)(2,1)}, u32[]{:S(2)}) copy-start(bf16[4,128,128]{2,1,0:T(8,128)(2,1)} %param.22) | copy-start | bytes 393220
  132.3 35.0 %copy-start.10 = (s32[1,4096]{1,0:T(1,128)S(1)}, s32[1,4096]{1,0:T(1,128)}, u32[]{:S(2)}) copy-start(s32[1,4096]{1,0:T(1,128)} %param.19) | copy-start | bytes 49156
  178.4 1.0 copy-start.4

commit v3 on v2

--- a/solution.py
+++ b/solution.py
@@ -57,6 +57,61 @@
         scratch_shapes=[pltpu.SemaphoreType.DMA((n,)), pltpu.SemaphoreType.DMA((n,)), pltpu.SemaphoreType.DMA],
         compiler_params=pltpu.CompilerParams(has_side_effects=True),
     )(x)
+
+
+def mlp_kernel(x_ref, w1_ref, w2_ref, w3_ref, o_ref):
+    def silu(v):
+        return v / (1.0 + jnp.exp(-v))
+
+    h = silu(jnp.dot(x_ref[...], w1_ref[...], preferred_element_type=jnp.float32))
+    h = h.astype(jnp.bfloat16)
+    for layer_id in range(w2_ref.shape[0]):
+        h = silu(jnp.dot(h, w2_ref[layer_id], preferred_element_type=jnp.float32))
+        h = h.astype(jnp.bfloat16)
+    o_ref[...] = jnp.dot(h, w3_ref[...], preferred_element_type=jnp.float32).astype(o_ref.dtype)
+
+
+def point_mlp(x, w1, w2, w3, block):
+    rows = x.shape[0]
+    full = lambda shape: pl.BlockSpec(shape, lambda i: (0,) * len(shape))
+    return pl.pallas_call(
+        mlp_kernel,
+        out_shape=jax.ShapeDtypeStruct((rows, w3.shape[1]), jnp.bfloat16),
+        grid=(rows // block,),
+        in_specs=[
+            pl.BlockSpec((block, x.shape[1]), lambda i: (i, 0)),
+            full(w1.shape),
+            full(w2.shape),
+            full(w3.shape),
+        ],
+        out_specs=pl.BlockSpec((block, w3.shape[1]), lambda i: (i, 0)),
+    )(x, w1, w2, w3)
+
+
+def permute_kernel(chunk, a_ref, b_ref, x_ref, o_ref):
+    total = jnp.zeros(o_ref.shape, jnp.float32)
+    keys = a_ref[...]
+    for start in range(0, x_ref.shape[0], chunk):
+        hits = (keys == b_ref[:, start : start + chunk]).astype(jnp.bfloat16)
+        total += jnp.dot(hits, x_ref[start : start + chunk, :], preferred_element_type=jnp.float32)
+    o_ref[...] = total.astype(o_ref.dtype)
+
+
+def permute_rows(a, b, x, block, chunk):
+    rows = a.shape[0]
+    a = a.reshape(rows, 1)
+    b = b.reshape(1, -1)
+    return pl.pallas_call(
+        functools.partial(permute_kernel, chunk),
+        out_shape=jax.ShapeDtypeStruct((rows, x.shape[1]), x.dtype),
+        grid=(rows // block,),
+        in_specs=[
+            pl.BlockSpec((block, 1), lambda i: (i, 0)),
+            pl.BlockSpec(b.shape, lambda i: (0, 0)),
+            pl.BlockSpec(x.shape, lambda i: (0, 0)),
+        ],
+        out_specs=pl.BlockSpec((block, x.shape[1]), lambda i: (i, 0)),
+    )(a, b, x)
 
 
 def padded_2(block, sides, width):
@@ -128,16 +183,7 @@
     head_width = width // HEADS
     inducing_count = inducing.shape[0]
 
-    hidden = jax.nn.silu(jnp.dot(points, embed_weight, preferred_element_type=jnp.float32)).astype(
-        jnp.bfloat16
-    )
-    for layer_id in range(inner_weights.shape[0]):
-        hidden = jax.nn.silu(
-            jnp.dot(hidden, inner_weights[layer_id], preferred_element_type=jnp.float32)
-        ).astype(jnp.bfloat16)
-    features = jnp.dot(hidden, output_weight, preferred_element_type=jnp.float32).astype(
-        jnp.bfloat16
-    )
+    features = point_mlp(points, embed_weight, inner_weights, output_weight, 512)
 
     own_counts = lax.dynamic_index_in_dim(counts, own_index, 0, keepdims=False)
     own_offsets = jnp.cumsum(own_counts) - own_counts
@@ -157,12 +203,12 @@
     band_table = (local_pos[:, :, None] == band_ids[None, None, :]).astype(jnp.bfloat16)
 
     order = point_order[0]
-    ordered = gather_rows(order, features, 512).reshape(along_x, band, width)
+    ordered = permute_rows(order, jnp.arange(point_count, dtype=jnp.int32), features, 256, 512).reshape(along_x, band, width)
     outgoing = jnp.einsum(
         "xrp,xpe->xre", band_table, ordered, preferred_element_type=jnp.float32
     ).astype(jnp.bfloat16)
     outgoing = outgoing.reshape(devices, quota, width)
-    arrived = exchange(outgoing, along_x, along_y)
+    arrived = lax.all_to_all(outgoing, ("tx", "ty"), split_axis=0, concat_axis=0, tiled=True)
     all_rows = arrived.reshape(devices * quota, width)
 
     inbound = counts.reshape(devices, along_x, TLX, along_y, TLY)
@@ -258,14 +304,18 @@
         + jnp.dot(second_attended, second_proj[3], preferred_element_type=jnp.float32)
     ).astype(jnp.bfloat16)
 
-    coming = exchange(result.reshape(devices, quota, width), along_x, along_y)
+    coming = lax.all_to_all(
+        result.reshape(devices, quota, width), ("tx", "ty"), split_axis=0, concat_axis=0, tiled=True
+    )
     returned = jnp.einsum(
         "xrp,xre->xpe",
         band_table,
         coming.reshape(along_x, band, width),
         preferred_element_type=jnp.float32,
     ).astype(jnp.bfloat16)
-    return scatter_rows(order, returned.reshape(point_count, width), 512)
+    return permute_rows(
+        jnp.arange(point_count, dtype=jnp.int32), order, returned.reshape(point_count, width), 256, 512
+    )
 
 
 def solution(mesh):

time: 181 us -> 154 us (0.85)
  matrix products: 78.8 us -> 22.4 us
  blocking collectives: 0 us -> 27.2 us
  Pallas kernels: 67.2 us -> 40.6 us
  waiting for transfers between devices: 6.55 us -> 23.6 us
  starting transfers between devices: 9.34 us -> 20 us
  local copies, waits for them, and re-layouts: 12.5 us -> 15.4 us
    dot_general x18 -> x0, matrix products: 48.8 us -> none  [the longest x8 22.5 us: pick_block(): jnp.dot(table, rows, preferred_element_type=jnp.float32)]
    all_to_all x0 -> x1, blocking collectives: none -> 27.2 us  [body(): lax.all_to_all(result.reshape(devices, quota, width), ('tx', 'ty'), split...]
    pallas_call x2 -> x3, Pallas kernels: 67.2 us -> 40.6 us  [the longest x2 30.9 us: permute_rows(): pl.pallas_call(functools.partial(permute_kernel, chunk), out_shape=jax.Sh...]
    all_to_all x0 -> x1, waiting for transfers between devices: none -> 16.4 us  [body(): lax.all_to_all(outgoing, ('tx', 'ty'), split_axis=0, concat_axis=0, tiled...]
    all_to_all x0 -> x1, starting transfers between devices: none -> 11.5 us  [body(): lax.all_to_all(outgoing, ('tx', 'ty'), split_axis=0, concat_axis=0, tiled...]
    dot_general x2, matrix products: 5.42 us -> 2.7 us  [body(): totals = jnp.dot(weights, row_mask, precision=lax.Precision.HIGHEST)]
    another operation x7 -> x5, local copies, waits for them, and re-layouts: 0.75 us -> 3.19 us  [the longest x1 2.71 us: permute_rows(): a = a.reshape(rows, 1)]
    iota x0 -> x2, local copies, waits for them, and re-layouts: none -> 2.09 us  [body(): jnp.arange(point_count, dtype=jnp.int32)]
  transfers between devices with their start and end apart: 4 -> 5, of which waited for: 2 -> 4; matrix products, arithmetic and copies ran while one was open for 1% -> 2% of each run, Pallas kernels for 0% -> 0%
where the time goes in v3:
time: 154 us; the launch traced here: 152 us
  Pallas kernels  40.6 us (26%)
  blocking collectives  27.2 us (18%)
  waiting for transfers between devices  23.6 us (15%)
  matrix products  22.4 us (15%)
  starting transfers between devices  20 us (13%)
  local copies, waits for them, and re-layouts  15.4 us (10%)
  other arithmetic  2.17 us (1%)
    pallas_call x2, Pallas kernels, permute_rows(): pl.pallas_call(functools.partial(permute_kernel, chunk), out_shape=jax.Sh...  30.9 us
    all_to_all x1, blocking collectives, body(): lax.all_to_all(result.reshape(devices, quota, width), ('tx', 'ty'), split...  27.2 us
    all_to_all x1, waiting for transfers between devices, body(): lax.all_to_all(outgoing, ('tx', 'ty'), split_axis=0, concat_axis=0, tiled...  16.4 us
    all_to_all x1, starting transfers between devices, body(): lax.all_to_all(outgoing, ('tx', 'ty'), split_axis=0, concat_axis=0, tiled...  11.5 us
    pallas_call x1, Pallas kernels, point_mlp(): pl.pallas_call(mlp_kernel, out_shape=jax.ShapeDtypeStruct((rows, w3.shape...  9.7 us
    ppermute x2, waiting for transfers between devices, padded_2(): lax.ppermute(lax.slice_in_dim(block, 0, width, axis=dim), axis, backward)  6.91 us
    ppermute x2, starting transfers between devices, padded_2(): lax.ppermute(lax.slice_in_dim(block, block.shape[dim] - width, None, axis...  5.15 us
    dot_general x2, matrix products, body(): jnp.dot(point_queries[:, lower:upper], second_keys[:, lower:upper].T, pre...  4.9 us
  transfers between devices with their start and end apart: 5, of which 4 were waited for; matrix products, arithmetic and copies ran while one was open for 2% of the time, Pallas kernels for 0%

profile of v3, /device:TPU:1, one launch (start us, length us, event | category | flops | bytes accessed | tf_op | source)
XLA Modules:
  0.0 152.0 jit_solution(16892156898619261266)
XLA Ops:
  0.0 0.5 broadcast.121
  0.5 1.4 fusion.74
  1.9 0.3 reduce-window.9
  2.2 0.2 reshape.257
  2.5 0.2 reshape.255
  2.7 0.1 slice_reduce_fusion.1
  3.0 0.1 add_subtract_fusion
  3.1 0.7 slice_reduce_fusion
  3.8 0.1 slice_add_fusion
  3.9 0.1 copy.75
  4.0 0.1 copy.77
  4.2 0.1 add.120
  4.7 0.1 copy.73
  4.9 0.1 lt.51
  5.2 2.7 %copy.79.a_ref = s32[4096,1]{1,0:T(8,128)} copy(s32[4096,1]{0,1:T(1,128)} %bitcast.212) | data formatting | bytes 32768 | tf_op jit(solution)/shard_map/reshape;squeeze | solution.py:102
  7.9 9.7 %shard_map.100.x_ref = bf16[4096,128]{1,0:T(8,128)(2,1)} custom-call(bf16[4096,128]{1,0:T(8,128)(2,1)} %x_ref.1, bf16[128,512]{1,0:T(8,128)(2,1)} %w1_ref.1, bf16[1,512,512]{2,1,0:T(8,128)(2,1)} %w2_ref.1, bf16[512,128]{1,0:T(8,128)(2,1)} %w3_ref.1), custom_call_target="tpu_custom_call" | custom-call | tf_op jit(solution)/shard_map/pallas_call | solution.py:77
  17.6 0.6 iota.30.b_ref
  18.2 15.4 %shard_map.101 = bf16[4096,128]{1,0:T(8,128)(2,1)} custom-call(s32[4096,1]{1,0:T(8,128)} %copy.79.a_ref, s32[1,4096]{1,0:T(1,128)} %iota.30.b_ref, bf16[4096,128]{1,0:T(8,128)(2,1)} %shard_map.100.x_ref), custom_call_target="tpu_custom_call" | custom-call | tf_op jit(solution)/shard_map/pallas_call | solution.py:104
  33.7 3.0 %fusion.13 = bf16[32,128,128]{2,1,0:T(8,128)(2,1)} fusion(bf16[32,128,128]{2,1,0:T(8,128)(2,1)} %bitcast.199, s32[32,128]{1,0:T(8,128)S(1)} %subtract_select_fusion), kind=kOutput, calls=%fused_computation.29 | convolution fusion | flops 135266304 | bytes 2113536 | tf_op jit(solution)/shard_map/xrp,xpe->xre/dot_general | solution.py:207
  36.7 11.5 %all-to-all-start = ((bf16[128,32,128]{2,1,0:T(8,128)(2,1)}), bf16[128,32,128]{2,1,0:T(8,128)(2,1)S(1)}, u32[]{:S(2)}, u32[]{:S(2)}) async-start(bf16[128,32,128]{2,1,0:T(8,128)(2,1)} %bitcast.6), calls=%async_computation | async-start | bytes 2097152 | tf_op jit(solution)/shard_map/all_to_all | solution.py:211
  48.2 0.1 copy.85
  48.4 0.1 copy.83
  48.5 0.1 copy.82
  48.6 0.2 multiply_reduce_fusion.3
  48.9 0.1 copy.86
  49.1 0.7 copy.95
  49.8 0.7 copy.81
  50.6 0.6 fusion.56
  51.2 16.4 %all-to-all-done = bf16[128,32,128]{2,1,0:T(8,128)(2,1)S(1)} async-done(((bf16[128,32,128]{2,1,0:T(8,128)(2,1)}), bf16[128,32,128]{2,1,0:T(8,128)(2,1)S(1)}, u32[]{:S(2)}, u32[]{:S(2)}) %all-to-all-start) | async-done | bytes 1048608 | tf_op jit(solution)/shard_map/all_to_all | solution.py:211
  67.6 0.5 multiply_reduce_fusion
  68.1 0.2 divide_convert_fusion
  68.3 0.5 fusion.5
  68.8 1.2 fusion.4
  70.0 1.7 %fusion.55 = f32[128,4]{0,1:T(4,128)} fusion(f32[128,4096]{1,0:T(8,128)S(1)} %fusion.5, s32[4096]{0:T(1024)S(1)} %eq.35), kind=kOutput, calls=%fused_computation.93 | convolution fusion | flops 25182208 | bytes 2115584 | tf_op jit(solution)/shard_map/dot_general | solution.py:245
  71.7 2.1 %convolution_convert_fusion = bf16[4096,128]{1,0:T(8,128)(2,1)} fusion(bf16[4096,128]{1,0:T(8,128)(2,1)S(1)} %bitcast.185, bf16[4,128,128]{2,1,0:T(8,128)(2,1)} %param.17), kind=kOutput, calls=%fused_computation.12 | convolution fusion | flops 134742016 | bytes 2129920 | tf_op jit(solution)/shard_map/dot_general | solution.py:228
  73.8 2.3 %copy.84 = bf16[4096,128]{0,1:T(8,128)(2,1)} copy(bf16[4096,128]{1,0:T(8,128)(2,1)} %convolution_convert_fusion) | data formatting | bytes 2097152 | tf_op jit(solution)/shard_map/convert_element_type | solution.py:228
  76.1 1.1 fusion.54
  77.2 0.2 copy-done.3
  77.3 0.3 broadcast_multiply_fusion
  77.6 1.3 copy-done.2
  78.9 0.7 fusion.21
  79.7 0.7 fusion.20
  80.4 1.0 fusion.16
  81.4 2.7 %collective-permute-start = (bf16[1,2,128,128]{3,2,1,0:T(8,128)(2,1)S(1)}, bf16[1,2,128,128]{3,2,1,0:T(8,128)(2,1)S(1)}, u32[]{:S(2)}, u32[]{:S(2)}) collective-permute-start(bf16[1,2,128,128]{3,2,1,0:T(8,128)(2,1)S(1)} %get-tuple-element.17), channel_id=1, source_target_pairs={{0,4},{4,8},{8,12},{12,16},{16,20},{20,24},{24,28},{28,32},{32,36}... | collective-permute-start | bytes 196616 | tf_op jit(solution)/shard_map/ppermute | solution.py:122
  84.1 1.9 %collective-permute-start.1 = (bf16[1,2,128,128]{3,2,1,0:T(8,128)(2,1)S(1)}, bf16[1,2,128,128]{3,2,1,0:T(8,128)(2,1)S(1)}, u32[]{:S(2)}, u32[]{:S(2)}) collective-permute-start(bf16[1,2,128,128]{3,2,1,0:T(8,128)(2,1)S(1)} %get-tuple-element.18), channel_id=1, source_target_pairs={{4,0},{8,4},{12,8},{16,12},{20,16},{24,20},{28,24},{32,28},{36,32}... | collective-permute-start | bytes 196616 | tf_op jit(solution)/shard_map/ppermute | solution.py:125
  86.1 0.5 multiply_reduce_fusion.1
  86.6 3.1 %collective-permute-done.1 = bf16[1,2,128,128]{3,2,1,0:T(8,128)(2,1)S(1)} collective-permute-done((bf16[1,2,128,128]{3,2,1,0:T(8,128)(2,1)S(1)}, bf16[1,2,128,128]{3,2,1,0:T(8,128)(2,1)S(1)}, u32[]{:S(2)}, u32[]{:S(2)}) %collective-permute-start.1) | collective-permute-done | bytes 65568 | tf_op jit(solution)/shard_map/ppermute | solution.py:125
  89.8 2.4 %collective-permute-start.2 = (bf16[4,1,128,128]{3,2,1,0:T(8,128)(2,1)S(1)}, bf16[4,1,128,128]{3,2,1,0:T(8,128)(2,1)S(1)}, u32[]{:S(2)}, u32[]{:S(2)}) collective-permute-start(bf16[4,1,128,128]{3,2,1,0:T(8,128)(2,1)S(1)} %get-tuple-element.14), channel_id=1, source_target_pairs={{0,1},{1,2},{2,3},{4,5},{5,6},{6,7},{8,9},{9,10},{10,11},{12,13},{... | collective-permute-start | bytes 393224 | tf_op jit(solution)/shard_map/ppermute | solution.py:122
  92.2 1.5 collective-permute-start.3
  93.7 0.2 divide_convert_fusion.1
  93.9 0.3 collective-permute-done.2
  94.2 3.8 %collective-permute-done.3 = bf16[4,1,128,128]{3,2,1,0:T(8,128)(2,1)S(1)} collective-permute-done((bf16[4,1,128,128]{3,2,1,0:T(8,128)(2,1)S(1)}, bf16[4,1,128,128]{3,2,1,0:T(8,128)(2,1)S(1)}, u32[]{:S(2)}, u32[]{:S(2)}) %collective-permute-start.3) | collective-permute-done | bytes 131104 | tf_op jit(solution)/shard_map/ppermute | solution.py:125
  98.2 0.4 fusion.17
  98.8 0.2 multiply_reduce_fusion.2
  99.0 0.2 convolution_convert_fusion.1
  99.3 1.3 fusion.31
  100.6 3.6 %fusion = (f32[4096]{0:T(1024)S(1)}, f32[4096]{0:T(1024)S(1)}, bf16[4096,512]{0,1:T(8,128)(2,1)S(1)}, bf16[4096,512]{0,1:T(8,128)(2,1)S(1)}) fusion(f32[4096,4]{0,1:T(4,128)S(1)} %get-tuple-element.23, f32[4096,512]{0,1:T(8,128)S(1)} %fusion.31, bf16[512,128]{0,1:T(8,128)(2,1)S(1)} %bitcast.204, bf16[4096,128]{0,1:T(8,128)(2,1)S(1)} %bitcast.194), kind=kOutput, calls=%fused_computation.2 | convolution fusion | flops 285204480 | bytes 17465344 | tf_op jit(solution)/shard_map/dot_general | solution.py:288
  104.2 0.8 fusion.7
  105.0 0.8 fusion.8
  105.9 0.5 fusion.6
  106.4 27.2 %all_to_all.10 = bf16[128,32,128]{2,1,0:T(8,128)(2,1)S(1)} all-to-all(bf16[128,32,128]{2,1,0:T(8,128)(2,1)S(1)} %bitcast.197), channel_id=1, replica_groups=mesh['tx'=32,'ty'=4] {'tx','ty'}, dimensions={0} | all-to-all | bytes 2097152 | tf_op jit(solution)/shard_map/all_to_all | solution.py:307
  133.6 1.5 fusion.14
  135.1 1.5 iota.29.a_ref
  136.6 15.4 %shard_map.102 = bf16[4096,128]{1,0:T(8,128)(2,1)} custom-call(s32[4096,1]{1,0:T(8,128)} %iota.29.a_ref, s32[1,4096]{1,0:T(1,128)} %b_ref.1, bf16[4096,128]{1,0:T(8,128)(2,1)} %bitcast.200), custom_call_target="tpu_custom_call" | custom-call | tf_op jit(solution)/shard_map/pallas_call | solution.py:104
  (72 shorter events, 1.7 us)
Async XLA Ops:
  0.0 98.2 %copy-start = (bf16[8,128,128]{2,1,0:T(8,128)(2,1)S(1)}, bf16[8,128,128]{2,1,0:T(8,128)(2,1)}, u32[]{:S(2)}) copy-start(bf16[8,128,128]{2,1,0:T(8,128)(2,1)} %param.19) | copy-start | bytes 786436
  33.7 3.0 %copy-start.5 = (s32[32,128]{1,0:T(8,128)}, s32[32,128]{1,0:T(8,128)S(1)}, u32[]{:S(2)}) copy-start(s32[32,128]{1,0:T(8,128)S(1)} %subtract_select_fusion) | copy-start | bytes 49156
  33.7 14.5 %copy-start.4 = (s32[128,512]{1,0:T(8,128)S(1)}, s32[128,512]{1,0:T(8,128)}, u32[]{:S(2)}) copy-start(s32[128,512]{1,0:T(8,128)} %param.14) | copy-start | bytes 786436
  33.7 14.6 %copy-start.12 = (bf16[4,128,128]{2,1,0:T(8,128)(2,1)S(1)}, bf16[4,128,128]{2,1,0:T(8,128)(2,1)}, u32[]{:S(2)}) copy-start(bf16[4,128,128]{2,1,0:T(8,128)(2,1)} %param.17) | copy-start | bytes 393220
  33.7 14.9 %copy-start.13 = (bf16[128,128]{1,0:T(8,128)(2,1)S(1)}, bf16[128,128]{1,0:T(8,128)(2,1)}, u32[]{:S(2)}) copy-start(bf16[128,128]{1,0:T(8,128)(2,1)} %param.16) | copy-start | bytes 98308
  36.7 12.4 %copy-start.10 = (bf16[4,128,128]{2,1,0:T(8,128)(2,1)S(1)}, bf16[4,128,128]{2,1,0:T(8,128)(2,1)}, u32[]{:S(2)}) copy-start(bf16[4,128,128]{2,1,0:T(8,128)(2,1)} %param.18) | copy-start | bytes 393220
  36.7 30.9 %all-to-all-start = ((bf16[128,32,128]{2,1,0:T(8,128)(2,1)}), bf16[128,32,128]{2,1,0:T(8,128)(2,1)S(1)}, u32[]{:S(2)}, u32[]{:S(2)}) async-start(bf16[128,32,128]{2,1,0:T(8,128)(2,1)} %bitcast.6), calls=%async_computation | async-start | bytes 2097152 | tf_op jit(solution)/shard_map/all_to_all | solution.py:211
  50.5 17.8 %copy-start.8 = (bf16[128,2,64]{0,2,1:T(8,128)(2,1)}, bf16[128,2,64]{0,2,1:T(8,128)(2,1)S(1)}, u32[]{:S(2)}) copy-start(bf16[128,2,64]{0,2,1:T(8,128)(2,1)S(1)} %divide_convert_fusion.3) | copy-start | bytes 98308
  68.8 2.9 %copy-start.1 = (f32[128,4096]{1,0:T(8,128)}, f32[128,4096]{1,0:T(8,128)S(1)}, u32[]{:S(2)}) copy-start(f32[128,4096]{1,0:T(8,128)S(1)} %fusion.5) | copy-start | bytes 6291460
  76.1 1.2 copy-start.3
  76.1 1.2 copy-start.7
  77.3 1.6 %copy-start.2 = (f32[128,4096]{1,0:T(8,128)S(1)}, f32[128,4096]{1,0:T(8,128)}, u32[]{:S(2)}) copy-start(f32[128,4096]{1,0:T(8,128)} %copy-done.1) | copy-start | bytes 6291460
  77.3 1.6 %copy-start.15 = (f32[128,4]{0,1:T(4,128)S(1)}, f32[128,4]{0,1:T(4,128)}, u32[]{:S(2)}) copy-start(f32[128,4]{0,1:T(4,128)} %fusion.55) | copy-start | bytes 6148
  79.6 6.4 %copy-start.9 = (bf16[128,128]{1,0:T(8,128)(2,1)S(1)}, bf16[128,128]{1,0:T(8,128)(2,1)}, u32[]{:S(2)}) copy-start(bf16[128,128]{1,0:T(8,128)(2,1)} %copy.81) | copy-start | bytes 98308
  81.4 5.2 %collective-permute-start = (bf16[1,2,128,128]{3,2,1,0:T(8,128)(2,1)S(1)}, bf16[1,2,128,128]{3,2,1,0:T(8,128)(2,1)S(1)}, u32[]{:S(2)}, u32[]{:S(2)}) collective-permute-start(bf16[1,2,128,128]{3,2,1,0:T(8,128)(2,1)S(1)} %get-tuple-element.17), channel_id=1, source_target_pairs={{0,4},{4,8},{8,12},{12,16},{16,20},{20,24},{24,28},{28,32},{32,36}... | collective-permute-start | bytes 196616 | tf_op jit(solution)/shard_map/ppermute | solution.py:122
  84.1 5.6 %collective-permute-start.1 = (bf16[1,2,128,128]{3,2,1,0:T(8,128)(2,1)S(1)}, bf16[1,2,128,128]{3,2,1,0:T(8,128)(2,1)S(1)}, u32[]{:S(2)}, u32[]{:S(2)}) collective-permute-start(bf16[1,2,128,128]{3,2,1,0:T(8,128)(2,1)S(1)} %get-tuple-element.18), channel_id=1, source_target_pairs={{4,0},{8,4},{12,8},{16,12},{20,16},{24,20},{28,24},{32,28},{36,32}... | collective-permute-start | bytes 196616 | tf_op jit(solution)/shard_map/ppermute | solution.py:125
  89.8 4.4 %collective-permute-start.2 = (bf16[4,1,128,128]{3,2,1,0:T(8,128)(2,1)S(1)}, bf16[4,1,128,128]{3,2,1,0:T(8,128)(2,1)S(1)}, u32[]{:S(2)}, u32[]{:S(2)}) collective-permute-start(bf16[4,1,128,128]{3,2,1,0:T(8,128)(2,1)S(1)} %get-tuple-element.14), channel_id=1, source_target_pairs={{0,1},{1,2},{2,3},{4,5},{5,6},{6,7},{8,9},{9,10},{10,11},{12,13},{... | collective-permute-start | bytes 393224 | tf_op jit(solution)/shard_map/ppermute | solution.py:122
  92.2 5.7 %collective-permute-start.3 = (bf16[4,1,128,128]{3,2,1,0:T(8,128)(2,1)S(1)}, bf16[4,1,128,128]{3,2,1,0:T(8,128)(2,1)S(1)}, u32[]{:S(2)}, u32[]{:S(2)}) collective-permute-start(bf16[4,1,128,128]{3,2,1,0:T(8,128)(2,1)S(1)} %get-tuple-element.13), channel_id=1, source_target_pairs={{1,0},{2,1},{3,2},{5,4},{6,5},{7,6},{9,8},{10,9},{11,10},{13,12},{... | collective-permute-start | bytes 393224 | tf_op jit(solution)/shard_map/ppermute | solution.py:125
  98.0 0.8 copy-start.14
  98.0 1.0 copy-start.11
  105.9 27.7 %copy-start.6 = (s32[32,128]{1,0:T(8,128)S(1)}, s32[32,128]{1,0:T(8,128)}, u32[]{:S(2)}) copy-start(s32[32,128]{1,0:T(8,128)} %copy-done.5) | copy-start | bytes 49156

commit v4 on v3

--- a/solution.py
+++ b/solution.py
@@ -112,6 +112,70 @@
         ],
         out_specs=pl.BlockSpec((block, x.shape[1]), lambda i: (i, 0)),
     )(a, b, x)
+
+
+def gather_kernel(unroll, pos_ref, order_ref, x_ref, o_ref):
+    def body(step, carry):
+        for lane in range(unroll):
+            row = step * unroll + lane
+            source = order_ref[pos_ref[row]]
+            o_ref[pl.ds(row, 1), :] = x_ref[pl.ds(source, 1), :]
+        return carry
+
+    lax.fori_loop(0, o_ref.shape[0] // unroll, body, 0)
+
+
+def scatter_kernel(unroll, pos_ref, order_ref, x_ref, o_ref):
+    def body(step, carry):
+        for lane in range(unroll):
+            row = step * unroll + lane
+            target = order_ref[pos_ref[row]]
+            o_ref[pl.ds(target, 1), :] = x_ref[pl.ds(row, 1), :]
+        return carry
+
+    lax.fori_loop(0, x_ref.shape[0] // unroll, body, 0)
+
+
+def move_rows(kernel, pos, order, x):
+    return pl.pallas_call(
+        functools.partial(kernel, 8),
+        out_shape=jax.ShapeDtypeStruct(x.shape, x.dtype),
+        in_specs=[
+            pl.BlockSpec(memory_space=pltpu.SMEM),
+            pl.BlockSpec(memory_space=pltpu.SMEM),
+            pl.BlockSpec(memory_space=pltpu.VMEM),
+        ],
+        out_specs=pl.BlockSpec(memory_space=pltpu.VMEM),
+    )(pos, order, x)
+
+
+def halo(block):
+    count_x = lax.axis_size("tx")
+    count_y = lax.axis_size("ty")
+
+    def shift(piece, step_x, step_y):
+        pairs = []
+        for source_x in range(count_x):
+            for source_y in range(count_y):
+                target_x = source_x + step_x
+                target_y = source_y + step_y
+                if 0 <= target_x < count_x and 0 <= target_y < count_y:
+                    pairs.append((source_x * count_y + source_y, target_x * count_y + target_y))
+        return lax.ppermute(piece, ("tx", "ty"), pairs)
+
+    last_x, last_y = block.shape[0] - 1, block.shape[1] - 1
+    low_x = shift(block[last_x:], 1, 0)
+    high_x = shift(block[:1], -1, 0)
+    low_y = shift(block[:, last_y:], 0, 1)
+    high_y = shift(block[:, :1], 0, -1)
+    low_low = shift(block[last_x:, last_y:], 1, 1)
+    low_high = shift(block[last_x:, :1], 1, -1)
+    high_low = shift(block[:1, last_y:], -1, 1)
+    high_high = shift(block[:1, :1], -1, -1)
+    top = jnp.concatenate([low_low, low_x, low_high], axis=1)
+    middle = jnp.concatenate([low_y, block, high_y], axis=1)
+    bottom = jnp.concatenate([high_low, high_x, high_high], axis=1)
+    return jnp.concatenate([top, middle, bottom], axis=0)
 
 
 def padded_2(block, sides, width):
@@ -199,14 +263,10 @@
         first_start[:, :, None] + slot_ids[None, None, :],
         second_start[:, :, None] + slot_ids[None, None, :] - first_len[:, :, None],
     ).reshape(along_x, band)
-    band_ids = jnp.arange(band, dtype=jnp.int32)
-    band_table = (local_pos[:, :, None] == band_ids[None, None, :]).astype(jnp.bfloat16)
-
+    send_pos = (local_pos + band_start).reshape(-1)
     order = point_order[0]
-    ordered = permute_rows(order, jnp.arange(point_count, dtype=jnp.int32), features, 256, 512).reshape(along_x, band, width)
-    outgoing = jnp.einsum(
-        "xrp,xpe->xre", band_table, ordered, preferred_element_type=jnp.float32
-    ).astype(jnp.bfloat16)
+    outgoing = move_rows(gather_kernel, send_pos, order, features.astype(jnp.float32))
+    outgoing = outgoing.astype(jnp.bfloat16)
     outgoing = outgoing.reshape(devices, quota, width)
     arrived = lax.all_to_all(outgoing, ("tx", "ty"), split_axis=0, concat_axis=0, tiled=True)
     all_rows = arrived.reshape(devices * quota, width)
@@ -259,7 +319,7 @@
         )
     ).astype(jnp.bfloat16)
     tile_grid = summary.reshape(TLX, TLY, inducing_count, width)
-    padded = padded_2(tile_grid, (("tx", 0), ("ty", 1)), 1)
+    padded = halo(tile_grid)
     stacked = jnp.stack(
         [
             padded[1 + steps[0] : 1 + steps[0] + TLX, 1 + steps[1] : 1 + steps[1] + TLY]
@@ -307,15 +367,10 @@
     coming = lax.all_to_all(
         result.reshape(devices, quota, width), ("tx", "ty"), split_axis=0, concat_axis=0, tiled=True
     )
-    returned = jnp.einsum(
-        "xrp,xre->xpe",
-        band_table,
-        coming.reshape(along_x, band, width),
-        preferred_element_type=jnp.float32,
-    ).astype(jnp.bfloat16)
-    return permute_rows(
-        jnp.arange(point_count, dtype=jnp.int32), order, returned.reshape(point_count, width), 256, 512
-    )
+    returned = move_rows(
+        scatter_kernel, send_pos, order, coming.reshape(point_count, width).astype(jnp.float32)
+    )
+    return returned.astype(jnp.bfloat16)
 
 
 def solution(mesh):

time: 154 us -> 155 us (level)
  starting transfers between devices: 20 us -> 33 us
  Pallas kernels: 40.6 us -> 29.8 us
  other arithmetic: 2.17 us -> 12.5 us
  waiting for transfers between devices: 23.6 us -> 17.4 us
  local copies, waits for them, and re-layouts: 15.4 us -> 10.5 us
  blocking collectives: 27.2 us -> 30 us
  matrix products: 22.4 us -> 20.4 us
    ppermute x4 -> x8, starting transfers between devices: 8.55 us -> 21.5 us  [shift(): return lax.ppermute(piece, ('tx', 'ty'), pairs)]
    pallas_call x2, Pallas kernels: 30.9 us -> 20.1 us  [move_rows(): pl.pallas_call(functools.partial(kernel, 8), out_shape=jax.ShapeDtypeStru...]
    convert_element_type x0 -> x5, other arithmetic: none -> 9.67 us  [the longest x1 2.71 us: body(): features.astype(jnp.float32)]
    ppermute x4 -> x8, waiting for transfers between devices: 7.17 us -> 0.91 us  [shift(): return lax.ppermute(piece, ('tx', 'ty'), pairs)]
    dot_general x2 -> x0, matrix products: 4.43 us -> none  [the longest x1 2.97 us: body(): jnp.einsum('xrp,xpe->xre', band_table, ordered, preferred_element_type=jn...]
    all_to_all x1, blocking collectives: 27.2 us -> 30 us  [body(): lax.all_to_all(result.reshape(devices, quota, width), ('tx', 'ty'), split...]
    another operation x5 -> x4, local copies, waits for them, and re-layouts: 3.19 us -> 0.47 us  [the longest x1 2.71 us: permute_rows(): a = a.reshape(rows, 1)]
    iota x2 -> x0, local copies, waits for them, and re-layouts: 2.09 us -> none  [body(): jnp.arange(point_count, dtype=jnp.int32)]
  transfers between devices with their start and end apart: 5 -> 9, of which waited for: 4 -> 2; matrix products, arithmetic and copies ran while one was open for 2% -> 2% of each run, Pallas kernels for 0% -> 0%
where the time goes in v4:
time: 155 us; the launch traced here: 154 us
  starting transfers between devices  33 us (21%)
  blocking collectives  30 us (19%)
  Pallas kernels  29.8 us (19%)
  matrix products  20.4 us (13%)
  waiting for transfers between devices  17.4 us (11%)
  other arithmetic  12.5 us (8%)
  local copies, waits for them, and re-layouts  10.5 us (7%)
    all_to_all x1, blocking collectives, body(): lax.all_to_all(result.reshape(devices, quota, width), ('tx', 'ty'), split...  30 us
    ppermute x8, starting transfers between devices, shift(): return lax.ppermute(piece, ('tx', 'ty'), pairs)  21.5 us
    pallas_call x2, Pallas kernels, move_rows(): pl.pallas_call(functools.partial(kernel, 8), out_shape=jax.ShapeDtypeStru...  20.1 us
    all_to_all x1, waiting for transfers between devices, body(): lax.all_to_all(outgoing, ('tx', 'ty'), split_axis=0, concat_axis=0, tiled...  16.5 us
    all_to_all x1, starting transfers between devices, body(): lax.all_to_all(outgoing, ('tx', 'ty'), split_axis=0, concat_axis=0, tiled...  11.5 us
    pallas_call x1, Pallas kernels, point_mlp(): pl.pallas_call(mlp_kernel, out_shape=jax.ShapeDtypeStruct((rows, w3.shape...  9.73 us
    dot_general x2, matrix products, body(): jnp.dot(point_queries[:, lower:upper], second_keys[:, lower:upper].T, pre...  4.91 us
    dot_general x2, matrix products, body(): totals = jnp.dot(weights, row_mask, precision=lax.Precision.HIGHEST)  3.79 us
  transfers between devices with their start and end apart: 9, of which 2 were waited for; matrix products, arithmetic and copies ran while one was open for 2% of the time, Pallas kernels for 0%

profile of v4, /device:TPU:1, one launch (start us, length us, event | category | flops | bytes accessed | tf_op | source)
XLA Modules:
  0.0 154.2 jit_solution(5641631665917479363)
XLA Ops:
  0.0 0.5 broadcast.112
  0.5 1.4 fusion.72
  1.9 0.3 reduce-window.9
  2.3 0.2 reshape.216
  2.5 0.1 slice_reduce_fusion.1
  2.8 0.2 reshape.214
  3.0 0.1 slice_add_fusion
  3.1 0.1 add_subtract_fusion
  3.2 0.7 slice_reduce_fusion
  4.2 0.1 lt.56
  4.5 0.1 copy.53
  4.8 0.1 add.127
  5.2 9.7 %shard_map.100 = bf16[4096,128]{1,0:T(8,128)(2,1)} custom-call(bf16[4096,128]{1,0:T(8,128)(2,1)} %x_ref.1, bf16[128,512]{1,0:T(8,128)(2,1)} %w1_ref.1, bf16[1,512,512]{2,1,0:T(8,128)(2,1)} %w2_ref.1, bf16[512,128]{1,0:T(8,128)(2,1)} %w3_ref.1), custom_call_target="tpu_custom_call" | custom-call | tf_op jit(solution)/shard_map/pallas_call | solution.py:77
  14.9 2.7 %convert_element_type.93.x_ref = f32[4096,128]{1,0:T(8,128)} convert(bf16[4096,128]{1,0:T(8,128)(2,1)} %shard_map.100) | non-fusion elementwise | flops 524288 | bytes 3145728 | tf_op jit(solution)/shard_map/convert_element_type | solution.py:268
  17.6 0.7 fusion.65.pos_ref
  18.3 10.2 %shard_map.101 = f32[4096,128]{1,0:T(8,128)} custom-call(s32[4096]{0:T(1024)} %fusion.65.pos_ref, s32[4096]{0:T(1024)} %bitcast.206, f32[4096,128]{1,0:T(8,128)} %convert_element_type.93.x_ref), custom_call_target="tpu_custom_call" | custom-call | tf_op jit(solution)/shard_map/pallas_call | solution.py:140
  28.5 2.7 %convert_element_type.94 = bf16[4096,128]{1,0:T(8,128)(2,1)} convert(f32[4096,128]{1,0:T(8,128)} %shard_map.101) | non-fusion elementwise | flops 524288 | bytes 3145728 | tf_op jit(solution)/shard_map/convert_element_type | solution.py:269
  31.2 11.5 %all-to-all-start = ((bf16[128,32,128]{2,1,0:T(8,128)(2,1)}), bf16[128,32,128]{2,1,0:T(8,128)(2,1)S(1)}, u32[]{:S(2)}, u32[]{:S(2)}) async-start(bf16[128,32,128]{2,1,0:T(8,128)(2,1)} %bitcast.7), calls=%async_computation | async-start | bytes 2097152 | tf_op jit(solution)/shard_map/all_to_all | solution.py:271
  42.7 0.1 copy.61
  42.9 0.1 copy.58
  43.0 0.1 copy.59
  43.1 0.2 multiply_reduce_fusion.3
  43.4 0.7 copy.64
  44.1 0.7 copy.57
  44.8 0.1 copy.62
  45.0 0.6 fusion.51
  45.7 16.5 %all-to-all-done = bf16[128,32,128]{2,1,0:T(8,128)(2,1)S(1)} async-done(((bf16[128,32,128]{2,1,0:T(8,128)(2,1)}), bf16[128,32,128]{2,1,0:T(8,128)(2,1)S(1)}, u32[]{:S(2)}, u32[]{:S(2)}) %all-to-all-start) | async-done | bytes 1048608 | tf_op jit(solution)/shard_map/all_to_all | solution.py:271
  62.1 0.5 multiply_reduce_fusion
  62.6 0.2 divide_convert_fusion
  62.8 1.8 %fusion.4 = f32[128,4096]{1,0:T(8,128)} fusion(bf16[4096,128]{0,1:T(8,128)(2,1)S(1)} %bitcast.192, bf16[128,128]{0,1:T(8,128)(2,1)S(1)} %bitcast.200), kind=kOutput, calls=%fused_computation.8 | convolution fusion | flops 67633152 | bytes 2637824 | tf_op jit(solution)/shard_map/dot_general | solution.py:299
  64.7 1.2 fusion.5
  65.9 2.1 %convolution_convert_fusion = bf16[4096,128]{1,0:T(8,128)(2,1)} fusion(bf16[4096,128]{1,0:T(8,128)(2,1)S(1)} %bitcast.181, bf16[4,128,128]{2,1,0:T(8,128)(2,1)} %param.17), kind=kOutput, calls=%fused_computation.12 | convolution fusion | flops 134742016 | bytes 2129920 | tf_op jit(solution)/shard_map/dot_general | solution.py:288
  68.0 2.3 %copy.60 = bf16[4096,128]{0,1:T(8,128)(2,1)} copy(bf16[4096,128]{1,0:T(8,128)(2,1)} %convolution_convert_fusion) | data formatting | bytes 2097152 | tf_op jit(solution)/shard_map/convert_element_type | solution.py:288
  70.3 2.7 %fusion.49 = f32[128,4]{0,1:T(4,128)S(1)} fusion(f32[128,4096]{1,0:T(8,128)} %fusion.4, s32[4096]{0:T(1024)S(1)} %eq.19), kind=kOutput, calls=%fused_computation.86 | convolution fusion | flops 25182208 | bytes 2115584 | tf_op jit(solution)/shard_map/dot_general | solution.py:305
  73.0 1.1 fusion.50
  74.1 0.3 broadcast_multiply_fusion
  74.4 1.3 copy-done.1
  75.7 0.7 fusion.14
  76.4 0.7 fusion.15
  77.2 1.0 fusion.11
  78.2 0.5 multiply_reduce_fusion.1
  78.7 2.7 %collective-permute-start.5 = (bf16[1,1,128,128]{3,2,1,0:T(8,128)(2,1)S(1)}, bf16[1,1,128,128]{3,2,1,0:T(8,128)(2,1)S(1)}, u32[]{:S(2)}, u32[]{:S(2)}) collective-permute-start(bf16[1,1,128,128]{3,2,1,0:T(8,128)(2,1)S(1)} %get-tuple-element.15), channel_id=1, source_target_pairs={{4,1},{5,2},{6,3},{8,5},{9,6},{10,7},{12,9},{13,10},{14,11},{16,13... | collective-permute-start | bytes 98312 | tf_op jit(solution)/shard_map/ppermute | solution.py:164
  81.5 1.3 collective-permute-start.7
  82.8 1.3 collective-permute-start.2
  84.1 5.8 %collective-permute-start = (bf16[1,1,128,128]{3,2,1,0:T(8,128)(2,1)S(1)}, bf16[1,1,128,128]{3,2,1,0:T(8,128)(2,1)S(1)}, u32[]{:S(2)}, u32[]{:S(2)}) collective-permute-start(bf16[1,1,128,128]{3,2,1,0:T(8,128)(2,1)S(1)} %get-tuple-element.18), channel_id=1, source_target_pairs={{0,5},{1,6},{2,7},{4,9},{5,10},{6,11},{8,13},{9,14},{10,15},{12,17... | collective-permute-start | bytes 98312 | tf_op jit(solution)/shard_map/ppermute | solution.py:164
  89.9 3.4 %collective-permute-start.3 = (bf16[2,1,128,128]{3,2,1,0:T(8,128)(2,1)S(1)}, bf16[2,1,128,128]{3,2,1,0:T(8,128)(2,1)S(1)}, u32[]{:S(2)}, u32[]{:S(2)}) collective-permute-start(bf16[2,1,128,128]{3,2,1,0:T(8,128)(2,1)S(1)} %get-tuple-element.21), channel_id=1, source_target_pairs={{0,1},{1,2},{2,3},{4,5},{5,6},{6,7},{8,9},{9,10},{10,11},{12,13},{... | collective-permute-start | bytes 196616 | tf_op jit(solution)/shard_map/ppermute | solution.py:164
  93.3 1.3 collective-permute-start.4
  94.6 2.6 %collective-permute-start.6 = (bf16[1,2,128,128]{3,2,1,0:T(8,128)(2,1)S(1)}, bf16[1,2,128,128]{3,2,1,0:T(8,128)(2,1)S(1)}, u32[]{:S(2)}, u32[]{:S(2)}) collective-permute-start(bf16[1,2,128,128]{3,2,1,0:T(8,128)(2,1)S(1)} %get-tuple-element.19), channel_id=1, source_target_pairs={{4,0},{5,1},{6,2},{7,3},{8,4},{9,5},{10,6},{11,7},{12,8},{13,9},{1... | collective-permute-start | bytes 196616 | tf_op jit(solution)/shard_map/ppermute | solution.py:164
  97.2 3.2 %collective-permute-start.1 = (bf16[1,2,128,128]{3,2,1,0:T(8,128)(2,1)S(1)}, bf16[1,2,128,128]{3,2,1,0:T(8,128)(2,1)S(1)}, u32[]{:S(2)}, u32[]{:S(2)}) collective-permute-start(bf16[1,2,128,128]{3,2,1,0:T(8,128)(2,1)S(1)} %get-tuple-element.20), channel_id=1, source_target_pairs={{0,4},{1,5},{2,6},{3,7},{4,8},{5,9},{6,10},{7,11},{8,12},{9,13},{1... | collective-permute-start | bytes 196616 | tf_op jit(solution)/shard_map/ppermute | solution.py:164
  100.4 0.2 divide_convert_fusion.1
  100.6 0.9 collective-permute-done.1
  101.8 0.4 fusion.21
  102.3 0.2 copy-done.8
  102.5 0.2 convolution_convert_fusion.1
  102.7 0.2 multiply_reduce_fusion.2
  103.0 1.3 fusion.25
  104.3 3.6 %fusion = (f32[4096]{0:T(1024)S(1)}, f32[4096]{0:T(1024)S(1)}, bf16[4096,512]{0,1:T(8,128)(2,1)S(1)}, bf16[4096,512]{0,1:T(8,128)(2,1)S(1)}) fusion(f32[4096,4]{0,1:T(4,128)S(1)} %get-tuple-element.27, f32[4096,512]{0,1:T(8,128)S(1)} %fusion.25, bf16[512,128]{0,1:T(8,128)(2,1)S(1)} %bitcast.198, bf16[4096,128]{0,1:T(8,128)(2,1)S(1)} %bitcast.191), kind=kOutput, calls=%fused_computation.2 | convolution fusion | flops 285204480 | bytes 17465344 | tf_op jit(solution)/shard_map/dot_general | solution.py:348
  107.9 0.8 fusion.7
  108.8 0.8 fusion.8
  109.6 0.5 fusion.6
  110.1 30.0 %all_to_all.10 = bf16[128,32,128]{2,1,0:T(8,128)(2,1)S(1)} all-to-all(bf16[128,32,128]{2,1,0:T(8,128)(2,1)S(1)} %bitcast.194), channel_id=1, replica_groups=mesh['tx'=32,'ty'=4] {'tx','ty'}, dimensions={0} | all-to-all | bytes 2097152 | tf_op jit(solution)/shard_map/all_to_all | solution.py:367
  140.1 1.6 %bitcast_convert_fusion.x_ref = f32[4096,128]{1,0:T(8,128)} fusion(bf16[128,32,128]{2,1,0:T(8,128)(2,1)S(1)} %all_to_all.10), kind=kLoop, calls=%fused_computation.36 | loop fusion | flops 524288 | bytes 3145728 | tf_op jit(solution)/shard_map/convert_element_type | solution.py:371
  141.7 9.9 %shard_map.102 = f32[4096,128]{1,0:T(8,128)} custom-call(s32[4096]{0:T(1024)} %fusion.65.pos_ref, s32[4096]{0:T(1024)} %bitcast.207, f32[4096,128]{1,0:T(8,128)} %bitcast_convert_fusion.x_ref), custom_call_target="tpu_custom_call" | custom-call | tf_op jit(solution)/shard_map/pallas_call | solution.py:140
  151.6 2.7 %convert_element_type.120 = bf16[4096,128]{1,0:T(8,128)(2,1)} convert(f32[4096,128]{1,0:T(8,128)} %shard_map.102) | non-fusion elementwise | flops 524288 | bytes 3145728 | tf_op jit(solution)/shard_map/convert_element_type | solution.py:373
  (72 shorter events, 1.9 us)
Async XLA Ops:
  0.0 101.8 %copy-start = (bf16[8,128,128]{2,1,0:T(8,128)(2,1)S(1)}, bf16[8,128,128]{2,1,0:T(8,128)(2,1)}, u32[]{:S(2)}) copy-start(bf16[8,128,128]{2,1,0:T(8,128)(2,1)} %param.19) | copy-start | bytes 786436
  28.5 14.2 %copy-start.3 = (s32[128,512]{1,0:T(8,128)S(1)}, s32[128,512]{1,0:T(8,128)}, u32[]{:S(2)}) copy-start(s32[128,512]{1,0:T(8,128)} %param.14) | copy-start | bytes 786436
  31.2 11.7 %copy-start.10 = (bf16[128,128]{1,0:T(8,128)(2,1)S(1)}, bf16[128,128]{1,0:T(8,128)(2,1)}, u32[]{:S(2)}) copy-start(bf16[128,128]{1,0:T(8,128)(2,1)} %param.16) | copy-start | bytes 98308
  31.2 11.7 %copy-start.9 = (bf16[4,128,128]{2,1,0:T(8,128)(2,1)S(1)}, bf16[4,128,128]{2,1,0:T(8,128)(2,1)}, u32[]{:S(2)}) copy-start(bf16[4,128,128]{2,1,0:T(8,128)(2,1)} %param.17) | copy-start | bytes 393220
  31.2 12.1 %copy-start.7 = (bf16[4,128,128]{2,1,0:T(8,128)(2,1)S(1)}, bf16[4,128,128]{2,1,0:T(8,128)(2,1)}, u32[]{:S(2)}) copy-start(bf16[4,128,128]{2,1,0:T(8,128)(2,1)} %param.18) | copy-start | bytes 393220
  31.2 30.9 %all-to-all-start = ((bf16[128,32,128]{2,1,0:T(8,128)(2,1)}), bf16[128,32,128]{2,1,0:T(8,128)(2,1)S(1)}, u32[]{:S(2)}, u32[]{:S(2)}) async-start(bf16[128,32,128]{2,1,0:T(8,128)(2,1)} %bitcast.7), calls=%async_computation | async-start | bytes 2097152 | tf_op jit(solution)/shard_map/all_to_all | solution.py:271
  45.0 17.8 %copy-start.5 = (bf16[128,2,64]{0,2,1:T(8,128)(2,1)}, bf16[128,2,64]{0,2,1:T(8,128)(2,1)S(1)}, u32[]{:S(2)}) copy-start(bf16[128,2,64]{0,2,1:T(8,128)(2,1)S(1)} %divide_convert_fusion.3) | copy-start | bytes 98308
  70.3 3.8 %copy-start.2 = (bf16[4096,128]{0,1:T(8,128)(2,1)S(1)}, bf16[4096,128]{0,1:T(8,128)(2,1)}, u32[]{:S(2)}) copy-start(bf16[4096,128]{0,1:T(8,128)(2,1)} %copy.60) | copy-start | bytes 3145732
  70.3 3.8 %copy-start.4 = (bf16[4096,4]{0,1:T(4,128)(2,1)S(1)}, bf16[4096,4]{0,1:T(4,128)(2,1)}, u32[]{:S(2)}) copy-start(bf16[4096,4]{0,1:T(4,128)(2,1)} %get-tuple-element.28) | copy-start | bytes 98308
  74.1 1.6 %copy-start.1 = (f32[128,4096]{1,0:T(8,128)S(1)}, f32[128,4096]{1,0:T(8,128)}, u32[]{:S(2)}) copy-start(f32[128,4096]{1,0:T(8,128)} %fusion.4) | copy-start | bytes 6291460
  76.4 1.8 %copy-start.6 = (bf16[128,128]{1,0:T(8,128)(2,1)S(1)}, bf16[128,128]{1,0:T(8,128)(2,1)}, u32[]{:S(2)}) copy-start(bf16[128,128]{1,0:T(8,128)(2,1)} %copy.57) | copy-start | bytes 98308
  78.7 14.6 %collective-permute-start.5 = (bf16[1,1,128,128]{3,2,1,0:T(8,128)(2,1)S(1)}, bf16[1,1,128,128]{3,2,1,0:T(8,128)(2,1)S(1)}, u32[]{:S(2)}, u32[]{:S(2)}) collective-permute-start(bf16[1,1,128,128]{3,2,1,0:T(8,128)(2,1)S(1)} %get-tuple-element.15), channel_id=1, source_target_pairs={{4,1},{5,2},{6,3},{8,5},{9,6},{10,7},{12,9},{13,10},{14,11},{16,13... | collective-permute-start | bytes 98312 | tf_op jit(solution)/shard_map/ppermute | solution.py:164
  81.5 13.1 %collective-permute-start.7 = (bf16[1,1,128,128]{3,2,1,0:T(8,128)(2,1)S(1)}, bf16[1,1,128,128]{3,2,1,0:T(8,128)(2,1)S(1)}, u32[]{:S(2)}, u32[]{:S(2)}) collective-permute-start(bf16[1,1,128,128]{3,2,1,0:T(8,128)(2,1)S(1)} %get-tuple-element.16), channel_id=1, source_target_pairs={{5,0},{6,1},{7,2},{9,4},{10,5},{11,6},{13,8},{14,9},{15,10},{17,12... | collective-permute-start | bytes 98312 | tf_op jit(solution)/shard_map/ppermute | solution.py:164
  82.8 14.4 %collective-permute-start.2 = (bf16[1,1,128,128]{3,2,1,0:T(8,128)(2,1)S(1)}, bf16[1,1,128,128]{3,2,1,0:T(8,128)(2,1)S(1)}, u32[]{:S(2)}, u32[]{:S(2)}) collective-permute-start(bf16[1,1,128,128]{3,2,1,0:T(8,128)(2,1)S(1)} %get-tuple-element.17), channel_id=1, source_target_pairs={{1,4},{2,5},{3,6},{5,8},{6,9},{7,10},{9,12},{10,13},{11,14},{13,16... | collective-permute-start | bytes 98312 | tf_op jit(solution)/shard_map/ppermute | solution.py:164
  84.1 16.5 %collective-permute-start = (bf16[1,1,128,128]{3,2,1,0:T(8,128)(2,1)S(1)}, bf16[1,1,128,128]{3,2,1,0:T(8,128)(2,1)S(1)}, u32[]{:S(2)}, u32[]{:S(2)}) collective-permute-start(bf16[1,1,128,128]{3,2,1,0:T(8,128)(2,1)S(1)} %get-tuple-element.18), channel_id=1, source_target_pairs={{0,5},{1,6},{2,7},{4,9},{5,10},{6,11},{8,13},{9,14},{10,15},{12,17... | collective-permute-start | bytes 98312 | tf_op jit(solution)/shard_map/ppermute | solution.py:164
  89.9 10.7 %collective-permute-start.3 = (bf16[2,1,128,128]{3,2,1,0:T(8,128)(2,1)S(1)}, bf16[2,1,128,128]{3,2,1,0:T(8,128)(2,1)S(1)}, u32[]{:S(2)}, u32[]{:S(2)}) collective-permute-start(bf16[2,1,128,128]{3,2,1,0:T(8,128)(2,1)S(1)} %get-tuple-element.21), channel_id=1, source_target_pairs={{0,1},{1,2},{2,3},{4,5},{5,6},{6,7},{8,9},{9,10},{10,11},{12,13},{... | collective-permute-start | bytes 196616 | tf_op jit(solution)/shard_map/ppermute | solution.py:164
  93.3 7.3 %collective-permute-start.4 = (bf16[2,1,128,128]{3,2,1,0:T(8,128)(2,1)S(1)}, bf16[2,1,128,128]{3,2,1,0:T(8,128)(2,1)S(1)}, u32[]{:S(2)}, u32[]{:S(2)}) collective-permute-start(bf16[2,1,128,128]{3,2,1,0:T(8,128)(2,1)S(1)} %get-tuple-element.22), channel_id=1, source_target_pairs={{1,0},{2,1},{3,2},{5,4},{6,5},{7,6},{9,8},{10,9},{11,10},{13,12},{... | collective-permute-start | bytes 196616 | tf_op jit(solution)/shard_map/ppermute | solution.py:164
  94.6 6.0 %collective-permute-start.6 = (bf16[1,2,128,128]{3,2,1,0:T(8,128)(2,1)S(1)}, bf16[1,2,128,128]{3,2,1,0:T(8,128)(2,1)S(1)}, u32[]{:S(2)}, u32[]{:S(2)}) collective-permute-start(bf16[1,2,128,128]{3,2,1,0:T(8,128)(2,1)S(1)} %get-tuple-element.19), channel_id=1, source_target_pairs={{4,0},{5,1},{6,2},{7,3},{8,4},{9,5},{10,6},{11,7},{12,8},{13,9},{1... | collective-permute-start | bytes 196616 | tf_op jit(solution)/shard_map/ppermute | solution.py:164
  97.2 4.3 %collective-permute-start.1 = (bf16[1,2,128,128]{3,2,1,0:T(8,128)(2,1)S(1)}, bf16[1,2,128,128]{3,2,1,0:T(8,128)(2,1)S(1)}, u32[]{:S(2)}, u32[]{:S(2)}) collective-permute-start(bf16[1,2,128,128]{3,2,1,0:T(8,128)(2,1)S(1)} %get-tuple-element.20), channel_id=1, source_target_pairs={{0,4},{1,5},{2,6},{3,7},{4,8},{5,9},{6,10},{7,11},{8,12},{9,13},{1... | collective-permute-start | bytes 196616 | tf_op jit(solution)/shard_map/ppermute | solution.py:164
  101.6 0.9 copy-start.8
  101.7 1.1 copy-start.11

commit v5 on v4

--- a/solution.py
+++ b/solution.py
@@ -114,68 +114,123 @@
     )(a, b, x)
 
 
-def gather_kernel(unroll, pos_ref, order_ref, x_ref, o_ref):
+def gather_kernel(unroll, pos_ref, order_ref, x_ref, o_ref, rows_in, rows_out):
+    rows_in[...] = x_ref[...].astype(jnp.float32)
+
     def body(step, carry):
         for lane in range(unroll):
             row = step * unroll + lane
             source = order_ref[pos_ref[row]]
-            o_ref[pl.ds(row, 1), :] = x_ref[pl.ds(source, 1), :]
+            rows_out[pl.ds(row, 1), :] = rows_in[pl.ds(source, 1), :]
         return carry
 
     lax.fori_loop(0, o_ref.shape[0] // unroll, body, 0)
-
-
-def scatter_kernel(unroll, pos_ref, order_ref, x_ref, o_ref):
+    o_ref[...] = rows_out[...].astype(o_ref.dtype)
+
+
+def scatter_kernel(unroll, pos_ref, order_ref, x_ref, o_ref, rows_in, rows_out):
+    rows_in[...] = x_ref[...].astype(jnp.float32)
+
     def body(step, carry):
         for lane in range(unroll):
             row = step * unroll + lane
             target = order_ref[pos_ref[row]]
-            o_ref[pl.ds(target, 1), :] = x_ref[pl.ds(row, 1), :]
+            rows_out[pl.ds(target, 1), :] = rows_in[pl.ds(row, 1), :]
         return carry
 
     lax.fori_loop(0, x_ref.shape[0] // unroll, body, 0)
+    o_ref[...] = rows_out[...].astype(o_ref.dtype)
 
 
 def move_rows(kernel, pos, order, x):
     return pl.pallas_call(
         functools.partial(kernel, 8),
-        out_shape=jax.ShapeDtypeStruct(x.shape, x.dtype),
+        out_shape=jax.ShapeDtypeStruct(x.shape, jnp.bfloat16),
         in_specs=[
             pl.BlockSpec(memory_space=pltpu.SMEM),
             pl.BlockSpec(memory_space=pltpu.SMEM),
             pl.BlockSpec(memory_space=pltpu.VMEM),
         ],
         out_specs=pl.BlockSpec(memory_space=pltpu.VMEM),
+        scratch_shapes=[pltpu.VMEM(x.shape, jnp.float32), pltpu.VMEM(x.shape, jnp.float32)],
     )(pos, order, x)
+
+
+def halo_kernel(count_x, count_y, x_ref, o_ref, send_sem, recv_sem, local_sem):
+    index_x = lax.axis_index("tx")
+    index_y = lax.axis_index("ty")
+    size_x, size_y = x_ref.shape[0], x_ref.shape[1]
+    mesh_ids = pl.DeviceIdType.MESH
+    steps = [(a, b) for a in (-1, 0, 1) for b in (-1, 0, 1) if (a, b) != (0, 0)]
+
+    def inside(px, py):
+        return (px >= 0) & (px < count_x) & (py >= 0) & (py < count_y)
+
+    def ranges(step, size):
+        if step == 1:
+            return pl.ds(size - 1, 1), pl.ds(0, 1)
+        if step == -1:
+            return pl.ds(0, 1), pl.ds(size + 1, 1)
+        return pl.ds(0, size), pl.ds(1, size)
+
+    barrier = pltpu.get_barrier_semaphore()
+    for a, b in steps:
+        @pl.when(inside(index_x + a, index_y + b))
+        def _():
+            pl.semaphore_signal(
+                barrier, 1, device_id=(index_x + a, index_y + b), device_id_type=mesh_ids
+            )
+    peers = sum(inside(index_x + a, index_y + b).astype(jnp.int32) for a, b in steps)
+    pl.semaphore_wait(barrier, peers)
+
+    center = pltpu.make_async_copy(
+        x_ref, o_ref.at[pl.ds(1, size_x), pl.ds(1, size_y)], local_sem
+    )
+    center.start()
+    copies = []
+    for k, (a, b) in enumerate(steps):
+        source_x, target_x = ranges(a, size_x)
+        source_y, target_y = ranges(b, size_y)
+        copy = pltpu.make_async_remote_copy(
+            src_ref=x_ref.at[source_x, source_y],
+            dst_ref=o_ref.at[target_x, target_y],
+            send_sem=send_sem.at[k],
+            recv_sem=recv_sem.at[k],
+            device_id=(index_x + a, index_y + b),
+            device_id_type=mesh_ids,
+        )
+        copies.append(copy)
+        pl.when(inside(index_x + a, index_y + b))(copy.start)
+    for k, (a, b) in enumerate(steps):
+        source_x, target_x = ranges(a, size_x)
+        source_y, target_y = ranges(b, size_y)
+
+        @pl.when(jnp.logical_not(inside(index_x - a, index_y - b)))
+        def _():
+            piece = o_ref.at[target_x, target_y]
+            piece[...] = jnp.zeros(piece.shape, piece.dtype)
+    for k, (a, b) in enumerate(steps):
+        pl.when(inside(index_x + a, index_y + b))(copies[k].wait_send)
+        pl.when(inside(index_x - a, index_y - b))(copies[k].wait_recv)
+    center.wait()
 
 
 def halo(block):
     count_x = lax.axis_size("tx")
     count_y = lax.axis_size("ty")
-
-    def shift(piece, step_x, step_y):
-        pairs = []
-        for source_x in range(count_x):
-            for source_y in range(count_y):
-                target_x = source_x + step_x
-                target_y = source_y + step_y
-                if 0 <= target_x < count_x and 0 <= target_y < count_y:
-                    pairs.append((source_x * count_y + source_y, target_x * count_y + target_y))
-        return lax.ppermute(piece, ("tx", "ty"), pairs)
-
-    last_x, last_y = block.shape[0] - 1, block.shape[1] - 1
-    low_x = shift(block[last_x:], 1, 0)
-    high_x = shift(block[:1], -1, 0)
-    low_y = shift(block[:, last_y:], 0, 1)
-    high_y = shift(block[:, :1], 0, -1)
-    low_low = shift(block[last_x:, last_y:], 1, 1)
-    low_high = shift(block[last_x:, :1], 1, -1)
-    high_low = shift(block[:1, last_y:], -1, 1)
-    high_high = shift(block[:1, :1], -1, -1)
-    top = jnp.concatenate([low_low, low_x, low_high], axis=1)
-    middle = jnp.concatenate([low_y, block, high_y], axis=1)
-    bottom = jnp.concatenate([high_low, high_x, high_high], axis=1)
-    return jnp.concatenate([top, middle, bottom], axis=0)
+    shape = (block.shape[0] + 2, block.shape[1] + 2) + block.shape[2:]
+    return pl.pallas_call(
+        functools.partial(halo_kernel, count_x, count_y),
+        out_shape=jax.ShapeDtypeStruct(shape, block.dtype),
+        in_specs=[pl.BlockSpec(memory_space=pltpu.VMEM)],
+        out_specs=pl.BlockSpec(memory_space=pltpu.VMEM),
+        scratch_shapes=[
+            pltpu.SemaphoreType.DMA((8,)),
+            pltpu.SemaphoreType.DMA((8,)),
+            pltpu.SemaphoreType.DMA,
+        ],
+        compiler_params=pltpu.CompilerParams(collective_id=0, has_side_effects=True),
+    )(block)
 
 
 def padded_2(block, sides, width):
@@ -265,8 +320,7 @@
     ).reshape(along_x, band)
     send_pos = (local_pos + band_start).reshape(-1)
     order = point_order[0]
-    outgoing = move_rows(gather_kernel, send_pos, order, features.astype(jnp.float32))
-    outgoing = outgoing.astype(jnp.bfloat16)
+    outgoing = move_rows(gather_kernel, send_pos, order, features)
     outgoing = outgoing.reshape(devices, quota, width)
     arrived = lax.all_to_all(outgoing, ("tx", "ty"), split_axis=0, concat_axis=0, tiled=True)
     all_rows = arrived.reshape(devices * quota, width)
@@ -368,9 +422,9 @@
         result.reshape(devices, quota, width), ("tx", "ty"), split_axis=0, concat_axis=0, tiled=True
     )
     returned = move_rows(
-        scatter_kernel, send_pos, order, coming.reshape(point_count, width).astype(jnp.float32)
-    )
-    return returned.astype(jnp.bfloat16)
+        scatter_kernel, send_pos, order, coming.reshape(point_count, width)
+    )
+    return returned
 
 
 def solution(mesh):

time: 155 us -> 134 us (0.86)
  starting transfers between devices: 33 us -> 11.5 us
  other arithmetic: 12.5 us -> 3.34 us
  local copies, waits for them, and re-layouts: 10.5 us -> 17.8 us
  Pallas kernels: 29.8 us -> 36.3 us
  blocking collectives: 30 us -> 25.3 us
  matrix products: 20.4 us -> 22.3 us
    ppermute x8 -> x0, starting transfers between devices: 21.5 us -> none  [shift(): return lax.ppermute(piece, ('tx', 'ty'), pairs)]
    convert_element_type x4 -> x0, other arithmetic: 9.63 us -> none  [the longest x1 2.71 us: body(): features.astype(jnp.float32)]
    pallas_call x0 -> x1, Pallas kernels: none -> 7.31 us  [halo(): pl.pallas_call(functools.partial(halo_kernel, count_x, count_y), out_shap...]
    unnamed x30 -> x38, local copies, waits for them, and re-layouts: 1.74 us -> 8.2 us
    all_to_all x1, blocking collectives: 30 us -> 25.3 us  [body(): lax.all_to_all(result.reshape(devices, quota, width), ('tx', 'ty'), split...]
  transfers between devices with their start and end apart: 9 -> 1, of which waited for: 2 -> 1; matrix products, arithmetic and copies ran while one was open for 2% -> 2% of each run, Pallas kernels for 0% -> 0%
where the time goes in v5:
time: 134 us; the launch traced here: 133 us
  Pallas kernels  36.3 us (27%)
  blocking collectives  25.3 us (19%)
  matrix products  22.3 us (17%)
  local copies, waits for them, and re-layouts  17.8 us (13%)
  waiting for transfers between devices  16.5 us (12%)
  starting transfers between devices  11.5 us (9%)
  other arithmetic  3.34 us (2%)
    all_to_all x1, blocking collectives, body(): lax.all_to_all(result.reshape(devices, quota, width), ('tx', 'ty'), split...  25.3 us
    pallas_call x2, Pallas kernels, move_rows(): pl.pallas_call(functools.partial(kernel, 8), out_shape=jax.ShapeDtypeStru...  19.3 us
    all_to_all x1, waiting for transfers between devices, body(): lax.all_to_all(outgoing, ('tx', 'ty'), split_axis=0, concat_axis=0, tiled...  16.5 us
    all_to_all x1, starting transfers between devices, body(): lax.all_to_all(outgoing, ('tx', 'ty'), split_axis=0, concat_axis=0, tiled...  11.5 us
    pallas_call x1, Pallas kernels, point_mlp(): pl.pallas_call(mlp_kernel, out_shape=jax.ShapeDtypeStruct((rows, w3.shape...  9.7 us
    unnamed x38, local copies, waits for them, and re-layouts  8.2 us
    pallas_call x1, Pallas kernels, halo(): pl.pallas_call(functools.partial(halo_kernel, count_x, count_y), out_shap...  7.31 us
    dot_general x2, matrix products, body(): jnp.dot(point_queries[:, lower:upper], second_keys[:, lower:upper].T, pre...  4.92 us
  transfers between devices with their start and end apart: 1, of which 1 were waited for; matrix products, arithmetic and copies ran while one was open for 2% of the time, Pallas kernels for 0%

profile of v5, /device:TPU:1, one launch (start us, length us, event | category | flops | bytes accessed | tf_op | source)
XLA Modules:
  0.0 133.5 jit_solution(6854056170948655284)
XLA Ops:
  0.0 0.5 broadcast.112
  0.5 1.4 %fusion.62 = (s32[512]{0:T(512)S(1)}, s32[1,512]{1,0:T(1,128)S(1)}) fusion(s32[]{:T(128)} %broadcast.112, s32[128,512]{1,0:T(8,128)} %param.14, s32[]{:T(128)S(6)} %select_n.22), kind=kLoop, calls=%fused_computation.115 | loop fusion | bytes 6152 | tf_op jit(solution)/shard_map/jit(dynamic_index_in_dim)/dynamic_slice | solution.py:307
  1.9 0.3 reduce-window.9
  2.3 0.2 reshape.214
  2.5 0.1 slice_reduce_fusion.1
  2.8 0.2 reshape.212
  3.0 0.1 slice_add_fusion
  3.1 0.1 add_subtract_fusion
  3.2 0.7 slice_reduce_fusion
  4.0 0.1 copy.51
  4.2 0.1 lt.56
  4.3 0.1 lt.57
  4.4 0.1 copy.55
  4.5 0.1 copy.53
  4.8 0.1 add.127
  4.9 0.1 add.128
  5.2 0.7 fusion.55.pos_ref
  5.9 9.7 %shard_map.100.x_ref = bf16[4096,128]{1,0:T(8,128)(2,1)} custom-call(bf16[4096,128]{1,0:T(8,128)(2,1)} %x_ref.1, bf16[128,512]{1,0:T(8,128)(2,1)} %w1_ref.1, bf16[1,512,512]{2,1,0:T(8,128)(2,1)} %w2_ref.1, bf16[512,128]{1,0:T(8,128)(2,1)} %w3_ref.1), custom_call_target="tpu_custom_call" | custom-call | tf_op jit(solution)/shard_map/pallas_call | solution.py:77
  15.6 9.8 %shard_map.101 = bf16[4096,128]{1,0:T(8,128)(2,1)} custom-call(s32[4096]{0:T(1024)} %fusion.55.pos_ref, s32[4096]{0:T(1024)} %bitcast.182, bf16[4096,128]{1,0:T(8,128)(2,1)} %shard_map.100.x_ref), custom_call_target="tpu_custom_call" | custom-call | tf_op jit(solution)/shard_map/pallas_call | solution.py:146
  25.4 11.5 %all-to-all-start = ((bf16[128,32,128]{2,1,0:T(8,128)(2,1)}), bf16[128,32,128]{2,1,0:T(8,128)(2,1)S(1)}, u32[]{:S(2)}, u32[]{:S(2)}) async-start(bf16[128,32,128]{2,1,0:T(8,128)(2,1)} %bitcast.167), calls=%async_computation | async-start | bytes 2097152 | tf_op jit(solution)/shard_map/all_to_all | solution.py:325
  36.9 0.1 copy.61
  37.1 0.1 copy.58
  37.2 0.1 copy.59
  37.4 0.2 multiply_reduce_fusion.3
  37.6 0.7 copy.64
  38.3 0.7 copy.57
  39.1 0.1 copy.62
  39.3 0.6 fusion.41
  39.9 16.5 %all-to-all-done = bf16[128,32,128]{2,1,0:T(8,128)(2,1)S(1)} async-done(((bf16[128,32,128]{2,1,0:T(8,128)(2,1)}), bf16[128,32,128]{2,1,0:T(8,128)(2,1)S(1)}, u32[]{:S(2)}, u32[]{:S(2)}) %all-to-all-start) | async-done | bytes 1048608 | tf_op jit(solution)/shard_map/all_to_all | solution.py:325
  56.4 0.5 multiply_reduce_fusion
  56.9 0.2 divide_convert_fusion
  57.1 1.8 %fusion.4 = f32[128,4096]{1,0:T(8,128)} fusion(bf16[4096,128]{0,1:T(8,128)(2,1)S(1)} %bitcast.164, bf16[128,128]{0,1:T(8,128)(2,1)S(1)} %bitcast.176), kind=kOutput, calls=%fused_computation.8 | convolution fusion | flops 67633152 | bytes 2637824 | tf_op jit(solution)/shard_map/dot_general | solution.py:353
  58.8 1.2 fusion.5
  60.0 2.1 %convolution_convert_fusion = bf16[4096,128]{1,0:T(8,128)(2,1)} fusion(bf16[4096,128]{1,0:T(8,128)(2,1)S(1)} %bitcast.159, bf16[4,128,128]{2,1,0:T(8,128)(2,1)} %param.17), kind=kOutput, calls=%fused_computation.12 | convolution fusion | flops 134742016 | bytes 2129920 | tf_op jit(solution)/shard_map/dot_general | solution.py:342
  62.2 2.3 %copy.60 = bf16[4096,128]{0,1:T(8,128)(2,1)} copy(bf16[4096,128]{1,0:T(8,128)(2,1)} %convolution_convert_fusion) | data formatting | bytes 2097152 | tf_op jit(solution)/shard_map/convert_element_type | solution.py:342
  64.4 2.6 %fusion.39 = f32[128,4]{0,1:T(4,128)S(1)} fusion(f32[128,4096]{1,0:T(8,128)} %fusion.4, s32[4096]{0:T(1024)S(1)} %eq.19), kind=kOutput, calls=%fused_computation.71 | convolution fusion | flops 25182208 | bytes 2115584 | tf_op jit(solution)/shard_map/dot_general | solution.py:359
  67.1 1.1 fusion.40
  68.2 1.8 %multiply_reduce_fusion.1 = (f32[4096,2]{0,1:T(2,128)S(1)}, f32[4096,2,64]{0,2,1:T(8,128)}) fusion(bf16[4096,128,1]{1,0,2:T(8,128)(2,1)S(1)} %bitcast.160, bf16[2,64,128]{2,1,0:T(8,128)(2,1)S(1)} %bitcast.178), kind=kOutput, calls=%fused_computation.25 | convolution fusion | flops 135258112 | bytes 3211264 | tf_op jit(solution)/shard_map/dot_general | solution.py:389
  70.0 0.6 add_sqrt_fusion.1
  70.6 0.3 broadcast_multiply_fusion
  70.9 1.3 copy-done.1
  72.2 0.7 fusion.14
  73.0 0.7 fusion.15
  73.7 1.6 %fusion.11 = bf16[4,128,128]{2,1,0:T(8,128)(2,1)} fusion(bf16[128,4,64]{0,2,1:T(8,128)(2,1)S(1)} %fusion.14, bf16[128,4,64]{0,2,1:T(8,128)(2,1)S(1)} %fusion.15, f32[128,128]{1,0:T(8,128)S(1)} %convert_element_type.82, bf16[4,128,128]{2,1,0:T(8,128)(2,1)} %param.17), kind=kOutput, calls=%fused_computation.27 | convolution fusion | flops 17170432 | bytes 360448 | tf_op jit(solution)/shard_map/tic,ce->tie/dot_general | solution.py:371
  75.3 7.3 %shard_map.102 = bf16[4,4,128,128]{3,2,1,0:T(8,128)(2,1)} custom-call(bf16[2,2,128,128]{3,2,1,0:T(8,128)(2,1)} %bitcast.169), custom_call_target="tpu_custom_call" | custom-call | tf_op jit(solution)/shard_map/pallas_call | solution.py:222
  82.7 1.0 bitcast_dynamic-update-slice_fusion.7
  83.6 1.0 bitcast_dynamic-update-slice_fusion.6
  84.6 0.9 bitcast_dynamic-update-slice_fusion.5
  85.5 0.9 bitcast_dynamic-update-slice_fusion.4
  86.5 1.1 bitcast_dynamic-update-slice_fusion.3
  87.6 0.9 bitcast_dynamic-update-slice_fusion.2
  88.5 0.9 bitcast_dynamic-update-slice_fusion.1
  89.4 0.9 bitcast_dynamic-update-slice_fusion
  90.4 0.4 fusion.21
  90.9 0.2 convolution_convert_fusion.1
  91.1 0.2 multiply_reduce_fusion.2
  91.4 0.2 divide_convert_fusion.1
  91.6 1.3 fusion.25
  92.9 3.6 %fusion = (f32[4096]{0:T(1024)S(1)}, f32[4096]{0:T(1024)S(1)}, bf16[4096,512]{0,1:T(8,128)(2,1)S(1)}, bf16[4096,512]{0,1:T(8,128)(2,1)S(1)}) fusion(f32[4096,4]{0,1:T(4,128)S(1)} %get-tuple-element.17, f32[4096,512]{0,1:T(8,128)S(1)} %fusion.25, bf16[512,128]{0,1:T(8,128)(2,1)S(1)} %bitcast.174, bf16[4096,128]{0,1:T(8,128)(2,1)S(1)} %bitcast.163), kind=kOutput, calls=%fused_computation.2 | convolution fusion | flops 285204480 | bytes 17465344 | tf_op jit(solution)/shard_map/dot_general | solution.py:402
  96.5 0.8 fusion.7
  97.4 0.8 fusion.8
  98.2 0.5 fusion.6
  98.7 25.3 %all_to_all.10 = bf16[128,32,128]{2,1,0:T(8,128)(2,1)} all-to-all(bf16[128,32,128]{2,1,0:T(8,128)(2,1)S(1)} %bitcast.166), channel_id=1, replica_groups=mesh['tx'=32,'ty'=4] {'tx','ty'}, dimensions={0} | all-to-all | bytes 2097152 | tf_op jit(solution)/shard_map/all_to_all | solution.py:421
  124.0 9.4 %shard_map.103 = bf16[4096,128]{1,0:T(8,128)(2,1)} custom-call(s32[4096]{0:T(1024)} %fusion.55.pos_ref, s32[4096]{0:T(1024)} %bitcast.183, bf16[4096,128]{1,0:T(8,128)(2,1)} %bitcast.168), custom_call_target="tpu_custom_call" | custom-call | tf_op jit(solution)/shard_map/pallas_call | solution.py:146
  (55 shorter events, 1.2 us)
Async XLA Ops:
  0.0 90.4 %copy-start = (bf16[8,128,128]{2,1,0:T(8,128)(2,1)S(1)}, bf16[8,128,128]{2,1,0:T(8,128)(2,1)}, u32[]{:S(2)}) copy-start(bf16[8,128,128]{2,1,0:T(8,128)(2,1)} %param.19) | copy-start | bytes 786436
  15.6 21.4 %copy-start.5 = (s32[128,512]{1,0:T(8,128)S(1)}, s32[128,512]{1,0:T(8,128)}, u32[]{:S(2)}) copy-start(s32[128,512]{1,0:T(8,128)} %param.14) | copy-start | bytes 786436
  15.6 21.5 %copy-start.13 = (bf16[128,128]{1,0:T(8,128)(2,1)S(1)}, bf16[128,128]{1,0:T(8,128)(2,1)}, u32[]{:S(2)}) copy-start(bf16[128,128]{1,0:T(8,128)(2,1)} %param.16) | copy-start | bytes 98308
  15.6 21.5 %copy-start.12 = (bf16[4,128,128]{2,1,0:T(8,128)(2,1)S(1)}, bf16[4,128,128]{2,1,0:T(8,128)(2,1)}, u32[]{:S(2)}) copy-start(bf16[4,128,128]{2,1,0:T(8,128)(2,1)} %param.17) | copy-start | bytes 393220
  25.4 12.1 %copy-start.10 = (bf16[4,128,128]{2,1,0:T(8,128)(2,1)S(1)}, bf16[4,128,128]{2,1,0:T(8,128)(2,1)}, u32[]{:S(2)}) copy-start(bf16[4,128,128]{2,1,0:T(8,128)(2,1)} %param.18) | copy-start | bytes 393220
  25.4 30.9 %all-to-all-start = ((bf16[128,32,128]{2,1,0:T(8,128)(2,1)}), bf16[128,32,128]{2,1,0:T(8,128)(2,1)S(1)}, u32[]{:S(2)}, u32[]{:S(2)}) async-start(bf16[128,32,128]{2,1,0:T(8,128)(2,1)} %bitcast.167), calls=%async_computation | async-start | bytes 2097152 | tf_op jit(solution)/shard_map/all_to_all | solution.py:325
  39.3 17.8 %copy-start.7 = (bf16[128,2,64]{0,2,1:T(8,128)(2,1)}, bf16[128,2,64]{0,2,1:T(8,128)(2,1)S(1)}, u32[]{:S(2)}) copy-start(bf16[128,2,64]{0,2,1:T(8,128)(2,1)S(1)} %divide_convert_fusion.3) | copy-start | bytes 98308
  64.4 3.7 %copy-start.8 = (bf16[128,128]{1,0:T(8,128)(2,1)S(1)}, bf16[128,128]{1,0:T(8,128)(2,1)}, u32[]{:S(2)}) copy-start(bf16[128,128]{1,0:T(8,128)(2,1)} %copy.57) | copy-start | bytes 98308
  68.2 2.5 %copy-start.3 = (bf16[4096,128]{0,1:T(8,128)(2,1)S(1)}, bf16[4096,128]{0,1:T(8,128)(2,1)}, u32[]{:S(2)}) copy-start(bf16[4096,128]{0,1:T(8,128)(2,1)} %copy.60) | copy-start | bytes 3145732
  68.2 2.5 %copy-start.6 = (bf16[4096,4]{0,1:T(4,128)(2,1)S(1)}, bf16[4096,4]{0,1:T(4,128)(2,1)}, u32[]{:S(2)}) copy-start(bf16[4096,4]{0,1:T(4,128)(2,1)} %get-tuple-element.18) | copy-start | bytes 98308
  70.6 1.6 %copy-start.1 = (f32[128,4096]{1,0:T(8,128)S(1)}, f32[128,4096]{1,0:T(8,128)}, u32[]{:S(2)}) copy-start(f32[128,4096]{1,0:T(8,128)} %fusion.4) | copy-start | bytes 6291460
  82.7 8.2 %copy-start.4 = (bf16[4,128,128]{2,1,0:T(8,128)(2,1)S(1)}, bf16[4,128,128]{2,1,0:T(8,128)(2,1)}, u32[]{:S(2)}) copy-start(bf16[4,128,128]{2,1,0:T(8,128)(2,1)} %fusion.11) | copy-start | bytes 393220
  83.6 7.3 %copy-start.11 = (bf16[4,128,128]{2,1,0:T(8,128)(2,1)S(1)}, bf16[4,128,128]{2,1,0:T(8,128)(2,1)}, u32[]{:S(2)}) copy-start(bf16[4,128,128]{2,1,0:T(8,128)(2,1)} %param.18) | copy-start | bytes 393220
  84.6 6.5 %copy-start.14 = (bf16[128,128]{1,0:T(8,128)(2,1)S(1)}, bf16[128,128]{1,0:T(8,128)(2,1)}, u32[]{:S(2)}) copy-start(bf16[128,128]{1,0:T(8,128)(2,1)} %copy.64) | copy-start | bytes 98308
  86.5 4.9 %copy-start.2 = (f32[4096,2,64]{0,2,1:T(8,128)S(1)}, f32[4096,2,64]{0,2,1:T(8,128)}, u32[]{:S(2)}) copy-start(f32[4096,2,64]{0,2,1:T(8,128)} %get-tuple-element.22) | copy-start | bytes 6291460
  86.5 4.9 %copy-start.9 = (f32[4096,2]{0,1:T(2,128)S(1)}, f32[4096,2]{0,1:T(2,128)}, u32[]{:S(2)}) copy-start(f32[4096,2]{0,1:T(2,128)} %add_sqrt_fusion.1) | copy-start | bytes 98308

commit v6 on v5

--- a/solution.py
+++ b/solution.py
@@ -15,48 +15,6 @@
 sharpness = 32.0
 epsilon = 1e-06
 neighbour_steps = ((-1, -1), (-1, 0), (-1, 1), (0, -1), (0, 1), (1, -1), (1, 0), (1, 1))
-
-
-def exchange_kernel(n, ny, x_ref, o_ref, send_sem, recv_sem, local_sem):
-    me = lax.axis_index("tx") * ny + lax.axis_index("ty")
-
-    def copy_to(d):
-        return pltpu.make_async_remote_copy(
-            src_ref=x_ref.at[d], dst_ref=o_ref.at[me], send_sem=send_sem.at[d],
-            recv_sem=recv_sem.at[me], device_id=(d // ny, d % ny),
-            device_id_type=pl.DeviceIdType.MESH)
-
-    def copy_from(s):
-        return pltpu.make_async_remote_copy(
-            src_ref=x_ref.at[s], dst_ref=o_ref.at[s], send_sem=send_sem.at[s],
-            recv_sem=recv_sem.at[s], device_id=(s // ny, s % ny),
-            device_id_type=pl.DeviceIdType.MESH)
-
-    local = pltpu.make_async_copy(x_ref.at[me], o_ref.at[me], local_sem)
-    local.start()
-
-    def start(k, carry):
-        copy_to(lax.rem(me + k, n)).start()
-        return carry
-    lax.fori_loop(1, n, start, 0)
-
-    def finish(k, carry):
-        copy_to(lax.rem(me + k, n)).wait_send()
-        copy_from(lax.rem(me + n - k, n)).wait_recv()
-        return carry
-    lax.fori_loop(1, n, finish, 0)
-    local.wait()
-
-def exchange(x, nx, ny):
-    n = nx * ny
-    return pl.pallas_call(
-        functools.partial(exchange_kernel, n, ny),
-        out_shape=jax.ShapeDtypeStruct(x.shape, x.dtype),
-        in_specs=[pl.BlockSpec(memory_space=pltpu.VMEM)],
-        out_specs=pl.BlockSpec(memory_space=pltpu.VMEM),
-        scratch_shapes=[pltpu.SemaphoreType.DMA((n,)), pltpu.SemaphoreType.DMA((n,)), pltpu.SemaphoreType.DMA],
-        compiler_params=pltpu.CompilerParams(has_side_effects=True),
-    )(x)
 
 
 def mlp_kernel(x_ref, w1_ref, w2_ref, w3_ref, o_ref):
@@ -88,32 +46,6 @@
     )(x, w1, w2, w3)
 
 
-def permute_kernel(chunk, a_ref, b_ref, x_ref, o_ref):
-    total = jnp.zeros(o_ref.shape, jnp.float32)
-    keys = a_ref[...]
-    for start in range(0, x_ref.shape[0], chunk):
-        hits = (keys == b_ref[:, start : start + chunk]).astype(jnp.bfloat16)
-        total += jnp.dot(hits, x_ref[start : start + chunk, :], preferred_element_type=jnp.float32)
-    o_ref[...] = total.astype(o_ref.dtype)
-
-
-def permute_rows(a, b, x, block, chunk):
-    rows = a.shape[0]
-    a = a.reshape(rows, 1)
-    b = b.reshape(1, -1)
-    return pl.pallas_call(
-        functools.partial(permute_kernel, chunk),
-        out_shape=jax.ShapeDtypeStruct((rows, x.shape[1]), x.dtype),
-        grid=(rows // block,),
-        in_specs=[
-            pl.BlockSpec((block, 1), lambda i: (i, 0)),
-            pl.BlockSpec(b.shape, lambda i: (0, 0)),
-            pl.BlockSpec(x.shape, lambda i: (0, 0)),
-        ],
-        out_specs=pl.BlockSpec((block, x.shape[1]), lambda i: (i, 0)),
-    )(a, b, x)
-
-
 def gather_kernel(unroll, pos_ref, order_ref, x_ref, o_ref, rows_in, rows_out):
     rows_in[...] = x_ref[...].astype(jnp.float32)
 
@@ -156,7 +88,7 @@
     )(pos, order, x)
 
 
-def halo_kernel(count_x, count_y, x_ref, o_ref, send_sem, recv_sem, local_sem):
+def mix_kernel(count_x, count_y, x_ref, mixing_ref, o_ref, padded, send_sem, recv_sem, local_sem):
     index_x = lax.axis_index("tx")
     index_y = lax.axis_index("ty")
     size_x, size_y = x_ref.shape[0], x_ref.shape[1]
@@ -184,7 +116,7 @@
     pl.semaphore_wait(barrier, peers)
 
     center = pltpu.make_async_copy(
-        x_ref, o_ref.at[pl.ds(1, size_x), pl.ds(1, size_y)], local_sem
+        x_ref, padded.at[pl.ds(1, size_x), pl.ds(1, size_y)], local_sem
     )
     center.start()
     copies = []
@@ -193,7 +125,7 @@
         source_y, target_y = ranges(b, size_y)
         copy = pltpu.make_async_remote_copy(
             src_ref=x_ref.at[source_x, source_y],
-            dst_ref=o_ref.at[target_x, target_y],
+            dst_ref=padded.at[target_x, target_y],
             send_sem=send_sem.at[k],
             recv_sem=recv_sem.at[k],
             device_id=(index_x + a, index_y + b),
@@ -207,43 +139,41 @@
 
         @pl.when(jnp.logical_not(inside(index_x - a, index_y - b)))
         def _():
-            piece = o_ref.at[target_x, target_y]
+            piece = padded.at[target_x, target_y]
             piece[...] = jnp.zeros(piece.shape, piece.dtype)
     for k, (a, b) in enumerate(steps):
         pl.when(inside(index_x + a, index_y + b))(copies[k].wait_send)
         pl.when(inside(index_x - a, index_y - b))(copies[k].wait_recv)
     center.wait()
-
-
-def halo(block):
+    for tile_x in range(size_x):
+        for tile_y in range(size_y):
+            total = x_ref[tile_x, tile_y].astype(jnp.float32)
+            for k, (a, b) in enumerate(steps):
+                total += jnp.dot(
+                    padded[1 + tile_x + a, 1 + tile_y + b],
+                    mixing_ref[k],
+                    preferred_element_type=jnp.float32,
+                )
+            o_ref[tile_x, tile_y] = total.astype(o_ref.dtype)
+
+
+def mix_tiles(block, mixing):
     count_x = lax.axis_size("tx")
     count_y = lax.axis_size("ty")
     shape = (block.shape[0] + 2, block.shape[1] + 2) + block.shape[2:]
     return pl.pallas_call(
-        functools.partial(halo_kernel, count_x, count_y),
-        out_shape=jax.ShapeDtypeStruct(shape, block.dtype),
-        in_specs=[pl.BlockSpec(memory_space=pltpu.VMEM)],
+        functools.partial(mix_kernel, count_x, count_y),
+        out_shape=jax.ShapeDtypeStruct(block.shape, block.dtype),
+        in_specs=[pl.BlockSpec(memory_space=pltpu.VMEM)] * 2,
         out_specs=pl.BlockSpec(memory_space=pltpu.VMEM),
         scratch_shapes=[
+            pltpu.VMEM(shape, block.dtype),
             pltpu.SemaphoreType.DMA((8,)),
             pltpu.SemaphoreType.DMA((8,)),
             pltpu.SemaphoreType.DMA,
         ],
         compiler_params=pltpu.CompilerParams(collective_id=0, has_side_effects=True),
-    )(block)
-
-
-def padded_2(block, sides, width):
-    for axis, dim in sides:
-        count = lax.axis_size(axis)
-        forward = [(i, i + 1) for i in range(count - 1)]
-        backward = [(target, source) for source, target in forward]
-        low = lax.ppermute(
-            lax.slice_in_dim(block, block.shape[dim] - width, None, axis=dim), axis, forward
-        )
-        high = lax.ppermute(lax.slice_in_dim(block, 0, width, axis=dim), axis, backward)
-        block = jnp.concatenate([low, block, high], axis=dim)
-    return block
+    )(block, mixing)
 
 
 def unit_heads(projected, head_count):
@@ -252,28 +182,6 @@
     )
     magnitude = jnp.sqrt(jnp.sum(pieces * pieces, axis=-1, keepdims=True) + epsilon)
     return (pieces / magnitude).reshape(projected.shape).astype(jnp.bfloat16)
-
-
-def gather_rows(order, rows, block):
-    column_ids = jnp.arange(rows.shape[0], dtype=jnp.int32)
-
-    def pick_block(index_block):
-        table = (index_block[:, None] == column_ids[None, :]).astype(jnp.bfloat16)
-        return jnp.dot(table, rows, preferred_element_type=jnp.float32).astype(jnp.bfloat16)
-
-    picked = lax.map(pick_block, order.reshape(-1, block))
-    return picked.reshape(order.shape[0], rows.shape[1])
-
-
-def scatter_rows(order, rows, block):
-    target_ids = jnp.arange(rows.shape[0], dtype=jnp.int32).reshape(-1, block)
-
-    def place_block(target_block):
-        table = (target_block[:, None] == order[None, :]).astype(jnp.bfloat16)
-        return jnp.dot(table, rows, preferred_element_type=jnp.float32).astype(jnp.bfloat16)
-
-    placed = lax.map(place_block, target_ids)
-    return placed.reshape(rows.shape[0], rows.shape[1])
 
 
 def body(
@@ -373,16 +281,7 @@
         )
     ).astype(jnp.bfloat16)
     tile_grid = summary.reshape(TLX, TLY, inducing_count, width)
-    padded = halo(tile_grid)
-    stacked = jnp.stack(
-        [
-            padded[1 + steps[0] : 1 + steps[0] + TLX, 1 + steps[1] : 1 + steps[1] + TLY]
-            for steps in neighbour_steps
-        ]
-    )
-    mixture = tile_grid.astype(jnp.float32) + jnp.einsum(
-        "dxyic,dce->xyie", stacked, mixing, preferred_element_type=jnp.float32
-    )
+    mixture = mix_tiles(tile_grid, mixing)
     mixture = mixture.astype(jnp.bfloat16).reshape(per_device * inducing_count, width)
 
     point_queries = unit_heads(

time: 134 us -> 128 us (0.955)
  local copies, waits for them, and re-layouts: 17.8 us -> 8.93 us
  waiting for transfers between devices: 16.5 us -> 18.2 us
    unnamed x38 -> x13, local copies, waits for them, and re-layouts: 8.2 us -> 1.42 us
    all_to_all x1, waiting for transfers between devices: 16.5 us -> 18.2 us  [body(): lax.all_to_all(outgoing, ('tx', 'ty'), split_axis=0, concat_axis=0, tiled...]
    convert_element_type x4, other arithmetic: 0.41 us -> 1.99 us  [unit_heads(): return (pieces / magnitude).reshape(projected.shape).astype(jnp.bfloat16)]
  transfers between devices with their start and end apart: 1 -> 1, of which waited for: 1 -> 1; matrix products, arithmetic and copies ran while one was open for 2% -> 1% of each run, Pallas kernels for 0% -> 0%
where the time goes in v6:
time: 128 us
  Pallas kernels  36.7 us (29%)
  blocking collectives  25.3 us (20%)
  matrix products  23 us (18%)
  waiting for transfers between devices  18.2 us (14%)
  starting transfers between devices  11.5 us (9%)
  local copies, waits for them, and re-layouts  8.93 us (7%)
  other arithmetic  3.69 us (3%)
    all_to_all x1, blocking collectives, body(): lax.all_to_all(result.reshape(devices, quota, width), ('tx', 'ty'), split...  25.3 us
    pallas_call x2, Pallas kernels, move_rows(): pl.pallas_call(functools.partial(kernel, 8), out_shape=jax.ShapeDtypeStru...  19.3 us
    all_to_all x1, waiting for transfers between devices, body(): lax.all_to_all(outgoing, ('tx', 'ty'), split_axis=0, concat_axis=0, tiled...  18.2 us
    all_to_all x1, starting transfers between devices, body(): lax.all_to_all(outgoing, ('tx', 'ty'), split_axis=0, concat_axis=0, tiled...  11.5 us
    pallas_call x1, Pallas kernels, point_mlp(): pl.pallas_call(mlp_kernel, out_shape=jax.ShapeDtypeStruct((rows, w3.shape...  9.7 us
    pallas_call x1, Pallas kernels, mix_tiles(): pl.pallas_call(functools.partial(mix_kernel, count_x, count_y), out_shape...  7.71 us
    dot_general x2, matrix products, body(): jnp.dot(point_queries[:, lower:upper], second_keys[:, lower:upper].T, pre...  4.91 us
    dot_general x2, matrix products, body(): totals = jnp.dot(weights, row_mask, precision=lax.Precision.HIGHEST)  3.71 us
  transfers between devices with their start and end apart: 1, of which 1 were waited for; matrix products, arithmetic and copies ran while one was open for 1% of the time, Pallas kernels for 0%

profile of v6, /device:TPU:1, one launch (start us, length us, event | category | flops | bytes accessed | tf_op | source)
XLA Modules:
  0.0 127.7 jit_solution(10718154625078204377)
XLA Ops:
  0.0 0.5 broadcast.112
  0.5 1.4 %fusion.58 = (s32[512]{0:T(512)S(1)}, s32[1,512]{1,0:T(1,128)S(1)}) fusion(s32[]{:T(128)} %broadcast.112, s32[128,512]{1,0:T(8,128)} %param.14, s32[]{:T(128)S(6)} %select_n.22), kind=kLoop, calls=%fused_computation.102 | loop fusion | bytes 6152 | tf_op jit(solution)/shard_map/jit(dynamic_index_in_dim)/dynamic_slice | solution.py:215
  1.9 0.3 reduce-window.9
  2.2 0.1 slice.87
  2.3 0.2 reshape.214
  2.5 0.1 slice_reduce_fusion.1
  2.6 0.1 broadcast.93
  2.7 0.1 reshape.216
  2.8 0.2 reshape.212
  3.0 0.1 slice_add_fusion
  3.1 0.1 add_subtract_fusion
  3.2 0.7 slice_reduce_fusion
  3.9 0.1 lt.52
  4.0 0.1 copy.47
  4.1 0.1 copy.48
  4.2 0.1 lt.56
  4.3 0.1 lt.57
  4.4 0.1 copy.51
  4.5 0.1 copy.49
  4.6 0.1 copy.52
  4.7 0.1 copy.50
  4.8 0.1 add.124
  4.9 0.1 add.125
  5.0 0.1 add.127
  5.1 0.1 add.128
  5.2 0.7 fusion.51.pos_ref
  5.9 9.7 %shard_map.100.x_ref = bf16[4096,128]{1,0:T(8,128)(2,1)} custom-call(bf16[4096,128]{1,0:T(8,128)(2,1)} %x_ref.1, bf16[128,512]{1,0:T(8,128)(2,1)} %w1_ref.1, bf16[1,512,512]{2,1,0:T(8,128)(2,1)} %w2_ref.1, bf16[512,128]{1,0:T(8,128)(2,1)} %w3_ref.1), custom_call_target="tpu_custom_call" | custom-call | tf_op jit(solution)/shard_map/pallas_call | solution.py:35
  15.6 9.8 %shard_map.101 = bf16[4096,128]{1,0:T(8,128)(2,1)} custom-call(s32[4096]{0:T(1024)} %fusion.51.pos_ref, s32[4096]{0:T(1024)} %bitcast.156, bf16[4096,128]{1,0:T(8,128)(2,1)} %shard_map.100.x_ref), custom_call_target="tpu_custom_call" | custom-call | tf_op jit(solution)/shard_map/pallas_call | solution.py:78
  25.4 11.5 %all-to-all-start = ((bf16[128,32,128]{2,1,0:T(8,128)(2,1)}), bf16[128,32,128]{2,1,0:T(8,128)(2,1)S(1)}, u32[]{:S(2)}, u32[]{:S(2)}) async-start(bf16[128,32,128]{2,1,0:T(8,128)(2,1)} %bitcast.142), calls=%async_computation | async-start | bytes 2097152 | tf_op jit(solution)/shard_map/all_to_all | solution.py:233
  36.9 0.1 copy.57
  37.1 0.0 copy-done.5
  37.1 0.1 copy.54
  37.2 0.1 copy.55
  37.4 0.2 multiply_reduce_fusion.3
  37.6 0.1 copy.60
  37.7 0.1 copy.53
  37.9 0.1 copy.58
  38.0 0.1 eq.19
  38.1 18.2 %all-to-all-done = bf16[128,32,128]{2,1,0:T(8,128)(2,1)S(1)} async-done(((bf16[128,32,128]{2,1,0:T(8,128)(2,1)}), bf16[128,32,128]{2,1,0:T(8,128)(2,1)S(1)}, u32[]{:S(2)}, u32[]{:S(2)}) %all-to-all-start) | async-done | bytes 1048608 | tf_op jit(solution)/shard_map/all_to_all | solution.py:233
  56.4 0.5 multiply_reduce_fusion
  56.9 0.2 divide_convert_fusion
  57.1 1.8 %fusion.4 = f32[128,4096]{1,0:T(8,128)} fusion(bf16[4096,128]{0,1:T(8,128)(2,1)S(1)} %bitcast.139, bf16[128,128]{0,1:T(8,128)(2,1)S(1)} %bitcast.150), kind=kOutput, calls=%fused_computation.8 | convolution fusion | flops 67633152 | bytes 2637824 | tf_op jit(solution)/shard_map/dot_general | solution.py:261
  58.8 0.5 fusion.5
  59.3 2.1 %convolution_convert_fusion = bf16[4096,128]{1,0:T(8,128)(2,1)} fusion(bf16[4096,128]{1,0:T(8,128)(2,1)S(1)} %bitcast.134, bf16[4,128,128]{2,1,0:T(8,128)(2,1)} %param.17), kind=kOutput, calls=%fused_computation.12 | convolution fusion | flops 134742016 | bytes 2129920 | tf_op jit(solution)/shard_map/dot_general | solution.py:250
  61.5 2.3 %copy.56 = bf16[4096,128]{0,1:T(8,128)(2,1)} copy(bf16[4096,128]{1,0:T(8,128)(2,1)} %convolution_convert_fusion) | data formatting | bytes 2097152 | tf_op jit(solution)/shard_map/convert_element_type | solution.py:250
  63.7 2.6 %fusion.35 = f32[128,4]{0,1:T(4,128)S(1)} fusion(f32[128,4096]{1,0:T(8,128)} %fusion.4, s32[4096]{0:T(1024)S(1)} %eq.19), kind=kOutput, calls=%fused_computation.58 | convolution fusion | flops 25182208 | bytes 2115584 | tf_op jit(solution)/shard_map/dot_general | solution.py:267
  66.4 1.1 fusion.36
  67.4 1.8 %multiply_reduce_fusion.1 = (f32[4096,2]{0,1:T(2,128)S(1)}, f32[4096,2,64]{0,2,1:T(8,128)}) fusion(bf16[4096,128,1]{1,0,2:T(8,128)(2,1)S(1)} %bitcast.135, bf16[2,64,128]{2,1,0:T(8,128)(2,1)S(1)} %bitcast.152), kind=kOutput, calls=%fused_computation.25 | convolution fusion | flops 135258112 | bytes 3211264 | tf_op jit(solution)/shard_map/dot_general | solution.py:288
  69.3 0.3 broadcast_multiply_fusion
  69.6 1.3 %copy-done = f32[128,4096]{1,0:T(8,128)S(1)} copy-done((f32[128,4096]{1,0:T(8,128)S(1)}, f32[128,4096]{1,0:T(8,128)}, u32[]{:S(2)}) %copy-start) | copy-done | bytes 2097176
  70.9 0.7 fusion.14
  71.6 0.7 fusion.15
  72.4 1.6 %fusion.11 = bf16[4,128,128]{2,1,0:T(8,128)(2,1)} fusion(bf16[128,4,64]{0,2,1:T(8,128)(2,1)S(1)} %fusion.14, bf16[128,4,64]{0,2,1:T(8,128)(2,1)S(1)} %fusion.15, f32[128,128]{1,0:T(8,128)S(1)} %convert_element_type.76, bf16[4,128,128]{2,1,0:T(8,128)(2,1)} %param.17), kind=kOutput, calls=%fused_computation.27 | convolution fusion | flops 17170432 | bytes 360448 | tf_op jit(solution)/shard_map/tic,ce->tie/dot_general | solution.py:279
  74.0 7.7 %shard_map.102 = bf16[2,2,128,128]{3,2,1,0:T(8,128)(2,1)} custom-call(bf16[2,2,128,128]{3,2,1,0:T(8,128)(2,1)} %bitcast.148, bf16[8,128,128]{2,1,0:T(8,128)(2,1)} %mixing_ref.1), custom_call_target="tpu_custom_call" | custom-call | tf_op jit(solution)/shard_map/pallas_call | solution.py:164
  81.7 1.1 convolution_convert_fusion.1
  82.9 1.1 multiply_reduce_fusion.2
  84.0 1.8 %divide_convert_fusion.1 = bf16[4096,2,64]{0,2,1:T(8,128)(2,1)S(1)} fusion(f32[4096,2,64]{0,2,1:T(8,128)} %get-tuple-element.22, f32[4096,2]{0,1:T(2,128)S(1)} %add_sqrt_fusion.1), kind=kLoop, calls=%fused_computation.24 | loop fusion | flops 1048576 | bytes 3178496 | tf_op jit(solution)/shard_map/convert_element_type | solution.py:184
  85.8 1.3 %fusion.23 = f32[4096,512]{0,1:T(8,128)S(1)} fusion(bf16[4096,128]{0,1:T(8,128)(2,1)S(1)} %bitcast.137, bf16[512,128]{0,1:T(8,128)(2,1)S(1)} %bitcast.146), kind=kOutput, calls=%fused_computation.40 | convolution fusion | flops 268435456 | bytes 8978432 | tf_op jit(solution)/shard_map/dot_general | solution.py:301
  87.1 3.6 %fusion = (f32[4096]{0:T(1024)S(1)}, f32[4096]{0:T(1024)S(1)}, bf16[4096,512]{0,1:T(8,128)(2,1)S(1)}, bf16[4096,512]{0,1:T(8,128)(2,1)S(1)}) fusion(f32[4096,4]{0,1:T(4,128)S(1)} %get-tuple-element.17, f32[4096,512]{0,1:T(8,128)S(1)} %fusion.23, bf16[512,128]{0,1:T(8,128)(2,1)S(1)} %bitcast.147, bf16[4096,128]{0,1:T(8,128)(2,1)S(1)} %bitcast.138), kind=kOutput, calls=%fused_computation.2 | convolution fusion | flops 285204480 | bytes 17465344 | tf_op jit(solution)/shard_map/dot_general | solution.py:301
  90.7 0.8 fusion.7
  91.6 0.8 fusion.8
  92.4 0.5 fusion.6
  92.9 25.3 %all_to_all.10 = bf16[128,32,128]{2,1,0:T(8,128)(2,1)} all-to-all(bf16[128,32,128]{2,1,0:T(8,128)(2,1)S(1)} %bitcast.141), channel_id=1, replica_groups=mesh['tx'=32,'ty'=4] {'tx','ty'}, dimensions={0} | all-to-all | bytes 2097152 | tf_op jit(solution)/shard_map/all_to_all | solution.py:320
  118.2 9.4 %shard_map.103 = bf16[4096,128]{1,0:T(8,128)(2,1)} custom-call(s32[4096]{0:T(1024)} %fusion.51.pos_ref, s32[4096]{0:T(1024)} %bitcast.157, bf16[4096,128]{1,0:T(8,128)(2,1)} %bitcast.143), custom_call_target="tpu_custom_call" | custom-call | tf_op jit(solution)/shard_map/pallas_call | solution.py:78
  (27 shorter events, 0.3 us)
Async XLA Ops:
  15.6 21.4 %copy-start.2 = (s32[128,512]{1,0:T(8,128)S(1)}, s32[128,512]{1,0:T(8,128)}, u32[]{:S(2)}) copy-start(s32[128,512]{1,0:T(8,128)} %param.14) | copy-start | bytes 786436
  15.6 21.5 %copy-start.5 = (bf16[128,128]{1,0:T(8,128)(2,1)S(1)}, bf16[128,128]{1,0:T(8,128)(2,1)}, u32[]{:S(2)}) copy-start(bf16[128,128]{1,0:T(8,128)(2,1)} %param.16) | copy-start | bytes 98308
  15.6 21.5 %copy-start.4 = (bf16[4,128,128]{2,1,0:T(8,128)(2,1)S(1)}, bf16[4,128,128]{2,1,0:T(8,128)(2,1)}, u32[]{:S(2)}) copy-start(bf16[4,128,128]{2,1,0:T(8,128)(2,1)} %param.17) | copy-start | bytes 393220
  25.4 12.1 %copy-start.3 = (bf16[4,128,128]{2,1,0:T(8,128)(2,1)S(1)}, bf16[4,128,128]{2,1,0:T(8,128)(2,1)}, u32[]{:S(2)}) copy-start(bf16[4,128,128]{2,1,0:T(8,128)(2,1)} %param.18) | copy-start | bytes 393220
  25.4 30.9 %all-to-all-start = ((bf16[128,32,128]{2,1,0:T(8,128)(2,1)}), bf16[128,32,128]{2,1,0:T(8,128)(2,1)S(1)}, u32[]{:S(2)}, u32[]{:S(2)}) async-start(bf16[128,32,128]{2,1,0:T(8,128)(2,1)} %bitcast.142), calls=%async_computation | async-start | bytes 2097152 | tf_op jit(solution)/shard_map/all_to_all | solution.py:233
  67.4 1.9 %copy-start.1 = (bf16[4096,128]{0,1:T(8,128)(2,1)S(1)}, bf16[4096,128]{0,1:T(8,128)(2,1)}, u32[]{:S(2)}) copy-start(bf16[4096,128]{0,1:T(8,128)(2,1)} %copy.56) | copy-start | bytes 3145732
  69.3 1.6 %copy-start = (f32[128,4096]{1,0:T(8,128)S(1)}, f32[128,4096]{1,0:T(8,128)}, u32[]{:S(2)}) copy-start(f32[128,4096]{1,0:T(8,128)} %fusion.4) | copy-start | bytes 6291460

commit v7 on v6

--- a/solution.py
+++ b/solution.py
@@ -182,6 +182,70 @@
     )
     magnitude = jnp.sqrt(jnp.sum(pieces * pieces, axis=-1, keepdims=True) + epsilon)
     return (pieces / magnitude).reshape(projected.shape).astype(jnp.bfloat16)
+
+
+def unit_rows(projected, head_width):
+    lanes = lax.broadcasted_iota(jnp.int32, projected.shape, projected.ndim - 1)
+    squares = projected * projected
+    magnitude = jnp.zeros_like(projected)
+    for head_id in range(projected.shape[-1] // head_width):
+        in_head = (lanes >= head_id * head_width) & (lanes < (head_id + 1) * head_width)
+        total = jnp.sum(jnp.where(in_head, squares, 0.0), axis=-1, keepdims=True)
+        magnitude = jnp.where(in_head, jnp.sqrt(total + epsilon), magnitude)
+    return (projected / magnitude).astype(jnp.bfloat16)
+
+
+def summary_kernel(rows_ref, column_mask_ref, lane_mask_ref, inducing_ref, proj_ref, o_ref):
+    width = rows_ref.shape[1]
+    head_width = width // HEADS
+    tiles = column_mask_ref.shape[1]
+    rows = rows_ref[...]
+    queries = unit_rows(
+        jnp.dot(inducing_ref[...], proj_ref[0], preferred_element_type=jnp.float32), head_width
+    )
+    keys = unit_rows(jnp.dot(rows, proj_ref[1], preferred_element_type=jnp.float32), head_width)
+    values = jnp.dot(rows, proj_ref[2], preferred_element_type=jnp.float32).astype(jnp.bfloat16)
+    column_mask = column_mask_ref[...]
+    lane_mask = lane_mask_ref[...]
+    heads_out = []
+    for head_id in range(HEADS):
+        lower = head_id * head_width
+        upper = lower + head_width
+        scores = lax.dot_general(
+            queries[:, lower:upper],
+            keys[:, lower:upper],
+            (((1,), (1,)), ((), ())),
+            preferred_element_type=jnp.float32,
+        )
+        weights = jnp.exp(sharpness * scores)
+        rounded = weights.astype(jnp.bfloat16)
+        head_values = values[:, lower:upper]
+        masked = jnp.concatenate(
+            [head_values * column_mask[:, t : t + 1] for t in range(tiles)], axis=1
+        )
+        numer = jnp.dot(rounded, masked, preferred_element_type=jnp.float32)
+        per_tile = []
+        for t in range(tiles):
+            totals = jnp.sum(weights * lane_mask[t : t + 1, :], axis=1, keepdims=True)
+            per_tile.append(numer[:, t * head_width : (t + 1) * head_width] / totals)
+        heads_out.append(per_tile)
+    inducing = inducing_ref[...].astype(jnp.float32)
+    for t in range(tiles):
+        attended = jnp.concatenate([heads_out[h][t] for h in range(HEADS)], axis=1)
+        attended = attended.astype(jnp.bfloat16)
+        o_ref[t] = (
+            inducing + jnp.dot(attended, proj_ref[3], preferred_element_type=jnp.float32)
+        ).astype(o_ref.dtype)
+
+
+def summarize(rows, row_mask, inducing, proj):
+    tiles = row_mask.shape[1]
+    return pl.pallas_call(
+        summary_kernel,
+        out_shape=jax.ShapeDtypeStruct((tiles,) + inducing.shape, jnp.bfloat16),
+        in_specs=[pl.BlockSpec(memory_space=pltpu.VMEM)] * 5,
+        out_specs=pl.BlockSpec(memory_space=pltpu.VMEM),
+    )(rows, row_mask.astype(jnp.bfloat16), row_mask.T, inducing, proj)
 
 
 def body(
@@ -244,42 +308,7 @@
     tile_ids = jnp.arange(per_device, dtype=jnp.int32)
     row_mask = (row_tile[:, None] == tile_ids[None, :]).astype(jnp.float32)
 
-    first_keys = unit_heads(
-        jnp.dot(all_rows, first_proj[1], preferred_element_type=jnp.float32), HEADS
-    )
-    first_values = jnp.dot(all_rows, first_proj[2], preferred_element_type=jnp.float32).astype(
-        jnp.bfloat16
-    )
-    inducing_queries = unit_heads(
-        jnp.dot(inducing, first_proj[0], preferred_element_type=jnp.float32), HEADS
-    )
-    masked_values = first_values[:, None, :] * row_mask.astype(jnp.bfloat16)[:, :, None]
-    heads_out = []
-    for head_id in range(HEADS):
-        lower = head_id * head_width
-        upper = lower + head_width
-        scores = jnp.dot(
-            inducing_queries[:, lower:upper],
-            first_keys[:, lower:upper].T,
-            preferred_element_type=jnp.float32,
-        )
-        weights = jnp.exp(sharpness * scores)
-        totals = jnp.dot(weights, row_mask, precision=lax.Precision.HIGHEST)
-        numer = jnp.dot(
-            weights.astype(jnp.bfloat16),
-            masked_values[:, :, lower:upper].reshape(-1, per_device * head_width),
-            preferred_element_type=jnp.float32,
-        ).reshape(inducing_count, per_device, head_width)
-        heads_out.append(numer / totals[:, :, None])
-    first_attended = (
-        jnp.concatenate(heads_out, axis=2).astype(jnp.bfloat16).transpose(1, 0, 2)
-    )
-    summary = (
-        inducing.astype(jnp.float32)[None]
-        + jnp.einsum(
-            "tic,ce->tie", first_attended, first_proj[3], preferred_element_type=jnp.float32
-        )
-    ).astype(jnp.bfloat16)
+    summary = summarize(all_rows, row_mask, inducing, first_proj)
     tile_grid = summary.reshape(TLX, TLY, inducing_count, width)
     mixture = mix_tiles(tile_grid, mixing)
     mixture = mixture.astype(jnp.bfloat16).reshape(per_device * inducing_count, width)

time: 128 us -> 120 us (0.938)
  matrix products: 23 us -> 9.78 us
  Pallas kernels: 36.7 us -> 46.9 us
  waiting for transfers between devices: 18.2 us -> 14.8 us
  local copies, waits for them, and re-layouts: 8.93 us -> 6.58 us
    dot_general x10 -> x0, matrix products: 11.8 us -> none  [the longest x2 3.71 us: body(): totals = jnp.dot(weights, row_mask, precision=lax.Precision.HIGHEST)]
    pallas_call x0 -> x1, Pallas kernels: none -> 10.2 us  [summarize(): pl.pallas_call(summary_kernel, out_shape=jax.ShapeDtypeStruct((tiles,) +...]
    all_to_all x1, waiting for transfers between devices: 18.2 us -> 14.8 us  [body(): lax.all_to_all(outgoing, ('tx', 'ty'), split_axis=0, concat_axis=0, tiled...]
    convert_element_type x1 -> x2, other arithmetic: 0.02 us -> 3.36 us  [body(): row_mask = (row_tile[:, None] == tile_ids[None, :]).astype(jnp.float32)]
    convert_element_type x4 -> x2, other arithmetic: 1.99 us -> 0.21 us  [unit_heads(): return (pieces / magnitude).reshape(projected.shape).astype(jnp.bfloat16)]
    convert_element_type x1, local copies, waits for them, and re-layouts: 2.27 us -> 0.63 us  [body(): row_mask = (row_tile[:, None] == tile_ids[None, :]).astype(jnp.float32)]
    dot_general x1, matrix products: 1.83 us -> 0.46 us  [body(): jnp.dot(all_rows, second_proj[0], preferred_element_type=jnp.float32)]
  transfers between devices with their start and end apart: 1 -> 1, of which waited for: 1 -> 1; matrix products, arithmetic and copies ran while one was open for 1% -> 4% of each run, Pallas kernels for 0% -> 0%
where the time goes in v7:
time: 120 us
  Pallas kernels  46.9 us (39%)
  blocking collectives  25.3 us (21%)
  waiting for transfers between devices  14.8 us (12%)
  starting transfers between devices  11.5 us (10%)
  matrix products  9.78 us (8%)
  local copies, waits for them, and re-layouts  6.58 us (5%)
  other arithmetic  4.89 us (4%)
    all_to_all x1, blocking collectives, body(): lax.all_to_all(result.reshape(devices, quota, width), ('tx', 'ty'), split...  25.3 us
    pallas_call x2, Pallas kernels, move_rows(): pl.pallas_call(functools.partial(kernel, 8), out_shape=jax.ShapeDtypeStru...  19.3 us
    all_to_all x1, waiting for transfers between devices, body(): lax.all_to_all(outgoing, ('tx', 'ty'), split_axis=0, concat_axis=0, tiled...  14.8 us
    all_to_all x1, starting transfers between devices, body(): lax.all_to_all(outgoing, ('tx', 'ty'), split_axis=0, concat_axis=0, tiled...  11.5 us
    pallas_call x1, Pallas kernels, summarize(): pl.pallas_call(summary_kernel, out_shape=jax.ShapeDtypeStruct((tiles,) +...  10.2 us
    pallas_call x1, Pallas kernels, point_mlp(): pl.pallas_call(mlp_kernel, out_shape=jax.ShapeDtypeStruct((rows, w3.shape...  9.7 us
    pallas_call x1, Pallas kernels, mix_tiles(): pl.pallas_call(functools.partial(mix_kernel, count_x, count_y), out_shape...  7.69 us
    dot_general x2, matrix products, body(): jnp.dot(point_queries[:, lower:upper], second_keys[:, lower:upper].T, pre...  4.92 us
  transfers between devices with their start and end apart: 1, of which 1 were waited for; matrix products, arithmetic and copies ran while one was open for 4% of the time, Pallas kernels for 0%

profile of v7, /device:TPU:1, one launch (start us, length us, event | category | flops | bytes accessed | tf_op | source)
XLA Modules:
  0.0 120.0 jit_solution(15083106712913148189)
XLA Ops:
  0.0 0.5 broadcast.75
  0.5 1.4 %fusion.29 = (s32[512]{0:T(512)S(1)}, s32[1,512]{1,0:T(1,128)S(1)}) fusion(s32[]{:T(128)} %broadcast.75, s32[128,512]{1,0:T(8,128)} %param.14, s32[]{:T(128)S(6)} %select_n.22), kind=kLoop, calls=%fused_computation.58 | loop fusion | bytes 6152 | tf_op jit(solution)/shard_map/jit(dynamic_index_in_dim)/dynamic_slice | solution.py:279
  1.9 0.3 reduce-window.9
  2.2 0.1 slice.57
  2.3 0.2 reshape.155
  2.5 0.1 slice_reduce_fusion.1
  2.6 0.1 broadcast.62
  2.7 0.1 reshape.157
  2.8 0.2 reshape.153
  3.0 0.1 slice_add_fusion
  3.1 0.1 add_subtract_fusion
  3.2 0.0 copy-start.2
  3.2 0.7 slice_reduce_fusion
  4.0 0.1 lt.52
  4.0 0.1 copy.51
  4.1 0.1 copy.52
  4.2 0.1 lt.56
  4.3 0.1 lt.57
  4.4 0.1 copy.55
  4.5 0.1 copy.53
  4.6 0.1 copy.56
  4.7 0.1 copy.54
  4.8 0.1 add.100
  4.9 0.1 add.101
  5.0 0.1 add.103
  5.1 0.1 add.104
  5.2 0.7 fusion.26.pos_ref
  5.9 9.7 %shard_map.100.x_ref = bf16[4096,128]{1,0:T(8,128)(2,1)} custom-call(bf16[4096,128]{1,0:T(8,128)(2,1)} %x_ref.1, bf16[128,512]{1,0:T(8,128)(2,1)} %w1_ref.1, bf16[1,512,512]{2,1,0:T(8,128)(2,1)} %w2_ref.1, bf16[512,128]{1,0:T(8,128)(2,1)} %w3_ref.1), custom_call_target="tpu_custom_call" | custom-call | tf_op jit(solution)/shard_map/pallas_call | solution.py:35
  15.6 0.0 copy-start.3
  15.6 9.9 %shard_map.101 = bf16[4096,128]{1,0:T(8,128)(2,1)} custom-call(s32[4096]{0:T(1024)} %fusion.26.pos_ref, s32[4096]{0:T(1024)} %bitcast.88, bf16[4096,128]{1,0:T(8,128)(2,1)} %shard_map.100.x_ref), custom_call_target="tpu_custom_call" | custom-call | tf_op jit(solution)/shard_map/pallas_call | solution.py:78
  25.5 11.5 %all-to-all-start = ((bf16[128,32,128]{2,1,0:T(8,128)(2,1)}), bf16[128,32,128]{2,1,0:T(8,128)(2,1)S(1)}, u32[]{:S(2)}, u32[]{:S(2)}) async-start(bf16[128,32,128]{2,1,0:T(8,128)(2,1)} %bitcast.78), calls=%async_computation | async-start | bytes 2097152 | tf_op jit(solution)/shard_map/all_to_all | solution.py:297
  37.0 0.0 copy-done.2
  37.0 0.1 copy.58
  37.2 0.1 copy.59
  37.3 0.1 eq.22
  37.4 2.7 %fusion.7 = (f32[4096,4]{1,0:T(8,128)S(1)}, bf16[4096,4]{1,0:T(8,128)(2,1)}) fusion(s32[4096]{0:T(1024)S(1)} %eq.22), kind=kLoop, calls=%fused_computation.15 | loop fusion | flops 49152 | bytes 114688 | tf_op jit(solution)/shard_map/convert_element_type | solution.py:309
  40.1 0.0 copy-done.3
  40.1 0.1 copy.61
  40.2 0.1 copy.57
  40.3 0.6 copy.62
  41.0 0.6 fusion.20.lane_mask_ref
  41.6 14.8 %all-to-all-done = bf16[128,32,128]{2,1,0:T(8,128)(2,1)S(1)} async-done(((bf16[128,32,128]{2,1,0:T(8,128)(2,1)}), bf16[128,32,128]{2,1,0:T(8,128)(2,1)S(1)}, u32[]{:S(2)}, u32[]{:S(2)}) %all-to-all-start) | async-done | bytes 1048608 | tf_op jit(solution)/shard_map/all_to_all | solution.py:297
  56.4 0.0 copy-start
  56.4 0.5 multiply_reduce_fusion
  56.9 0.5 copy-done
  57.4 10.2 %shard_map.102 = bf16[4,128,128]{2,1,0:T(8,128)(2,1)} custom-call(bf16[4096,128]{1,0:T(8,128)(2,1)} %bitcast.73, bf16[4096,4]{1,0:T(8,128)(2,1)} %get-tuple-element.16.column_mask_ref, f32[4,4096]{1,0:T(4,128)} %fusion.20.lane_mask_ref, bf16[128,128]{1,0:T(8,128)(2,1)} %inducing_ref.1, bf16[4,128,128]{2,1,0:T(8,128)(2,1)} %proj_ref.1), custom_call_target="tpu_custom_call" | custom-call | tf_op jit(solution)/shard_map/pallas_call | solution.py:243
  67.5 7.7 %shard_map.103 = bf16[2,2,128,128]{3,2,1,0:T(8,128)(2,1)} custom-call(bf16[2,2,128,128]{3,2,1,0:T(8,128)(2,1)} %bitcast.84, bf16[8,128,128]{2,1,0:T(8,128)(2,1)} %mixing_ref.1), custom_call_target="tpu_custom_call" | custom-call | tf_op jit(solution)/shard_map/pallas_call | solution.py:164
  75.2 1.1 convolution_convert_fusion
  76.4 1.1 multiply_reduce_fusion.1
  77.5 0.2 divide_convert_fusion
  77.7 1.3 %fusion.12 = f32[4096,512]{0,1:T(8,128)S(1)} fusion(bf16[4096,128]{0,1:T(8,128)(2,1)S(1)} %bitcast.75, bf16[512,128]{0,1:T(8,128)(2,1)S(1)} %bitcast.82), kind=kOutput, calls=%fused_computation.21 | convolution fusion | flops 268435456 | bytes 8978432 | tf_op jit(solution)/shard_map/dot_general | solution.py:330
  79.0 3.6 %fusion = (f32[4096]{0:T(1024)S(1)}, f32[4096]{0:T(1024)S(1)}, bf16[4096,512]{0,1:T(8,128)(2,1)S(1)}, bf16[4096,512]{0,1:T(8,128)(2,1)S(1)}) fusion(f32[4096,4]{0,1:T(4,128)S(1)} %copy.62, f32[4096,512]{0,1:T(8,128)S(1)} %fusion.12, bf16[512,128]{0,1:T(8,128)(2,1)S(1)} %bitcast.83, bf16[4096,128]{0,1:T(8,128)(2,1)S(1)} %bitcast.76), kind=kOutput, calls=%fused_computation.2 | convolution fusion | flops 285204480 | bytes 17465344 | tf_op jit(solution)/shard_map/dot_general | solution.py:330
  82.6 0.8 fusion.5
  83.5 0.0 copy-start.1
  83.5 0.8 fusion.6
  84.4 0.4 copy-done.1
  84.7 0.5 fusion.4
  85.2 25.3 %all_to_all.10 = bf16[128,32,128]{2,1,0:T(8,128)(2,1)} all-to-all(bf16[128,32,128]{2,1,0:T(8,128)(2,1)S(1)} %bitcast.77), channel_id=1, replica_groups=mesh['tx'=32,'ty'=4] {'tx','ty'}, dimensions={0} | all-to-all | bytes 2097152 | tf_op jit(solution)/shard_map/all_to_all | solution.py:349
  110.5 9.4 %shard_map.104 = bf16[4096,128]{1,0:T(8,128)(2,1)} custom-call(s32[4096]{0:T(1024)} %fusion.26.pos_ref, s32[4096]{0:T(1024)} %bitcast.89, bf16[4096,128]{1,0:T(8,128)(2,1)} %bitcast.79), custom_call_target="tpu_custom_call" | custom-call | tf_op jit(solution)/shard_map/pallas_call | solution.py:78
  (11 shorter events, 0.2 us)
Async XLA Ops:
  3.2 33.8 %copy-start.2 = (s32[128,512]{1,0:T(8,128)S(1)}, s32[128,512]{1,0:T(8,128)}, u32[]{:S(2)}) copy-start(s32[128,512]{1,0:T(8,128)} %param.14) | copy-start | bytes 786436
  15.6 24.5 %copy-start.3 = (bf16[4,128,128]{2,1,0:T(8,128)(2,1)S(1)}, bf16[4,128,128]{2,1,0:T(8,128)(2,1)}, u32[]{:S(2)}) copy-start(bf16[4,128,128]{2,1,0:T(8,128)(2,1)} %param.18) | copy-start | bytes 393220
  25.5 30.9 %all-to-all-start = ((bf16[128,32,128]{2,1,0:T(8,128)(2,1)}), bf16[128,32,128]{2,1,0:T(8,128)(2,1)S(1)}, u32[]{:S(2)}, u32[]{:S(2)}) async-start(bf16[128,32,128]{2,1,0:T(8,128)(2,1)} %bitcast.78), calls=%async_computation | async-start | bytes 2097152 | tf_op jit(solution)/shard_map/all_to_all | solution.py:297
  56.4 1.0 copy-start
  83.5 1.2 %copy-start.1 = (bf16[128,32,128]{2,1,0:T(8,128)(2,1)S(1)}, bf16[128,32,128]{2,1,0:T(8,128)(2,1)}, u32[]{:S(2)}) copy-start(bf16[128,32,128]{2,1,0:T(8,128)(2,1)} %copy-done) | copy-start | bytes 3145732

commit v8 on v7

--- a/solution.py
+++ b/solution.py
@@ -246,6 +246,56 @@
         in_specs=[pl.BlockSpec(memory_space=pltpu.VMEM)] * 5,
         out_specs=pl.BlockSpec(memory_space=pltpu.VMEM),
     )(rows, row_mask.astype(jnp.bfloat16), row_mask.T, inducing, proj)
+
+
+def finish_kernel(rows_ref, row_tile_ref, mixture_ref, proj_ref, o_ref):
+    width = rows_ref.shape[1]
+    head_width = width // HEADS
+    keys_per_tile = mixture_ref.shape[0] // TLX // TLY
+    mixture = mixture_ref[...]
+    keys = unit_rows(jnp.dot(mixture, proj_ref[1], preferred_element_type=jnp.float32), head_width)
+    values = jnp.dot(mixture, proj_ref[2], preferred_element_type=jnp.float32).astype(jnp.bfloat16)
+    rows = rows_ref[...]
+    queries = unit_rows(jnp.dot(rows, proj_ref[0], preferred_element_type=jnp.float32), head_width)
+    key_tile = lax.broadcasted_iota(jnp.int32, (rows.shape[0], mixture.shape[0]), 1) // keys_per_tile
+    own = key_tile == row_tile_ref[...]
+    heads_out = []
+    for head_id in range(HEADS):
+        lower = head_id * head_width
+        upper = lower + head_width
+        scores = lax.dot_general(
+            queries[:, lower:upper],
+            keys[:, lower:upper],
+            (((1,), (1,)), ((), ())),
+            preferred_element_type=jnp.float32,
+        )
+        weights = jnp.where(own, jnp.exp(sharpness * scores), 0.0)
+        totals = jnp.sum(weights, axis=1, keepdims=True)
+        numer = jnp.dot(
+            weights.astype(jnp.bfloat16), values[:, lower:upper], preferred_element_type=jnp.float32
+        )
+        heads_out.append(numer / totals)
+    attended = jnp.concatenate(heads_out, axis=1).astype(jnp.bfloat16)
+    o_ref[...] = (
+        rows.astype(jnp.float32) + jnp.dot(attended, proj_ref[3], preferred_element_type=jnp.float32)
+    ).astype(o_ref.dtype)
+
+
+def finish(rows, row_tile, mixture, proj, block):
+    count = rows.shape[0]
+    full = lambda shape: pl.BlockSpec(shape, lambda i: (0,) * len(shape))
+    return pl.pallas_call(
+        finish_kernel,
+        out_shape=jax.ShapeDtypeStruct(rows.shape, jnp.bfloat16),
+        grid=(count // block,),
+        in_specs=[
+            pl.BlockSpec((block, rows.shape[1]), lambda i: (i, 0)),
+            pl.BlockSpec((block, 1), lambda i: (i, 0)),
+            full(mixture.shape),
+            full(proj.shape),
+        ],
+        out_specs=pl.BlockSpec((block, rows.shape[1]), lambda i: (i, 0)),
+    )(rows, row_tile.reshape(count, 1), mixture, proj)
 
 
 def body(
@@ -313,38 +363,7 @@
     mixture = mix_tiles(tile_grid, mixing)
     mixture = mixture.astype(jnp.bfloat16).reshape(per_device * inducing_count, width)
 
-    point_queries = unit_heads(
-        jnp.dot(all_rows, second_proj[0], preferred_element_type=jnp.float32), HEADS
-    )
-    second_keys = unit_heads(
-        jnp.dot(mixture, second_proj[1], preferred_element_type=jnp.float32), HEADS
-    )
-    second_values = jnp.dot(mixture, second_proj[2], preferred_element_type=jnp.float32).astype(
-        jnp.bfloat16
-    )
-    key_mask = jnp.repeat(row_mask, inducing_count, axis=1)
-    heads_out = []
-    for head_id in range(HEADS):
-        lower = head_id * head_width
-        upper = lower + head_width
-        scores = jnp.dot(
-            point_queries[:, lower:upper],
-            second_keys[:, lower:upper].T,
-            preferred_element_type=jnp.float32,
-        )
-        weights = jnp.exp(sharpness * scores) * key_mask
-        totals = jnp.sum(weights, axis=1, keepdims=True)
-        numer = jnp.dot(
-            weights.astype(jnp.bfloat16),
-            second_values[:, lower:upper],
-            preferred_element_type=jnp.float32,
-        )
-        heads_out.append(numer / totals)
-    second_attended = jnp.concatenate(heads_out, axis=1).astype(jnp.bfloat16)
-    result = (
-        all_rows.astype(jnp.float32)
-        + jnp.dot(second_attended, second_proj[3], preferred_element_type=jnp.float32)
-    ).astype(jnp.bfloat16)
+    result = finish(all_rows, row_tile, mixture, second_proj, 512)
 
     coming = lax.all_to_all(
         result.reshape(devices, quota, width), ("tx", "ty"), split_axis=0, concat_axis=0, tiled=True

time: 120 us -> 126 us (1.050)
  Pallas kernels: 46.9 us -> 62.5 us
  matrix products: 9.78 us -> 0 us
  local copies, waits for them, and re-layouts: 6.58 us -> 9.36 us
  waiting for transfers between devices: 14.8 us -> 12.2 us
    pallas_call x0 -> x1, Pallas kernels: none -> 15.7 us  [finish(): pl.pallas_call(finish_kernel, out_shape=jax.ShapeDtypeStruct(rows.shape,...]
    dot_general x8 -> x0, matrix products: 9.78 us -> none  [the longest x2 4.92 us: body(): jnp.dot(point_queries[:, lower:upper], second_keys[:, lower:upper].T, pre...]
    another operation x4 -> x5, local copies, waits for them, and re-layouts: 0.47 us -> 3.98 us  [the longest x1 3.51 us: finish(): row_tile.reshape(count, 1)]
    convert_element_type x2 -> x1, other arithmetic: 3.36 us -> 0.66 us  [body(): row_mask = (row_tile[:, None] == tile_ids[None, :]).astype(jnp.float32)]
    all_to_all x1, waiting for transfers between devices: 14.8 us -> 12.2 us  [body(): lax.all_to_all(outgoing, ('tx', 'ty'), split_axis=0, concat_axis=0, tiled...]
    convert_element_type x2 -> x1, other arithmetic: 0.21 us -> 2.68 us  [summarize(): row_mask.astype(jnp.bfloat16)]
  transfers between devices with their start and end apart: 1 -> 1, of which waited for: 1 -> 1; matrix products, arithmetic and copies ran while one was open for 4% -> 6% of each run, Pallas kernels for 0% -> 0%
where the time goes in v8:
time: 126 us
  Pallas kernels  62.5 us (50%)
  blocking collectives  25.5 us (20%)
  waiting for transfers between devices  12.2 us (10%)
  starting transfers between devices  11.5 us (9%)
  local copies, waits for them, and re-layouts  9.36 us (7%)
  other arithmetic  4.61 us (4%)
    all_to_all x1, blocking collectives, body(): lax.all_to_all(result.reshape(devices, quota, width), ('tx', 'ty'), split...  25.5 us
    pallas_call x2, Pallas kernels, move_rows(): pl.pallas_call(functools.partial(kernel, 8), out_shape=jax.ShapeDtypeStru...  19.3 us
    pallas_call x1, Pallas kernels, finish(): pl.pallas_call(finish_kernel, out_shape=jax.ShapeDtypeStruct(rows.shape,...  15.7 us
    all_to_all x1, waiting for transfers between devices, body(): lax.all_to_all(outgoing, ('tx', 'ty'), split_axis=0, concat_axis=0, tiled...  12.2 us
    all_to_all x1, starting transfers between devices, body(): lax.all_to_all(outgoing, ('tx', 'ty'), split_axis=0, concat_axis=0, tiled...  11.5 us
    pallas_call x1, Pallas kernels, summarize(): pl.pallas_call(summary_kernel, out_shape=jax.ShapeDtypeStruct((tiles,) +...  10.2 us
    pallas_call x1, Pallas kernels, point_mlp(): pl.pallas_call(mlp_kernel, out_shape=jax.ShapeDtypeStruct((rows, w3.shape...  9.7 us
    pallas_call x1, Pallas kernels, mix_tiles(): pl.pallas_call(functools.partial(mix_kernel, count_x, count_y), out_shape...  7.7 us
  transfers between devices with their start and end apart: 1, of which 1 were waited for; matrix products, arithmetic and copies ran while one was open for 6% of the time, Pallas kernels for 0%

profile of v8, /device:TPU:1, one launch (start us, length us, event | category | flops | bytes accessed | tf_op | source)
XLA Modules:
  0.0 125.8 jit_solution(1933908324422458094)
XLA Ops:
  0.0 0.5 broadcast.55
  0.5 1.4 %fusion.4 = (s32[512]{0:T(512)S(1)}, s32[1,512]{1,0:T(1,128)S(1)}) fusion(s32[]{:T(128)} %broadcast.55, s32[128,512]{1,0:T(8,128)} %param.14, s32[]{:T(128)S(6)} %select_n.22), kind=kLoop, calls=%fused_computation.20 | loop fusion | bytes 6152 | tf_op jit(solution)/shard_map/jit(dynamic_index_in_dim)/dynamic_slice | solution.py:329
  1.9 0.3 reduce-window.9
  2.2 0.1 slice.27
  2.3 0.2 reshape.130
  2.5 0.1 slice_reduce_fusion.1
  2.6 0.1 broadcast.47
  2.7 0.1 reshape.132
  2.8 0.2 reshape.128
  3.0 0.1 slice_add_fusion
  3.1 0.1 add_subtract_fusion
  3.2 0.7 slice_reduce_fusion
  3.9 0.1 lt.52
  4.0 0.1 copy.43
  4.1 0.1 copy.44
  4.2 0.1 lt.56
  4.3 0.1 lt.57
  4.4 0.1 copy.47
  4.5 0.1 copy.45
  4.6 0.1 copy.48
  4.7 0.1 copy.46
  4.8 0.1 add.75
  4.9 0.1 add.76
  5.0 0.1 add.78
  5.1 0.1 add.79
  5.2 0.7 fusion.2.pos_ref
  5.9 9.7 %shard_map.100.x_ref = bf16[4096,128]{1,0:T(8,128)(2,1)} custom-call(bf16[4096,128]{1,0:T(8,128)(2,1)} %x_ref.1, bf16[128,512]{1,0:T(8,128)(2,1)} %w1_ref.1, bf16[1,512,512]{2,1,0:T(8,128)(2,1)} %w2_ref.1, bf16[512,128]{1,0:T(8,128)(2,1)} %w3_ref.1), custom_call_target="tpu_custom_call" | custom-call | tf_op jit(solution)/shard_map/pallas_call | solution.py:35
  15.6 0.0 copy-start.1
  15.6 9.8 %shard_map.101 = bf16[4096,128]{1,0:T(8,128)(2,1)} custom-call(s32[4096]{0:T(1024)} %fusion.2.pos_ref, s32[4096]{0:T(1024)} %bitcast.40, bf16[4096,128]{1,0:T(8,128)(2,1)} %shard_map.100.x_ref), custom_call_target="tpu_custom_call" | custom-call | tf_op jit(solution)/shard_map/pallas_call | solution.py:78
  25.4 11.5 %all-to-all-start = ((bf16[128,32,128]{2,1,0:T(8,128)(2,1)}), bf16[128,32,128]{2,1,0:T(8,128)(2,1)S(1)}, u32[]{:S(2)}, u32[]{:S(2)}) async-start(bf16[128,32,128]{2,1,0:T(8,128)(2,1)} %bitcast.35), calls=%async_computation | async-start | bytes 2097152 | tf_op jit(solution)/shard_map/all_to_all | solution.py:347
  36.9 0.0 copy-done.1
  36.9 0.1 copy.49
  37.1 0.1 copy.50
  37.2 0.1 eq.22
  37.3 0.7 fusion.lane_mask_ref
  38.0 3.5 %reshape_reshape.4.row_tile_ref = s32[4096,1]{1,0:T(8,128)} reshape(s32[128,32]{1,0:T(8,128)S(1)} %copy.50) | data formatting | bytes 32768 | tf_op jit(solution)/shard_map/reshape;reshape | solution.py:298
  41.5 2.7 %convert_convert_fusion.column_mask_ref = bf16[4096,4]{1,0:T(8,128)(2,1)} fusion(s32[4096]{0:T(1024)S(1)} %eq.22), kind=kLoop, calls=%fused_computation | loop fusion | flops 49152 | bytes 49152 | tf_op jit(solution)/shard_map/convert_element_type | solution.py:248
  44.2 12.2 %all-to-all-done = bf16[128,32,128]{2,1,0:T(8,128)(2,1)S(1)} async-done(((bf16[128,32,128]{2,1,0:T(8,128)(2,1)}), bf16[128,32,128]{2,1,0:T(8,128)(2,1)S(1)}, u32[]{:S(2)}, u32[]{:S(2)}) %all-to-all-start) | async-done | bytes 1048608 | tf_op jit(solution)/shard_map/all_to_all | solution.py:347
  56.3 0.0 copy-start
  56.3 1.0 copy-done
  57.3 10.2 %shard_map.102 = bf16[4,128,128]{2,1,0:T(8,128)(2,1)} custom-call(bf16[4096,128]{1,0:T(8,128)(2,1)} %bitcast.32, bf16[4096,4]{1,0:T(8,128)(2,1)} %convert_convert_fusion.column_mask_ref, f32[4,4096]{1,0:T(4,128)} %fusion.lane_mask_ref, bf16[128,128]{1,0:T(8,128)(2,1)} %inducing_ref.1, bf16[4,128,128]{2,1,0:T(8,128)(2,1)} %proj_ref.2), custom_call_target="tpu_custom_call" | custom-call | tf_op jit(solution)/shard_map/pallas_call | solution.py:243
  67.5 7.7 %shard_map.103 = bf16[2,2,128,128]{3,2,1,0:T(8,128)(2,1)} custom-call(bf16[2,2,128,128]{3,2,1,0:T(8,128)(2,1)} %bitcast.38, bf16[8,128,128]{2,1,0:T(8,128)(2,1)} %mixing_ref.1), custom_call_target="tpu_custom_call" | custom-call | tf_op jit(solution)/shard_map/pallas_call | solution.py:164
  75.2 15.7 %shard_map.104 = bf16[4096,128]{1,0:T(8,128)(2,1)} custom-call(bf16[4096,128]{1,0:T(8,128)(2,1)} %bitcast.33, s32[4096,1]{1,0:T(8,128)} %reshape_reshape.4.row_tile_ref, bf16[512,128]{1,0:T(8,128)(2,1)} %bitcast.37, bf16[4,128,128]{2,1,0:T(8,128)(2,1)} %proj_ref.3), custom_call_target="tpu_custom_call" | custom-call | tf_op jit(solution)/shard_map/pallas_call | solution.py:287
  90.9 25.5 %all_to_all.10 = bf16[128,32,128]{2,1,0:T(8,128)(2,1)} all-to-all(bf16[128,32,128]{2,1,0:T(8,128)(2,1)} %bitcast.34), channel_id=1, replica_groups=mesh['tx'=32,'ty'=4] {'tx','ty'}, dimensions={0} | all-to-all | bytes 2097152 | tf_op jit(solution)/shard_map/all_to_all | solution.py:368
  116.4 9.5 %shard_map.105 = bf16[4096,128]{1,0:T(8,128)(2,1)} custom-call(s32[4096]{0:T(1024)} %fusion.2.pos_ref, s32[4096]{0:T(1024)} %bitcast.41, bf16[4096,128]{1,0:T(8,128)(2,1)} %bitcast.36), custom_call_target="tpu_custom_call" | custom-call | tf_op jit(solution)/shard_map/pallas_call | solution.py:78
  (7 shorter events, 0.1 us)
Async XLA Ops:
  15.6 21.3 %copy-start.1 = (s32[128,512]{1,0:T(8,128)S(1)}, s32[128,512]{1,0:T(8,128)}, u32[]{:S(2)}) copy-start(s32[128,512]{1,0:T(8,128)} %param.14) | copy-start | bytes 786436
  25.4 30.9 %all-to-all-start = ((bf16[128,32,128]{2,1,0:T(8,128)(2,1)}), bf16[128,32,128]{2,1,0:T(8,128)(2,1)S(1)}, u32[]{:S(2)}, u32[]{:S(2)}) async-start(bf16[128,32,128]{2,1,0:T(8,128)(2,1)} %bitcast.35), calls=%async_computation | async-start | bytes 2097152 | tf_op jit(solution)/shard_map/all_to_all | solution.py:347
  56.3 1.0 copy-start

commit v9 on v8

--- a/solution.py
+++ b/solution.py
@@ -257,8 +257,8 @@
     values = jnp.dot(mixture, proj_ref[2], preferred_element_type=jnp.float32).astype(jnp.bfloat16)
     rows = rows_ref[...]
     queries = unit_rows(jnp.dot(rows, proj_ref[0], preferred_element_type=jnp.float32), head_width)
-    key_tile = lax.broadcasted_iota(jnp.int32, (rows.shape[0], mixture.shape[0]), 1) // keys_per_tile
-    own = key_tile == row_tile_ref[...]
+    row_tile = row_tile_ref[...]
+    tiles = mixture.shape[0] // keys_per_tile
     heads_out = []
     for head_id in range(HEADS):
         lower = head_id * head_width
@@ -269,11 +269,21 @@
             (((1,), (1,)), ((), ())),
             preferred_element_type=jnp.float32,
         )
-        weights = jnp.where(own, jnp.exp(sharpness * scores), 0.0)
+        own_scores = scores[:, :keys_per_tile]
+        for t in range(1, tiles):
+            own_scores = jnp.where(
+                row_tile == t, scores[:, t * keys_per_tile : (t + 1) * keys_per_tile], own_scores
+            )
+        weights = jnp.exp(sharpness * own_scores)
         totals = jnp.sum(weights, axis=1, keepdims=True)
-        numer = jnp.dot(
-            weights.astype(jnp.bfloat16), values[:, lower:upper], preferred_element_type=jnp.float32
-        )
+        rounded = weights.astype(jnp.bfloat16)
+        numer = jnp.zeros((rows.shape[0], head_width), jnp.float32)
+        for t in range(tiles):
+            numer += jnp.dot(
+                jnp.where(row_tile == t, rounded, jnp.zeros_like(rounded)),
+                values[t * keys_per_tile : (t + 1) * keys_per_tile, lower:upper],
+                preferred_element_type=jnp.float32,
+            )
         heads_out.append(numer / totals)
     attended = jnp.concatenate(heads_out, axis=1).astype(jnp.bfloat16)
     o_ref[...] = (

time: 126 us -> 128 us (1.016)
  Pallas kernels: 62.5 us -> 64.2 us
    pallas_call x1, Pallas kernels: 15.7 us -> 17.3 us  [finish(): pl.pallas_call(finish_kernel, out_shape=jax.ShapeDtypeStruct(rows.shape,...]
where the time goes in v9:
time: 128 us; the launch traced here: 127 us
  Pallas kernels  64.2 us (50%)
  blocking collectives  25.5 us (20%)
  waiting for transfers between devices  12.2 us (10%)
  starting transfers between devices  11.5 us (9%)
  local copies, waits for them, and re-layouts  9.36 us (7%)
  other arithmetic  4.61 us (4%)
    all_to_all x1, blocking collectives, body(): lax.all_to_all(result.reshape(devices, quota, width), ('tx', 'ty'), split...  25.5 us
    pallas_call x2, Pallas kernels, move_rows(): pl.pallas_call(functools.partial(kernel, 8), out_shape=jax.ShapeDtypeStru...  19.3 us
    pallas_call x1, Pallas kernels, finish(): pl.pallas_call(finish_kernel, out_shape=jax.ShapeDtypeStruct(rows.shape,...  17.3 us
    all_to_all x1, waiting for transfers between devices, body(): lax.all_to_all(outgoing, ('tx', 'ty'), split_axis=0, concat_axis=0, tiled...  12.2 us
    all_to_all x1, starting transfers between devices, body(): lax.all_to_all(outgoing, ('tx', 'ty'), split_axis=0, concat_axis=0, tiled...  11.5 us
    pallas_call x1, Pallas kernels, summarize(): pl.pallas_call(summary_kernel, out_shape=jax.ShapeDtypeStruct((tiles,) +...  10.2 us
    pallas_call x1, Pallas kernels, point_mlp(): pl.pallas_call(mlp_kernel, out_shape=jax.ShapeDtypeStruct((rows, w3.shape...  9.7 us
    pallas_call x1, Pallas kernels, mix_tiles(): pl.pallas_call(functools.partial(mix_kernel, count_x, count_y), out_shape...  7.7 us
  transfers between devices with their start and end apart: 1, of which 1 were waited for; matrix products, arithmetic and copies ran while one was open for 6% of the time, Pallas kernels for 0%

profile of v9, /device:TPU:1, one launch (start us, length us, event | category | flops | bytes accessed | tf_op | source)
XLA Modules:
  0.0 127.5 jit_solution(5075621414908804324)
XLA Ops:
  0.0 0.5 broadcast.55
  0.5 1.4 %fusion.4 = (s32[512]{0:T(512)S(1)}, s32[1,512]{1,0:T(1,128)S(1)}) fusion(s32[]{:T(128)} %broadcast.55, s32[128,512]{1,0:T(8,128)} %param.14, s32[]{:T(128)S(6)} %select_n.22), kind=kLoop, calls=%fused_computation.20 | loop fusion | bytes 6152 | tf_op jit(solution)/shard_map/jit(dynamic_index_in_dim)/dynamic_slice | solution.py:339
  1.9 0.3 reduce-window.9
  2.2 0.1 slice.27
  2.3 0.2 reshape.130
  2.5 0.1 slice_reduce_fusion.1
  2.6 0.1 broadcast.47
  2.7 0.1 reshape.132
  2.8 0.2 reshape.128
  3.0 0.1 slice_add_fusion
  3.1 0.1 add_subtract_fusion
  3.2 0.7 slice_reduce_fusion
  3.9 0.1 lt.52
  4.0 0.1 copy.43
  4.1 0.1 copy.44
  4.2 0.1 lt.56
  4.3 0.1 lt.57
  4.4 0.1 copy.47
  4.5 0.1 copy.45
  4.6 0.1 copy.48
  4.7 0.1 copy.46
  4.8 0.1 add.75
  4.9 0.1 add.76
  5.0 0.1 add.78
  5.1 0.1 add.79
  5.2 0.7 fusion.2.pos_ref
  5.9 9.7 %shard_map.100.x_ref = bf16[4096,128]{1,0:T(8,128)(2,1)} custom-call(bf16[4096,128]{1,0:T(8,128)(2,1)} %x_ref.1, bf16[128,512]{1,0:T(8,128)(2,1)} %w1_ref.1, bf16[1,512,512]{2,1,0:T(8,128)(2,1)} %w2_ref.1, bf16[512,128]{1,0:T(8,128)(2,1)} %w3_ref.1), custom_call_target="tpu_custom_call" | custom-call | tf_op jit(solution)/shard_map/pallas_call | solution.py:35
  15.6 0.0 copy-start.1
  15.6 9.8 %shard_map.101 = bf16[4096,128]{1,0:T(8,128)(2,1)} custom-call(s32[4096]{0:T(1024)} %fusion.2.pos_ref, s32[4096]{0:T(1024)} %bitcast.40, bf16[4096,128]{1,0:T(8,128)(2,1)} %shard_map.100.x_ref), custom_call_target="tpu_custom_call" | custom-call | tf_op jit(solution)/shard_map/pallas_call | solution.py:78
  25.4 11.5 %all-to-all-start = ((bf16[128,32,128]{2,1,0:T(8,128)(2,1)}), bf16[128,32,128]{2,1,0:T(8,128)(2,1)S(1)}, u32[]{:S(2)}, u32[]{:S(2)}) async-start(bf16[128,32,128]{2,1,0:T(8,128)(2,1)} %bitcast.35), calls=%async_computation | async-start | bytes 2097152 | tf_op jit(solution)/shard_map/all_to_all | solution.py:357
  36.9 0.0 copy-done.1
  36.9 0.1 copy.49
  37.1 0.1 copy.50
  37.2 0.1 eq.22
  37.3 0.7 fusion.lane_mask_ref
  38.0 3.5 %reshape_reshape.4.row_tile_ref = s32[4096,1]{1,0:T(8,128)} reshape(s32[128,32]{1,0:T(8,128)S(1)} %copy.50) | data formatting | bytes 32768 | tf_op jit(solution)/shard_map/reshape;reshape | solution.py:308
  41.5 2.7 %convert_convert_fusion.column_mask_ref = bf16[4096,4]{1,0:T(8,128)(2,1)} fusion(s32[4096]{0:T(1024)S(1)} %eq.22), kind=kLoop, calls=%fused_computation | loop fusion | flops 49152 | bytes 49152 | tf_op jit(solution)/shard_map/convert_element_type | solution.py:248
  44.2 12.2 %all-to-all-done = bf16[128,32,128]{2,1,0:T(8,128)(2,1)S(1)} async-done(((bf16[128,32,128]{2,1,0:T(8,128)(2,1)}), bf16[128,32,128]{2,1,0:T(8,128)(2,1)S(1)}, u32[]{:S(2)}, u32[]{:S(2)}) %all-to-all-start) | async-done | bytes 1048608 | tf_op jit(solution)/shard_map/all_to_all | solution.py:357
  56.3 0.0 copy-start
  56.3 1.0 copy-done
  57.3 10.2 %shard_map.102 = bf16[4,128,128]{2,1,0:T(8,128)(2,1)} custom-call(bf16[4096,128]{1,0:T(8,128)(2,1)} %bitcast.32, bf16[4096,4]{1,0:T(8,128)(2,1)} %convert_convert_fusion.column_mask_ref, f32[4,4096]{1,0:T(4,128)} %fusion.lane_mask_ref, bf16[128,128]{1,0:T(8,128)(2,1)} %inducing_ref.1, bf16[4,128,128]{2,1,0:T(8,128)(2,1)} %proj_ref.2), custom_call_target="tpu_custom_call" | custom-call | tf_op jit(solution)/shard_map/pallas_call | solution.py:243
  67.5 7.7 %shard_map.103 = bf16[2,2,128,128]{3,2,1,0:T(8,128)(2,1)} custom-call(bf16[2,2,128,128]{3,2,1,0:T(8,128)(2,1)} %bitcast.38, bf16[8,128,128]{2,1,0:T(8,128)(2,1)} %mixing_ref.1), custom_call_target="tpu_custom_call" | custom-call | tf_op jit(solution)/shard_map/pallas_call | solution.py:164
  75.2 17.3 %shard_map.104 = bf16[4096,128]{1,0:T(8,128)(2,1)} custom-call(bf16[4096,128]{1,0:T(8,128)(2,1)} %bitcast.33, s32[4096,1]{1,0:T(8,128)} %reshape_reshape.4.row_tile_ref, bf16[512,128]{1,0:T(8,128)(2,1)} %bitcast.37, bf16[4,128,128]{2,1,0:T(8,128)(2,1)} %proj_ref.3), custom_call_target="tpu_custom_call" | custom-call | tf_op jit(solution)/shard_map/pallas_call | solution.py:297
  92.5 25.5 %all_to_all.10 = bf16[128,32,128]{2,1,0:T(8,128)(2,1)} all-to-all(bf16[128,32,128]{2,1,0:T(8,128)(2,1)} %bitcast.34), channel_id=1, replica_groups=mesh['tx'=32,'ty'=4] {'tx','ty'}, dimensions={0} | all-to-all | bytes 2097152 | tf_op jit(solution)/shard_map/all_to_all | solution.py:378
  118.0 9.5 %shard_map.105 = bf16[4096,128]{1,0:T(8,128)(2,1)} custom-call(s32[4096]{0:T(1024)} %fusion.2.pos_ref, s32[4096]{0:T(1024)} %bitcast.41, bf16[4096,128]{1,0:T(8,128)(2,1)} %bitcast.36), custom_call_target="tpu_custom_call" | custom-call | tf_op jit(solution)/shard_map/pallas_call | solution.py:78
  (7 shorter events, 0.1 us)
Async XLA Ops:
  15.6 21.3 %copy-start.1 = (s32[128,512]{1,0:T(8,128)S(1)}, s32[128,512]{1,0:T(8,128)}, u32[]{:S(2)}) copy-start(s32[128,512]{1,0:T(8,128)} %param.14) | copy-start | bytes 786436
  25.4 30.9 %all-to-all-start = ((bf16[128,32,128]{2,1,0:T(8,128)(2,1)}), bf16[128,32,128]{2,1,0:T(8,128)(2,1)S(1)}, u32[]{:S(2)}, u32[]{:S(2)}) async-start(bf16[128,32,128]{2,1,0:T(8,128)(2,1)} %bitcast.35), calls=%async_computation | async-start | bytes 2097152 | tf_op jit(solution)/shard_map/all_to_all | solution.py:357
  56.3 1.0 copy-start

commit v10 on v9

--- a/solution.py
+++ b/solution.py
@@ -248,17 +248,16 @@
     )(rows, row_mask.astype(jnp.bfloat16), row_mask.T, inducing, proj)
 
 
-def finish_kernel(rows_ref, row_tile_ref, mixture_ref, proj_ref, o_ref):
+def finish_kernel(rows_ref, row_tile_ref, keys_ref, values_ref, proj_ref, o_ref):
     width = rows_ref.shape[1]
     head_width = width // HEADS
-    keys_per_tile = mixture_ref.shape[0] // TLX // TLY
-    mixture = mixture_ref[...]
-    keys = unit_rows(jnp.dot(mixture, proj_ref[1], preferred_element_type=jnp.float32), head_width)
-    values = jnp.dot(mixture, proj_ref[2], preferred_element_type=jnp.float32).astype(jnp.bfloat16)
+    keys_per_tile = keys_ref.shape[0] // TLX // TLY
+    keys = keys_ref[...]
+    values = values_ref[...]
     rows = rows_ref[...]
     queries = unit_rows(jnp.dot(rows, proj_ref[0], preferred_element_type=jnp.float32), head_width)
     row_tile = row_tile_ref[...]
-    tiles = mixture.shape[0] // keys_per_tile
+    tiles = keys.shape[0] // keys_per_tile
     heads_out = []
     for head_id in range(HEADS):
         lower = head_id * head_width
@@ -293,6 +292,8 @@
 
 def finish(rows, row_tile, mixture, proj, block):
     count = rows.shape[0]
+    keys = unit_heads(jnp.dot(mixture, proj[1], preferred_element_type=jnp.float32), HEADS)
+    values = jnp.dot(mixture, proj[2], preferred_element_type=jnp.float32).astype(jnp.bfloat16)
     full = lambda shape: pl.BlockSpec(shape, lambda i: (0,) * len(shape))
     return pl.pallas_call(
         finish_kernel,
@@ -301,11 +302,12 @@
         in_specs=[
             pl.BlockSpec((block, rows.shape[1]), lambda i: (i, 0)),
             pl.BlockSpec((block, 1), lambda i: (i, 0)),
-            full(mixture.shape),
+            full(keys.shape),
+            full(values.shape),
             full(proj.shape),
         ],
         out_specs=pl.BlockSpec((block, rows.shape[1]), lambda i: (i, 0)),
-    )(rows, row_tile.reshape(count, 1), mixture, proj)
+    )(rows, row_tile.reshape(count, 1), keys, values, proj)
 
 
 def body(

time: 128 us -> 129 us (level)
  Pallas kernels: 64.2 us -> 61.3 us
  matrix products: 0 us -> 2.83 us
    pallas_call x1, Pallas kernels: 17.3 us -> 14.5 us  [finish(): pl.pallas_call(finish_kernel, out_shape=jax.ShapeDtypeStruct(rows.shape,...]
    dot_general x0 -> x2, matrix products: none -> 2.83 us  [the longest x1 1.72 us: finish(): jnp.dot(mixture, proj[2], preferred_element_type=jnp.float32)]
where the time goes in v10:
time: 129 us; the launch traced here: 128 us
  Pallas kernels  61.3 us (48%)
  blocking collectives  25.5 us (20%)
  waiting for transfers between devices  12 us (9%)
  starting transfers between devices  11.5 us (9%)
  local copies, waits for them, and re-layouts  10.2 us (8%)
  other arithmetic  4.67 us (4%)
  matrix products  2.83 us (2%)
    all_to_all x1, blocking collectives, body(): lax.all_to_all(result.reshape(devices, quota, width), ('tx', 'ty'), split...  25.5 us
    pallas_call x2, Pallas kernels, move_rows(): pl.pallas_call(functools.partial(kernel, 8), out_shape=jax.ShapeDtypeStru...  19.3 us
    pallas_call x1, Pallas kernels, finish(): pl.pallas_call(finish_kernel, out_shape=jax.ShapeDtypeStruct(rows.shape,...  14.5 us
    all_to_all x1, waiting for transfers between devices, body(): lax.all_to_all(outgoing, ('tx', 'ty'), split_axis=0, concat_axis=0, tiled...  12 us
    all_to_all x1, starting transfers between devices, body(): lax.all_to_all(outgoing, ('tx', 'ty'), split_axis=0, concat_axis=0, tiled...  11.5 us
    pallas_call x1, Pallas kernels, summarize(): pl.pallas_call(summary_kernel, out_shape=jax.ShapeDtypeStruct((tiles,) +...  10.2 us
    pallas_call x1, Pallas kernels, point_mlp(): pl.pallas_call(mlp_kernel, out_shape=jax.ShapeDtypeStruct((rows, w3.shape...  9.7 us
    pallas_call x1, Pallas kernels, mix_tiles(): pl.pallas_call(functools.partial(mix_kernel, count_x, count_y), out_shape...  7.7 us
  transfers between devices with their start and end apart: 1, of which 1 were waited for; matrix products, arithmetic and copies ran while one was open for 6% of the time, Pallas kernels for 0%

profile of v10, /device:TPU:1, one launch (start us, length us, event | category | flops | bytes accessed | tf_op | source)
XLA Modules:
  0.0 128.2 jit_solution(8001745824723273569)
XLA Ops:
  0.0 0.5 broadcast.60
  0.5 1.4 %fusion.6 = (s32[512]{0:T(512)S(1)}, s32[1,512]{1,0:T(1,128)S(1)}) fusion(s32[]{:T(128)} %broadcast.60, s32[128,512]{1,0:T(8,128)} %param.14, s32[]{:T(128)S(6)} %select_n.22), kind=kLoop, calls=%fused_computation.27 | loop fusion | bytes 6152 | tf_op jit(solution)/shard_map/jit(dynamic_index_in_dim)/dynamic_slice | solution.py:341
  1.9 0.3 reduce-window.9
  2.2 0.1 slice.33
  2.3 0.2 reshape.140
  2.5 0.1 slice_reduce_fusion.1
  2.6 0.1 broadcast.52
  2.7 0.1 reshape.142
  2.8 0.2 reshape.138
  3.0 0.1 slice_add_fusion
  3.1 0.1 add_subtract_fusion
  3.2 0.7 slice_reduce_fusion
  3.9 0.1 lt.52
  4.0 0.1 copy.51
  4.1 0.1 copy.52
  4.2 0.1 lt.56
  4.3 0.1 lt.57
  4.4 0.1 copy.55
  4.5 0.1 copy.53
  4.6 0.1 copy.56
  4.7 0.1 copy.54
  4.8 0.1 add.86
  4.9 0.1 add.87
  5.0 0.1 add.89
  5.1 0.1 add.90
  5.2 0.7 fusion.4.pos_ref
  5.9 9.7 %shard_map.100.x_ref = bf16[4096,128]{1,0:T(8,128)(2,1)} custom-call(bf16[4096,128]{1,0:T(8,128)(2,1)} %x_ref.1, bf16[128,512]{1,0:T(8,128)(2,1)} %w1_ref.1, bf16[1,512,512]{2,1,0:T(8,128)(2,1)} %w2_ref.1, bf16[512,128]{1,0:T(8,128)(2,1)} %w3_ref.1), custom_call_target="tpu_custom_call" | custom-call | tf_op jit(solution)/shard_map/pallas_call | solution.py:35
  15.6 0.0 copy-start.2
  15.6 9.8 %shard_map.101 = bf16[4096,128]{1,0:T(8,128)(2,1)} custom-call(s32[4096]{0:T(1024)} %fusion.4.pos_ref, s32[4096]{0:T(1024)} %bitcast.57, bf16[4096,128]{1,0:T(8,128)(2,1)} %shard_map.100.x_ref), custom_call_target="tpu_custom_call" | custom-call | tf_op jit(solution)/shard_map/pallas_call | solution.py:78
  25.4 0.0 copy-start.1
  25.4 11.5 %all-to-all-start = ((bf16[128,32,128]{2,1,0:T(8,128)(2,1)}), bf16[128,32,128]{2,1,0:T(8,128)(2,1)S(1)}, u32[]{:S(2)}, u32[]{:S(2)}) async-start(bf16[128,32,128]{2,1,0:T(8,128)(2,1)} %bitcast.48), calls=%async_computation | async-start | bytes 2097152 | tf_op jit(solution)/shard_map/all_to_all | solution.py:359
  36.9 0.0 copy-done.2
  36.9 0.1 copy.57
  37.1 0.1 copy.58
  37.2 0.1 eq.22
  37.3 3.5 %reshape_reshape.4.row_tile_ref = s32[4096,1]{1,0:T(8,128)} reshape(s32[128,32]{1,0:T(8,128)S(1)} %copy.58) | data formatting | bytes 32768 | tf_op jit(solution)/shard_map/reshape;reshape | solution.py:310
  40.9 0.6 fusion.lane_mask_ref
  41.5 0.0 copy-done.1
  41.5 0.1 copy.61
  41.6 2.7 %convert_convert_fusion.column_mask_ref = bf16[4096,4]{1,0:T(8,128)(2,1)} fusion(s32[4096]{0:T(1024)S(1)} %eq.22), kind=kLoop, calls=%fused_computation | loop fusion | flops 49152 | bytes 49152 | tf_op jit(solution)/shard_map/convert_element_type | solution.py:248
  44.3 12.0 %all-to-all-done = bf16[128,32,128]{2,1,0:T(8,128)(2,1)S(1)} async-done(((bf16[128,32,128]{2,1,0:T(8,128)(2,1)}), bf16[128,32,128]{2,1,0:T(8,128)(2,1)S(1)}, u32[]{:S(2)}, u32[]{:S(2)}) %all-to-all-start) | async-done | bytes 1048608 | tf_op jit(solution)/shard_map/all_to_all | solution.py:359
  56.3 0.0 copy-start
  56.3 1.0 copy-done
  57.3 10.2 %shard_map.102 = bf16[4,128,128]{2,1,0:T(8,128)(2,1)} custom-call(bf16[4096,128]{1,0:T(8,128)(2,1)} %bitcast.46, bf16[4096,4]{1,0:T(8,128)(2,1)} %convert_convert_fusion.column_mask_ref, f32[4,4096]{1,0:T(4,128)} %fusion.lane_mask_ref, bf16[128,128]{1,0:T(8,128)(2,1)} %inducing_ref.1, bf16[4,128,128]{2,1,0:T(8,128)(2,1)} %proj_ref.2), custom_call_target="tpu_custom_call" | custom-call | tf_op jit(solution)/shard_map/pallas_call | solution.py:243
  67.5 7.7 %shard_map.103 = bf16[2,2,128,128]{3,2,1,0:T(8,128)(2,1)} custom-call(bf16[2,2,128,128]{3,2,1,0:T(8,128)(2,1)} %bitcast.54, bf16[8,128,128]{2,1,0:T(8,128)(2,1)} %mixing_ref.1), custom_call_target="tpu_custom_call" | custom-call | tf_op jit(solution)/shard_map/pallas_call | solution.py:164
  75.2 1.7 %convolution_convert_fusion.values_ref = bf16[512,128]{1,0:T(8,128)(2,1)} fusion(bf16[512,128]{1,0:T(8,128)(2,1)} %bitcast.51, bf16[4,128,128]{2,1,0:T(8,128)(2,1)S(1)} %copy-done.1), kind=kOutput, calls=%fused_computation.2 | convolution fusion | flops 16842752 | bytes 294912 | tf_op jit(solution)/shard_map/dot_general | solution.py:296
  76.9 1.1 multiply_reduce_fusion
  78.1 0.8 copy.63.keys_ref
  78.8 14.5 %shard_map.104 = bf16[4096,128]{1,0:T(8,128)(2,1)} custom-call(bf16[4096,128]{1,0:T(8,128)(2,1)} %bitcast.47, s32[4096,1]{1,0:T(8,128)} %reshape_reshape.4.row_tile_ref, bf16[512,128]{1,0:T(8,128)(2,1)} %copy.63.keys_ref, bf16[512,128]{1,0:T(8,128)(2,1)} %convolution_convert_fusion.values_ref, bf16[4,128,128]{2,1,0:T(8,128)(2,1)} %proj_ref.3), custom_call_target="tpu_custom_call" | custom-call | tf_op jit(solution)/shard_map/pallas_call | solution.py:298
  93.3 25.5 %all_to_all.10 = bf16[128,32,128]{2,1,0:T(8,128)(2,1)} all-to-all(bf16[128,32,128]{2,1,0:T(8,128)(2,1)} %bitcast.50), channel_id=1, replica_groups=mesh['tx'=32,'ty'=4] {'tx','ty'}, dimensions={0} | all-to-all | bytes 2097152 | tf_op jit(solution)/shard_map/all_to_all | solution.py:380
  118.8 9.4 %shard_map.105 = bf16[4096,128]{1,0:T(8,128)(2,1)} custom-call(s32[4096]{0:T(1024)} %fusion.4.pos_ref, s32[4096]{0:T(1024)} %bitcast.58, bf16[4096,128]{1,0:T(8,128)(2,1)} %bitcast.49), custom_call_target="tpu_custom_call" | custom-call | tf_op jit(solution)/shard_map/pallas_call | solution.py:78
  (10 shorter events, 0.2 us)
Async XLA Ops:
  15.6 21.3 %copy-start.2 = (s32[128,512]{1,0:T(8,128)S(1)}, s32[128,512]{1,0:T(8,128)}, u32[]{:S(2)}) copy-start(s32[128,512]{1,0:T(8,128)} %param.14) | copy-start | bytes 786436
  25.4 16.1 %copy-start.1 = (bf16[4,128,128]{2,1,0:T(8,128)(2,1)S(1)}, bf16[4,128,128]{2,1,0:T(8,128)(2,1)}, u32[]{:S(2)}) copy-start(bf16[4,128,128]{2,1,0:T(8,128)(2,1)} %proj_ref.3) | copy-start | bytes 393220
  25.4 30.9 %all-to-all-start = ((bf16[128,32,128]{2,1,0:T(8,128)(2,1)}), bf16[128,32,128]{2,1,0:T(8,128)(2,1)S(1)}, u32[]{:S(2)}, u32[]{:S(2)}) async-start(bf16[128,32,128]{2,1,0:T(8,128)(2,1)} %bitcast.48), calls=%async_computation | async-start | bytes 2097152 | tf_op jit(solution)/shard_map/all_to_all | solution.py:359
  56.3 1.0 copy-start

commit v11 on v7

--- a/solution.py
+++ b/solution.py
@@ -76,7 +76,7 @@
 
 def move_rows(kernel, pos, order, x):
     return pl.pallas_call(
-        functools.partial(kernel, 8),
+        functools.partial(kernel, 32),
         out_shape=jax.ShapeDtypeStruct(x.shape, jnp.bfloat16),
         in_specs=[
             pl.BlockSpec(memory_space=pltpu.SMEM),
@@ -274,7 +274,7 @@
     head_width = width // HEADS
     inducing_count = inducing.shape[0]
 
-    features = point_mlp(points, embed_weight, inner_weights, output_weight, 512)
+    features = point_mlp(points, embed_weight, inner_weights, output_weight, 2048)
 
     own_counts = lax.dynamic_index_in_dim(counts, own_index, 0, keepdims=False)
     own_offsets = jnp.cumsum(own_counts) - own_counts

time: 120 us -> 115 us (0.958)
  Pallas kernels: 46.9 us -> 41 us
    pallas_call x2, Pallas kernels: 19.3 us -> 15.1 us  [move_rows(): pl.pallas_call(functools.partial(kernel, 32), out_shape=jax.ShapeDtypeStr...]
    pallas_call x1, Pallas kernels: 9.7 us -> 8.09 us  [point_mlp(): pl.pallas_call(mlp_kernel, out_shape=jax.ShapeDtypeStruct((rows, w3.shape...]
where the time goes in v11:
time: 115 us; the launch traced here: 114 us
  Pallas kernels  41 us (36%)
  blocking collectives  25.3 us (22%)
  waiting for transfers between devices  14.8 us (13%)
  starting transfers between devices  11.5 us (10%)
  matrix products  9.78 us (9%)
  local copies, waits for them, and re-layouts  6.58 us (6%)
  other arithmetic  4.89 us (4%)
    all_to_all x1, blocking collectives, body(): lax.all_to_all(result.reshape(devices, quota, width), ('tx', 'ty'), split...  25.3 us
    pallas_call x2, Pallas kernels, move_rows(): pl.pallas_call(functools.partial(kernel, 32), out_shape=jax.ShapeDtypeStr...  15.1 us
    all_to_all x1, waiting for transfers between devices, body(): lax.all_to_all(outgoing, ('tx', 'ty'), split_axis=0, concat_axis=0, tiled...  14.8 us
    all_to_all x1, starting transfers between devices, body(): lax.all_to_all(outgoing, ('tx', 'ty'), split_axis=0, concat_axis=0, tiled...  11.5 us
    pallas_call x1, Pallas kernels, summarize(): pl.pallas_call(summary_kernel, out_shape=jax.ShapeDtypeStruct((tiles,) +...  10.2 us
    pallas_call x1, Pallas kernels, point_mlp(): pl.pallas_call(mlp_kernel, out_shape=jax.ShapeDtypeStruct((rows, w3.shape...  8.09 us
    pallas_call x1, Pallas kernels, mix_tiles(): pl.pallas_call(functools.partial(mix_kernel, count_x, count_y), out_shape...  7.69 us
    dot_general x2, matrix products, body(): jnp.dot(point_queries[:, lower:upper], second_keys[:, lower:upper].T, pre...  4.92 us
  transfers between devices with their start and end apart: 1, of which 1 were waited for; matrix products, arithmetic and copies ran while one was open for 4% of the time, Pallas kernels for 0%

profile of v11, /device:TPU:1, one launch (start us, length us, event | category | flops | bytes accessed | tf_op | source)
XLA Modules:
  0.0 114.1 jit_solution(4007729627651501508)
XLA Ops:
  0.0 0.5 broadcast.75
  0.5 1.4 %fusion.29 = (s32[512]{0:T(512)S(1)}, s32[1,512]{1,0:T(1,128)S(1)}) fusion(s32[]{:T(128)} %broadcast.75, s32[128,512]{1,0:T(8,128)} %param.14, s32[]{:T(128)S(6)} %select_n.22), kind=kLoop, calls=%fused_computation.58 | loop fusion | bytes 6152 | tf_op jit(solution)/shard_map/jit(dynamic_index_in_dim)/dynamic_slice | solution.py:279
  1.9 0.3 reduce-window.9
  2.2 0.1 slice.57
  2.3 0.2 reshape.155
  2.5 0.1 slice_reduce_fusion.1
  2.6 0.1 broadcast.62
  2.7 0.1 reshape.157
  2.8 0.2 reshape.153
  3.0 0.1 slice_add_fusion
  3.1 0.1 add_subtract_fusion
  3.2 0.0 copy-start.2
  3.2 0.7 slice_reduce_fusion
  4.0 0.1 lt.52
  4.0 0.1 copy.51
  4.1 0.1 copy.52
  4.2 0.1 lt.56
  4.3 0.1 lt.57
  4.4 0.1 copy.55
  4.5 0.1 copy.53
  4.6 0.1 copy.56
  4.7 0.1 copy.54
  4.8 0.1 add.100
  4.9 0.1 add.101
  5.0 0.1 add.103
  5.1 0.1 add.104
  5.2 0.7 fusion.26.pos_ref
  5.9 8.1 %shard_map.100.x_ref = bf16[4096,128]{1,0:T(8,128)(2,1)} custom-call(bf16[4096,128]{1,0:T(8,128)(2,1)} %x_ref.1, bf16[128,512]{1,0:T(8,128)(2,1)} %w1_ref.1, bf16[1,512,512]{2,1,0:T(8,128)(2,1)} %w2_ref.1, bf16[512,128]{1,0:T(8,128)(2,1)} %w3_ref.1), custom_call_target="tpu_custom_call" | custom-call | tf_op jit(solution)/shard_map/pallas_call | solution.py:35
  14.0 0.0 copy-start.3
  14.0 7.7 %shard_map.101 = bf16[4096,128]{1,0:T(8,128)(2,1)} custom-call(s32[4096]{0:T(1024)} %fusion.26.pos_ref, s32[4096]{0:T(1024)} %bitcast.88, bf16[4096,128]{1,0:T(8,128)(2,1)} %shard_map.100.x_ref), custom_call_target="tpu_custom_call" | custom-call | tf_op jit(solution)/shard_map/pallas_call | solution.py:78
  21.6 11.5 %all-to-all-start = ((bf16[128,32,128]{2,1,0:T(8,128)(2,1)}), bf16[128,32,128]{2,1,0:T(8,128)(2,1)S(1)}, u32[]{:S(2)}, u32[]{:S(2)}) async-start(bf16[128,32,128]{2,1,0:T(8,128)(2,1)} %bitcast.78), calls=%async_computation | async-start | bytes 2097152 | tf_op jit(solution)/shard_map/all_to_all | solution.py:297
  33.2 0.0 copy-done.2
  33.2 0.1 copy.58
  33.4 0.1 copy.59
  33.5 0.1 eq.22
  33.6 2.7 %fusion.7 = (f32[4096,4]{1,0:T(8,128)S(1)}, bf16[4096,4]{1,0:T(8,128)(2,1)}) fusion(s32[4096]{0:T(1024)S(1)} %eq.22), kind=kLoop, calls=%fused_computation.15 | loop fusion | flops 49152 | bytes 114688 | tf_op jit(solution)/shard_map/convert_element_type | solution.py:309
  36.3 0.0 copy-done.3
  36.3 0.1 copy.61
  36.4 0.1 copy.57
  36.5 0.6 copy.62
  37.2 0.6 fusion.20.lane_mask_ref
  37.8 14.8 %all-to-all-done = bf16[128,32,128]{2,1,0:T(8,128)(2,1)S(1)} async-done(((bf16[128,32,128]{2,1,0:T(8,128)(2,1)}), bf16[128,32,128]{2,1,0:T(8,128)(2,1)S(1)}, u32[]{:S(2)}, u32[]{:S(2)}) %all-to-all-start) | async-done | bytes 1048608 | tf_op jit(solution)/shard_map/all_to_all | solution.py:297
  52.6 0.0 copy-start
  52.6 0.5 multiply_reduce_fusion
  53.1 0.5 copy-done
  53.5 10.2 %shard_map.102 = bf16[4,128,128]{2,1,0:T(8,128)(2,1)} custom-call(bf16[4096,128]{1,0:T(8,128)(2,1)} %bitcast.73, bf16[4096,4]{1,0:T(8,128)(2,1)} %get-tuple-element.16.column_mask_ref, f32[4,4096]{1,0:T(4,128)} %fusion.20.lane_mask_ref, bf16[128,128]{1,0:T(8,128)(2,1)} %inducing_ref.1, bf16[4,128,128]{2,1,0:T(8,128)(2,1)} %proj_ref.1), custom_call_target="tpu_custom_call" | custom-call | tf_op jit(solution)/shard_map/pallas_call | solution.py:243
  63.7 7.7 %shard_map.103 = bf16[2,2,128,128]{3,2,1,0:T(8,128)(2,1)} custom-call(bf16[2,2,128,128]{3,2,1,0:T(8,128)(2,1)} %bitcast.84, bf16[8,128,128]{2,1,0:T(8,128)(2,1)} %mixing_ref.1), custom_call_target="tpu_custom_call" | custom-call | tf_op jit(solution)/shard_map/pallas_call | solution.py:164
  71.4 1.1 convolution_convert_fusion
  72.5 1.1 multiply_reduce_fusion.1
  73.7 0.2 divide_convert_fusion
  73.9 1.3 %fusion.12 = f32[4096,512]{0,1:T(8,128)S(1)} fusion(bf16[4096,128]{0,1:T(8,128)(2,1)S(1)} %bitcast.75, bf16[512,128]{0,1:T(8,128)(2,1)S(1)} %bitcast.82), kind=kOutput, calls=%fused_computation.21 | convolution fusion | flops 268435456 | bytes 8978432 | tf_op jit(solution)/shard_map/dot_general | solution.py:330
  75.2 3.6 %fusion = (f32[4096]{0:T(1024)S(1)}, f32[4096]{0:T(1024)S(1)}, bf16[4096,512]{0,1:T(8,128)(2,1)S(1)}, bf16[4096,512]{0,1:T(8,128)(2,1)S(1)}) fusion(f32[4096,4]{0,1:T(4,128)S(1)} %copy.62, f32[4096,512]{0,1:T(8,128)S(1)} %fusion.12, bf16[512,128]{0,1:T(8,128)(2,1)S(1)} %bitcast.83, bf16[4096,128]{0,1:T(8,128)(2,1)S(1)} %bitcast.76), kind=kOutput, calls=%fused_computation.2 | convolution fusion | flops 285204480 | bytes 17465344 | tf_op jit(solution)/shard_map/dot_general | solution.py:330
  78.8 0.8 fusion.5
  79.7 0.0 copy-start.1
  79.7 0.8 fusion.6
  80.5 0.4 copy-done.1
  80.9 0.5 fusion.4
  81.4 25.3 %all_to_all.10 = bf16[128,32,128]{2,1,0:T(8,128)(2,1)} all-to-all(bf16[128,32,128]{2,1,0:T(8,128)(2,1)S(1)} %bitcast.77), channel_id=1, replica_groups=mesh['tx'=32,'ty'=4] {'tx','ty'}, dimensions={0} | all-to-all | bytes 2097152 | tf_op jit(solution)/shard_map/all_to_all | solution.py:349
  106.7 7.4 %shard_map.104 = bf16[4096,128]{1,0:T(8,128)(2,1)} custom-call(s32[4096]{0:T(1024)} %fusion.26.pos_ref, s32[4096]{0:T(1024)} %bitcast.89, bf16[4096,128]{1,0:T(8,128)(2,1)} %bitcast.79), custom_call_target="tpu_custom_call" | custom-call | tf_op jit(solution)/shard_map/pallas_call | solution.py:78
  (11 shorter events, 0.2 us)
Async XLA Ops:
  3.2 29.9 %copy-start.2 = (s32[128,512]{1,0:T(8,128)S(1)}, s32[128,512]{1,0:T(8,128)}, u32[]{:S(2)}) copy-start(s32[128,512]{1,0:T(8,128)} %param.14) | copy-start | bytes 786436
  14.0 22.3 %copy-start.3 = (bf16[4,128,128]{2,1,0:T(8,128)(2,1)S(1)}, bf16[4,128,128]{2,1,0:T(8,128)(2,1)}, u32[]{:S(2)}) copy-start(bf16[4,128,128]{2,1,0:T(8,128)(2,1)} %param.18) | copy-start | bytes 393220
  21.6 30.9 %all-to-all-start = ((bf16[128,32,128]{2,1,0:T(8,128)(2,1)}), bf16[128,32,128]{2,1,0:T(8,128)(2,1)S(1)}, u32[]{:S(2)}, u32[]{:S(2)}) async-start(bf16[128,32,128]{2,1,0:T(8,128)(2,1)} %bitcast.78), calls=%async_computation | async-start | bytes 2097152 | tf_op jit(solution)/shard_map/all_to_all | solution.py:297
  52.6 1.0 copy-start
  79.7 1.2 %copy-start.1 = (bf16[128,32,128]{2,1,0:T(8,128)(2,1)S(1)}, bf16[128,32,128]{2,1,0:T(8,128)(2,1)}, u32[]{:S(2)}) copy-start(bf16[128,32,128]{2,1,0:T(8,128)(2,1)} %copy-done) | copy-start | bytes 3145732

commit v12 on v11

--- a/solution.py
+++ b/solution.py
@@ -185,14 +185,17 @@
 
 
 def unit_rows(projected, head_width):
-    lanes = lax.broadcasted_iota(jnp.int32, projected.shape, projected.ndim - 1)
-    squares = projected * projected
-    magnitude = jnp.zeros_like(projected)
-    for head_id in range(projected.shape[-1] // head_width):
-        in_head = (lanes >= head_id * head_width) & (lanes < (head_id + 1) * head_width)
-        total = jnp.sum(jnp.where(in_head, squares, 0.0), axis=-1, keepdims=True)
-        magnitude = jnp.where(in_head, jnp.sqrt(total + epsilon), magnitude)
-    return (projected / magnitude).astype(jnp.bfloat16)
+    width = projected.shape[-1]
+    lane_head = lax.broadcasted_iota(jnp.int32, (width, width), 0) // head_width
+    column_head = lax.broadcasted_iota(jnp.int32, (width, width), 1) // head_width
+    same_head = (lane_head == column_head).astype(jnp.float32)
+    totals = jnp.dot(
+        projected * projected,
+        same_head,
+        precision=lax.Precision.HIGHEST,
+        preferred_element_type=jnp.float32,
+    )
+    return (projected / jnp.sqrt(totals + epsilon)).astype(jnp.bfloat16)
 
 
 def summary_kernel(rows_ref, column_mask_ref, lane_mask_ref, inducing_ref, proj_ref, o_ref):

time: 115 us -> 114 us (level)
  no operation moved by 1% of the time
where the time goes in v12:
time: 114 us; the launch traced here: 113 us
  Pallas kernels  40.4 us (35%)
  blocking collectives  25.3 us (22%)
  waiting for transfers between devices  14.8 us (13%)
  starting transfers between devices  11.5 us (10%)
  matrix products  9.78 us (9%)
  local copies, waits for them, and re-layouts  6.58 us (6%)
  other arithmetic  4.89 us (4%)
    all_to_all x1, blocking collectives, body(): lax.all_to_all(result.reshape(devices, quota, width), ('tx', 'ty'), split...  25.3 us
    pallas_call x2, Pallas kernels, move_rows(): pl.pallas_call(functools.partial(kernel, 32), out_shape=jax.ShapeDtypeStr...  15.1 us
    all_to_all x1, waiting for transfers between devices, body(): lax.all_to_all(outgoing, ('tx', 'ty'), split_axis=0, concat_axis=0, tiled...  14.8 us
    all_to_all x1, starting transfers between devices, body(): lax.all_to_all(outgoing, ('tx', 'ty'), split_axis=0, concat_axis=0, tiled...  11.5 us
    pallas_call x1, Pallas kernels, summarize(): pl.pallas_call(summary_kernel, out_shape=jax.ShapeDtypeStruct((tiles,) +...  9.49 us
    pallas_call x1, Pallas kernels, point_mlp(): pl.pallas_call(mlp_kernel, out_shape=jax.ShapeDtypeStruct((rows, w3.shape...  8.09 us
    pallas_call x1, Pallas kernels, mix_tiles(): pl.pallas_call(functools.partial(mix_kernel, count_x, count_y), out_shape...  7.7 us
    dot_general x2, matrix products, body(): jnp.dot(point_queries[:, lower:upper], second_keys[:, lower:upper].T, pre...  4.92 us
  transfers between devices with their start and end apart: 1, of which 1 were waited for; matrix products, arithmetic and copies ran while one was open for 4% of the time, Pallas kernels for 0%

profile of v12, /device:TPU:1, one launch (start us, length us, event | category | flops | bytes accessed | tf_op | source)
XLA Modules:
  0.0 113.5 jit_solution(7281805907841877885)
XLA Ops:
  0.0 0.5 broadcast.75
  0.5 1.4 %fusion.29 = (s32[512]{0:T(512)S(1)}, s32[1,512]{1,0:T(1,128)S(1)}) fusion(s32[]{:T(128)} %broadcast.75, s32[128,512]{1,0:T(8,128)} %param.14, s32[]{:T(128)S(6)} %select_n.22), kind=kLoop, calls=%fused_computation.58 | loop fusion | bytes 6152 | tf_op jit(solution)/shard_map/jit(dynamic_index_in_dim)/dynamic_slice | solution.py:282
  1.9 0.3 reduce-window.9
  2.2 0.1 slice.57
  2.3 0.2 reshape.155
  2.5 0.1 slice_reduce_fusion.1
  2.6 0.1 broadcast.62
  2.7 0.1 reshape.157
  2.8 0.2 reshape.153
  3.0 0.1 slice_add_fusion
  3.1 0.1 add_subtract_fusion
  3.2 0.0 copy-start.2
  3.2 0.7 slice_reduce_fusion
  4.0 0.1 lt.52
  4.0 0.1 copy.51
  4.1 0.1 copy.52
  4.2 0.1 lt.56
  4.3 0.1 lt.57
  4.4 0.1 copy.55
  4.5 0.1 copy.53
  4.6 0.1 copy.56
  4.7 0.1 copy.54
  4.8 0.1 add.100
  4.9 0.1 add.101
  5.0 0.1 add.103
  5.1 0.1 add.104
  5.2 0.7 fusion.26.pos_ref
  5.9 8.1 %shard_map.100.x_ref = bf16[4096,128]{1,0:T(8,128)(2,1)} custom-call(bf16[4096,128]{1,0:T(8,128)(2,1)} %x_ref.1, bf16[128,512]{1,0:T(8,128)(2,1)} %w1_ref.1, bf16[1,512,512]{2,1,0:T(8,128)(2,1)} %w2_ref.1, bf16[512,128]{1,0:T(8,128)(2,1)} %w3_ref.1), custom_call_target="tpu_custom_call" | custom-call | tf_op jit(solution)/shard_map/pallas_call | solution.py:35
  14.0 0.0 copy-start.3
  14.0 7.7 %shard_map.101 = bf16[4096,128]{1,0:T(8,128)(2,1)} custom-call(s32[4096]{0:T(1024)} %fusion.26.pos_ref, s32[4096]{0:T(1024)} %bitcast.88, bf16[4096,128]{1,0:T(8,128)(2,1)} %shard_map.100.x_ref), custom_call_target="tpu_custom_call" | custom-call | tf_op jit(solution)/shard_map/pallas_call | solution.py:78
  21.6 11.5 %all-to-all-start = ((bf16[128,32,128]{2,1,0:T(8,128)(2,1)}), bf16[128,32,128]{2,1,0:T(8,128)(2,1)S(1)}, u32[]{:S(2)}, u32[]{:S(2)}) async-start(bf16[128,32,128]{2,1,0:T(8,128)(2,1)} %bitcast.78), calls=%async_computation | async-start | bytes 2097152 | tf_op jit(solution)/shard_map/all_to_all | solution.py:300
  33.2 0.0 copy-done.2
  33.2 0.1 copy.58
  33.4 0.1 copy.59
  33.5 0.1 eq.22
  33.6 2.7 %fusion.7 = (f32[4096,4]{1,0:T(8,128)S(1)}, bf16[4096,4]{1,0:T(8,128)(2,1)}) fusion(s32[4096]{0:T(1024)S(1)} %eq.22), kind=kLoop, calls=%fused_computation.15 | loop fusion | flops 49152 | bytes 114688 | tf_op jit(solution)/shard_map/convert_element_type | solution.py:312
  36.3 0.0 copy-done.3
  36.3 0.1 copy.61
  36.4 0.1 copy.57
  36.5 0.6 copy.62
  37.2 0.6 fusion.20.lane_mask_ref
  37.8 14.8 %all-to-all-done = bf16[128,32,128]{2,1,0:T(8,128)(2,1)S(1)} async-done(((bf16[128,32,128]{2,1,0:T(8,128)(2,1)}), bf16[128,32,128]{2,1,0:T(8,128)(2,1)S(1)}, u32[]{:S(2)}, u32[]{:S(2)}) %all-to-all-start) | async-done | bytes 1048608 | tf_op jit(solution)/shard_map/all_to_all | solution.py:300
  52.6 0.0 copy-start
  52.6 0.5 multiply_reduce_fusion
  53.1 0.5 copy-done
  53.5 9.5 %shard_map.102 = bf16[4,128,128]{2,1,0:T(8,128)(2,1)} custom-call(bf16[4096,128]{1,0:T(8,128)(2,1)} %bitcast.73, bf16[4096,4]{1,0:T(8,128)(2,1)} %get-tuple-element.16.column_mask_ref, f32[4,4096]{1,0:T(4,128)} %fusion.20.lane_mask_ref, bf16[128,128]{1,0:T(8,128)(2,1)} %inducing_ref.1, bf16[4,128,128]{2,1,0:T(8,128)(2,1)} %proj_ref.1), custom_call_target="tpu_custom_call" | custom-call | tf_op jit(solution)/shard_map/pallas_call | solution.py:246
  63.0 7.7 %shard_map.103 = bf16[2,2,128,128]{3,2,1,0:T(8,128)(2,1)} custom-call(bf16[2,2,128,128]{3,2,1,0:T(8,128)(2,1)} %bitcast.84, bf16[8,128,128]{2,1,0:T(8,128)(2,1)} %mixing_ref.1), custom_call_target="tpu_custom_call" | custom-call | tf_op jit(solution)/shard_map/pallas_call | solution.py:164
  70.7 1.1 convolution_convert_fusion
  71.9 1.1 multiply_reduce_fusion.1
  73.0 0.2 divide_convert_fusion
  73.2 1.3 %fusion.12 = f32[4096,512]{0,1:T(8,128)S(1)} fusion(bf16[4096,128]{0,1:T(8,128)(2,1)S(1)} %bitcast.75, bf16[512,128]{0,1:T(8,128)(2,1)S(1)} %bitcast.82), kind=kOutput, calls=%fused_computation.21 | convolution fusion | flops 268435456 | bytes 8978432 | tf_op jit(solution)/shard_map/dot_general | solution.py:333
  74.5 3.6 %fusion = (f32[4096]{0:T(1024)S(1)}, f32[4096]{0:T(1024)S(1)}, bf16[4096,512]{0,1:T(8,128)(2,1)S(1)}, bf16[4096,512]{0,1:T(8,128)(2,1)S(1)}) fusion(f32[4096,4]{0,1:T(4,128)S(1)} %copy.62, f32[4096,512]{0,1:T(8,128)S(1)} %fusion.12, bf16[512,128]{0,1:T(8,128)(2,1)S(1)} %bitcast.83, bf16[4096,128]{0,1:T(8,128)(2,1)S(1)} %bitcast.76), kind=kOutput, calls=%fused_computation.2 | convolution fusion | flops 285204480 | bytes 17465344 | tf_op jit(solution)/shard_map/dot_general | solution.py:333
  78.2 0.8 fusion.5
  79.0 0.0 copy-start.1
  79.0 0.8 fusion.6
  79.9 0.4 copy-done.1
  80.2 0.5 fusion.4
  80.7 25.3 %all_to_all.10 = bf16[128,32,128]{2,1,0:T(8,128)(2,1)} all-to-all(bf16[128,32,128]{2,1,0:T(8,128)(2,1)S(1)} %bitcast.77), channel_id=1, replica_groups=mesh['tx'=32,'ty'=4] {'tx','ty'}, dimensions={0} | all-to-all | bytes 2097152 | tf_op jit(solution)/shard_map/all_to_all | solution.py:352
  106.0 7.4 %shard_map.104 = bf16[4096,128]{1,0:T(8,128)(2,1)} custom-call(s32[4096]{0:T(1024)} %fusion.26.pos_ref, s32[4096]{0:T(1024)} %bitcast.89, bf16[4096,128]{1,0:T(8,128)(2,1)} %bitcast.79), custom_call_target="tpu_custom_call" | custom-call | tf_op jit(solution)/shard_map/pallas_call | solution.py:78
  (11 shorter events, 0.2 us)
Async XLA Ops:
  3.2 29.9 %copy-start.2 = (s32[128,512]{1,0:T(8,128)S(1)}, s32[128,512]{1,0:T(8,128)}, u32[]{:S(2)}) copy-start(s32[128,512]{1,0:T(8,128)} %param.14) | copy-start | bytes 786436
  14.0 22.3 %copy-start.3 = (bf16[4,128,128]{2,1,0:T(8,128)(2,1)S(1)}, bf16[4,128,128]{2,1,0:T(8,128)(2,1)}, u32[]{:S(2)}) copy-start(bf16[4,128,128]{2,1,0:T(8,128)(2,1)} %param.18) | copy-start | bytes 393220
  21.6 30.9 %all-to-all-start = ((bf16[128,32,128]{2,1,0:T(8,128)(2,1)}), bf16[128,32,128]{2,1,0:T(8,128)(2,1)S(1)}, u32[]{:S(2)}, u32[]{:S(2)}) async-start(bf16[128,32,128]{2,1,0:T(8,128)(2,1)} %bitcast.78), calls=%async_computation | async-start | bytes 2097152 | tf_op jit(solution)/shard_map/all_to_all | solution.py:300
  52.6 1.0 copy-start
  79.0 1.2 %copy-start.1 = (bf16[128,32,128]{2,1,0:T(8,128)(2,1)S(1)}, bf16[128,32,128]{2,1,0:T(8,128)(2,1)}, u32[]{:S(2)}) copy-start(bf16[128,32,128]{2,1,0:T(8,128)(2,1)} %copy-done) | copy-start | bytes 3145732

commit v13 on v12

--- a/solution.py
+++ b/solution.py
@@ -76,7 +76,7 @@
 
 def move_rows(kernel, pos, order, x):
     return pl.pallas_call(
-        functools.partial(kernel, 32),
+        functools.partial(kernel, 64),
         out_shape=jax.ShapeDtypeStruct(x.shape, jnp.bfloat16),
         in_specs=[
             pl.BlockSpec(memory_space=pltpu.SMEM),

time: 114 us -> 113 us (level)
  no operation moved by 1% of the time
where the time goes in v13:
time: 113 us
  Pallas kernels  39.7 us (35%)
  blocking collectives  25.3 us (22%)
  waiting for transfers between devices  14.8 us (13%)
  starting transfers between devices  11.5 us (10%)
  matrix products  9.78 us (9%)
  local copies, waits for them, and re-layouts  6.58 us (6%)
  other arithmetic  4.89 us (4%)
    all_to_all x1, blocking collectives, body(): lax.all_to_all(result.reshape(devices, quota, width), ('tx', 'ty'), split...  25.3 us
    all_to_all x1, waiting for transfers between devices, body(): lax.all_to_all(outgoing, ('tx', 'ty'), split_axis=0, concat_axis=0, tiled...  14.8 us
    pallas_call x2, Pallas kernels, move_rows(): pl.pallas_call(functools.partial(kernel, 64), out_shape=jax.ShapeDtypeStr...  14.4 us
    all_to_all x1, starting transfers between devices, body(): lax.all_to_all(outgoing, ('tx', 'ty'), split_axis=0, concat_axis=0, tiled...  11.5 us
    pallas_call x1, Pallas kernels, summarize(): pl.pallas_call(summary_kernel, out_shape=jax.ShapeDtypeStruct((tiles,) +...  9.49 us
    pallas_call x1, Pallas kernels, point_mlp(): pl.pallas_call(mlp_kernel, out_shape=jax.ShapeDtypeStruct((rows, w3.shape...  8.09 us
    pallas_call x1, Pallas kernels, mix_tiles(): pl.pallas_call(functools.partial(mix_kernel, count_x, count_y), out_shape...  7.7 us
    dot_general x2, matrix products, body(): jnp.dot(point_queries[:, lower:upper], second_keys[:, lower:upper].T, pre...  4.92 us
  transfers between devices with their start and end apart: 1, of which 1 were waited for; matrix products, arithmetic and copies ran while one was open for 4% of the time, Pallas kernels for 0%

profile of v13, /device:TPU:1, one launch (start us, length us, event | category | flops | bytes accessed | tf_op | source)
XLA Modules:
  0.0 112.7 jit_solution(13596331743656243239)
XLA Ops:
  0.0 0.5 broadcast.75
  0.5 1.4 %fusion.29 = (s32[512]{0:T(512)S(1)}, s32[1,512]{1,0:T(1,128)S(1)}) fusion(s32[]{:T(128)} %broadcast.75, s32[128,512]{1,0:T(8,128)} %param.14, s32[]{:T(128)S(6)} %select_n.22), kind=kLoop, calls=%fused_computation.58 | loop fusion | bytes 6152 | tf_op jit(solution)/shard_map/jit(dynamic_index_in_dim)/dynamic_slice | solution.py:282
  1.9 0.3 reduce-window.9
  2.2 0.1 slice.57
  2.3 0.2 reshape.155
  2.5 0.1 slice_reduce_fusion.1
  2.6 0.1 broadcast.62
  2.7 0.1 reshape.157
  2.8 0.2 reshape.153
  3.0 0.1 slice_add_fusion
  3.1 0.1 add_subtract_fusion
  3.2 0.0 copy-start.2
  3.2 0.7 slice_reduce_fusion
  4.0 0.1 lt.52
  4.0 0.1 copy.51
  4.1 0.1 copy.52
  4.2 0.1 lt.56
  4.3 0.1 lt.57
  4.4 0.1 copy.55
  4.5 0.1 copy.53
  4.6 0.1 copy.56
  4.7 0.1 copy.54
  4.8 0.1 add.100
  4.9 0.1 add.101
  5.0 0.1 add.103
  5.1 0.1 add.104
  5.2 0.7 fusion.26.pos_ref
  5.9 8.1 %shard_map.100.x_ref = bf16[4096,128]{1,0:T(8,128)(2,1)} custom-call(bf16[4096,128]{1,0:T(8,128)(2,1)} %x_ref.1, bf16[128,512]{1,0:T(8,128)(2,1)} %w1_ref.1, bf16[1,512,512]{2,1,0:T(8,128)(2,1)} %w2_ref.1, bf16[512,128]{1,0:T(8,128)(2,1)} %w3_ref.1), custom_call_target="tpu_custom_call" | custom-call | tf_op jit(solution)/shard_map/pallas_call | solution.py:35
  14.0 0.0 copy-start.3
  14.0 7.3 %shard_map.101 = bf16[4096,128]{1,0:T(8,128)(2,1)} custom-call(s32[4096]{0:T(1024)} %fusion.26.pos_ref, s32[4096]{0:T(1024)} %bitcast.88, bf16[4096,128]{1,0:T(8,128)(2,1)} %shard_map.100.x_ref), custom_call_target="tpu_custom_call" | custom-call | tf_op jit(solution)/shard_map/pallas_call | solution.py:78
  21.3 11.5 %all-to-all-start = ((bf16[128,32,128]{2,1,0:T(8,128)(2,1)}), bf16[128,32,128]{2,1,0:T(8,128)(2,1)S(1)}, u32[]{:S(2)}, u32[]{:S(2)}) async-start(bf16[128,32,128]{2,1,0:T(8,128)(2,1)} %bitcast.78), calls=%async_computation | async-start | bytes 2097152 | tf_op jit(solution)/shard_map/all_to_all | solution.py:300
  32.8 0.0 copy-done.2
  32.8 0.1 copy.58
  33.0 0.1 copy.59
  33.1 0.1 eq.22
  33.2 2.7 %fusion.7 = (f32[4096,4]{1,0:T(8,128)S(1)}, bf16[4096,4]{1,0:T(8,128)(2,1)}) fusion(s32[4096]{0:T(1024)S(1)} %eq.22), kind=kLoop, calls=%fused_computation.15 | loop fusion | flops 49152 | bytes 114688 | tf_op jit(solution)/shard_map/convert_element_type | solution.py:312
  35.9 0.0 copy-done.3
  35.9 0.1 copy.61
  36.0 0.1 copy.57
  36.2 0.6 copy.62
  36.8 0.6 fusion.20.lane_mask_ref
  37.4 14.8 %all-to-all-done = bf16[128,32,128]{2,1,0:T(8,128)(2,1)S(1)} async-done(((bf16[128,32,128]{2,1,0:T(8,128)(2,1)}), bf16[128,32,128]{2,1,0:T(8,128)(2,1)S(1)}, u32[]{:S(2)}, u32[]{:S(2)}) %all-to-all-start) | async-done | bytes 1048608 | tf_op jit(solution)/shard_map/all_to_all | solution.py:300
  52.2 0.0 copy-start
  52.2 0.5 multiply_reduce_fusion
  52.7 0.5 copy-done
  53.2 9.5 %shard_map.102 = bf16[4,128,128]{2,1,0:T(8,128)(2,1)} custom-call(bf16[4096,128]{1,0:T(8,128)(2,1)} %bitcast.73, bf16[4096,4]{1,0:T(8,128)(2,1)} %get-tuple-element.16.column_mask_ref, f32[4,4096]{1,0:T(4,128)} %fusion.20.lane_mask_ref, bf16[128,128]{1,0:T(8,128)(2,1)} %inducing_ref.1, bf16[4,128,128]{2,1,0:T(8,128)(2,1)} %proj_ref.1), custom_call_target="tpu_custom_call" | custom-call | tf_op jit(solution)/shard_map/pallas_call | solution.py:246
  62.7 7.7 %shard_map.103 = bf16[2,2,128,128]{3,2,1,0:T(8,128)(2,1)} custom-call(bf16[2,2,128,128]{3,2,1,0:T(8,128)(2,1)} %bitcast.84, bf16[8,128,128]{2,1,0:T(8,128)(2,1)} %mixing_ref.1), custom_call_target="tpu_custom_call" | custom-call | tf_op jit(solution)/shard_map/pallas_call | solution.py:164
  70.4 1.1 convolution_convert_fusion
  71.5 1.1 multiply_reduce_fusion.1
  72.6 0.2 divide_convert_fusion
  72.9 1.3 %fusion.12 = f32[4096,512]{0,1:T(8,128)S(1)} fusion(bf16[4096,128]{0,1:T(8,128)(2,1)S(1)} %bitcast.75, bf16[512,128]{0,1:T(8,128)(2,1)S(1)} %bitcast.82), kind=kOutput, calls=%fused_computation.21 | convolution fusion | flops 268435456 | bytes 8978432 | tf_op jit(solution)/shard_map/dot_general | solution.py:333
  74.2 3.6 %fusion = (f32[4096]{0:T(1024)S(1)}, f32[4096]{0:T(1024)S(1)}, bf16[4096,512]{0,1:T(8,128)(2,1)S(1)}, bf16[4096,512]{0,1:T(8,128)(2,1)S(1)}) fusion(f32[4096,4]{0,1:T(4,128)S(1)} %copy.62, f32[4096,512]{0,1:T(8,128)S(1)} %fusion.12, bf16[512,128]{0,1:T(8,128)(2,1)S(1)} %bitcast.83, bf16[4096,128]{0,1:T(8,128)(2,1)S(1)} %bitcast.76), kind=kOutput, calls=%fused_computation.2 | convolution fusion | flops 285204480 | bytes 17465344 | tf_op jit(solution)/shard_map/dot_general | solution.py:333
  77.8 0.8 fusion.5
  78.6 0.0 copy-start.1
  78.7 0.8 fusion.6
  79.5 0.4 copy-done.1
  79.9 0.5 fusion.4
  80.4 25.3 %all_to_all.10 = bf16[128,32,128]{2,1,0:T(8,128)(2,1)} all-to-all(bf16[128,32,128]{2,1,0:T(8,128)(2,1)S(1)} %bitcast.77), channel_id=1, replica_groups=mesh['tx'=32,'ty'=4] {'tx','ty'}, dimensions={0} | all-to-all | bytes 2097152 | tf_op jit(solution)/shard_map/all_to_all | solution.py:352
  105.7 7.1 %shard_map.104 = bf16[4096,128]{1,0:T(8,128)(2,1)} custom-call(s32[4096]{0:T(1024)} %fusion.26.pos_ref, s32[4096]{0:T(1024)} %bitcast.89, bf16[4096,128]{1,0:T(8,128)(2,1)} %bitcast.79), custom_call_target="tpu_custom_call" | custom-call | tf_op jit(solution)/shard_map/pallas_call | solution.py:78
  (11 shorter events, 0.2 us)
Async XLA Ops:
  3.2 29.6 %copy-start.2 = (s32[128,512]{1,0:T(8,128)S(1)}, s32[128,512]{1,0:T(8,128)}, u32[]{:S(2)}) copy-start(s32[128,512]{1,0:T(8,128)} %param.14) | copy-start | bytes 786436
  14.0 21.9 %copy-start.3 = (bf16[4,128,128]{2,1,0:T(8,128)(2,1)S(1)}, bf16[4,128,128]{2,1,0:T(8,128)(2,1)}, u32[]{:S(2)}) copy-start(bf16[4,128,128]{2,1,0:T(8,128)(2,1)} %param.18) | copy-start | bytes 393220
  21.3 30.9 %all-to-all-start = ((bf16[128,32,128]{2,1,0:T(8,128)(2,1)}), bf16[128,32,128]{2,1,0:T(8,128)(2,1)S(1)}, u32[]{:S(2)}, u32[]{:S(2)}) async-start(bf16[128,32,128]{2,1,0:T(8,128)(2,1)} %bitcast.78), calls=%async_computation | async-start | bytes 2097152 | tf_op jit(solution)/shard_map/all_to_all | solution.py:300
  52.2 1.0 copy-start
  78.6 1.2 %copy-start.1 = (bf16[128,32,128]{2,1,0:T(8,128)(2,1)S(1)}, bf16[128,32,128]{2,1,0:T(8,128)(2,1)}, u32[]{:S(2)}) copy-start(bf16[128,32,128]{2,1,0:T(8,128)(2,1)} %copy-done) | copy-start | bytes 3145732

commit v14 on v13

--- a/solution.py
+++ b/solution.py
@@ -88,7 +88,22 @@
     )(pos, order, x)
 
 
-def mix_kernel(count_x, count_y, x_ref, mixing_ref, o_ref, padded, send_sem, recv_sem, local_sem):
+def mix_kernel(
+    count_x,
+    count_y,
+    x_ref,
+    mixing_ref,
+    rows_ref,
+    proj_ref,
+    queries_ref,
+    keys_ref,
+    values_ref,
+    padded,
+    mixed,
+    send_sem,
+    recv_sem,
+    local_sem,
+):
     index_x = lax.axis_index("tx")
     index_y = lax.axis_index("ty")
     size_x, size_y = x_ref.shape[0], x_ref.shape[1]
@@ -141,6 +156,10 @@
         def _():
             piece = padded.at[target_x, target_y]
             piece[...] = jnp.zeros(piece.shape, piece.dtype)
+    head_width = rows_ref.shape[1] // HEADS
+    queries_ref[...] = unit_rows(
+        jnp.dot(rows_ref[...], proj_ref[0], preferred_element_type=jnp.float32), head_width
+    )
     for k, (a, b) in enumerate(steps):
         pl.when(inside(index_x + a, index_y + b))(copies[k].wait_send)
         pl.when(inside(index_x - a, index_y - b))(copies[k].wait_recv)
@@ -154,26 +173,40 @@
                     mixing_ref[k],
                     preferred_element_type=jnp.float32,
                 )
-            o_ref[tile_x, tile_y] = total.astype(o_ref.dtype)
-
-
-def mix_tiles(block, mixing):
+            tile_rows = pl.ds((tile_x * size_y + tile_y) * x_ref.shape[2], x_ref.shape[2])
+            mixed[tile_rows, :] = total.astype(mixed.dtype)
+    mixture = mixed[...]
+    keys_ref[...] = unit_rows(
+        jnp.dot(mixture, proj_ref[1], preferred_element_type=jnp.float32), head_width
+    )
+    values_ref[...] = jnp.dot(mixture, proj_ref[2], preferred_element_type=jnp.float32).astype(
+        values_ref.dtype
+    )
+
+
+def mix_tiles(block, mixing, rows, proj):
     count_x = lax.axis_size("tx")
     count_y = lax.axis_size("ty")
     shape = (block.shape[0] + 2, block.shape[1] + 2) + block.shape[2:]
+    keys_shape = (block.shape[0] * block.shape[1] * block.shape[2], block.shape[3])
     return pl.pallas_call(
         functools.partial(mix_kernel, count_x, count_y),
-        out_shape=jax.ShapeDtypeStruct(block.shape, block.dtype),
-        in_specs=[pl.BlockSpec(memory_space=pltpu.VMEM)] * 2,
-        out_specs=pl.BlockSpec(memory_space=pltpu.VMEM),
+        out_shape=(
+            jax.ShapeDtypeStruct(rows.shape, jnp.bfloat16),
+            jax.ShapeDtypeStruct(keys_shape, jnp.bfloat16),
+            jax.ShapeDtypeStruct(keys_shape, jnp.bfloat16),
+        ),
+        in_specs=[pl.BlockSpec(memory_space=pltpu.VMEM)] * 4,
+        out_specs=[pl.BlockSpec(memory_space=pltpu.VMEM)] * 3,
         scratch_shapes=[
             pltpu.VMEM(shape, block.dtype),
+            pltpu.VMEM(keys_shape, jnp.bfloat16),
             pltpu.SemaphoreType.DMA((8,)),
             pltpu.SemaphoreType.DMA((8,)),
             pltpu.SemaphoreType.DMA,
         ],
         compiler_params=pltpu.CompilerParams(collective_id=0, has_side_effects=True),
-    )(block, mixing)
+    )(block, mixing, rows, proj)
 
 
 def unit_heads(projected, head_count):
@@ -313,17 +346,8 @@
 
     summary = summarize(all_rows, row_mask, inducing, first_proj)
     tile_grid = summary.reshape(TLX, TLY, inducing_count, width)
-    mixture = mix_tiles(tile_grid, mixing)
-    mixture = mixture.astype(jnp.bfloat16).reshape(per_device * inducing_count, width)
-
-    point_queries = unit_heads(
-        jnp.dot(all_rows, second_proj[0], preferred_element_type=jnp.float32), HEADS
-    )
-    second_keys = unit_heads(
-        jnp.dot(mixture, second_proj[1], preferred_element_type=jnp.float32), HEADS
-    )
-    second_values = jnp.dot(mixture, second_proj[2], preferred_element_type=jnp.float32).astype(
-        jnp.bfloat16
+    point_queries, second_keys, second_values = mix_tiles(
+        tile_grid, mixing, all_rows, second_proj
     )
     key_mask = jnp.repeat(row_mask, inducing_count, axis=1)
     heads_out = []

time: 113 us -> 114 us (level)
  Pallas kernels: 39.7 us -> 40.9 us
    dot_general x3 -> x0, matrix products: 2.69 us -> none  [the longest x1 1.12 us: body(): jnp.dot(mixture, second_proj[2], preferred_element_type=jnp.float32)]
    dot_general x2, matrix products: 4.92 us -> 6.29 us  [body(): jnp.dot(point_queries[:, lower:upper], second_keys[:, lower:upper].T, pre...]
    pallas_call x1, Pallas kernels: 7.7 us -> 8.98 us  [mix_tiles(): pl.pallas_call(functools.partial(mix_kernel, count_x, count_y), out_shape...]
where the time goes in v14:
time: 114 us
  Pallas kernels  40.9 us (36%)
  blocking collectives  25.3 us (22%)
  waiting for transfers between devices  15 us (13%)
  starting transfers between devices  11.5 us (10%)
  matrix products  9.37 us (8%)
  local copies, waits for them, and re-layouts  6.74 us (6%)
  other arithmetic  4.63 us (4%)
    all_to_all x1, blocking collectives, body(): lax.all_to_all(result.reshape(devices, quota, width), ('tx', 'ty'), split...  25.3 us
    all_to_all x1, waiting for transfers between devices, body(): lax.all_to_all(outgoing, ('tx', 'ty'), split_axis=0, concat_axis=0, tiled...  15 us
    pallas_call x2, Pallas kernels, move_rows(): pl.pallas_call(functools.partial(kernel, 64), out_shape=jax.ShapeDtypeStr...  14.3 us
    all_to_all x1, starting transfers between devices, body(): lax.all_to_all(outgoing, ('tx', 'ty'), split_axis=0, concat_axis=0, tiled...  11.5 us
    pallas_call x1, Pallas kernels, summarize(): pl.pallas_call(summary_kernel, out_shape=jax.ShapeDtypeStruct((tiles,) +...  9.49 us
    pallas_call x1, Pallas kernels, mix_tiles(): pl.pallas_call(functools.partial(mix_kernel, count_x, count_y), out_shape...  8.98 us
    pallas_call x1, Pallas kernels, point_mlp(): pl.pallas_call(mlp_kernel, out_shape=jax.ShapeDtypeStruct((rows, w3.shape...  8.09 us
    dot_general x2, matrix products, body(): jnp.dot(point_queries[:, lower:upper], second_keys[:, lower:upper].T, pre...  6.29 us
  transfers between devices with their start and end apart: 1, of which 1 were waited for; matrix products, arithmetic and copies ran while one was open for 4% of the time, Pallas kernels for 0%

profile of v14, /device:TPU:1, one launch (start us, length us, event | category | flops | bytes accessed | tf_op | source)
XLA Modules:
  0.0 113.7 jit_solution(13655873387001831119)
XLA Ops:
  0.0 0.5 broadcast.65
  0.5 1.4 %fusion.27 = (s32[512]{0:T(512)S(1)}, s32[1,512]{1,0:T(1,128)S(1)}) fusion(s32[]{:T(128)} %broadcast.65, s32[128,512]{1,0:T(8,128)} %param.14, s32[]{:T(128)S(6)} %select_n.22), kind=kLoop, calls=%fused_computation.47 | loop fusion | bytes 6152 | tf_op jit(solution)/shard_map/jit(dynamic_index_in_dim)/dynamic_slice | solution.py:315
  1.9 0.3 reduce-window.9
  2.2 0.1 slice.48
  2.3 0.2 reshape.132
  2.5 0.1 slice_reduce_fusion.1
  2.6 0.1 broadcast.52
  2.7 0.1 reshape.134
  2.8 0.2 reshape.130
  3.0 0.1 slice_add_fusion
  3.1 0.1 add_subtract_fusion
  3.2 0.0 copy-start.4
  3.2 0.7 slice_reduce_fusion
  4.0 0.1 lt.52
  4.0 0.1 copy.43
  4.1 0.1 copy.44
  4.2 0.1 lt.56
  4.3 0.1 lt.57
  4.4 0.1 copy.47
  4.5 0.1 copy.45
  4.6 0.1 copy.48
  4.7 0.1 copy.46
  4.8 0.1 add.78
  4.9 0.1 add.79
  5.0 0.1 add.81
  5.1 0.1 add.82
  5.2 0.7 fusion.24.pos_ref
  5.9 8.1 %shard_map.100.x_ref = bf16[4096,128]{1,0:T(8,128)(2,1)} custom-call(bf16[4096,128]{1,0:T(8,128)(2,1)} %x_ref.1, bf16[128,512]{1,0:T(8,128)(2,1)} %w1_ref.1, bf16[1,512,512]{2,1,0:T(8,128)(2,1)} %w2_ref.1, bf16[512,128]{1,0:T(8,128)(2,1)} %w3_ref.1), custom_call_target="tpu_custom_call" | custom-call | tf_op jit(solution)/shard_map/pallas_call | solution.py:35
  14.0 7.2 %shard_map.101 = bf16[4096,128]{1,0:T(8,128)(2,1)} custom-call(s32[4096]{0:T(1024)} %fusion.24.pos_ref, s32[4096]{0:T(1024)} %bitcast.55, bf16[4096,128]{1,0:T(8,128)(2,1)} %shard_map.100.x_ref), custom_call_target="tpu_custom_call" | custom-call | tf_op jit(solution)/shard_map/pallas_call | solution.py:78
  21.2 11.5 %all-to-all-start = ((bf16[128,32,128]{2,1,0:T(8,128)(2,1)}), bf16[128,32,128]{2,1,0:T(8,128)(2,1)S(1)}, u32[]{:S(2)}, u32[]{:S(2)}) async-start(bf16[128,32,128]{2,1,0:T(8,128)(2,1)} %bitcast.51), calls=%async_computation | async-start | bytes 2097152 | tf_op jit(solution)/shard_map/all_to_all | solution.py:333
  32.7 0.0 copy-done.4
  32.7 0.1 copy.49
  32.9 0.1 copy.50
  33.0 0.1 eq.22
  33.1 2.7 %fusion.7 = (f32[4096,4]{1,0:T(8,128)S(1)}, bf16[4096,4]{1,0:T(8,128)(2,1)}) fusion(s32[4096]{0:T(1024)S(1)} %eq.22), kind=kLoop, calls=%fused_computation.13 | loop fusion | flops 49152 | bytes 114688 | tf_op jit(solution)/shard_map/convert_element_type | solution.py:345
  35.8 0.6 copy.52
  36.4 0.6 fusion.20.lane_mask_ref
  37.1 15.0 %all-to-all-done = bf16[128,32,128]{2,1,0:T(8,128)(2,1)S(1)} async-done(((bf16[128,32,128]{2,1,0:T(8,128)(2,1)}), bf16[128,32,128]{2,1,0:T(8,128)(2,1)S(1)}, u32[]{:S(2)}, u32[]{:S(2)}) %all-to-all-start) | async-done | bytes 1048608 | tf_op jit(solution)/shard_map/all_to_all | solution.py:333
  52.1 0.0 copy-start
  52.1 1.0 copy-done
  53.1 9.5 %shard_map.102 = bf16[4,128,128]{2,1,0:T(8,128)(2,1)} custom-call(bf16[4096,128]{1,0:T(8,128)(2,1)} %bitcast.47, bf16[4096,4]{1,0:T(8,128)(2,1)} %get-tuple-element.20.column_mask_ref, f32[4,4096]{1,0:T(4,128)} %fusion.20.lane_mask_ref, bf16[128,128]{1,0:T(8,128)(2,1)} %inducing_ref.1, bf16[4,128,128]{2,1,0:T(8,128)(2,1)} %proj_ref.2), custom_call_target="tpu_custom_call" | custom-call | tf_op jit(solution)/shard_map/pallas_call | solution.py:279
  62.6 9.0 %shard_map.103 = (bf16[4096,128]{1,0:T(8,128)(2,1)}, bf16[512,128]{1,0:T(8,128)(2,1)}, bf16[512,128]{1,0:T(8,128)(2,1)}) custom-call(bf16[2,2,128,128]{3,2,1,0:T(8,128)(2,1)} %bitcast.53, bf16[8,128,128]{2,1,0:T(8,128)(2,1)} %mixing_ref.1, bf16[4096,128]{1,0:T(8,128)(2,1)} %bitcast.48, bf16[4,128,128]{2,1,0:T(8,128)(2,1)} %proj_ref.3), custom_call_target="tpu_custom_call" | custom-call | tf_op jit(solution)/shard_map/pallas_call | solution.py:192
  71.6 0.0 copy-start.2
  71.6 0.0 copy-start.3
  71.6 2.7 %fusion.11 = f32[4096,512]{0,1:T(8,128)S(1)} fusion(bf16[4096,128]{1,0:T(8,128)(2,1)} %get-tuple-element.8, bf16[512,128]{1,0:T(8,128)(2,1)} %get-tuple-element.9), kind=kOutput, calls=%fused_computation.17 | convolution fusion | flops 268435456 | bytes 9568256 | tf_op jit(solution)/shard_map/dot_general | solution.py:357
  74.2 0.0 copy-done.2
  74.3 0.0 copy-done.3
  74.3 0.0 copy-start.5
  74.3 3.6 %fusion = (f32[4096]{0:T(1024)S(1)}, f32[4096]{0:T(1024)S(1)}, bf16[4096,512]{0,1:T(8,128)(2,1)S(1)}, bf16[4096,512]{0,1:T(8,128)(2,1)S(1)}) fusion(f32[4096,4]{0,1:T(4,128)S(1)} %copy.52, f32[4096,512]{0,1:T(8,128)S(1)} %fusion.11, bf16[512,128]{1,0:T(8,128)(2,1)S(1)} %copy-done.3, bf16[4096,128]{1,0:T(8,128)(2,1)S(1)} %copy-done.2), kind=kOutput, calls=%fused_computation.2 | convolution fusion | flops 285204480 | bytes 18055168 | tf_op jit(solution)/shard_map/dot_general | solution.py:357
  77.9 0.0 copy-done.5
  77.9 0.9 fusion.5
  78.8 0.0 copy-start.1
  78.8 1.0 fusion.6
  79.8 0.3 copy-done.1
  80.1 1.2 %fusion.4 = bf16[4096,128]{1,0:T(8,128)(2,1)S(1)} fusion(bf16[4096,128]{1,0:T(8,128)(2,1)S(1)} %bitcast.49, bf16[4096,64]{0,1:T(8,128)(2,1)S(1)} %fusion.6, bf16[4096,64]{0,1:T(8,128)(2,1)S(1)} %fusion.5, bf16[4,128,128]{2,1,0:T(8,128)(2,1)} %proj_ref.3), kind=kOutput, calls=%fused_computation.7 | convolution fusion | flops 137887744 | bytes 3178496 | tf_op jit(solution)/shard_map/dot_general | solution.py:373
  81.3 25.3 %all_to_all.10 = bf16[128,32,128]{2,1,0:T(8,128)(2,1)} all-to-all(bf16[128,32,128]{2,1,0:T(8,128)(2,1)S(1)} %bitcast.50), channel_id=1, replica_groups=mesh['tx'=32,'ty'=4] {'tx','ty'}, dimensions={0} | all-to-all | bytes 2097152 | tf_op jit(solution)/shard_map/all_to_all | solution.py:376
  106.6 7.1 %shard_map.104 = bf16[4096,128]{1,0:T(8,128)(2,1)} custom-call(s32[4096]{0:T(1024)} %fusion.24.pos_ref, s32[4096]{0:T(1024)} %bitcast.56, bf16[4096,128]{1,0:T(8,128)(2,1)} %bitcast.52), custom_call_target="tpu_custom_call" | custom-call | tf_op jit(solution)/shard_map/pallas_call | solution.py:78
  (7 shorter events, 0.1 us)
Async XLA Ops:
  3.2 29.5 %copy-start.4 = (s32[128,512]{1,0:T(8,128)S(1)}, s32[128,512]{1,0:T(8,128)}, u32[]{:S(2)}) copy-start(s32[128,512]{1,0:T(8,128)} %param.14) | copy-start | bytes 786436
  21.2 30.9 %all-to-all-start = ((bf16[128,32,128]{2,1,0:T(8,128)(2,1)}), bf16[128,32,128]{2,1,0:T(8,128)(2,1)S(1)}, u32[]{:S(2)}, u32[]{:S(2)}) async-start(bf16[128,32,128]{2,1,0:T(8,128)(2,1)} %bitcast.51), calls=%async_computation | async-start | bytes 2097152 | tf_op jit(solution)/shard_map/all_to_all | solution.py:333
  52.1 1.0 copy-start
  71.6 2.7 %copy-start.2 = (bf16[4096,128]{1,0:T(8,128)(2,1)S(1)}, bf16[4096,128]{1,0:T(8,128)(2,1)}, u32[]{:S(2)}) copy-start(bf16[4096,128]{1,0:T(8,128)(2,1)} %get-tuple-element.8) | copy-start | bytes 3145732
  71.6 2.7 %copy-start.3 = (bf16[512,128]{1,0:T(8,128)(2,1)S(1)}, bf16[512,128]{1,0:T(8,128)(2,1)}, u32[]{:S(2)}) copy-start(bf16[512,128]{1,0:T(8,128)(2,1)} %get-tuple-element.9) | copy-start | bytes 393220
  74.3 3.7 %copy-start.5 = (bf16[512,128]{1,0:T(8,128)(2,1)S(1)}, bf16[512,128]{1,0:T(8,128)(2,1)}, u32[]{:S(2)}) copy-start(bf16[512,128]{1,0:T(8,128)(2,1)} %get-tuple-element.10) | copy-start | bytes 393220
  78.8 1.2 %copy-start.1 = (bf16[128,32,128]{2,1,0:T(8,128)(2,1)S(1)}, bf16[128,32,128]{2,1,0:T(8,128)(2,1)}, u32[]{:S(2)}) copy-start(bf16[128,32,128]{2,1,0:T(8,128)(2,1)} %copy-done) | copy-start | bytes 3145732

commit v15 on v13

--- a/solution.py
+++ b/solution.py
@@ -325,7 +325,7 @@
     second_values = jnp.dot(mixture, second_proj[2], preferred_element_type=jnp.float32).astype(
         jnp.bfloat16
     )
-    key_mask = jnp.repeat(row_mask, inducing_count, axis=1)
+    own_tile = row_mask > 0
     heads_out = []
     for head_id in range(HEADS):
         lower = head_id * head_width
@@ -334,11 +334,13 @@
             point_queries[:, lower:upper],
             second_keys[:, lower:upper].T,
             preferred_element_type=jnp.float32,
-        )
-        weights = jnp.exp(sharpness * scores) * key_mask
+        ).reshape(-1, per_device, inducing_count)
+        own_scores = jnp.sum(jnp.where(own_tile[:, :, None], scores, 0.0), axis=1)
+        weights = jnp.exp(sharpness * own_scores)
         totals = jnp.sum(weights, axis=1, keepdims=True)
+        spread = jnp.where(own_tile[:, :, None], weights[:, None, :], 0.0)
         numer = jnp.dot(
-            weights.astype(jnp.bfloat16),
+            spread.reshape(-1, per_device * inducing_count).astype(jnp.bfloat16),
             second_values[:, lower:upper],
             preferred_element_type=jnp.float32,
         )

time: 113 us -> 130 us (1.15)
  other arithmetic: 4.89 us -> 16.3 us
  matrix products: 9.78 us -> 14.2 us
    reduce_sum x0 -> x2, other arithmetic: none -> 9.11 us  [the longest x1 8.5 us: body(): own_scores = jnp.sum(jnp.where(own_tile[:, :, None], scores, 0.0), axis=1)]
    dot_general x2, matrix products: 4.92 us -> 9.01 us  [body(): jnp.dot(point_queries[:, lower:upper], second_keys[:, lower:upper].T, pre...]
    gt x0 -> x1, other arithmetic: none -> 2.72 us  [body(): own_tile = row_mask > 0]
    convert_element_type x2 -> x1, other arithmetic: 3.36 us -> 0.65 us  [body(): row_mask = (row_tile[:, None] == tile_ids[None, :]).astype(jnp.float32)]
    convert_element_type x0 -> x1, other arithmetic: none -> 1.7 us  [body(): spread.reshape(-1, per_device * inducing_count).astype(jnp.bfloat16)]
where the time goes in v15:
time: 130 us; the launch traced here: 129 us
  Pallas kernels  39.7 us (31%)
  blocking collectives  25.3 us (19%)
  other arithmetic  16.3 us (13%)
  waiting for transfers between devices  14.7 us (11%)
  matrix products  14.2 us (11%)
  starting transfers between devices  11.5 us (9%)
  local copies, waits for them, and re-layouts  7.44 us (6%)
    all_to_all x1, blocking collectives, body(): lax.all_to_all(result.reshape(devices, quota, width), ('tx', 'ty'), split...  25.3 us
    all_to_all x1, waiting for transfers between devices, body(): lax.all_to_all(outgoing, ('tx', 'ty'), split_axis=0, concat_axis=0, tiled...  14.7 us
    pallas_call x2, Pallas kernels, move_rows(): pl.pallas_call(functools.partial(kernel, 64), out_shape=jax.ShapeDtypeStr...  14.4 us
    all_to_all x1, starting transfers between devices, body(): lax.all_to_all(outgoing, ('tx', 'ty'), split_axis=0, concat_axis=0, tiled...  11.5 us
    pallas_call x1, Pallas kernels, summarize(): pl.pallas_call(summary_kernel, out_shape=jax.ShapeDtypeStruct((tiles,) +...  9.49 us
    dot_general x2, matrix products, body(): jnp.dot(point_queries[:, lower:upper], second_keys[:, lower:upper].T, pre...  9.01 us
    reduce_sum x1, other arithmetic, body(): own_scores = jnp.sum(jnp.where(own_tile[:, :, None], scores, 0.0), axis=1)  8.5 us
    pallas_call x1, Pallas kernels, point_mlp(): pl.pallas_call(mlp_kernel, out_shape=jax.ShapeDtypeStruct((rows, w3.shape...  8.1 us
  transfers between devices with their start and end apart: 1, of which 1 were waited for; matrix products, arithmetic and copies ran while one was open for 4% of the time, Pallas kernels for 0%

profile of v15, /device:TPU:1, one launch (start us, length us, event | category | flops | bytes accessed | tf_op | source)
XLA Modules:
  0.0 129.4 jit_solution(17367055180102033559)
XLA Ops:
  0.0 0.5 broadcast.111
  0.5 1.4 %fusion.25 = (s32[512]{0:T(512)S(1)}, s32[1,512]{1,0:T(1,128)S(1)}) fusion(s32[]{:T(128)} %broadcast.111, s32[128,512]{1,0:T(8,128)} %param.14, s32[]{:T(128)S(6)} %select_n.40), kind=kLoop, calls=%fused_computation.60 | loop fusion | bytes 6152 | tf_op jit(solution)/shard_map/jit(dynamic_index_in_dim)/dynamic_slice | solution.py:282
  1.9 0.3 reduce-window.9
  2.2 0.1 slice.57
  2.3 0.2 reshape.203
  2.5 0.1 slice_reduce_fusion.1
  2.6 0.1 broadcast.96
  2.7 0.1 reshape.205
  2.8 0.2 reshape.201
  3.0 0.1 slice_add_fusion
  3.1 0.1 add_subtract_fusion
  3.2 0.7 slice_reduce_fusion
  3.9 0.1 lt.52
  4.0 0.1 copy.51
  4.1 0.1 copy.52
  4.2 0.1 lt.56
  4.3 0.1 lt.57
  4.4 0.1 copy.55
  4.5 0.1 copy.53
  4.6 0.1 copy.56
  4.7 0.1 copy.54
  4.8 0.1 add.100
  4.9 0.1 add.101
  5.0 0.1 add.103
  5.1 0.1 add.104
  5.2 0.7 fusion.20.pos_ref
  5.9 8.1 %shard_map.100.x_ref = bf16[4096,128]{1,0:T(8,128)(2,1)} custom-call(bf16[4096,128]{1,0:T(8,128)(2,1)} %x_ref.1, bf16[128,512]{1,0:T(8,128)(2,1)} %w1_ref.1, bf16[1,512,512]{2,1,0:T(8,128)(2,1)} %w2_ref.1, bf16[512,128]{1,0:T(8,128)(2,1)} %w3_ref.1), custom_call_target="tpu_custom_call" | custom-call | tf_op jit(solution)/shard_map/pallas_call | solution.py:35
  14.0 0.0 copy-start.3
  14.0 7.3 %shard_map.101 = bf16[4096,128]{1,0:T(8,128)(2,1)} custom-call(s32[4096]{0:T(1024)} %fusion.20.pos_ref, s32[4096]{0:T(1024)} %bitcast.85, bf16[4096,128]{1,0:T(8,128)(2,1)} %shard_map.100.x_ref), custom_call_target="tpu_custom_call" | custom-call | tf_op jit(solution)/shard_map/pallas_call | solution.py:78
  21.3 0.0 copy-start.4
  21.3 11.5 %all-to-all-start = ((bf16[128,32,128]{2,1,0:T(8,128)(2,1)}), bf16[128,32,128]{2,1,0:T(8,128)(2,1)S(1)}, u32[]{:S(2)}, u32[]{:S(2)}) async-start(bf16[128,32,128]{2,1,0:T(8,128)(2,1)} %bitcast.75), calls=%async_computation | async-start | bytes 2097152 | tf_op jit(solution)/shard_map/all_to_all | solution.py:300
  32.8 0.0 copy-done.3
  32.8 0.1 copy.57
  33.0 0.1 copy.58
  33.1 0.1 eq.26
  33.2 2.7 %convert_compare_fusion = (pred[4096,4]{1,0:T(8,128)(4,1)S(1)}, bf16[4096,4]{1,0:T(8,128)(2,1)}) fusion(s32[4096]{0:T(1024)S(1)} %eq.26), kind=kLoop, calls=%fused_computation.11 | loop fusion | flops 65536 | bytes 65536 | tf_op jit(solution)/shard_map/gt | solution.py:328
  35.9 0.0 copy-done.4
  35.9 0.1 copy.62
  36.0 0.1 copy.61
  36.1 0.7 copy.60
  36.8 0.6 fusion.14.lane_mask_ref
  37.5 14.7 %all-to-all-done = bf16[128,32,128]{2,1,0:T(8,128)(2,1)S(1)} async-done(((bf16[128,32,128]{2,1,0:T(8,128)(2,1)}), bf16[128,32,128]{2,1,0:T(8,128)(2,1)S(1)}, u32[]{:S(2)}, u32[]{:S(2)}) %all-to-all-start) | async-done | bytes 1048608 | tf_op jit(solution)/shard_map/all_to_all | solution.py:300
  52.2 1.0 copy-done
  53.2 9.5 %shard_map.102 = bf16[4,128,128]{2,1,0:T(8,128)(2,1)} custom-call(bf16[4096,128]{1,0:T(8,128)(2,1)} %bitcast.67, bf16[4096,4]{1,0:T(8,128)(2,1)} %get-tuple-element.16.column_mask_ref, f32[4,4096]{1,0:T(4,128)} %fusion.14.lane_mask_ref, bf16[128,128]{1,0:T(8,128)(2,1)} %inducing_ref.1, bf16[4,128,128]{2,1,0:T(8,128)(2,1)} %proj_ref.1), custom_call_target="tpu_custom_call" | custom-call | tf_op jit(solution)/shard_map/pallas_call | solution.py:246
  62.7 7.7 %shard_map.103 = bf16[2,2,128,128]{3,2,1,0:T(8,128)(2,1)} custom-call(bf16[2,2,128,128]{3,2,1,0:T(8,128)(2,1)} %bitcast.81, bf16[8,128,128]{2,1,0:T(8,128)(2,1)} %mixing_ref.1), custom_call_target="tpu_custom_call" | custom-call | tf_op jit(solution)/shard_map/pallas_call | solution.py:164
  70.4 1.1 multiply_reduce_fusion.1
  71.5 1.7 %multiply_reduce_fusion = (f32[4096,2]{0,1:T(2,128)S(1)}, f32[4096,2,64]{0,2,1:T(8,128)S(1)}) fusion(bf16[4096,128,1]{1,0,2:T(8,128)(2,1)} %bitcast.68, bf16[2,64,128]{2,1,0:T(8,128)(2,1)S(1)} %bitcast.83), kind=kOutput, calls=%fused_computation.15 | convolution fusion | flops 135258112 | bytes 3211264 | tf_op jit(solution)/shard_map/dot_general | solution.py:320
  73.3 0.2 divide_convert_fusion
  73.5 4.5 %fusion.6 = f32[4096,512]{0,1:T(8,128)} fusion(bf16[4096,128]{0,1:T(8,128)(2,1)S(1)} %bitcast.70, bf16[512,128]{0,1:T(8,128)(2,1)S(1)} %bitcast.79), kind=kOutput, calls=%fused_computation.21 | convolution fusion | flops 268435456 | bytes 8978432 | tf_op jit(solution)/shard_map/dot_general | solution.py:333
  78.0 4.5 %fusion.8 = f32[4096,512]{0,1:T(8,128)} fusion(bf16[4096,128]{0,1:T(8,128)(2,1)S(1)} %bitcast.71, bf16[512,128]{0,1:T(8,128)(2,1)S(1)} %bitcast.80), kind=kOutput, calls=%fused_computation.23 | convolution fusion | flops 268435456 | bytes 8978432 | tf_op jit(solution)/shard_map/dot_general | solution.py:333
  82.5 8.5 %select_reduce_fusion.1 = (f32[4096,128]{0,1:T(8,128)S(1)}, f32[4096,128]{0,1:T(8,128)S(1)}) fusion(f32[4096,4,128]{0,2,1:T(8,128)} %bitcast.66, pred[4096,4]{0,1:T(4,128)(4,1)S(1)} %copy.60, f32[4096,4,128]{0,2,1:T(8,128)} %bitcast.65), kind=kLoop, calls=%fused_computation.3 | loop fusion | flops 7340032 | bytes 20987904 | tf_op jit(solution)/shard_map/reduce_sum | solution.py:338
  91.0 0.6 fusion.23
  91.6 0.0 copy-start.2
  91.6 0.6 multiply_exponential_fusion
  92.2 0.3 copy-done.2
  92.5 0.2 convolution_convert_fusion
  92.7 1.7 %select_convert_fusion.1 = (bf16[4096,4,128]{0,2,1:T(8,128)(2,1)S(1)}, bf16[4096,4,128]{0,2,1:T(8,128)(2,1)S(1)}) fusion(bf16[4096,128]{0,1:T(8,128)(2,1)S(1)} %get-tuple-element.24, pred[4096,4]{0,1:T(4,128)(4,1)S(1)} %copy.60, bf16[4096,128]{0,1:T(8,128)(2,1)S(1)} %get-tuple-element.23), kind=kLoop, calls=%fused_computation.2 | loop fusion | flops 4194304 | bytes 10502144 | tf_op jit(solution)/shard_map/convert_element_type | solution.py:343
  94.4 0.8 fusion.1
  95.3 0.0 copy-start.1
  95.3 0.8 fusion.2
  96.2 0.4 copy-done.1
  96.5 0.5 fusion
  97.0 25.3 %all_to_all.10 = bf16[128,32,128]{2,1,0:T(8,128)(2,1)} all-to-all(bf16[128,32,128]{2,1,0:T(8,128)(2,1)S(1)} %bitcast.74), channel_id=1, replica_groups=mesh['tx'=32,'ty'=4] {'tx','ty'}, dimensions={0} | all-to-all | bytes 2097152 | tf_op jit(solution)/shard_map/all_to_all | solution.py:354
  122.3 7.1 %shard_map.104 = bf16[4096,128]{1,0:T(8,128)(2,1)} custom-call(s32[4096]{0:T(1024)} %fusion.20.pos_ref, s32[4096]{0:T(1024)} %bitcast.86, bf16[4096,128]{1,0:T(8,128)(2,1)} %bitcast.76), custom_call_target="tpu_custom_call" | custom-call | tf_op jit(solution)/shard_map/pallas_call | solution.py:78
  (12 shorter events, 0.2 us)
Async XLA Ops:
  14.0 18.8 %copy-start.3 = (s32[128,512]{1,0:T(8,128)S(1)}, s32[128,512]{1,0:T(8,128)}, u32[]{:S(2)}) copy-start(s32[128,512]{1,0:T(8,128)} %param.14) | copy-start | bytes 786436
  21.3 14.6 %copy-start.4 = (bf16[4,128,128]{2,1,0:T(8,128)(2,1)S(1)}, bf16[4,128,128]{2,1,0:T(8,128)(2,1)}, u32[]{:S(2)}) copy-start(bf16[4,128,128]{2,1,0:T(8,128)(2,1)} %param.18) | copy-start | bytes 393220
  21.3 30.9 %all-to-all-start = ((bf16[128,32,128]{2,1,0:T(8,128)(2,1)}), bf16[128,32,128]{2,1,0:T(8,128)(2,1)S(1)}, u32[]{:S(2)}, u32[]{:S(2)}) async-start(bf16[128,32,128]{2,1,0:T(8,128)(2,1)} %bitcast.75), calls=%async_computation | async-start | bytes 2097152 | tf_op jit(solution)/shard_map/all_to_all | solution.py:300
  52.2 1.0 copy-start
  91.6 0.9 copy-start.2
  95.3 1.2 copy-start.1

commit v16 on v13

--- a/solution.py
+++ b/solution.py
@@ -210,34 +210,31 @@
     values = jnp.dot(rows, proj_ref[2], preferred_element_type=jnp.float32).astype(jnp.bfloat16)
     column_mask = column_mask_ref[...]
     lane_mask = lane_mask_ref[...]
-    heads_out = []
+    lane_head = lax.broadcasted_iota(jnp.int32, queries.shape, 1) // head_width
+    masked = [values * column_mask[:, t : t + 1] for t in range(tiles)]
+    attended = [jnp.zeros(queries.shape, jnp.float32) for t in range(tiles)]
     for head_id in range(HEADS):
-        lower = head_id * head_width
-        upper = lower + head_width
+        in_head = lane_head == head_id
+        head_queries = jnp.where(in_head, queries, jnp.zeros_like(queries))
         scores = lax.dot_general(
-            queries[:, lower:upper],
-            keys[:, lower:upper],
+            head_queries,
+            keys,
             (((1,), (1,)), ((), ())),
             preferred_element_type=jnp.float32,
         )
         weights = jnp.exp(sharpness * scores)
         rounded = weights.astype(jnp.bfloat16)
-        head_values = values[:, lower:upper]
-        masked = jnp.concatenate(
-            [head_values * column_mask[:, t : t + 1] for t in range(tiles)], axis=1
-        )
-        numer = jnp.dot(rounded, masked, preferred_element_type=jnp.float32)
-        per_tile = []
         for t in range(tiles):
+            numer = jnp.dot(rounded, masked[t], preferred_element_type=jnp.float32)
             totals = jnp.sum(weights * lane_mask[t : t + 1, :], axis=1, keepdims=True)
-            per_tile.append(numer[:, t * head_width : (t + 1) * head_width] / totals)
-        heads_out.append(per_tile)
+            attended[t] = jnp.where(in_head, numer / totals, attended[t])
     inducing = inducing_ref[...].astype(jnp.float32)
     for t in range(tiles):
-        attended = jnp.concatenate([heads_out[h][t] for h in range(HEADS)], axis=1)
-        attended = attended.astype(jnp.bfloat16)
         o_ref[t] = (
-            inducing + jnp.dot(attended, proj_ref[3], preferred_element_type=jnp.float32)
+            inducing
+            + jnp.dot(
+                attended[t].astype(jnp.bfloat16), proj_ref[3], preferred_element_type=jnp.float32
+            )
         ).astype(o_ref.dtype)
 
 

time: 113 us -> 115 us (1.018)
  Pallas kernels: 39.7 us -> 41.3 us
    pallas_call x1, Pallas kernels: 9.49 us -> 11.1 us  [summarize(): pl.pallas_call(summary_kernel, out_shape=jax.ShapeDtypeStruct((tiles,) +...]
where the time goes in v16:
time: 115 us; the launch traced here: 114 us
  Pallas kernels  41.3 us (36%)
  blocking collectives  25.3 us (22%)
  waiting for transfers between devices  14.8 us (13%)
  starting transfers between devices  11.5 us (10%)
  matrix products  9.78 us (9%)
  local copies, waits for them, and re-layouts  6.58 us (6%)
  other arithmetic  4.89 us (4%)
    all_to_all x1, blocking collectives, body(): lax.all_to_all(result.reshape(devices, quota, width), ('tx', 'ty'), split...  25.3 us
    all_to_all x1, waiting for transfers between devices, body(): lax.all_to_all(outgoing, ('tx', 'ty'), split_axis=0, concat_axis=0, tiled...  14.8 us
    pallas_call x2, Pallas kernels, move_rows(): pl.pallas_call(functools.partial(kernel, 64), out_shape=jax.ShapeDtypeStr...  14.4 us
    all_to_all x1, starting transfers between devices, body(): lax.all_to_all(outgoing, ('tx', 'ty'), split_axis=0, concat_axis=0, tiled...  11.5 us
    pallas_call x1, Pallas kernels, summarize(): pl.pallas_call(summary_kernel, out_shape=jax.ShapeDtypeStruct((tiles,) +...  11.1 us
    pallas_call x1, Pallas kernels, point_mlp(): pl.pallas_call(mlp_kernel, out_shape=jax.ShapeDtypeStruct((rows, w3.shape...  8.09 us
    pallas_call x1, Pallas kernels, mix_tiles(): pl.pallas_call(functools.partial(mix_kernel, count_x, count_y), out_shape...  7.69 us
    dot_general x2, matrix products, body(): jnp.dot(point_queries[:, lower:upper], second_keys[:, lower:upper].T, pre...  4.92 us
  transfers between devices with their start and end apart: 1, of which 1 were waited for; matrix products, arithmetic and copies ran while one was open for 4% of the time, Pallas kernels for 0%

profile of v16, /device:TPU:1, one launch (start us, length us, event | category | flops | bytes accessed | tf_op | source)
XLA Modules:
  0.0 114.4 jit_solution(3847515384627462389)
XLA Ops:
  0.0 0.5 broadcast.75
  0.5 1.4 %fusion.29 = (s32[512]{0:T(512)S(1)}, s32[1,512]{1,0:T(1,128)S(1)}) fusion(s32[]{:T(128)} %broadcast.75, s32[128,512]{1,0:T(8,128)} %param.14, s32[]{:T(128)S(6)} %select_n.22), kind=kLoop, calls=%fused_computation.58 | loop fusion | bytes 6152 | tf_op jit(solution)/shard_map/jit(dynamic_index_in_dim)/dynamic_slice | solution.py:279
  1.9 0.3 reduce-window.9
  2.2 0.1 slice.57
  2.3 0.2 reshape.155
  2.5 0.1 slice_reduce_fusion.1
  2.6 0.1 broadcast.62
  2.7 0.1 reshape.157
  2.8 0.2 reshape.153
  3.0 0.1 slice_add_fusion
  3.1 0.1 add_subtract_fusion
  3.2 0.0 copy-start.2
  3.2 0.7 slice_reduce_fusion
  4.0 0.1 lt.52
  4.0 0.1 copy.51
  4.1 0.1 copy.52
  4.2 0.1 lt.56
  4.3 0.1 lt.57
  4.4 0.1 copy.55
  4.5 0.1 copy.53
  4.6 0.1 copy.56
  4.7 0.1 copy.54
  4.8 0.1 add.100
  4.9 0.1 add.101
  5.0 0.1 add.103
  5.1 0.1 add.104
  5.2 0.7 fusion.26.pos_ref
  5.9 8.1 %shard_map.100.x_ref = bf16[4096,128]{1,0:T(8,128)(2,1)} custom-call(bf16[4096,128]{1,0:T(8,128)(2,1)} %x_ref.1, bf16[128,512]{1,0:T(8,128)(2,1)} %w1_ref.1, bf16[1,512,512]{2,1,0:T(8,128)(2,1)} %w2_ref.1, bf16[512,128]{1,0:T(8,128)(2,1)} %w3_ref.1), custom_call_target="tpu_custom_call" | custom-call | tf_op jit(solution)/shard_map/pallas_call | solution.py:35
  14.0 0.0 copy-start.3
  14.0 7.3 %shard_map.101 = bf16[4096,128]{1,0:T(8,128)(2,1)} custom-call(s32[4096]{0:T(1024)} %fusion.26.pos_ref, s32[4096]{0:T(1024)} %bitcast.88, bf16[4096,128]{1,0:T(8,128)(2,1)} %shard_map.100.x_ref), custom_call_target="tpu_custom_call" | custom-call | tf_op jit(solution)/shard_map/pallas_call | solution.py:78
  21.3 11.5 %all-to-all-start = ((bf16[128,32,128]{2,1,0:T(8,128)(2,1)}), bf16[128,32,128]{2,1,0:T(8,128)(2,1)S(1)}, u32[]{:S(2)}, u32[]{:S(2)}) async-start(bf16[128,32,128]{2,1,0:T(8,128)(2,1)} %bitcast.78), calls=%async_computation | async-start | bytes 2097152 | tf_op jit(solution)/shard_map/all_to_all | solution.py:297
  32.8 0.0 copy-done.2
  32.8 0.1 copy.58
  33.0 0.1 copy.59
  33.1 0.1 eq.22
  33.2 2.7 %fusion.7 = (f32[4096,4]{1,0:T(8,128)S(1)}, bf16[4096,4]{1,0:T(8,128)(2,1)}) fusion(s32[4096]{0:T(1024)S(1)} %eq.22), kind=kLoop, calls=%fused_computation.15 | loop fusion | flops 49152 | bytes 114688 | tf_op jit(solution)/shard_map/convert_element_type | solution.py:309
  35.9 0.0 copy-done.3
  35.9 0.1 copy.61
  36.0 0.1 copy.57
  36.2 0.6 copy.62
  36.8 0.6 fusion.20.lane_mask_ref
  37.4 14.8 %all-to-all-done = bf16[128,32,128]{2,1,0:T(8,128)(2,1)S(1)} async-done(((bf16[128,32,128]{2,1,0:T(8,128)(2,1)}), bf16[128,32,128]{2,1,0:T(8,128)(2,1)S(1)}, u32[]{:S(2)}, u32[]{:S(2)}) %all-to-all-start) | async-done | bytes 1048608 | tf_op jit(solution)/shard_map/all_to_all | solution.py:297
  52.2 0.0 copy-start
  52.2 0.5 multiply_reduce_fusion
  52.7 0.5 copy-done
  53.2 11.1 %shard_map.102 = bf16[4,128,128]{2,1,0:T(8,128)(2,1)} custom-call(bf16[4096,128]{1,0:T(8,128)(2,1)} %bitcast.73, bf16[4096,4]{1,0:T(8,128)(2,1)} %get-tuple-element.16.column_mask_ref, f32[4,4096]{1,0:T(4,128)} %fusion.20.lane_mask_ref, bf16[128,128]{1,0:T(8,128)(2,1)} %inducing_ref.1, bf16[4,128,128]{2,1,0:T(8,128)(2,1)} %proj_ref.1), custom_call_target="tpu_custom_call" | custom-call | tf_op jit(solution)/shard_map/pallas_call | solution.py:243
  64.3 7.7 %shard_map.103 = bf16[2,2,128,128]{3,2,1,0:T(8,128)(2,1)} custom-call(bf16[2,2,128,128]{3,2,1,0:T(8,128)(2,1)} %bitcast.84, bf16[8,128,128]{2,1,0:T(8,128)(2,1)} %mixing_ref.1), custom_call_target="tpu_custom_call" | custom-call | tf_op jit(solution)/shard_map/pallas_call | solution.py:164
  72.0 1.1 convolution_convert_fusion
  73.1 1.1 multiply_reduce_fusion.1
  74.2 0.2 divide_convert_fusion
  74.5 1.3 %fusion.12 = f32[4096,512]{0,1:T(8,128)S(1)} fusion(bf16[4096,128]{0,1:T(8,128)(2,1)S(1)} %bitcast.75, bf16[512,128]{0,1:T(8,128)(2,1)S(1)} %bitcast.82), kind=kOutput, calls=%fused_computation.21 | convolution fusion | flops 268435456 | bytes 8978432 | tf_op jit(solution)/shard_map/dot_general | solution.py:330
  75.8 3.6 %fusion = (f32[4096]{0:T(1024)S(1)}, f32[4096]{0:T(1024)S(1)}, bf16[4096,512]{0,1:T(8,128)(2,1)S(1)}, bf16[4096,512]{0,1:T(8,128)(2,1)S(1)}) fusion(f32[4096,4]{0,1:T(4,128)S(1)} %copy.62, f32[4096,512]{0,1:T(8,128)S(1)} %fusion.12, bf16[512,128]{0,1:T(8,128)(2,1)S(1)} %bitcast.83, bf16[4096,128]{0,1:T(8,128)(2,1)S(1)} %bitcast.76), kind=kOutput, calls=%fused_computation.2 | convolution fusion | flops 285204480 | bytes 17465344 | tf_op jit(solution)/shard_map/dot_general | solution.py:330
  79.4 0.8 fusion.5
  80.3 0.0 copy-start.1
  80.3 0.8 fusion.6
  81.1 0.4 copy-done.1
  81.5 0.5 fusion.4
  82.0 25.3 %all_to_all.10 = bf16[128,32,128]{2,1,0:T(8,128)(2,1)} all-to-all(bf16[128,32,128]{2,1,0:T(8,128)(2,1)S(1)} %bitcast.77), channel_id=1, replica_groups=mesh['tx'=32,'ty'=4] {'tx','ty'}, dimensions={0} | all-to-all | bytes 2097152 | tf_op jit(solution)/shard_map/all_to_all | solution.py:349
  107.3 7.1 %shard_map.104 = bf16[4096,128]{1,0:T(8,128)(2,1)} custom-call(s32[4096]{0:T(1024)} %fusion.26.pos_ref, s32[4096]{0:T(1024)} %bitcast.89, bf16[4096,128]{1,0:T(8,128)(2,1)} %bitcast.79), custom_call_target="tpu_custom_call" | custom-call | tf_op jit(solution)/shard_map/pallas_call | solution.py:78
  (11 shorter events, 0.2 us)
Async XLA Ops:
  3.2 29.6 %copy-start.2 = (s32[128,512]{1,0:T(8,128)S(1)}, s32[128,512]{1,0:T(8,128)}, u32[]{:S(2)}) copy-start(s32[128,512]{1,0:T(8,128)} %param.14) | copy-start | bytes 786436
  14.0 21.9 %copy-start.3 = (bf16[4,128,128]{2,1,0:T(8,128)(2,1)S(1)}, bf16[4,128,128]{2,1,0:T(8,128)(2,1)}, u32[]{:S(2)}) copy-start(bf16[4,128,128]{2,1,0:T(8,128)(2,1)} %param.18) | copy-start | bytes 393220
  21.3 30.9 %all-to-all-start = ((bf16[128,32,128]{2,1,0:T(8,128)(2,1)}), bf16[128,32,128]{2,1,0:T(8,128)(2,1)S(1)}, u32[]{:S(2)}, u32[]{:S(2)}) async-start(bf16[128,32,128]{2,1,0:T(8,128)(2,1)} %bitcast.78), calls=%async_computation | async-start | bytes 2097152 | tf_op jit(solution)/shard_map/all_to_all | solution.py:297
  52.2 1.0 copy-start
  80.3 1.2 %copy-start.1 = (bf16[128,32,128]{2,1,0:T(8,128)(2,1)S(1)}, bf16[128,32,128]{2,1,0:T(8,128)(2,1)}, u32[]{:S(2)}) copy-start(bf16[128,32,128]{2,1,0:T(8,128)(2,1)} %copy-done) | copy-start | bytes 3145732

commit v17 on v13

--- a/solution.py
+++ b/solution.py
@@ -44,6 +44,43 @@
         ],
         out_specs=pl.BlockSpec((block, w3.shape[1]), lambda i: (i, 0)),
     )(x, w1, w2, w3)
+
+
+def encode_kernel(unroll, block, pos_ref, order_ref, x_ref, w1_ref, w2_ref, w3_ref, o_ref, rows_in, rows_out):
+    def silu(v):
+        return v / (1.0 + jnp.exp(-v))
+
+    for start in range(0, x_ref.shape[0], block):
+        part = pl.ds(start, block)
+        h = silu(jnp.dot(x_ref[part, :], w1_ref[...], preferred_element_type=jnp.float32))
+        h = h.astype(jnp.bfloat16)
+        for layer_id in range(w2_ref.shape[0]):
+            h = silu(jnp.dot(h, w2_ref[layer_id], preferred_element_type=jnp.float32))
+            h = h.astype(jnp.bfloat16)
+        features = jnp.dot(h, w3_ref[...], preferred_element_type=jnp.float32)
+        rows_in[part, :] = features.astype(jnp.bfloat16).astype(jnp.float32)
+
+    def body(step, carry):
+        for lane in range(unroll):
+            row = step * unroll + lane
+            source = order_ref[pos_ref[row]]
+            rows_out[pl.ds(row, 1), :] = rows_in[pl.ds(source, 1), :]
+        return carry
+
+    lax.fori_loop(0, o_ref.shape[0] // unroll, body, 0)
+    o_ref[...] = rows_out[...].astype(o_ref.dtype)
+
+
+def encode_and_gather(pos, order, x, w1, w2, w3, block):
+    shape = (x.shape[0], w3.shape[1])
+    return pl.pallas_call(
+        functools.partial(encode_kernel, 64, block),
+        out_shape=jax.ShapeDtypeStruct(shape, jnp.bfloat16),
+        in_specs=[pl.BlockSpec(memory_space=pltpu.SMEM)] * 2
+        + [pl.BlockSpec(memory_space=pltpu.VMEM)] * 4,
+        out_specs=pl.BlockSpec(memory_space=pltpu.VMEM),
+        scratch_shapes=[pltpu.VMEM(shape, jnp.float32), pltpu.VMEM(shape, jnp.float32)],
+    )(pos, order, x, w1, w2, w3)
 
 
 def gather_kernel(unroll, pos_ref, order_ref, x_ref, o_ref, rows_in, rows_out):
@@ -277,7 +314,6 @@
     head_width = width // HEADS
     inducing_count = inducing.shape[0]
 
-    features = point_mlp(points, embed_weight, inner_weights, output_weight, 2048)
 
     own_counts = lax.dynamic_index_in_dim(counts, own_index, 0, keepdims=False)
     own_offsets = jnp.cumsum(own_counts) - own_counts
@@ -295,7 +331,9 @@
     ).reshape(along_x, band)
     send_pos = (local_pos + band_start).reshape(-1)
     order = point_order[0]
-    outgoing = move_rows(gather_kernel, send_pos, order, features)
+    outgoing = encode_and_gather(
+        send_pos, order, points, embed_weight, inner_weights, output_weight, 2048
+    )
     outgoing = outgoing.reshape(devices, quota, width)
     arrived = lax.all_to_all(outgoing, ("tx", "ty"), split_axis=0, concat_axis=0, tiled=True)
     all_rows = arrived.reshape(devices * quota, width)

time: 113 us -> 111 us (0.982)
  Pallas kernels: 39.7 us -> 37.1 us
    pallas_call x2 -> x1, Pallas kernels: 14.4 us -> 7.09 us  [move_rows(): pl.pallas_call(functools.partial(kernel, 64), out_shape=jax.ShapeDtypeStr...]
    pallas_call x1, Pallas kernels: 8.09 us -> 12.8 us  [encode_and_gather(): pl.pallas_call(functools.partial(encode_kernel, 64, block), out_shape=jax...]
where the time goes in v17:
time: 111 us; the launch traced here: 110 us
  Pallas kernels  37.1 us (33%)
  blocking collectives  25.3 us (23%)
  waiting for transfers between devices  14.8 us (13%)
  starting transfers between devices  11.5 us (10%)
  matrix products  9.78 us (9%)
  local copies, waits for them, and re-layouts  6.58 us (6%)
  other arithmetic  4.89 us (4%)
    all_to_all x1, blocking collectives, body(): lax.all_to_all(result.reshape(devices, quota, width), ('tx', 'ty'), split...  25.3 us
    all_to_all x1, waiting for transfers between devices, body(): lax.all_to_all(outgoing, ('tx', 'ty'), split_axis=0, concat_axis=0, tiled...  14.8 us
    pallas_call x1, Pallas kernels, encode_and_gather(): pl.pallas_call(functools.partial(encode_kernel, 64, block), out_shape=jax...  12.8 us
    all_to_all x1, starting transfers between devices, body(): lax.all_to_all(outgoing, ('tx', 'ty'), split_axis=0, concat_axis=0, tiled...  11.5 us
    pallas_call x1, Pallas kernels, summarize(): pl.pallas_call(summary_kernel, out_shape=jax.ShapeDtypeStruct((tiles,) +...  9.49 us
    pallas_call x1, Pallas kernels, mix_tiles(): pl.pallas_call(functools.partial(mix_kernel, count_x, count_y), out_shape...  7.7 us
    pallas_call x1, Pallas kernels, move_rows(): pl.pallas_call(functools.partial(kernel, 64), out_shape=jax.ShapeDtypeStr...  7.09 us
    dot_general x2, matrix products, body(): jnp.dot(point_queries[:, lower:upper], second_keys[:, lower:upper].T, pre...  4.92 us
  transfers between devices with their start and end apart: 1, of which 1 were waited for; matrix products, arithmetic and copies ran while one was open for 4% of the time, Pallas kernels for 0%

profile of v17, /device:TPU:1, one launch (start us, length us, event | category | flops | bytes accessed | tf_op | source)
XLA Modules:
  0.0 110.2 jit_solution(7108562590142851793)
XLA Ops:
  0.0 0.0 copy-start.2
  0.0 0.5 broadcast.75
  0.5 1.4 %fusion.29 = (s32[512]{0:T(512)S(1)}, s32[1,512]{1,0:T(1,128)S(1)}) fusion(s32[]{:T(128)} %broadcast.75, s32[128,512]{1,0:T(8,128)} %param.14, s32[]{:T(128)S(6)} %select_n.22), kind=kLoop, calls=%fused_computation.58 | loop fusion | bytes 6152 | tf_op jit(solution)/shard_map/jit(dynamic_index_in_dim)/dynamic_slice | solution.py:318
  1.9 0.3 reduce-window.9
  2.2 0.1 slice.57
  2.3 0.2 reshape.155
  2.5 0.1 slice_reduce_fusion.1
  2.6 0.1 broadcast.62
  2.7 0.1 reshape.157
  2.8 0.2 reshape.153
  3.0 0.1 slice_add_fusion
  3.1 0.1 add_subtract_fusion
  3.2 0.7 slice_reduce_fusion
  3.9 0.1 lt.52
  4.0 0.1 copy.51
  4.1 0.1 copy.52
  4.2 0.1 lt.56
  4.3 0.1 lt.57
  4.4 0.1 copy.55
  4.5 0.1 copy.53
  4.6 0.1 copy.56
  4.7 0.1 copy.54
  4.8 0.1 add.100
  4.9 0.1 add.101
  5.0 0.1 add.103
  5.1 0.1 add.104
  5.2 0.7 fusion.26.pos_ref
  5.9 0.0 copy-start.3
  5.9 12.8 %shard_map.100 = bf16[4096,128]{1,0:T(8,128)(2,1)} custom-call(s32[4096]{0:T(1024)} %fusion.26.pos_ref, s32[4096]{0:T(1024)} %bitcast.88, bf16[4096,128]{1,0:T(8,128)(2,1)} %x_ref.1, bf16[128,512]{1,0:T(8,128)(2,1)} %w1_ref.1, bf16[1,512,512]{2,1,0:T(8,128)(2,1)} %w2_ref.1, bf16[512,128]{1,0:T(8,128)(2,1)} %w3_ref.1), custom_call_target="tpu_custom_call" | custom-call | tf_op jit(solution)/shard_map/pallas_call | solution.py:76
  18.7 11.5 %all-to-all-start = ((bf16[128,32,128]{2,1,0:T(8,128)(2,1)}), bf16[128,32,128]{2,1,0:T(8,128)(2,1)S(1)}, u32[]{:S(2)}, u32[]{:S(2)}) async-start(bf16[128,32,128]{2,1,0:T(8,128)(2,1)} %bitcast.79), calls=%async_computation | async-start | bytes 2097152 | tf_op jit(solution)/shard_map/all_to_all | solution.py:338
  30.2 0.0 copy-done.2
  30.2 0.1 copy.58
  30.4 0.1 copy.59
  30.5 0.1 eq.22
  30.6 2.7 %fusion.7 = (f32[4096,4]{1,0:T(8,128)S(1)}, bf16[4096,4]{1,0:T(8,128)(2,1)}) fusion(s32[4096]{0:T(1024)S(1)} %eq.22), kind=kLoop, calls=%fused_computation.15 | loop fusion | flops 49152 | bytes 114688 | tf_op jit(solution)/shard_map/convert_element_type | solution.py:350
  33.3 0.0 copy-done.3
  33.3 0.1 copy.61
  33.5 0.1 copy.57
  33.6 0.6 copy.62
  34.2 0.6 fusion.20.lane_mask_ref
  34.9 14.8 %all-to-all-done = bf16[128,32,128]{2,1,0:T(8,128)(2,1)S(1)} async-done(((bf16[128,32,128]{2,1,0:T(8,128)(2,1)}), bf16[128,32,128]{2,1,0:T(8,128)(2,1)S(1)}, u32[]{:S(2)}, u32[]{:S(2)}) %all-to-all-start) | async-done | bytes 1048608 | tf_op jit(solution)/shard_map/all_to_all | solution.py:338
  49.6 0.0 copy-start
  49.6 0.5 multiply_reduce_fusion
  50.1 0.5 copy-done
  50.6 9.5 %shard_map.101 = bf16[4,128,128]{2,1,0:T(8,128)(2,1)} custom-call(bf16[4096,128]{1,0:T(8,128)(2,1)} %bitcast.73, bf16[4096,4]{1,0:T(8,128)(2,1)} %get-tuple-element.16.column_mask_ref, f32[4,4096]{1,0:T(4,128)} %fusion.20.lane_mask_ref, bf16[128,128]{1,0:T(8,128)(2,1)} %inducing_ref.1, bf16[4,128,128]{2,1,0:T(8,128)(2,1)} %proj_ref.1), custom_call_target="tpu_custom_call" | custom-call | tf_op jit(solution)/shard_map/pallas_call | solution.py:283
  60.1 7.7 %shard_map.102 = bf16[2,2,128,128]{3,2,1,0:T(8,128)(2,1)} custom-call(bf16[2,2,128,128]{3,2,1,0:T(8,128)(2,1)} %bitcast.84, bf16[8,128,128]{2,1,0:T(8,128)(2,1)} %mixing_ref.1), custom_call_target="tpu_custom_call" | custom-call | tf_op jit(solution)/shard_map/pallas_call | solution.py:201
  67.8 1.1 %convolution_convert_fusion = bf16[512,128]{0,1:T(8,128)(2,1)S(1)} fusion(bf16[512,128]{1,0:T(8,128)(2,1)} %bitcast.80, bf16[4,128,128]{2,1,0:T(8,128)(2,1)S(1)} %copy-done.3), kind=kOutput, calls=%fused_computation.16 | convolution fusion | flops 16842752 | bytes 294912 | tf_op jit(solution)/shard_map/dot_general | solution.py:363
  68.9 1.1 %multiply_reduce_fusion.1 = (f32[512,2]{0,1:T(2,128)S(1)}, f32[512,2,64]{0,2,1:T(8,128)S(1)}) fusion(bf16[512,128,1]{1,0,2:T(8,128)(2,1)} %bitcast.81, bf16[2,64,128]{2,1,0:T(8,128)(2,1)S(1)} %bitcast.87), kind=kOutput, calls=%fused_computation.26 | convolution fusion | flops 16907264 | bytes 430080 | tf_op jit(solution)/shard_map/dot_general | solution.py:361
  70.1 0.2 divide_convert_fusion
  70.3 1.3 %fusion.12 = f32[4096,512]{0,1:T(8,128)S(1)} fusion(bf16[4096,128]{0,1:T(8,128)(2,1)S(1)} %bitcast.75, bf16[512,128]{0,1:T(8,128)(2,1)S(1)} %bitcast.82), kind=kOutput, calls=%fused_computation.21 | convolution fusion | flops 268435456 | bytes 8978432 | tf_op jit(solution)/shard_map/dot_general | solution.py:371
  71.6 3.6 %fusion = (f32[4096]{0:T(1024)S(1)}, f32[4096]{0:T(1024)S(1)}, bf16[4096,512]{0,1:T(8,128)(2,1)S(1)}, bf16[4096,512]{0,1:T(8,128)(2,1)S(1)}) fusion(f32[4096,4]{0,1:T(4,128)S(1)} %copy.62, f32[4096,512]{0,1:T(8,128)S(1)} %fusion.12, bf16[512,128]{0,1:T(8,128)(2,1)S(1)} %bitcast.83, bf16[4096,128]{0,1:T(8,128)(2,1)S(1)} %bitcast.76), kind=kOutput, calls=%fused_computation.2 | convolution fusion | flops 285204480 | bytes 17465344 | tf_op jit(solution)/shard_map/dot_general | solution.py:371
  75.2 0.8 fusion.5
  76.1 0.0 copy-start.1
  76.1 0.8 fusion.6
  76.9 0.4 copy-done.1
  77.3 0.5 fusion.4
  77.8 25.3 %all_to_all.10 = bf16[128,32,128]{2,1,0:T(8,128)(2,1)} all-to-all(bf16[128,32,128]{2,1,0:T(8,128)(2,1)S(1)} %bitcast.77), channel_id=1, replica_groups=mesh['tx'=32,'ty'=4] {'tx','ty'}, dimensions={0} | all-to-all | bytes 2097152 | tf_op jit(solution)/shard_map/all_to_all | solution.py:390
  103.1 7.1 %shard_map.103 = bf16[4096,128]{1,0:T(8,128)(2,1)} custom-call(s32[4096]{0:T(1024)} %fusion.26.pos_ref, s32[4096]{0:T(1024)} %bitcast.89, bf16[4096,128]{1,0:T(8,128)(2,1)} %bitcast.78), custom_call_target="tpu_custom_call" | custom-call | tf_op jit(solution)/shard_map/pallas_call | solution.py:115
  (11 shorter events, 0.2 us)
Async XLA Ops:
  0.0 30.2 %copy-start.2 = (s32[128,512]{1,0:T(8,128)S(1)}, s32[128,512]{1,0:T(8,128)}, u32[]{:S(2)}) copy-start(s32[128,512]{1,0:T(8,128)} %param.14) | copy-start | bytes 786436
  5.9 27.4 %copy-start.3 = (bf16[4,128,128]{2,1,0:T(8,128)(2,1)S(1)}, bf16[4,128,128]{2,1,0:T(8,128)(2,1)}, u32[]{:S(2)}) copy-start(bf16[4,128,128]{2,1,0:T(8,128)(2,1)} %param.18) | copy-start | bytes 393220
  18.7 30.9 %all-to-all-start = ((bf16[128,32,128]{2,1,0:T(8,128)(2,1)}), bf16[128,32,128]{2,1,0:T(8,128)(2,1)S(1)}, u32[]{:S(2)}, u32[]{:S(2)}) async-start(bf16[128,32,128]{2,1,0:T(8,128)(2,1)} %bitcast.79), calls=%async_computation | async-start | bytes 2097152 | tf_op jit(solution)/shard_map/all_to_all | solution.py:338
  49.6 1.0 copy-start
  76.1 1.2 %copy-start.1 = (bf16[128,32,128]{2,1,0:T(8,128)(2,1)S(1)}, bf16[128,32,128]{2,1,0:T(8,128)(2,1)}, u32[]{:S(2)}) copy-start(bf16[128,32,128]{2,1,0:T(8,128)(2,1)} %copy-done) | copy-start | bytes 3145732

commit v18 on v17

--- a/solution.py
+++ b/solution.py
@@ -125,7 +125,22 @@
     )(pos, order, x)
 
 
-def mix_kernel(count_x, count_y, x_ref, mixing_ref, o_ref, padded, send_sem, recv_sem, local_sem):
+def mix_kernel(
+    count_x,
+    count_y,
+    rows_ref,
+    column_mask_ref,
+    lane_mask_ref,
+    inducing_ref,
+    proj_ref,
+    mixing_ref,
+    o_ref,
+    x_ref,
+    padded,
+    send_sem,
+    recv_sem,
+    local_sem,
+):
     index_x = lax.axis_index("tx")
     index_y = lax.axis_index("ty")
     size_x, size_y = x_ref.shape[0], x_ref.shape[1]
@@ -149,6 +164,10 @@
             pl.semaphore_signal(
                 barrier, 1, device_id=(index_x + a, index_y + b), device_id_type=mesh_ids
             )
+    def store(t, value):
+        x_ref[t // size_y, t % size_y] = value
+
+    summary_body(rows_ref, column_mask_ref, lane_mask_ref, inducing_ref, proj_ref, store)
     peers = sum(inside(index_x + a, index_y + b).astype(jnp.int32) for a, b in steps)
     pl.semaphore_wait(barrier, peers)
 
@@ -194,23 +213,25 @@
             o_ref[tile_x, tile_y] = total.astype(o_ref.dtype)
 
 
-def mix_tiles(block, mixing):
+def mix_tiles(rows, row_mask, inducing, first_proj, mixing):
     count_x = lax.axis_size("tx")
     count_y = lax.axis_size("ty")
-    shape = (block.shape[0] + 2, block.shape[1] + 2) + block.shape[2:]
+    tiles = (TLX, TLY) + inducing.shape
+    shape = (TLX + 2, TLY + 2) + inducing.shape
     return pl.pallas_call(
         functools.partial(mix_kernel, count_x, count_y),
-        out_shape=jax.ShapeDtypeStruct(block.shape, block.dtype),
-        in_specs=[pl.BlockSpec(memory_space=pltpu.VMEM)] * 2,
+        out_shape=jax.ShapeDtypeStruct(tiles, jnp.bfloat16),
+        in_specs=[pl.BlockSpec(memory_space=pltpu.VMEM)] * 6,
         out_specs=pl.BlockSpec(memory_space=pltpu.VMEM),
         scratch_shapes=[
-            pltpu.VMEM(shape, block.dtype),
+            pltpu.VMEM(tiles, jnp.bfloat16),
+            pltpu.VMEM(shape, jnp.bfloat16),
             pltpu.SemaphoreType.DMA((8,)),
             pltpu.SemaphoreType.DMA((8,)),
             pltpu.SemaphoreType.DMA,
         ],
         compiler_params=pltpu.CompilerParams(collective_id=0, has_side_effects=True),
-    )(block, mixing)
+    )(rows, row_mask.astype(jnp.bfloat16), row_mask.T, inducing, first_proj, mixing)
 
 
 def unit_heads(projected, head_count):
@@ -235,7 +256,7 @@
     return (projected / jnp.sqrt(totals + epsilon)).astype(jnp.bfloat16)
 
 
-def summary_kernel(rows_ref, column_mask_ref, lane_mask_ref, inducing_ref, proj_ref, o_ref):
+def summary_body(rows_ref, column_mask_ref, lane_mask_ref, inducing_ref, proj_ref, store):
     width = rows_ref.shape[1]
     head_width = width // HEADS
     tiles = column_mask_ref.shape[1]
@@ -273,19 +294,12 @@
     for t in range(tiles):
         attended = jnp.concatenate([heads_out[h][t] for h in range(HEADS)], axis=1)
         attended = attended.astype(jnp.bfloat16)
-        o_ref[t] = (
-            inducing + jnp.dot(attended, proj_ref[3], preferred_element_type=jnp.float32)
-        ).astype(o_ref.dtype)
-
-
-def summarize(rows, row_mask, inducing, proj):
-    tiles = row_mask.shape[1]
-    return pl.pallas_call(
-        summary_kernel,
-        out_shape=jax.ShapeDtypeStruct((tiles,) + inducing.shape, jnp.bfloat16),
-        in_specs=[pl.BlockSpec(memory_space=pltpu.VMEM)] * 5,
-        out_specs=pl.BlockSpec(memory_space=pltpu.VMEM),
-    )(rows, row_mask.astype(jnp.bfloat16), row_mask.T, inducing, proj)
+        store(
+            t,
+            (inducing + jnp.dot(attended, proj_ref[3], preferred_element_type=jnp.float32)).astype(
+                jnp.bfloat16
+            ),
+        )
 
 
 def body(
@@ -349,9 +363,7 @@
     tile_ids = jnp.arange(per_device, dtype=jnp.int32)
     row_mask = (row_tile[:, None] == tile_ids[None, :]).astype(jnp.float32)
 
-    summary = summarize(all_rows, row_mask, inducing, first_proj)
-    tile_grid = summary.reshape(TLX, TLY, inducing_count, width)
-    mixture = mix_tiles(tile_grid, mixing)
+    mixture = mix_tiles(all_rows, row_mask, inducing, first_proj, mixing)
     mixture = mixture.astype(jnp.bfloat16).reshape(per_device * inducing_count, width)
 
     point_queries = unit_heads(

time: 111 us -> 108 us (0.973)
  Pallas kernels: 37.1 us -> 34.2 us
    pallas_call x1 -> x0, Pallas kernels: 9.49 us -> none  [summarize(): pl.pallas_call(summary_kernel, out_shape=jax.ShapeDtypeStruct((tiles,) +...]
    pallas_call x1, Pallas kernels: 7.7 us -> 14.2 us  [mix_tiles(): pl.pallas_call(functools.partial(mix_kernel, count_x, count_y), out_shape...]
where the time goes in v18:
time: 108 us; the launch traced here: 107 us
  Pallas kernels  34.2 us (32%)
  blocking collectives  25.5 us (24%)
  waiting for transfers between devices  14.8 us (14%)
  starting transfers between devices  11.5 us (11%)
  matrix products  9.78 us (9%)
  local copies, waits for them, and re-layouts  6.58 us (6%)
  other arithmetic  4.89 us (5%)
    all_to_all x1, blocking collectives, body(): lax.all_to_all(result.reshape(devices, quota, width), ('tx', 'ty'), split...  25.5 us
    all_to_all x1, waiting for transfers between devices, body(): lax.all_to_all(outgoing, ('tx', 'ty'), split_axis=0, concat_axis=0, tiled...  14.8 us
    pallas_call x1, Pallas kernels, mix_tiles(): pl.pallas_call(functools.partial(mix_kernel, count_x, count_y), out_shape...  14.2 us
    pallas_call x1, Pallas kernels, encode_and_gather(): pl.pallas_call(functools.partial(encode_kernel, 64, block), out_shape=jax...  12.8 us
    all_to_all x1, starting transfers between devices, body(): lax.all_to_all(outgoing, ('tx', 'ty'), split_axis=0, concat_axis=0, tiled...  11.5 us
    pallas_call x1, Pallas kernels, move_rows(): pl.pallas_call(functools.partial(kernel, 64), out_shape=jax.ShapeDtypeStr...  7.1 us
    dot_general x2, matrix products, body(): jnp.dot(point_queries[:, lower:upper], second_keys[:, lower:upper].T, pre...  4.92 us
    convert_element_type x2, other arithmetic, body(): row_mask = (row_tile[:, None] == tile_ids[None, :]).astype(jnp.float32)  3.36 us
  transfers between devices with their start and end apart: 1, of which 1 were waited for; matrix products, arithmetic and copies ran while one was open for 4% of the time, Pallas kernels for 0%

profile of v18, /device:TPU:1, one launch (start us, length us, event | category | flops | bytes accessed | tf_op | source)
XLA Modules:
  0.0 107.4 jit_solution(4974888427792409470)
XLA Ops:
  0.0 0.0 copy-start.2
  0.0 0.5 broadcast.75
  0.5 1.4 %fusion.29 = (s32[512]{0:T(512)S(1)}, s32[1,512]{1,0:T(1,128)S(1)}) fusion(s32[]{:T(128)} %broadcast.75, s32[128,512]{1,0:T(8,128)} %param.14, s32[]{:T(128)S(6)} %select_n.22), kind=kLoop, calls=%fused_computation.58 | loop fusion | bytes 6152 | tf_op jit(solution)/shard_map/jit(dynamic_index_in_dim)/dynamic_slice | solution.py:332
  1.9 0.3 reduce-window.9
  2.2 0.1 slice.57
  2.3 0.2 reshape.152
  2.5 0.1 slice_reduce_fusion.1
  2.6 0.1 broadcast.62
  2.7 0.1 reshape.154
  2.8 0.2 reshape.150
  3.0 0.1 slice_add_fusion
  3.1 0.1 add_subtract_fusion
  3.2 0.7 slice_reduce_fusion
  3.9 0.1 lt.52
  4.0 0.1 copy.51
  4.1 0.1 copy.52
  4.2 0.1 lt.56
  4.3 0.1 lt.57
  4.4 0.1 copy.55
  4.5 0.1 copy.53
  4.6 0.1 copy.56
  4.7 0.1 copy.54
  4.8 0.1 add.100
  4.9 0.1 add.101
  5.0 0.1 add.103
  5.1 0.1 add.104
  5.2 0.7 fusion.26.pos_ref
  5.9 0.0 copy-start.3
  5.9 12.8 %shard_map.100 = bf16[4096,128]{1,0:T(8,128)(2,1)} custom-call(s32[4096]{0:T(1024)} %fusion.26.pos_ref, s32[4096]{0:T(1024)} %bitcast.86, bf16[4096,128]{1,0:T(8,128)(2,1)} %x_ref.1, bf16[128,512]{1,0:T(8,128)(2,1)} %w1_ref.1, bf16[1,512,512]{2,1,0:T(8,128)(2,1)} %w2_ref.1, bf16[512,128]{1,0:T(8,128)(2,1)} %w3_ref.1), custom_call_target="tpu_custom_call" | custom-call | tf_op jit(solution)/shard_map/pallas_call | solution.py:76
  18.7 11.5 %all-to-all-start = ((bf16[128,32,128]{2,1,0:T(8,128)(2,1)}), bf16[128,32,128]{2,1,0:T(8,128)(2,1)S(1)}, u32[]{:S(2)}, u32[]{:S(2)}) async-start(bf16[128,32,128]{2,1,0:T(8,128)(2,1)} %bitcast.78), calls=%async_computation | async-start | bytes 2097152 | tf_op jit(solution)/shard_map/all_to_all | solution.py:352
  30.2 0.0 copy-done.2
  30.2 0.1 copy.58
  30.4 0.1 copy.59
  30.5 0.1 eq.22
  30.6 2.7 %fusion.7 = (f32[4096,4]{1,0:T(8,128)S(1)}, bf16[4096,4]{1,0:T(8,128)(2,1)}) fusion(s32[4096]{0:T(1024)S(1)} %eq.22), kind=kLoop, calls=%fused_computation.15 | loop fusion | flops 49152 | bytes 114688 | tf_op jit(solution)/shard_map/convert_element_type | solution.py:364
  33.3 0.0 copy-done.3
  33.3 0.1 copy.61
  33.4 0.1 copy.57
  33.6 0.6 copy.62
  34.2 0.6 fusion.20.lane_mask_ref
  34.8 14.8 %all-to-all-done = bf16[128,32,128]{2,1,0:T(8,128)(2,1)S(1)} async-done(((bf16[128,32,128]{2,1,0:T(8,128)(2,1)}), bf16[128,32,128]{2,1,0:T(8,128)(2,1)S(1)}, u32[]{:S(2)}, u32[]{:S(2)}) %all-to-all-start) | async-done | bytes 1048608 | tf_op jit(solution)/shard_map/all_to_all | solution.py:352
  49.6 0.0 copy-start
  49.6 0.5 multiply_reduce_fusion
  50.1 0.5 copy-done
  50.6 14.2 %shard_map.101 = bf16[2,2,128,128]{3,2,1,0:T(8,128)(2,1)} custom-call(bf16[4096,128]{1,0:T(8,128)(2,1)} %bitcast.72, bf16[4096,4]{1,0:T(8,128)(2,1)} %get-tuple-element.16.column_mask_ref, f32[4,4096]{1,0:T(4,128)} %fusion.20.lane_mask_ref, bf16[128,128]{1,0:T(8,128)(2,1)} %inducing_ref.1, bf16[4,128,128]{2,1,0:T(8,128)(2,1)} %proj_ref.1, ...), custom_call_target="tpu_custom_call" | custom-call | tf_op jit(solution)/shard_map/pallas_call | solution.py:221
  64.9 1.1 %convolution_convert_fusion = bf16[512,128]{0,1:T(8,128)(2,1)S(1)} fusion(bf16[512,128]{1,0:T(8,128)(2,1)} %bitcast.79, bf16[4,128,128]{2,1,0:T(8,128)(2,1)S(1)} %copy-done.3), kind=kOutput, calls=%fused_computation.16 | convolution fusion | flops 16842752 | bytes 294912 | tf_op jit(solution)/shard_map/dot_general | solution.py:375
  66.0 1.1 %multiply_reduce_fusion.1 = (f32[512,2]{0,1:T(2,128)S(1)}, f32[512,2,64]{0,2,1:T(8,128)S(1)}) fusion(bf16[512,128,1]{1,0,2:T(8,128)(2,1)} %bitcast.80, bf16[2,64,128]{2,1,0:T(8,128)(2,1)S(1)} %bitcast.85), kind=kOutput, calls=%fused_computation.26 | convolution fusion | flops 16907264 | bytes 430080 | tf_op jit(solution)/shard_map/dot_general | solution.py:373
  67.1 0.2 divide_convert_fusion
  67.3 1.3 %fusion.12 = f32[4096,512]{0,1:T(8,128)S(1)} fusion(bf16[4096,128]{0,1:T(8,128)(2,1)S(1)} %bitcast.74, bf16[512,128]{0,1:T(8,128)(2,1)S(1)} %bitcast.81), kind=kOutput, calls=%fused_computation.21 | convolution fusion | flops 268435456 | bytes 8978432 | tf_op jit(solution)/shard_map/dot_general | solution.py:383
  68.6 3.6 %fusion = (f32[4096]{0:T(1024)S(1)}, f32[4096]{0:T(1024)S(1)}, bf16[4096,512]{0,1:T(8,128)(2,1)S(1)}, bf16[4096,512]{0,1:T(8,128)(2,1)S(1)}) fusion(f32[4096,4]{0,1:T(4,128)S(1)} %copy.62, f32[4096,512]{0,1:T(8,128)S(1)} %fusion.12, bf16[512,128]{0,1:T(8,128)(2,1)S(1)} %bitcast.82, bf16[4096,128]{0,1:T(8,128)(2,1)S(1)} %bitcast.75), kind=kOutput, calls=%fused_computation.2 | convolution fusion | flops 285204480 | bytes 17465344 | tf_op jit(solution)/shard_map/dot_general | solution.py:383
  72.3 0.8 fusion.5
  73.1 0.0 copy-start.1
  73.1 0.8 fusion.6
  74.0 0.4 copy-done.1
  74.4 0.5 fusion.4
  74.8 25.5 %all_to_all.10 = bf16[128,32,128]{2,1,0:T(8,128)(2,1)} all-to-all(bf16[128,32,128]{2,1,0:T(8,128)(2,1)S(1)} %bitcast.76), channel_id=1, replica_groups=mesh['tx'=32,'ty'=4] {'tx','ty'}, dimensions={0} | all-to-all | bytes 2097152 | tf_op jit(solution)/shard_map/all_to_all | solution.py:402
  100.3 7.1 %shard_map.102 = bf16[4096,128]{1,0:T(8,128)(2,1)} custom-call(s32[4096]{0:T(1024)} %fusion.26.pos_ref, s32[4096]{0:T(1024)} %bitcast.87, bf16[4096,128]{1,0:T(8,128)(2,1)} %bitcast.77), custom_call_target="tpu_custom_call" | custom-call | tf_op jit(solution)/shard_map/pallas_call | solution.py:115
  (11 shorter events, 0.2 us)
Async XLA Ops:
  0.0 30.2 %copy-start.2 = (s32[128,512]{1,0:T(8,128)S(1)}, s32[128,512]{1,0:T(8,128)}, u32[]{:S(2)}) copy-start(s32[128,512]{1,0:T(8,128)} %param.14) | copy-start | bytes 786436
  5.9 27.4 %copy-start.3 = (bf16[4,128,128]{2,1,0:T(8,128)(2,1)S(1)}, bf16[4,128,128]{2,1,0:T(8,128)(2,1)}, u32[]{:S(2)}) copy-start(bf16[4,128,128]{2,1,0:T(8,128)(2,1)} %param.18) | copy-start | bytes 393220
  18.7 30.9 %all-to-all-start = ((bf16[128,32,128]{2,1,0:T(8,128)(2,1)}), bf16[128,32,128]{2,1,0:T(8,128)(2,1)S(1)}, u32[]{:S(2)}, u32[]{:S(2)}) async-start(bf16[128,32,128]{2,1,0:T(8,128)(2,1)} %bitcast.78), calls=%async_computation | async-start | bytes 2097152 | tf_op jit(solution)/shard_map/all_to_all | solution.py:352
  49.6 1.0 copy-start
  73.1 1.2 %copy-start.1 = (bf16[128,32,128]{2,1,0:T(8,128)(2,1)S(1)}, bf16[128,32,128]{2,1,0:T(8,128)(2,1)}, u32[]{:S(2)}) copy-start(bf16[128,32,128]{2,1,0:T(8,128)(2,1)} %copy-done) | copy-start | bytes 3145732

commit v19 on v18

--- a/solution.py
+++ b/solution.py
@@ -330,13 +330,14 @@
 
 
     own_counts = lax.dynamic_index_in_dim(counts, own_index, 0, keepdims=False)
-    own_offsets = jnp.cumsum(own_counts) - own_counts
+    band_counts = own_counts.reshape(along_x, -1)
+    band_offsets = jnp.cumsum(band_counts, axis=1) - band_counts
     grid_counts = own_counts.reshape(along_x, TLX, along_y, TLY)
-    grid_offsets = own_offsets.reshape(along_x, TLX, along_y, TLY)
-    band_start = grid_offsets[:, 0, 0, 0][:, None]
+    grid_offsets = band_offsets.reshape(along_x, TLX, along_y, TLY)
+    band_start = (jnp.arange(along_x, dtype=jnp.int32) * band)[:, None]
     first_len = grid_counts[:, 0, :, 0] + grid_counts[:, 0, :, 1]
-    first_start = grid_offsets[:, 0, :, 0] - band_start
-    second_start = grid_offsets[:, 1, :, 0] - band_start
+    first_start = grid_offsets[:, 0, :, 0]
+    second_start = grid_offsets[:, 1, :, 0]
     slot_ids = jnp.arange(quota, dtype=jnp.int32)
     local_pos = jnp.where(
         slot_ids[None, None, :] < first_len[:, :, None],

time: 108 us -> 107 us (level)
  no operation moved by 1% of the time
where the time goes in v19:
time: 107 us; the launch traced here: 106 us
  Pallas kernels  34.2 us (32%)
  blocking collectives  25.5 us (24%)
  waiting for transfers between devices  14.8 us (14%)
  starting transfers between devices  11.5 us (11%)
  matrix products  9.78 us (9%)
  local copies, waits for them, and re-layouts  5.64 us (5%)
  other arithmetic  4.66 us (4%)
    all_to_all x1, blocking collectives, body(): lax.all_to_all(result.reshape(devices, quota, width), ('tx', 'ty'), split...  25.5 us
    all_to_all x1, waiting for transfers between devices, body(): lax.all_to_all(outgoing, ('tx', 'ty'), split_axis=0, concat_axis=0, tiled...  14.8 us
    pallas_call x1, Pallas kernels, mix_tiles(): pl.pallas_call(functools.partial(mix_kernel, count_x, count_y), out_shape...  14.2 us
    pallas_call x1, Pallas kernels, encode_and_gather(): pl.pallas_call(functools.partial(encode_kernel, 64, block), out_shape=jax...  12.8 us
    all_to_all x1, starting transfers between devices, body(): lax.all_to_all(outgoing, ('tx', 'ty'), split_axis=0, concat_axis=0, tiled...  11.5 us
    pallas_call x1, Pallas kernels, move_rows(): pl.pallas_call(functools.partial(kernel, 64), out_shape=jax.ShapeDtypeStr...  7.09 us
    dot_general x2, matrix products, body(): jnp.dot(point_queries[:, lower:upper], second_keys[:, lower:upper].T, pre...  4.92 us
    convert_element_type x2, other arithmetic, body(): row_mask = (row_tile[:, None] == tile_ids[None, :]).astype(jnp.float32)  3.36 us
  transfers between devices with their start and end apart: 1, of which 1 were waited for; matrix products, arithmetic and copies ran while one was open for 4% of the time, Pallas kernels for 0%

profile of v19, /device:TPU:1, one launch (start us, length us, event | category | flops | bytes accessed | tf_op | source)
XLA Modules:
  0.0 106.2 jit_solution(5290270618969426906)
XLA Ops:
  0.0 0.0 copy-start.2
  0.0 0.1 lt.52
  0.1 0.5 broadcast.46
  0.6 1.4 %fusion.29 = (s32[512]{0:T(512)S(1)}, s32[1,512]{1,0:T(1,128)S(1)}) fusion(s32[]{:T(128)} %broadcast.46, s32[128,512]{1,0:T(8,128)} %param.14, s32[]{:T(128)S(6)} %select_n.22), kind=kLoop, calls=%fused_computation.54 | loop fusion | bytes 6152 | tf_op jit(solution)/shard_map/jit(dynamic_index_in_dim)/dynamic_slice | solution.py:332
  2.0 0.1 reshape.96
  2.1 0.2 reduce_window_sum.24
  2.2 0.1 copy.46
  2.3 0.2 copy.47
  2.5 0.2 reshape.95
  2.7 0.1 slice_add_fusion
  2.8 0.1 copy.44
  3.0 0.1 copy.50
  3.1 0.1 copy.48
  3.2 0.1 copy.49
  3.3 0.1 copy.51
  3.3 0.1 copy.45
  3.4 0.1 lt.56
  3.5 0.1 lt.57
  3.6 0.1 add.109
  3.7 0.1 add.110
  3.8 0.1 add.105
  3.9 0.1 add.106
  4.0 0.7 fusion.26.pos_ref
  4.7 0.0 copy-start.3
  4.7 12.8 %shard_map.100 = bf16[4096,128]{1,0:T(8,128)(2,1)} custom-call(s32[4096]{0:T(1024)} %fusion.26.pos_ref, s32[4096]{0:T(1024)} %bitcast.85, bf16[4096,128]{1,0:T(8,128)(2,1)} %x_ref.1, bf16[128,512]{1,0:T(8,128)(2,1)} %w1_ref.1, bf16[1,512,512]{2,1,0:T(8,128)(2,1)} %w2_ref.1, bf16[512,128]{1,0:T(8,128)(2,1)} %w3_ref.1), custom_call_target="tpu_custom_call" | custom-call | tf_op jit(solution)/shard_map/pallas_call | solution.py:76
  17.5 11.5 %all-to-all-start = ((bf16[128,32,128]{2,1,0:T(8,128)(2,1)}), bf16[128,32,128]{2,1,0:T(8,128)(2,1)S(1)}, u32[]{:S(2)}, u32[]{:S(2)}) async-start(bf16[128,32,128]{2,1,0:T(8,128)(2,1)} %bitcast.77), calls=%async_computation | async-start | bytes 2097152 | tf_op jit(solution)/shard_map/all_to_all | solution.py:353
  29.0 0.0 copy-done.2
  29.1 0.1 copy.53
  29.3 0.1 copy.54
  29.4 0.1 eq.22
  29.4 2.7 %fusion.7 = (f32[4096,4]{1,0:T(8,128)S(1)}, bf16[4096,4]{1,0:T(8,128)(2,1)}) fusion(s32[4096]{0:T(1024)S(1)} %eq.22), kind=kLoop, calls=%fused_computation.15 | loop fusion | flops 49152 | bytes 114688 | tf_op jit(solution)/shard_map/convert_element_type | solution.py:365
  32.2 0.0 copy-done.3
  32.2 0.1 copy.56
  32.3 0.1 copy.52
  32.4 0.6 copy.57
  33.0 0.6 fusion.20.lane_mask_ref
  33.7 14.8 %all-to-all-done = bf16[128,32,128]{2,1,0:T(8,128)(2,1)S(1)} async-done(((bf16[128,32,128]{2,1,0:T(8,128)(2,1)}), bf16[128,32,128]{2,1,0:T(8,128)(2,1)S(1)}, u32[]{:S(2)}, u32[]{:S(2)}) %all-to-all-start) | async-done | bytes 1048608 | tf_op jit(solution)/shard_map/all_to_all | solution.py:353
  48.5 0.0 copy-start
  48.5 0.5 multiply_reduce_fusion
  49.0 0.5 copy-done
  49.4 14.2 %shard_map.101 = bf16[2,2,128,128]{3,2,1,0:T(8,128)(2,1)} custom-call(bf16[4096,128]{1,0:T(8,128)(2,1)} %bitcast.71, bf16[4096,4]{1,0:T(8,128)(2,1)} %get-tuple-element.16.column_mask_ref, f32[4,4096]{1,0:T(4,128)} %fusion.20.lane_mask_ref, bf16[128,128]{1,0:T(8,128)(2,1)} %inducing_ref.1, bf16[4,128,128]{2,1,0:T(8,128)(2,1)} %proj_ref.1, ...), custom_call_target="tpu_custom_call" | custom-call | tf_op jit(solution)/shard_map/pallas_call | solution.py:221
  63.7 1.1 %convolution_convert_fusion = bf16[512,128]{0,1:T(8,128)(2,1)S(1)} fusion(bf16[512,128]{1,0:T(8,128)(2,1)} %bitcast.78, bf16[4,128,128]{2,1,0:T(8,128)(2,1)S(1)} %copy-done.3), kind=kOutput, calls=%fused_computation.16 | convolution fusion | flops 16842752 | bytes 294912 | tf_op jit(solution)/shard_map/dot_general | solution.py:376
  64.8 1.1 %multiply_reduce_fusion.1 = (f32[512,2]{0,1:T(2,128)S(1)}, f32[512,2,64]{0,2,1:T(8,128)S(1)}) fusion(bf16[512,128,1]{1,0,2:T(8,128)(2,1)} %bitcast.79, bf16[2,64,128]{2,1,0:T(8,128)(2,1)S(1)} %bitcast.84), kind=kOutput, calls=%fused_computation.26 | convolution fusion | flops 16907264 | bytes 430080 | tf_op jit(solution)/shard_map/dot_general | solution.py:374
  66.0 0.2 divide_convert_fusion
  66.2 1.3 %fusion.12 = f32[4096,512]{0,1:T(8,128)S(1)} fusion(bf16[4096,128]{0,1:T(8,128)(2,1)S(1)} %bitcast.73, bf16[512,128]{0,1:T(8,128)(2,1)S(1)} %bitcast.80), kind=kOutput, calls=%fused_computation.21 | convolution fusion | flops 268435456 | bytes 8978432 | tf_op jit(solution)/shard_map/dot_general | solution.py:384
  67.5 3.6 %fusion = (f32[4096]{0:T(1024)S(1)}, f32[4096]{0:T(1024)S(1)}, bf16[4096,512]{0,1:T(8,128)(2,1)S(1)}, bf16[4096,512]{0,1:T(8,128)(2,1)S(1)}) fusion(f32[4096,4]{0,1:T(4,128)S(1)} %copy.57, f32[4096,512]{0,1:T(8,128)S(1)} %fusion.12, bf16[512,128]{0,1:T(8,128)(2,1)S(1)} %bitcast.81, bf16[4096,128]{0,1:T(8,128)(2,1)S(1)} %bitcast.74), kind=kOutput, calls=%fused_computation.2 | convolution fusion | flops 285204480 | bytes 17465344 | tf_op jit(solution)/shard_map/dot_general | solution.py:384
  71.1 0.8 fusion.5
  72.0 0.0 copy-start.1
  72.0 0.8 fusion.6
  72.8 0.4 copy-done.1
  73.2 0.5 fusion.4
  73.7 25.5 %all_to_all.10 = bf16[128,32,128]{2,1,0:T(8,128)(2,1)} all-to-all(bf16[128,32,128]{2,1,0:T(8,128)(2,1)S(1)} %bitcast.75), channel_id=1, replica_groups=mesh['tx'=32,'ty'=4] {'tx','ty'}, dimensions={0} | all-to-all | bytes 2097152 | tf_op jit(solution)/shard_map/all_to_all | solution.py:403
  99.1 7.1 %shard_map.102 = bf16[4096,128]{1,0:T(8,128)(2,1)} custom-call(s32[4096]{0:T(1024)} %fusion.26.pos_ref, s32[4096]{0:T(1024)} %bitcast.86, bf16[4096,128]{1,0:T(8,128)(2,1)} %bitcast.76), custom_call_target="tpu_custom_call" | custom-call | tf_op jit(solution)/shard_map/pallas_call | solution.py:115
  (11 shorter events, 0.2 us)
Async XLA Ops:
  0.0 29.0 %copy-start.2 = (s32[128,512]{1,0:T(8,128)S(1)}, s32[128,512]{1,0:T(8,128)}, u32[]{:S(2)}) copy-start(s32[128,512]{1,0:T(8,128)} %param.14) | copy-start | bytes 786436
  4.7 27.4 %copy-start.3 = (bf16[4,128,128]{2,1,0:T(8,128)(2,1)S(1)}, bf16[4,128,128]{2,1,0:T(8,128)(2,1)}, u32[]{:S(2)}) copy-start(bf16[4,128,128]{2,1,0:T(8,128)(2,1)} %param.18) | copy-start | bytes 393220
  17.5 30.9 %all-to-all-start = ((bf16[128,32,128]{2,1,0:T(8,128)(2,1)}), bf16[128,32,128]{2,1,0:T(8,128)(2,1)S(1)}, u32[]{:S(2)}, u32[]{:S(2)}) async-start(bf16[128,32,128]{2,1,0:T(8,128)(2,1)} %bitcast.77), calls=%async_computation | async-start | bytes 2097152 | tf_op jit(solution)/shard_map/all_to_all | solution.py:353
  48.5 1.0 copy-start
  72.0 1.2 %copy-start.1 = (bf16[128,32,128]{2,1,0:T(8,128)(2,1)S(1)}, bf16[128,32,128]{2,1,0:T(8,128)(2,1)}, u32[]{:S(2)}) copy-start(bf16[128,32,128]{2,1,0:T(8,128)(2,1)} %copy-done) | copy-start | bytes 3145732

commit v20 on v19

--- a/solution.py
+++ b/solution.py
@@ -329,7 +329,11 @@
     inducing_count = inducing.shape[0]
 
 
-    own_counts = lax.dynamic_index_in_dim(counts, own_index, 0, keepdims=False)
+    source_ids = jnp.arange(devices, dtype=jnp.int32)
+    own_row = (source_ids == own_index).astype(jnp.bfloat16)[None, :]
+    own_counts = jnp.dot(
+        own_row, counts.astype(jnp.bfloat16), preferred_element_type=jnp.float32
+    )[0].astype(jnp.int32)
     band_counts = own_counts.reshape(along_x, -1)
     band_offsets = jnp.cumsum(band_counts, axis=1) - band_counts
     grid_counts = own_counts.reshape(along_x, TLX, along_y, TLY)

time: 107 us -> 106 us (level)
  local copies, waits for them, and re-layouts: 5.64 us -> 3.75 us
  matrix products: 9.78 us -> 10.9 us
    dynamic_slice x2 -> x0, local copies, waits for them, and re-layouts: 1.9 us -> none  [body(): own_counts = lax.dynamic_index_in_dim(counts, own_index, 0, keepdims=False)]
    dot_general x0 -> x1, matrix products: none -> 1.15 us  [body(): jnp.dot(own_row, counts.astype(jnp.bfloat16), preferred_element_type=jnp....]
where the time goes in v20:
time: 106 us; the launch traced here: 105 us
  Pallas kernels  34.2 us (32%)
  blocking collectives  25.4 us (24%)
  waiting for transfers between devices  14.8 us (14%)
  starting transfers between devices  11.5 us (11%)
  matrix products  10.9 us (10%)
  other arithmetic  4.66 us (4%)
  local copies, waits for them, and re-layouts  3.75 us (4%)
    all_to_all x1, blocking collectives, body(): lax.all_to_all(result.reshape(devices, quota, width), ('tx', 'ty'), split...  25.4 us
    all_to_all x1, waiting for transfers between devices, body(): lax.all_to_all(outgoing, ('tx', 'ty'), split_axis=0, concat_axis=0, tiled...  14.8 us
    pallas_call x1, Pallas kernels, mix_tiles(): pl.pallas_call(functools.partial(mix_kernel, count_x, count_y), out_shape...  14.3 us
    pallas_call x1, Pallas kernels, encode_and_gather(): pl.pallas_call(functools.partial(encode_kernel, 64, block), out_shape=jax...  12.8 us
    all_to_all x1, starting transfers between devices, body(): lax.all_to_all(outgoing, ('tx', 'ty'), split_axis=0, concat_axis=0, tiled...  11.5 us
    pallas_call x1, Pallas kernels, move_rows(): pl.pallas_call(functools.partial(kernel, 64), out_shape=jax.ShapeDtypeStr...  7.09 us
    dot_general x2, matrix products, body(): jnp.dot(point_queries[:, lower:upper], second_keys[:, lower:upper].T, pre...  4.92 us
    convert_element_type x2, other arithmetic, body(): row_mask = (row_tile[:, None] == tile_ids[None, :]).astype(jnp.float32)  3.36 us
  transfers between devices with their start and end apart: 1, of which 1 were waited for; matrix products, arithmetic and copies ran while one was open for 4% of the time, Pallas kernels for 0%

profile of v20, /device:TPU:1, one launch (start us, length us, event | category | flops | bytes accessed | tf_op | source)
XLA Modules:
  0.0 105.5 jit_solution(9728922676372449437)
XLA Ops:
  0.0 0.0 copy-start.2
  0.0 1.1 %fusion.16 = f32[1,512]{1,0:T(1,128)S(1)} fusion(s32[128,512]{1,0:T(8,128)} %param.14, s32[]{:T(128)S(6)} %add.96), kind=kOutput, calls=%fused_computation.27 | convolution fusion | flops 196736 | bytes 264196 | tf_op jit(solution)/shard_map/dot_general | solution.py:334
  1.2 0.1 convert_element_type.59
  1.2 0.2 convert_element_type.58
  1.5 0.1 lt.48
  1.5 0.2 reduce_window_sum.24
  1.7 0.1 copy.46
  1.8 0.2 copy.47
  1.9 0.1 slice_add_fusion
  2.1 0.1 copy.44
  2.2 0.1 copy.50
  2.3 0.1 copy.48
  2.4 0.1 copy.49
  2.5 0.1 copy.51
  2.6 0.1 copy.45
  2.7 0.1 lt.51
  2.8 0.1 lt.52
  2.9 0.1 add.104
  3.0 0.1 add.105
  3.1 0.1 add.100
  3.2 0.1 add.101
  3.3 0.7 fusion.28.pos_ref
  4.0 0.0 copy-start.3
  4.0 12.8 %shard_map.100 = bf16[4096,128]{1,0:T(8,128)(2,1)} custom-call(s32[4096]{0:T(1024)} %fusion.28.pos_ref, s32[4096]{0:T(1024)} %bitcast.88, bf16[4096,128]{1,0:T(8,128)(2,1)} %x_ref.1, bf16[128,512]{1,0:T(8,128)(2,1)} %w1_ref.1, bf16[1,512,512]{2,1,0:T(8,128)(2,1)} %w2_ref.1, bf16[512,128]{1,0:T(8,128)(2,1)} %w3_ref.1), custom_call_target="tpu_custom_call" | custom-call | tf_op jit(solution)/shard_map/pallas_call | solution.py:76
  16.8 11.5 %all-to-all-start = ((bf16[128,32,128]{2,1,0:T(8,128)(2,1)}), bf16[128,32,128]{2,1,0:T(8,128)(2,1)S(1)}, u32[]{:S(2)}, u32[]{:S(2)}) async-start(bf16[128,32,128]{2,1,0:T(8,128)(2,1)} %bitcast.80), calls=%async_computation | async-start | bytes 2097152 | tf_op jit(solution)/shard_map/all_to_all | solution.py:357
  28.3 0.0 copy-done.2
  28.3 0.1 copy.53
  28.5 0.1 copy.54
  28.6 0.1 eq.32
  28.7 2.7 %fusion.7 = (f32[4096,4]{1,0:T(8,128)S(1)}, bf16[4096,4]{1,0:T(8,128)(2,1)}) fusion(s32[4096]{0:T(1024)S(1)} %eq.32), kind=kLoop, calls=%fused_computation.15 | loop fusion | flops 49152 | bytes 114688 | tf_op jit(solution)/shard_map/convert_element_type | solution.py:369
  31.4 0.0 copy-done.3
  31.4 0.1 copy.56
  31.5 0.1 copy.52
  31.7 0.6 copy.57
  32.3 0.6 fusion.22.lane_mask_ref
  32.9 14.8 %all-to-all-done = bf16[128,32,128]{2,1,0:T(8,128)(2,1)S(1)} async-done(((bf16[128,32,128]{2,1,0:T(8,128)(2,1)}), bf16[128,32,128]{2,1,0:T(8,128)(2,1)S(1)}, u32[]{:S(2)}, u32[]{:S(2)}) %all-to-all-start) | async-done | bytes 1048608 | tf_op jit(solution)/shard_map/all_to_all | solution.py:357
  47.7 0.0 copy-start
  47.7 0.5 multiply_reduce_fusion
  48.2 0.5 copy-done
  48.7 14.3 %shard_map.101 = bf16[2,2,128,128]{3,2,1,0:T(8,128)(2,1)} custom-call(bf16[4096,128]{1,0:T(8,128)(2,1)} %bitcast.74, bf16[4096,4]{1,0:T(8,128)(2,1)} %get-tuple-element.14.column_mask_ref, f32[4,4096]{1,0:T(4,128)} %fusion.22.lane_mask_ref, bf16[128,128]{1,0:T(8,128)(2,1)} %inducing_ref.1, bf16[4,128,128]{2,1,0:T(8,128)(2,1)} %proj_ref.1, ...), custom_call_target="tpu_custom_call" | custom-call | tf_op jit(solution)/shard_map/pallas_call | solution.py:221
  63.0 1.1 %convolution_convert_fusion = bf16[512,128]{0,1:T(8,128)(2,1)S(1)} fusion(bf16[512,128]{1,0:T(8,128)(2,1)} %bitcast.81, bf16[4,128,128]{2,1,0:T(8,128)(2,1)S(1)} %copy-done.3), kind=kOutput, calls=%fused_computation.16 | convolution fusion | flops 16842752 | bytes 294912 | tf_op jit(solution)/shard_map/dot_general | solution.py:380
  64.1 1.1 %multiply_reduce_fusion.1 = (f32[512,2]{0,1:T(2,128)S(1)}, f32[512,2,64]{0,2,1:T(8,128)S(1)}) fusion(bf16[512,128,1]{1,0,2:T(8,128)(2,1)} %bitcast.82, bf16[2,64,128]{2,1,0:T(8,128)(2,1)S(1)} %bitcast.87), kind=kOutput, calls=%fused_computation.26 | convolution fusion | flops 16907264 | bytes 430080 | tf_op jit(solution)/shard_map/dot_general | solution.py:378
  65.2 0.2 divide_convert_fusion
  65.4 1.3 %fusion.12 = f32[4096,512]{0,1:T(8,128)S(1)} fusion(bf16[4096,128]{0,1:T(8,128)(2,1)S(1)} %bitcast.76, bf16[512,128]{0,1:T(8,128)(2,1)S(1)} %bitcast.83), kind=kOutput, calls=%fused_computation.21 | convolution fusion | flops 268435456 | bytes 8978432 | tf_op jit(solution)/shard_map/dot_general | solution.py:388
  66.7 3.6 %fusion = (f32[4096]{0:T(1024)S(1)}, f32[4096]{0:T(1024)S(1)}, bf16[4096,512]{0,1:T(8,128)(2,1)S(1)}, bf16[4096,512]{0,1:T(8,128)(2,1)S(1)}) fusion(f32[4096,4]{0,1:T(4,128)S(1)} %copy.57, f32[4096,512]{0,1:T(8,128)S(1)} %fusion.12, bf16[512,128]{0,1:T(8,128)(2,1)S(1)} %bitcast.84, bf16[4096,128]{0,1:T(8,128)(2,1)S(1)} %bitcast.77), kind=kOutput, calls=%fused_computation.2 | convolution fusion | flops 285204480 | bytes 17465344 | tf_op jit(solution)/shard_map/dot_general | solution.py:388
  70.4 0.8 fusion.5
  71.2 0.0 copy-start.1
  71.2 0.8 fusion.6
  72.1 0.4 copy-done.1
  72.5 0.5 fusion.4
  72.9 25.4 %all_to_all.10 = bf16[128,32,128]{2,1,0:T(8,128)(2,1)} all-to-all(bf16[128,32,128]{2,1,0:T(8,128)(2,1)S(1)} %bitcast.78), channel_id=1, replica_groups=mesh['tx'=32,'ty'=4] {'tx','ty'}, dimensions={0} | all-to-all | bytes 2097152 | tf_op jit(solution)/shard_map/all_to_all | solution.py:407
  98.4 7.1 %shard_map.102 = bf16[4096,128]{1,0:T(8,128)(2,1)} custom-call(s32[4096]{0:T(1024)} %fusion.28.pos_ref, s32[4096]{0:T(1024)} %bitcast.89, bf16[4096,128]{1,0:T(8,128)(2,1)} %bitcast.79), custom_call_target="tpu_custom_call" | custom-call | tf_op jit(solution)/shard_map/pallas_call | solution.py:115
  (12 shorter events, 0.2 us)
Async XLA Ops:
  0.0 28.3 %copy-start.2 = (s32[128,512]{1,0:T(8,128)S(1)}, s32[128,512]{1,0:T(8,128)}, u32[]{:S(2)}) copy-start(s32[128,512]{1,0:T(8,128)} %param.14) | copy-start | bytes 786436
  4.0 27.4 %copy-start.3 = (bf16[4,128,128]{2,1,0:T(8,128)(2,1)S(1)}, bf16[4,128,128]{2,1,0:T(8,128)(2,1)}, u32[]{:S(2)}) copy-start(bf16[4,128,128]{2,1,0:T(8,128)(2,1)} %param.18) | copy-start | bytes 393220
  16.8 30.9 %all-to-all-start = ((bf16[128,32,128]{2,1,0:T(8,128)(2,1)}), bf16[128,32,128]{2,1,0:T(8,128)(2,1)S(1)}, u32[]{:S(2)}, u32[]{:S(2)}) async-start(bf16[128,32,128]{2,1,0:T(8,128)(2,1)} %bitcast.80), calls=%async_computation | async-start | bytes 2097152 | tf_op jit(solution)/shard_map/all_to_all | solution.py:357
  47.7 1.0 copy-start
  71.2 1.2 %copy-start.1 = (bf16[128,32,128]{2,1,0:T(8,128)(2,1)S(1)}, bf16[128,32,128]{2,1,0:T(8,128)(2,1)}, u32[]{:S(2)}) copy-start(bf16[128,32,128]{2,1,0:T(8,128)(2,1)} %copy-done) | copy-start | bytes 3145732

commit v21 on v20

--- a/solution.py
+++ b/solution.py
@@ -48,7 +48,7 @@
 
 def encode_kernel(unroll, block, pos_ref, order_ref, x_ref, w1_ref, w2_ref, w3_ref, o_ref, rows_in, rows_out):
     def silu(v):
-        return v / (1.0 + jnp.exp(-v))
+        return v * (0.5 + 0.5 * jnp.tanh(0.5 * v))
 
     for start in range(0, x_ref.shape[0], block):
         part = pl.ds(start, block)

time: 106 us -> 105 us (level)
  no operation moved by 1% of the time
where the time goes in v21:
time: 105 us
  Pallas kernels  33.6 us (32%)
  blocking collectives  25.5 us (24%)
  waiting for transfers between devices  14.8 us (14%)
  starting transfers between devices  11.5 us (11%)
  matrix products  10.9 us (10%)
  other arithmetic  4.66 us (4%)
  local copies, waits for them, and re-layouts  3.75 us (4%)
    all_to_all x1, blocking collectives, body(): lax.all_to_all(result.reshape(devices, quota, width), ('tx', 'ty'), split...  25.5 us
    all_to_all x1, waiting for transfers between devices, body(): lax.all_to_all(outgoing, ('tx', 'ty'), split_axis=0, concat_axis=0, tiled...  14.8 us
    pallas_call x1, Pallas kernels, mix_tiles(): pl.pallas_call(functools.partial(mix_kernel, count_x, count_y), out_shape...  14.2 us
    pallas_call x1, Pallas kernels, encode_and_gather(): pl.pallas_call(functools.partial(encode_kernel, 64, block), out_shape=jax...  12.3 us
    all_to_all x1, starting transfers between devices, body(): lax.all_to_all(outgoing, ('tx', 'ty'), split_axis=0, concat_axis=0, tiled...  11.5 us
    pallas_call x1, Pallas kernels, move_rows(): pl.pallas_call(functools.partial(kernel, 64), out_shape=jax.ShapeDtypeStr...  7.09 us
    dot_general x2, matrix products, body(): jnp.dot(point_queries[:, lower:upper], second_keys[:, lower:upper].T, pre...  4.92 us
    convert_element_type x2, other arithmetic, body(): row_mask = (row_tile[:, None] == tile_ids[None, :]).astype(jnp.float32)  3.36 us
  transfers between devices with their start and end apart: 1, of which 1 were waited for; matrix products, arithmetic and copies ran while one was open for 4% of the time, Pallas kernels for 0%

profile of v21, /device:TPU:1, one launch (start us, length us, event | category | flops | bytes accessed | tf_op | source)
XLA Modules:
  0.0 104.9 jit_solution(7712748395821193443)
XLA Ops:
  0.0 0.0 copy-start.2
  0.0 1.1 %fusion.16 = f32[1,512]{1,0:T(1,128)S(1)} fusion(s32[128,512]{1,0:T(8,128)} %param.14, s32[]{:T(128)S(6)} %add.96), kind=kOutput, calls=%fused_computation.27 | convolution fusion | flops 196736 | bytes 264196 | tf_op jit(solution)/shard_map/dot_general | solution.py:334
  1.2 0.1 convert_element_type.59
  1.2 0.2 convert_element_type.58
  1.5 0.1 lt.48
  1.5 0.2 reduce_window_sum.24
  1.7 0.1 copy.46
  1.8 0.2 copy.47
  1.9 0.1 slice_add_fusion
  2.1 0.1 copy.44
  2.2 0.1 copy.50
  2.3 0.1 copy.48
  2.4 0.1 copy.49
  2.5 0.1 copy.51
  2.6 0.1 copy.45
  2.7 0.1 lt.51
  2.8 0.1 lt.52
  2.9 0.1 add.104
  3.0 0.1 add.105
  3.1 0.1 add.100
  3.2 0.1 add.101
  3.3 0.7 fusion.28.pos_ref
  4.0 0.0 copy-start.3
  4.0 12.3 %shard_map.100 = bf16[4096,128]{1,0:T(8,128)(2,1)} custom-call(s32[4096]{0:T(1024)} %fusion.28.pos_ref, s32[4096]{0:T(1024)} %bitcast.88, bf16[4096,128]{1,0:T(8,128)(2,1)} %x_ref.1, bf16[128,512]{1,0:T(8,128)(2,1)} %w1_ref.1, bf16[1,512,512]{2,1,0:T(8,128)(2,1)} %w2_ref.1, bf16[512,128]{1,0:T(8,128)(2,1)} %w3_ref.1), custom_call_target="tpu_custom_call" | custom-call | tf_op jit(solution)/shard_map/pallas_call | solution.py:76
  16.2 11.5 %all-to-all-start = ((bf16[128,32,128]{2,1,0:T(8,128)(2,1)}), bf16[128,32,128]{2,1,0:T(8,128)(2,1)S(1)}, u32[]{:S(2)}, u32[]{:S(2)}) async-start(bf16[128,32,128]{2,1,0:T(8,128)(2,1)} %bitcast.80), calls=%async_computation | async-start | bytes 2097152 | tf_op jit(solution)/shard_map/all_to_all | solution.py:357
  27.7 0.0 copy-done.2
  27.8 0.1 copy.53
  28.0 0.1 copy.54
  28.1 0.1 eq.32
  28.1 2.7 %fusion.7 = (f32[4096,4]{1,0:T(8,128)S(1)}, bf16[4096,4]{1,0:T(8,128)(2,1)}) fusion(s32[4096]{0:T(1024)S(1)} %eq.32), kind=kLoop, calls=%fused_computation.15 | loop fusion | flops 49152 | bytes 114688 | tf_op jit(solution)/shard_map/convert_element_type | solution.py:369
  30.9 0.0 copy-done.3
  30.9 0.1 copy.56
  31.0 0.1 copy.52
  31.1 0.6 copy.57
  31.7 0.6 fusion.22.lane_mask_ref
  32.4 14.8 %all-to-all-done = bf16[128,32,128]{2,1,0:T(8,128)(2,1)S(1)} async-done(((bf16[128,32,128]{2,1,0:T(8,128)(2,1)}), bf16[128,32,128]{2,1,0:T(8,128)(2,1)S(1)}, u32[]{:S(2)}, u32[]{:S(2)}) %all-to-all-start) | async-done | bytes 1048608 | tf_op jit(solution)/shard_map/all_to_all | solution.py:357
  47.2 0.0 copy-start
  47.2 0.5 multiply_reduce_fusion
  47.7 0.5 copy-done
  48.1 14.2 %shard_map.101 = bf16[2,2,128,128]{3,2,1,0:T(8,128)(2,1)} custom-call(bf16[4096,128]{1,0:T(8,128)(2,1)} %bitcast.74, bf16[4096,4]{1,0:T(8,128)(2,1)} %get-tuple-element.14.column_mask_ref, f32[4,4096]{1,0:T(4,128)} %fusion.22.lane_mask_ref, bf16[128,128]{1,0:T(8,128)(2,1)} %inducing_ref.1, bf16[4,128,128]{2,1,0:T(8,128)(2,1)} %proj_ref.1, ...), custom_call_target="tpu_custom_call" | custom-call | tf_op jit(solution)/shard_map/pallas_call | solution.py:221
  62.4 1.1 %convolution_convert_fusion = bf16[512,128]{0,1:T(8,128)(2,1)S(1)} fusion(bf16[512,128]{1,0:T(8,128)(2,1)} %bitcast.81, bf16[4,128,128]{2,1,0:T(8,128)(2,1)S(1)} %copy-done.3), kind=kOutput, calls=%fused_computation.16 | convolution fusion | flops 16842752 | bytes 294912 | tf_op jit(solution)/shard_map/dot_general | solution.py:380
  63.5 1.1 %multiply_reduce_fusion.1 = (f32[512,2]{0,1:T(2,128)S(1)}, f32[512,2,64]{0,2,1:T(8,128)S(1)}) fusion(bf16[512,128,1]{1,0,2:T(8,128)(2,1)} %bitcast.82, bf16[2,64,128]{2,1,0:T(8,128)(2,1)S(1)} %bitcast.87), kind=kOutput, calls=%fused_computation.26 | convolution fusion | flops 16907264 | bytes 430080 | tf_op jit(solution)/shard_map/dot_general | solution.py:378
  64.7 0.2 divide_convert_fusion
  64.9 1.3 %fusion.12 = f32[4096,512]{0,1:T(8,128)S(1)} fusion(bf16[4096,128]{0,1:T(8,128)(2,1)S(1)} %bitcast.76, bf16[512,128]{0,1:T(8,128)(2,1)S(1)} %bitcast.83), kind=kOutput, calls=%fused_computation.21 | convolution fusion | flops 268435456 | bytes 8978432 | tf_op jit(solution)/shard_map/dot_general | solution.py:388
  66.2 3.6 %fusion = (f32[4096]{0:T(1024)S(1)}, f32[4096]{0:T(1024)S(1)}, bf16[4096,512]{0,1:T(8,128)(2,1)S(1)}, bf16[4096,512]{0,1:T(8,128)(2,1)S(1)}) fusion(f32[4096,4]{0,1:T(4,128)S(1)} %copy.57, f32[4096,512]{0,1:T(8,128)S(1)} %fusion.12, bf16[512,128]{0,1:T(8,128)(2,1)S(1)} %bitcast.84, bf16[4096,128]{0,1:T(8,128)(2,1)S(1)} %bitcast.77), kind=kOutput, calls=%fused_computation.2 | convolution fusion | flops 285204480 | bytes 17465344 | tf_op jit(solution)/shard_map/dot_general | solution.py:388
  69.8 0.8 fusion.5
  70.7 0.0 copy-start.1
  70.7 0.8 fusion.6
  71.5 0.4 copy-done.1
  71.9 0.5 fusion.4
  72.4 25.5 %all_to_all.10 = bf16[128,32,128]{2,1,0:T(8,128)(2,1)} all-to-all(bf16[128,32,128]{2,1,0:T(8,128)(2,1)S(1)} %bitcast.78), channel_id=1, replica_groups=mesh['tx'=32,'ty'=4] {'tx','ty'}, dimensions={0} | all-to-all | bytes 2097152 | tf_op jit(solution)/shard_map/all_to_all | solution.py:407
  97.8 7.1 %shard_map.102 = bf16[4096,128]{1,0:T(8,128)(2,1)} custom-call(s32[4096]{0:T(1024)} %fusion.28.pos_ref, s32[4096]{0:T(1024)} %bitcast.89, bf16[4096,128]{1,0:T(8,128)(2,1)} %bitcast.79), custom_call_target="tpu_custom_call" | custom-call | tf_op jit(solution)/shard_map/pallas_call | solution.py:115
  (12 shorter events, 0.2 us)
Async XLA Ops:
  0.0 27.7 %copy-start.2 = (s32[128,512]{1,0:T(8,128)S(1)}, s32[128,512]{1,0:T(8,128)}, u32[]{:S(2)}) copy-start(s32[128,512]{1,0:T(8,128)} %param.14) | copy-start | bytes 786436
  4.0 26.9 %copy-start.3 = (bf16[4,128,128]{2,1,0:T(8,128)(2,1)S(1)}, bf16[4,128,128]{2,1,0:T(8,128)(2,1)}, u32[]{:S(2)}) copy-start(bf16[4,128,128]{2,1,0:T(8,128)(2,1)} %param.18) | copy-start | bytes 393220
  16.2 30.9 %all-to-all-start = ((bf16[128,32,128]{2,1,0:T(8,128)(2,1)}), bf16[128,32,128]{2,1,0:T(8,128)(2,1)S(1)}, u32[]{:S(2)}, u32[]{:S(2)}) async-start(bf16[128,32,128]{2,1,0:T(8,128)(2,1)} %bitcast.80), calls=%async_computation | async-start | bytes 2097152 | tf_op jit(solution)/shard_map/all_to_all | solution.py:357
  47.2 1.0 copy-start
  70.7 1.2 %copy-start.1 = (bf16[128,32,128]{2,1,0:T(8,128)(2,1)S(1)}, bf16[128,32,128]{2,1,0:T(8,128)(2,1)}, u32[]{:S(2)}) copy-start(bf16[128,32,128]{2,1,0:T(8,128)(2,1)} %copy-done) | copy-start | bytes 3145732

commit v22 on v20

--- a/solution.py
+++ b/solution.py
@@ -46,7 +46,9 @@
     )(x, w1, w2, w3)
 
 
-def encode_kernel(unroll, block, pos_ref, order_ref, x_ref, w1_ref, w2_ref, w3_ref, o_ref, rows_in, rows_out):
+def encode_kernel(
+    unroll, block, pos_ref, order_ref, x_ref, w1_ref, w2_ref, w3_ref, o_ref, index_ref, rows_in, rows_out
+):
     def silu(v):
         return v / (1.0 + jnp.exp(-v))
 
@@ -64,6 +66,7 @@
         for lane in range(unroll):
             row = step * unroll + lane
             source = order_ref[pos_ref[row]]
+            index_ref[row] = source
             rows_out[pl.ds(row, 1), :] = rows_in[pl.ds(source, 1), :]
         return carry
 
@@ -75,10 +78,13 @@
     shape = (x.shape[0], w3.shape[1])
     return pl.pallas_call(
         functools.partial(encode_kernel, 64, block),
-        out_shape=jax.ShapeDtypeStruct(shape, jnp.bfloat16),
+        out_shape=(
+            jax.ShapeDtypeStruct(shape, jnp.bfloat16),
+            jax.ShapeDtypeStruct(pos.shape, jnp.int32),
+        ),
         in_specs=[pl.BlockSpec(memory_space=pltpu.SMEM)] * 2
         + [pl.BlockSpec(memory_space=pltpu.VMEM)] * 4,
-        out_specs=pl.BlockSpec(memory_space=pltpu.VMEM),
+        out_specs=[pl.BlockSpec(memory_space=pltpu.VMEM), pl.BlockSpec(memory_space=pltpu.SMEM)],
         scratch_shapes=[pltpu.VMEM(shape, jnp.float32), pltpu.VMEM(shape, jnp.float32)],
     )(pos, order, x, w1, w2, w3)
 
@@ -97,18 +103,28 @@
     o_ref[...] = rows_out[...].astype(o_ref.dtype)
 
 
-def scatter_kernel(unroll, pos_ref, order_ref, x_ref, o_ref, rows_in, rows_out):
+def scatter_kernel(unroll, index_ref, x_ref, o_ref, rows_in, rows_out):
     rows_in[...] = x_ref[...].astype(jnp.float32)
 
     def body(step, carry):
         for lane in range(unroll):
             row = step * unroll + lane
-            target = order_ref[pos_ref[row]]
+            target = index_ref[row]
             rows_out[pl.ds(target, 1), :] = rows_in[pl.ds(row, 1), :]
         return carry
 
     lax.fori_loop(0, x_ref.shape[0] // unroll, body, 0)
     o_ref[...] = rows_out[...].astype(o_ref.dtype)
+
+
+def place_rows(index, x):
+    return pl.pallas_call(
+        functools.partial(scatter_kernel, 64),
+        out_shape=jax.ShapeDtypeStruct(x.shape, jnp.bfloat16),
+        in_specs=[pl.BlockSpec(memory_space=pltpu.SMEM), pl.BlockSpec(memory_space=pltpu.VMEM)],
+        out_specs=pl.BlockSpec(memory_space=pltpu.VMEM),
+        scratch_shapes=[pltpu.VMEM(x.shape, jnp.float32), pltpu.VMEM(x.shape, jnp.float32)],
+    )(index, x)
 
 
 def move_rows(kernel, pos, order, x):
@@ -350,7 +366,7 @@
     ).reshape(along_x, band)
     send_pos = (local_pos + band_start).reshape(-1)
     order = point_order[0]
-    outgoing = encode_and_gather(
+    outgoing, send_index = encode_and_gather(
         send_pos, order, points, embed_weight, inner_weights, output_weight, 2048
     )
     outgoing = outgoing.reshape(devices, quota, width)
@@ -407,9 +423,7 @@
     coming = lax.all_to_all(
         result.reshape(devices, quota, width), ("tx", "ty"), split_axis=0, concat_axis=0, tiled=True
     )
-    returned = move_rows(
-        scatter_kernel, send_pos, order, coming.reshape(point_count, width)
-    )
+    returned = place_rows(send_index, coming.reshape(point_count, width))
     return returned
 
 

time: 106 us -> 107 us (level)
  no operation moved by 1% of the time
where the time goes in v22:
time: 107 us; the launch traced here: 106 us
  Pallas kernels  35.1 us (33%)
  blocking collectives  25.5 us (24%)
  waiting for transfers between devices  14.8 us (14%)
  starting transfers between devices  11.5 us (11%)
  matrix products  10.9 us (10%)
  other arithmetic  4.65 us (4%)
  local copies, waits for them, and re-layouts  3.76 us (4%)
    all_to_all x1, blocking collectives, body(): lax.all_to_all(result.reshape(devices, quota, width), ('tx', 'ty'), split...  25.5 us
    pallas_call x1, Pallas kernels, encode_and_gather(): pl.pallas_call(functools.partial(encode_kernel, 64, block), out_shape=(ja...  14.9 us
    all_to_all x1, waiting for transfers between devices, body(): lax.all_to_all(outgoing, ('tx', 'ty'), split_axis=0, concat_axis=0, tiled...  14.8 us
    pallas_call x1, Pallas kernels, mix_tiles(): pl.pallas_call(functools.partial(mix_kernel, count_x, count_y), out_shape...  14.3 us
    all_to_all x1, starting transfers between devices, body(): lax.all_to_all(outgoing, ('tx', 'ty'), split_axis=0, concat_axis=0, tiled...  11.5 us
    pallas_call x1, Pallas kernels, place_rows(): pl.pallas_call(functools.partial(scatter_kernel, 64), out_shape=jax.Shape...  5.98 us
    dot_general x2, matrix products, body(): jnp.dot(point_queries[:, lower:upper], second_keys[:, lower:upper].T, pre...  4.92 us
    convert_element_type x2, other arithmetic, body(): row_mask = (row_tile[:, None] == tile_ids[None, :]).astype(jnp.float32)  3.36 us
  transfers between devices with their start and end apart: 1, of which 1 were waited for; matrix products, arithmetic and copies ran while one was open for 4% of the time, Pallas kernels for 0%

profile of v22, /device:TPU:1, one launch (start us, length us, event | category | flops | bytes accessed | tf_op | source)
XLA Modules:
  0.0 106.5 jit_solution(15483455528258149065)
XLA Ops:
  0.0 0.0 copy-start.2
  0.0 1.1 %fusion.16 = f32[1,512]{1,0:T(1,128)S(1)} fusion(s32[128,512]{1,0:T(8,128)} %param.14, s32[]{:T(128)S(6)} %add.96), kind=kOutput, calls=%fused_computation.27 | convolution fusion | flops 196736 | bytes 264196 | tf_op jit(solution)/shard_map/dot_general | solution.py:350
  1.2 0.1 convert_element_type.59
  1.2 0.2 convert_element_type.58
  1.5 0.1 lt.48
  1.5 0.2 reduce_window_sum.24
  1.7 0.1 copy.46
  1.8 0.2 copy.47
  1.9 0.1 slice_add_fusion
  2.1 0.1 copy.44
  2.2 0.1 copy.50
  2.3 0.1 copy.48
  2.4 0.1 copy.49
  2.5 0.1 copy.51
  2.6 0.1 copy.45
  2.7 0.0 copy-start.3
  2.7 0.1 lt.51
  2.8 0.1 lt.52
  2.9 0.1 add.104
  3.0 0.1 add.105
  3.1 0.1 add.100
  3.2 0.1 add.101
  3.3 0.7 fusion.28.pos_ref
  4.0 14.9 %shard_map.100 = (bf16[4096,128]{1,0:T(8,128)(2,1)}, s32[4096]{0:T(1024)}) custom-call(s32[4096]{0:T(1024)} %fusion.28.pos_ref, s32[4096]{0:T(1024)} %bitcast.89, bf16[4096,128]{1,0:T(8,128)(2,1)} %x_ref.1, bf16[128,512]{1,0:T(8,128)(2,1)} %w1_ref.1, bf16[1,512,512]{2,1,0:T(8,128)(2,1)} %w2_ref.1, bf16[512,128]{1,0:T(8,128)(2,1)} %w3_ref.1), custom_call_target="tpu_custom_call" | custom-call | tf_op jit(solution)/shard_map/pallas_call | solution.py:79
  18.9 11.5 %all-to-all-start = ((bf16[128,32,128]{2,1,0:T(8,128)(2,1)}), bf16[128,32,128]{2,1,0:T(8,128)(2,1)S(1)}, u32[]{:S(2)}, u32[]{:S(2)}) async-start(bf16[128,32,128]{2,1,0:T(8,128)(2,1)} %bitcast.82), calls=%async_computation | async-start | bytes 2097152 | tf_op jit(solution)/shard_map/all_to_all | solution.py:373
  30.4 0.0 copy-done.2
  30.4 0.1 copy.53
  30.6 0.1 copy.54
  30.7 0.1 eq.32
  30.8 2.7 %fusion.7 = (f32[4096,4]{1,0:T(8,128)S(1)}, bf16[4096,4]{1,0:T(8,128)(2,1)}) fusion(s32[4096]{0:T(1024)S(1)} %eq.32), kind=kLoop, calls=%fused_computation.15 | loop fusion | flops 49152 | bytes 114688 | tf_op jit(solution)/shard_map/convert_element_type | solution.py:385
  33.5 0.0 copy-done.3
  33.5 0.1 copy.56
  33.6 0.1 copy.52
  33.7 0.6 copy.57
  34.4 0.6 fusion.22.lane_mask_ref
  35.0 14.8 %all-to-all-done = bf16[128,32,128]{2,1,0:T(8,128)(2,1)S(1)} async-done(((bf16[128,32,128]{2,1,0:T(8,128)(2,1)}), bf16[128,32,128]{2,1,0:T(8,128)(2,1)S(1)}, u32[]{:S(2)}, u32[]{:S(2)}) %all-to-all-start) | async-done | bytes 1048608 | tf_op jit(solution)/shard_map/all_to_all | solution.py:373
  49.8 0.0 copy-start
  49.8 0.5 multiply_reduce_fusion
  50.3 0.5 copy-done
  50.8 14.3 %shard_map.101 = bf16[2,2,128,128]{3,2,1,0:T(8,128)(2,1)} custom-call(bf16[4096,128]{1,0:T(8,128)(2,1)} %bitcast.74, bf16[4096,4]{1,0:T(8,128)(2,1)} %get-tuple-element.18.column_mask_ref, f32[4,4096]{1,0:T(4,128)} %fusion.22.lane_mask_ref, bf16[128,128]{1,0:T(8,128)(2,1)} %inducing_ref.1, bf16[4,128,128]{2,1,0:T(8,128)(2,1)} %proj_ref.1, ...), custom_call_target="tpu_custom_call" | custom-call | tf_op jit(solution)/shard_map/pallas_call | solution.py:237
  65.0 1.1 %convolution_convert_fusion = bf16[512,128]{0,1:T(8,128)(2,1)S(1)} fusion(bf16[512,128]{1,0:T(8,128)(2,1)} %bitcast.80, bf16[4,128,128]{2,1,0:T(8,128)(2,1)S(1)} %copy-done.3), kind=kOutput, calls=%fused_computation.16 | convolution fusion | flops 16842752 | bytes 294912 | tf_op jit(solution)/shard_map/dot_general | solution.py:396
  66.2 1.1 %multiply_reduce_fusion.1 = (f32[512,2]{0,1:T(2,128)S(1)}, f32[512,2,64]{0,2,1:T(8,128)S(1)}) fusion(bf16[512,128,1]{1,0,2:T(8,128)(2,1)} %bitcast.81, bf16[2,64,128]{2,1,0:T(8,128)(2,1)S(1)} %bitcast.87), kind=kOutput, calls=%fused_computation.26 | convolution fusion | flops 16907264 | bytes 430080 | tf_op jit(solution)/shard_map/dot_general | solution.py:394
  67.3 0.2 divide_convert_fusion
  67.5 1.3 %fusion.12 = f32[4096,512]{0,1:T(8,128)S(1)} fusion(bf16[4096,128]{0,1:T(8,128)(2,1)S(1)} %bitcast.76, bf16[512,128]{0,1:T(8,128)(2,1)S(1)} %bitcast.83), kind=kOutput, calls=%fused_computation.21 | convolution fusion | flops 268435456 | bytes 8978432 | tf_op jit(solution)/shard_map/dot_general | solution.py:404
  68.8 3.6 %fusion = (f32[4096]{0:T(1024)S(1)}, f32[4096]{0:T(1024)S(1)}, bf16[4096,512]{0,1:T(8,128)(2,1)S(1)}, bf16[4096,512]{0,1:T(8,128)(2,1)S(1)}) fusion(f32[4096,4]{0,1:T(4,128)S(1)} %copy.57, f32[4096,512]{0,1:T(8,128)S(1)} %fusion.12, bf16[512,128]{0,1:T(8,128)(2,1)S(1)} %bitcast.84, bf16[4096,128]{0,1:T(8,128)(2,1)S(1)} %bitcast.77), kind=kOutput, calls=%fused_computation.2 | convolution fusion | flops 285204480 | bytes 17465344 | tf_op jit(solution)/shard_map/dot_general | solution.py:404
  72.4 0.8 fusion.5
  73.3 0.0 copy-start.1
  73.3 0.8 fusion.6
  74.2 0.4 copy-done.1
  74.5 0.5 fusion.4
  75.0 25.5 %all_to_all.10 = bf16[128,32,128]{2,1,0:T(8,128)(2,1)} all-to-all(bf16[128,32,128]{2,1,0:T(8,128)(2,1)S(1)} %bitcast.78), channel_id=1, replica_groups=mesh['tx'=32,'ty'=4] {'tx','ty'}, dimensions={0} | all-to-all | bytes 2097152 | tf_op jit(solution)/shard_map/all_to_all | solution.py:423
  100.5 6.0 %shard_map.102 = bf16[4096,128]{1,0:T(8,128)(2,1)} custom-call(s32[4096]{0:T(1024)} %get-tuple-element.7.index_ref, bf16[4096,128]{1,0:T(8,128)(2,1)} %bitcast.79), custom_call_target="tpu_custom_call" | custom-call | tf_op jit(solution)/shard_map/pallas_call | solution.py:121
  (12 shorter events, 0.2 us)
Async XLA Ops:
  0.0 30.4 %copy-start.2 = (s32[128,512]{1,0:T(8,128)S(1)}, s32[128,512]{1,0:T(8,128)}, u32[]{:S(2)}) copy-start(s32[128,512]{1,0:T(8,128)} %param.14) | copy-start | bytes 786436
  2.7 30.8 %copy-start.3 = (bf16[4,128,128]{2,1,0:T(8,128)(2,1)S(1)}, bf16[4,128,128]{2,1,0:T(8,128)(2,1)}, u32[]{:S(2)}) copy-start(bf16[4,128,128]{2,1,0:T(8,128)(2,1)} %param.18) | copy-start | bytes 393220
  18.9 30.9 %all-to-all-start = ((bf16[128,32,128]{2,1,0:T(8,128)(2,1)}), bf16[128,32,128]{2,1,0:T(8,128)(2,1)S(1)}, u32[]{:S(2)}, u32[]{:S(2)}) async-start(bf16[128,32,128]{2,1,0:T(8,128)(2,1)} %bitcast.82), calls=%async_computation | async-start | bytes 2097152 | tf_op jit(solution)/shard_map/all_to_all | solution.py:373
  49.8 1.0 copy-start
  73.3 1.2 %copy-start.1 = (bf16[128,32,128]{2,1,0:T(8,128)(2,1)S(1)}, bf16[128,32,128]{2,1,0:T(8,128)(2,1)}, u32[]{:S(2)}) copy-start(bf16[128,32,128]{2,1,0:T(8,128)(2,1)} %copy-done) | copy-start | bytes 3145732
